TPU v7x, 128 devices: a whole 4x4x4 slice. The times are simulated.
128 devices in a mesh: row: 8 (over x, core), col: 16 (over y, z).
Axes of the slice: x: 4, y: 4, z: 4, core: 2. Of those that a mesh axis runs over, the one named last changes fastest.
Arguments:
- trail: bfloat16 [16384, 16384], P('row', 'col'), may hold values from -0.046875 to 0.046875
- row_one: bfloat16 [128, 16384], P('row', 'col'), may hold values from -0.5 to 0.5
- row_two: bfloat16 [128, 16384], P('row', 'col'), may hold values from -0.5 to 0.5
- diag_one: float32 [128, 128], replicated, may hold values from -1 to 2, as said below
- diag_two: float32 [128, 128], replicated, may hold values from -1 to 2, as said below
- adj_trail: float32 [16384, 16384], P('row', 'col'), may hold values from -6 to 6
- adj_row_one: float32 [128, 16384], P('row', 'col'), may hold values from -6 to 6
- adj_row_two: float32 [128, 16384], P('row', 'col'), may hold values from -6 to 6
- adj_diag_one: float32 [128, 128], replicated, may hold values from -6 to 6
- adj_diag_two: float32 [128, 128], replicated, may hold values from -6 to 6
Outputs:
- grad_trail: bfloat16 [16384, 16384], P('row', 'col')
- grad_row_one: float32 [128, 16384], P('row', 'col')
- grad_row_two: float32 [128, 16384], P('row', 'col')
- grad_diag_one: float32 [128, 128], replicated
- grad_diag_two: float32 [128, 128], replicated
Inputs may be any that keep to these rules, and one draw needn't show every extreme that they name: `diag_one`: lower triangular with a positive diagonal. `diag_two`: lower triangular with a positive diagonal.
All inputs are finite; a program needn't handle non-finite values.
Results may differ from a plain program's by a relative error of at most 0.014.
Values may be sent and summed in bfloat16 or wider, within the bound.
A program may use at most 128 MiB of HBM per device.

v0:
```python
import jax
import jax.numpy as jnp
from jax import lax
from jax.sharding import PartitionSpec as P

exact_mode = lax.Precision.HIGHEST


def from_root(value, axis, source):
    kept = jnp.where(lax.axis_index(axis) == source, value, 0).astype(value.dtype)
    return lax.psum(kept, axis)


def halved_lower(matrix):
    order = matrix.shape[0]
    keep = jnp.tril(jnp.ones((order, order), matrix.dtype)) - 0.5 * jnp.eye(
        order, dtype=matrix.dtype
    )
    return matrix * keep


def inverse_lower(block):
    ident = jnp.eye(block.shape[0], dtype=block.dtype)
    return lax.linalg.triangular_solve(block, ident, left_side=True, lower=True)


def block_adjoint(block, inverse, seed_adj):
    inner = halved_lower(jnp.dot(block.T, seed_adj, precision=exact_mode))
    middle = jnp.dot(inverse.T, inner, precision=exact_mode)
    return halved_lower(jnp.dot(middle, inverse, precision=exact_mode))


def per_device(
    trail,
    row_one,
    row_two,
    diag_one,
    diag_two,
    adj_trail,
    adj_row_one,
    adj_row_two,
    adj_diag_one,
    adj_diag_two,
):
    panel = diag_one.shape[0]
    width = trail.shape[1]
    band = row_one.shape[0]
    last = width - panel
    col_count = lax.axis_size("col")
    col_here = lax.axis_index("col")
    row_start = lax.axis_index("row") * band
    here_one = col_here == col_count - 2
    here_two = col_here == col_count - 1
    full_one, full_two = (
        lax.all_gather(row_one, "row", axis=0, tiled=True),
        lax.all_gather(row_two, "row", axis=0, tiled=True),
    )

    def own_rows(matrix):
        return lax.dynamic_slice_in_dim(matrix, row_start, band, 0)

    def solve_panel(rows, inverse, root):
        whole = from_root(rows, "col", root)
        return jnp.dot(whole, inverse, precision=exact_mode).astype(jnp.bfloat16)

    def summed_block(partial_value, root):
        rows_sum = lax.psum(partial_value, "row")
        return from_root(rows_sum, "col", root)

    inverse_two = inverse_lower(diag_two)
    solved_two = solve_panel(adj_trail[:, last:], inverse_two, col_count - 1)
    partial_two = jnp.dot(solved_two.T, trail[:, last:], preferred_element_type=jnp.float32)
    seed_two = jnp.tril(adj_diag_two - summed_block(partial_two, col_count - 1))
    grad_diag_two = block_adjoint(diag_two, inverse_two, seed_two)
    mirror_two = own_rows(grad_diag_two + grad_diag_two.T)
    rest_two = jnp.dot(mirror_two, full_two.astype(jnp.float32), precision=exact_mode)
    inverse_one = inverse_lower(diag_one)
    crossed = lax.psum_scatter(
        jnp.dot(solved_two.T, trail, preferred_element_type=jnp.float32).astype(jnp.bfloat16),
        "row",
        scatter_dimension=0,
        tiled=True,
    ).astype(jnp.float32)
    adj_two = adj_row_two - crossed - rest_two
    adj_next = adj_trail - jnp.dot(solved_two, full_two, preferred_element_type=jnp.float32)
    stacked = jnp.concatenate([adj_two[:, last:], adj_next[:, last:]], 0)
    solved_one = solve_panel(stacked, inverse_one, col_count - 2)
    head_rows = solved_one[:band]
    tail_rows = solved_one[band:]
    partial_one = jnp.dot(
        head_rows.T, row_two[:, last:], preferred_element_type=jnp.float32
    ) + jnp.dot(tail_rows.T, trail[:, last:], preferred_element_type=jnp.float32)
    seed_one = jnp.tril(adj_diag_one - summed_block(partial_one, col_count - 2))
    grad_diag_one = block_adjoint(diag_one, inverse_one, seed_one)
    mirror_one = own_rows(grad_diag_one + grad_diag_one.T)
    rest_one = jnp.dot(mirror_one, full_one.astype(jnp.float32), precision=exact_mode)
    head_update = jnp.dot(head_rows, full_one, preferred_element_type=jnp.float32)
    two_left = adj_two - head_update
    trail_left = adj_next - jnp.dot(tail_rows, full_one, preferred_element_type=jnp.float32)
    crossed_one = lax.psum_scatter(
        (
            jnp.dot(head_rows.T, row_two, preferred_element_type=jnp.float32)
            + jnp.dot(tail_rows.T, trail, preferred_element_type=jnp.float32)
        ).astype(jnp.bfloat16),
        "row",
        scatter_dimension=0,
        tiled=True,
    ).astype(jnp.float32)
    one_left = adj_row_one - crossed_one - rest_one
    trail_block = jnp.where(
        here_one,
        tail_rows.astype(jnp.float32),
        jnp.where(here_two, solved_two.astype(jnp.float32), trail_left[:, last:]),
    )
    grad_trail = jnp.concatenate([trail_left[:, :last], trail_block], 1).astype(jnp.bfloat16)
    zero_block = jnp.zeros((band, panel), jnp.float32)
    one_block = jnp.where(here_one | here_two, zero_block, one_left[:, last:])
    grad_row_one = jnp.concatenate([one_left[:, :last], one_block], 1)
    two_block = jnp.where(
        here_one, head_rows.astype(jnp.float32), jnp.where(here_two, zero_block, two_left[:, last:])
    )
    grad_row_two = jnp.concatenate([two_left[:, :last], two_block], 1)
    return (grad_trail, grad_row_one, grad_row_two, grad_diag_one, grad_diag_two)


def solution(mesh):
    in_specs = (
        P("row", "col"),
        P("row", "col"),
        P("row", "col"),
        P(),
        P(),
        P("row", "col"),
        P("row", "col"),
        P("row", "col"),
        P(),
        P(),
    )
    out_specs = (P("row", "col"), P("row", "col"), P("row", "col"), P(), P())
    return jax.shard_map(
        per_device, mesh=mesh, in_specs=in_specs, out_specs=out_specs, check_vma=False
    )
```

profile of v0, /device:TPU:1, one launch (start us, length us, event | category | flops | bytes accessed | tf_op | source)
XLA Modules:
  0.0 562.1 jit_solution(18032866646956129577)
XLA Ops:
  7.2 0.0 all-reduce.7.cloned.1.call-start
  7.2 2.3 slice_select_fusion.1
  9.5 0.0 all-reduce.7.cloned.1.call-update
  9.5 0.0 all-reduce.9.cloned.1.call-start
  9.6 0.9 select_bitcast_fusion.1
  10.4 9.8 %custom-call.4 = f32[1,128,128]{1,2,0:T(8,128)S(1)} custom-call(f32[1,128,128]{2,1,0:T(8,128)S(1)} %select_bitcast_fusion.1), custom_call_target="InvertDiagBlocksLowerTriangular" | custom-call | tf_op jit(solution)/shard_map/triangular_solve/custom-call.1 | solution.py:24
  20.3 14.7 %all_gather.6 = bf16[128,1024]{1,0:T(8,128)(2,1)S(1)} all-gather(bf16[16,1024]{1,0:T(8,128)(2,1)} %param.14), channel_id=1, replica_groups=mesh['row'=8,'col'=16] {'row'}, dimensions={0}, use_global_device_ids=true | all-gather | bytes 294912 | tf_op jit(solution)/shard_map/all_gather | solution.py:56
  35.0 0.3 fusion.13
  35.3 65.5 %all-reduce.7.cloned.1.call-done = f32[2048,128]{1,0:T(8,128)} async-done(((f32[2048,128]{1,0:T(8,128)}), f32[2048,128]{1,0:T(8,128)}) %all-reduce.7.cloned.1.call-update) | async-done | bytes 1048592 | tf_op jit(solution)/shard_map/psum | solution.py:11
  100.8 2.2 convolution_convert_fusion.1
  103.0 2.0 fusion.6
  105.0 0.0 all-reduce.9.cloned.1.call-update
  105.0 0.0 all-reduce.11.cloned.1.call-start
  105.1 7.8 %convolution_subtract_fusion.1 = f32[2048,1024]{1,0:T(8,128)} fusion(f32[2048,1024]{1,0:T(8,128)} %param.17, bf16[2048,128]{1,0:T(8,128)(2,1)S(1)} %convolution_convert_fusion.1, bf16[128,1024]{1,0:T(8,128)(2,1)S(1)} %all_gather.6), kind=kOutput, calls=%fused_computation.2 | convolution fusion | flops 538968064 | bytes 17563648 | tf_op jit(solution)/shard_map/dot_general | solution.py:85
  113.0 49.3 %all-reduce.9.cloned.1.call-done = f32[128,128]{1,0:T(8,128)} async-done(((f32[128,128]{1,0:T(8,128)}), f32[128,128]{1,0:T(8,128)}) %all-reduce.9.cloned.1.call-update) | async-done | bytes 65552 | tf_op jit(solution)/shard_map/psum | solution.py:67
  162.2 0.6 broadcast_select_fusion.1
  162.9 0.0 all-reduce.11.cloned.1.call-update
  162.9 0.0 reduce-scatter.7.cloned.1.call-start
  163.0 3.7 convolution_convert_fusion.2
  166.7 0.0 reduce-scatter.7.cloned.1.call-update
  166.7 0.0 all-reduce.13.cloned.1.call-start
  166.8 80.1 %all-reduce.11.cloned.1.call-done = f32[128,128]{1,0:T(8,128)} async-done(((f32[128,128]{1,0:T(8,128)}), f32[128,128]{1,0:T(8,128)}) %all-reduce.11.cloned.1.call-update) | async-done | bytes 65552 | tf_op jit(solution)/shard_map/psum | solution.py:11
  246.9 1.1 fusion.2
  248.1 0.3 fusion.42
  248.3 0.2 fusion.25
  248.6 0.0 copy-start.4
  248.6 0.1 copy.62
  248.7 29.7 %reduce-scatter.7.cloned.1.call-done = bf16[16,1024]{1,0:T(8,128)(2,1)} async-done(((bf16[128,1024]{1,0:T(8,128)(2,1)}), bf16[16,1024]{1,0:T(8,128)(2,1)}) %reduce-scatter.7.cloned.1.call-update) | async-done | bytes 32784 | tf_op jit(solution)/shard_map/reduce_scatter | solution.py:78
  278.3 1.0 convolution_subtract_fusion.4
  279.3 1.0 maximum_select_fusion
  280.4 0.0 all-reduce.13.cloned.1.call-update
  280.4 0.0 all-reduce.15.cloned.1.call-start
  280.5 9.8 %custom-call.5 = f32[1,128,128]{1,2,0:T(8,128)S(1)} custom-call(f32[1,128,128]{2,1,0:T(8,128)S(1)} %select_bitcast_fusion), custom_call_target="InvertDiagBlocksLowerTriangular" | custom-call | tf_op jit(solution)/shard_map/triangular_solve/custom-call.1 | solution.py:24
  290.3 16.1 %all_gather.7 = bf16[128,1024]{1,0:T(8,128)(2,1)S(1)} all-gather(bf16[16,1024]{1,0:T(8,128)(2,1)S(1)} %copy-done.10), channel_id=1, replica_groups=mesh['row'=8,'col'=16] {'row'}, dimensions={0}, use_global_device_ids=true | all-gather | bytes 294912 | tf_op jit(solution)/shard_map/all_gather | solution.py:55
  306.5 0.3 fusion.11
  306.8 62.7 %all-reduce.13.cloned.1.call-done = f32[2064,128]{1,0:T(8,128)} async-done(((f32[2064,128]{1,0:T(8,128)}), f32[2064,128]{1,0:T(8,128)}) %all-reduce.13.cloned.1.call-update) | async-done | bytes 1056784 | tf_op jit(solution)/shard_map/psum | solution.py:11
  369.5 2.2 convolution_convert_fusion
  371.7 0.2 fusion.32
  371.9 0.2 fusion.36
  372.1 0.2 convolution_subtract_fusion.2
  372.3 6.7 %convolution_subtract_fusion = bf16[2048,1024]{1,0:T(8,128)(2,1)} fusion(f32[2048,1024]{1,0:T(8,128)} %convolution_subtract_fusion.1, bf16[128,1024]{1,0:T(8,128)(2,1)S(1)} %all_gather.7, bf16[2064,128]{1,0:T(8,128)(2,1)S(1)} %convolution_convert_fusion), kind=kOutput, calls=%fused_computation.1 | convolution fusion | flops 541065216 | bytes 13369344 | tf_op jit(solution)/shard_map/dot_general | solution.py:99
  378.9 2.0 convolution_add_fusion.1
  381.0 0.0 all-reduce.15.cloned.1.call-update
  381.0 0.0 all-reduce.17.cloned.1.call-start
  381.0 3.6 fusion
  384.7 1.2 fusion.4
  385.9 0.0 slice-start.1
  385.9 4.1 slice.97
  390.1 47.9 %all-reduce.15.cloned.1.call-done = f32[128,128]{1,0:T(8,128)} async-done(((f32[128,128]{1,0:T(8,128)}), f32[128,128]{1,0:T(8,128)}) %all-reduce.15.cloned.1.call-update) | async-done | bytes 65552 | tf_op jit(solution)/shard_map/psum | solution.py:67
  437.9 0.6 broadcast_select_fusion
  438.6 0.0 all-reduce.17.cloned.1.call-update
  438.6 0.0 reduce-scatter.9.cloned.1.call-start
  438.7 0.6 pad_maximum_fusion.2
  439.3 0.0 reduce-scatter.9.cloned.1.call-update
  439.4 0.0 copy-start.8
  439.4 4.7 pad_maximum_fusion
  444.1 78.5 %all-reduce.17.cloned.1.call-done = f32[128,128]{1,0:T(8,128)} async-done(((f32[128,128]{1,0:T(8,128)}), f32[128,128]{1,0:T(8,128)}) %all-reduce.17.cloned.1.call-update) | async-done | bytes 65552 | tf_op jit(solution)/shard_map/psum | solution.py:11
  522.6 1.1 fusion.1
  523.7 0.3 fusion.43
  524.0 0.2 fusion.24
  524.3 0.1 copy.67
  524.4 29.3 %reduce-scatter.9.cloned.1.call-done = bf16[16,1024]{1,0:T(8,128)(2,1)} async-done(((bf16[128,1024]{1,0:T(8,128)(2,1)}), bf16[16,1024]{1,0:T(8,128)(2,1)}) %reduce-scatter.9.cloned.1.call-update) | async-done | bytes 32784 | tf_op jit(solution)/shard_map/reduce_scatter | solution.py:100
  553.6 1.0 convolution_subtract_fusion.3
  554.6 0.6 pad_maximum_fusion.1
  (29 shorter events, 0.1 us)
Async XLA Ops:
  7.2 93.6 %all-reduce.7.cloned.1.call-start = ((), (), s32[]{:S(2)}) async-start(), calls=%async_computation.2 | async-start | bytes 2097152 | tf_op jit(solution)/shard_map/psum | solution.py:11
  9.5 152.7 %all-reduce.9.cloned.1.call-start = ((), (), s32[]{:S(2)}) async-start(), calls=%async_computation.3 | async-start | bytes 131072 | tf_op jit(solution)/shard_map/psum | solution.py:67
  105.0 141.9 %all-reduce.11.cloned.1.call-start = ((), (), s32[]{:S(2)}) async-start(), calls=%async_computation.4 | async-start | bytes 131072 | tf_op jit(solution)/shard_map/psum | solution.py:11
  112.9 134.0 %copy-start.1 = (f32[128,128]{1,0:T(8,128)S(1)}, f32[128,128]{1,0:T(8,128)}, u32[]{:S(2)}) copy-start(f32[128,128]{1,0:T(8,128)} %param.16) | copy-start | bytes 196612
  112.9 134.0 %copy-start.6 = (f32[128,128]{1,0:T(8,128)S(1)}, f32[128,128]{1,0:T(8,128)}, u32[]{:S(2)}) copy-start(f32[128,128]{1,0:T(8,128)} %param.21) | copy-start | bytes 196612
  112.9 165.4 %copy-start.7 = (f32[16,1024]{1,0:T(8,128)S(1)}, f32[16,1024]{1,0:T(8,128)}, u32[]{:S(2)}) copy-start(f32[16,1024]{1,0:T(8,128)} %param.19) | copy-start | bytes 196612
  162.9 116.4 %slice-start = ((f32[2048,1024]{1,0:T(8,128)}), f32[2048,128]{1,0:T(8,128)S(1)}, s32[]{:S(2)}) async-start(f32[2048,1024]{1,0:T(8,128)} %convolution_subtract_fusion.1), calls=%async_computation.10 | async-start | bytes 2097152 | tf_op jit(solution)/shard_map/slice | solution.py:86
  162.9 115.4 %reduce-scatter.7.cloned.1.call-start = ((), (), s32[]{:S(2)}) async-start(), calls=%async_computation.8 | async-start | bytes 294912 | tf_op jit(solution)/shard_map/reduce_scatter | solution.py:78
  166.7 113.8 %copy-start.2 = (f32[128,128]{1,0:T(8,128)S(1)}, f32[128,128]{1,0:T(8,128)}, u32[]{:S(2)}) copy-start(f32[128,128]{1,0:T(8,128)} %param.15) | copy-start | bytes 196612
  166.7 123.6 %copy-start.10 = (bf16[16,1024]{1,0:T(8,128)(2,1)S(1)}, bf16[16,1024]{1,0:T(8,128)(2,1)}, u32[]{:S(2)}) copy-start(bf16[16,1024]{1,0:T(8,128)(2,1)} %param.13) | copy-start | bytes 98308
  166.7 205.0 %copy-start.3 = (bf16[16,1024]{1,0:T(8,128)(2,1)S(1)}, bf16[16,1024]{1,0:T(8,128)(2,1)}, u32[]{:S(2)}) copy-start(bf16[16,1024]{1,0:T(8,128)(2,1)} %param.14) | copy-start | bytes 98308
  166.7 202.8 %all-reduce.13.cloned.1.call-start = ((), (), s32[]{:S(2)}) async-start(), calls=%async_computation.5 | async-start | bytes 2113536 | tf_op jit(solution)/shard_map/psum | solution.py:11
  248.6 130.4 %copy-start.4 = (f32[128,128]{1,0:T(8,128)}, f32[128,128]{1,0:T(8,128)S(1)}, u32[]{:S(2)}) copy-start(f32[128,128]{1,0:T(8,128)S(1)} %get-tuple-element.16) | copy-start | bytes 196612
  280.4 157.5 %all-reduce.15.cloned.1.call-start = ((), (), s32[]{:S(2)}) async-start(), calls=%async_computation.6 | async-start | bytes 131072 | tf_op jit(solution)/shard_map/psum | solution.py:67
  372.3 13.7 %copy-start = (f32[16,1024]{1,0:T(8,128)}, f32[16,1024]{1,0:T(8,128)S(1)}, u32[]{:S(2)}) copy-start(f32[16,1024]{1,0:T(8,128)S(1)} %convolution_subtract_fusion.2) | copy-start | bytes 196612
  381.0 141.6 %all-reduce.17.cloned.1.call-start = ((), (), s32[]{:S(2)}) async-start(), calls=%async_computation.7 | async-start | bytes 131072 | tf_op jit(solution)/shard_map/psum | solution.py:11
  385.9 52.7 %slice-start.1 = ((f32[16,1024]{1,0:T(8,128)}), f32[16,896]{1,0:T(8,128)S(1)}, s32[]{:S(2)}) async-start(f32[16,1024]{1,0:T(8,128)} %copy-done), calls=%async_computation.11 | async-start | bytes 114688 | tf_op jit(solution)/shard_map/slice | solution.py:122
  438.6 115.0 %reduce-scatter.9.cloned.1.call-start = ((), (), s32[]{:S(2)}) async-start(), calls=%async_computation.9 | async-start | bytes 294912 | tf_op jit(solution)/shard_map/reduce_scatter | solution.py:100
  439.4 83.2 %copy-start.8 = (f32[128,128]{1,0:T(8,128)S(1)}, f32[128,128]{1,0:T(8,128)}, u32[]{:S(2)}) copy-start(f32[128,128]{1,0:T(8,128)} %param.20) | copy-start | bytes 196612
  439.4 114.2 %copy-start.9 = (f32[16,1024]{1,0:T(8,128)S(1)}, f32[16,1024]{1,0:T(8,128)}, u32[]{:S(2)}) copy-start(f32[16,1024]{1,0:T(8,128)} %param.18) | copy-start | bytes 196612
  524.2 31.0 %copy-start.5 = (f32[128,128]{1,0:T(8,128)}, f32[128,128]{1,0:T(8,128)S(1)}, u32[]{:S(2)}) copy-start(f32[128,128]{1,0:T(8,128)S(1)} %get-tuple-element.18) | copy-start | bytes 196612
Sparse Core Ops, SparseCore 0:
  11.8 88.9 all-reduce.6
  105.2 57.0 all-reduce.8
  166.3 80.5 all-reduce.10
  249.7 28.6 reduce-scatter.6
  282.4 86.9 all-reduce.12
  381.1 56.7 all-reduce.14
  442.0 80.5 all-reduce.16
  525.0 28.6 reduce-scatter.8
where the time goes:
time: 565 us; the launch traced here: 562 us
  waiting for transfers between devices  443 us (78%)
  matrix products  36.6 us (6%)
  other arithmetic  32.3 us (6%)
  blocking collectives  30.9 us (5%)
  between operations  14.4 us (3%)
    psum x4, waiting for transfers between devices, from_root(): return lax.psum(kept, axis)  287 us
    psum x2, waiting for transfers between devices, summed_block(): rows_sum = lax.psum(partial_value, 'row')  97.2 us
    reduce_scatter x1, waiting for transfers between devices, per_device(): lax.psum_scatter(jnp.dot(solved_two.T, trail, preferred_element_type=jnp....  29.7 us
    reduce_scatter x1, waiting for transfers between devices, per_device(): lax.psum_scatter((jnp.dot(head_rows.T, row_two, preferred_element_type=jn...  29.3 us
    another operation x2, other arithmetic, inverse_lower(): return lax.linalg.triangular_solve(block, ident, left_side=True, lower=True)  19.6 us
    all_gather x1, blocking collectives, per_device(): lax.all_gather(row_one, 'row', axis=0, tiled=True)  16.1 us
    all_gather x1, blocking collectives, per_device(): lax.all_gather(row_two, 'row', axis=0, tiled=True)  14.7 us
  transfers between devices with their start and end apart: 8, of which 8 were waited for; matrix products, arithmetic and copies ran while one was open for 9% of the time, Pallas kernels for 0%

commit v1 on v0

v1 whole, which is shorter than its diff:
```python
import jax
import jax.numpy as jnp
from jax import lax
from jax.sharding import PartitionSpec as P

exact_mode = lax.Precision.HIGHEST


def tree_broadcast(value, axis, size, root):
    here = lax.axis_index(axis) ^ root
    step = 1
    while step < size:
        pairs = [(root ^ d, root ^ (d + step)) for d in range(step)]
        arrived = lax.ppermute(value, axis, pairs)
        take = (here >= step) & (here < 2 * step)
        value = jnp.where(take, arrived, value)
        step *= 2
    return value


def butterfly_sum(value, axis, size):
    step = 1
    while step < size:
        pairs = [(i, i ^ step) for i in range(size)]
        value = value + lax.ppermute(value, axis, pairs)
        step *= 2
    return value


def halving_scatter(value, axis, size):
    here = lax.axis_index(axis)
    band = value.shape[0] // size
    blocks = value.reshape(size, band, value.shape[1])
    step = size // 2
    while step >= 1:
        halves = blocks.reshape(2, step, band, value.shape[1])
        high = ((here // step) % 2) == 1
        keep = jnp.where(high, halves[1], halves[0])
        send = jnp.where(high, halves[0], halves[1])
        pairs = [(i, i ^ step) for i in range(size)]
        blocks = keep + lax.ppermute(send, axis, pairs)
        step //= 2
    return blocks.reshape(band, value.shape[1])


def doubling_gather(value, axis, size):
    here = lax.axis_index(axis)
    step = 1
    while step < size:
        pairs = [(i, i ^ step) for i in range(size)]
        other = lax.ppermute(value, axis, pairs)
        high = ((here // step) % 2) == 1
        value = jnp.where(
            high,
            jnp.concatenate([other, value], 0),
            jnp.concatenate([value, other], 0),
        )
        step *= 2
    return value


def halved_lower(matrix):
    order = matrix.shape[0]
    keep = jnp.tril(jnp.ones((order, order), matrix.dtype)) - 0.5 * jnp.eye(
        order, dtype=matrix.dtype
    )
    return matrix * keep


def inverse_lower(block):
    ident = jnp.eye(block.shape[0], dtype=block.dtype)
    return lax.linalg.triangular_solve(block, ident, left_side=True, lower=True)


def block_adjoint(block, inverse, seed_adj):
    inner = halved_lower(jnp.dot(block.T, seed_adj, precision=exact_mode))
    middle = jnp.dot(inverse.T, inner, precision=exact_mode)
    return halved_lower(jnp.dot(middle, inverse, precision=exact_mode))


def make_per_device(n_row, n_col):
    def per_device(
        trail,
        row_one,
        row_two,
        diag_one,
        diag_two,
        adj_trail,
        adj_row_one,
        adj_row_two,
        adj_diag_one,
        adj_diag_two,
    ):
        panel = diag_one.shape[0]
        width = trail.shape[1]
        band = row_one.shape[0]
        last = width - panel
        col_here = lax.axis_index("col")
        row_start = lax.axis_index("row") * band
        root_one = n_col - 2
        root_two = n_col - 1
        here_one = col_here == root_one
        here_two = col_here == root_two
        full_one = doubling_gather(row_one, "row", n_row)
        full_two = doubling_gather(row_two, "row", n_row)

        def own_rows(matrix):
            return lax.dynamic_slice_in_dim(matrix, row_start, band, 0)

        def solve_panel(rows, inverse, root):
            local = jnp.dot(rows, inverse, precision=exact_mode).astype(jnp.bfloat16)
            return tree_broadcast(local, "col", n_col, root)

        def summed_block(partial_value, root):
            rows_sum = butterfly_sum(partial_value, "row", n_row)
            return tree_broadcast(rows_sum, "col", n_col, root)

        inverse_two = inverse_lower(diag_two)
        solved_two = solve_panel(adj_trail[:, last:], inverse_two, root_two)
        partial_two = jnp.dot(solved_two.T, trail[:, last:], preferred_element_type=jnp.float32)
        seed_two = jnp.tril(adj_diag_two - summed_block(partial_two, root_two))
        grad_diag_two = block_adjoint(diag_two, inverse_two, seed_two)
        mirror_two = own_rows(grad_diag_two + grad_diag_two.T)
        rest_two = jnp.dot(mirror_two, full_two.astype(jnp.float32), precision=exact_mode)
        inverse_one = inverse_lower(diag_one)
        crossed = halving_scatter(
            jnp.dot(solved_two.T, trail, preferred_element_type=jnp.float32), "row", n_row
        )
        adj_two = adj_row_two - crossed - rest_two
        adj_next = adj_trail - jnp.dot(solved_two, full_two, preferred_element_type=jnp.float32)
        stacked = jnp.concatenate([adj_two[:, last:], adj_next[:, last:]], 0)
        solved_one = solve_panel(stacked, inverse_one, root_one)
        head_rows = solved_one[:band]
        tail_rows = solved_one[band:]
        partial_one = jnp.dot(
            head_rows.T, row_two[:, last:], preferred_element_type=jnp.float32
        ) + jnp.dot(tail_rows.T, trail[:, last:], preferred_element_type=jnp.float32)
        seed_one = jnp.tril(adj_diag_one - summed_block(partial_one, root_one))
        grad_diag_one = block_adjoint(diag_one, inverse_one, seed_one)
        mirror_one = own_rows(grad_diag_one + grad_diag_one.T)
        rest_one = jnp.dot(mirror_one, full_one.astype(jnp.float32), precision=exact_mode)
        head_update = jnp.dot(head_rows, full_one, preferred_element_type=jnp.float32)
        two_left = adj_two - head_update
        trail_left = adj_next - jnp.dot(tail_rows, full_one, preferred_element_type=jnp.float32)
        crossed_one = halving_scatter(
            jnp.dot(head_rows.T, row_two, preferred_element_type=jnp.float32)
            + jnp.dot(tail_rows.T, trail, preferred_element_type=jnp.float32),
            "row",
            n_row,
        )
        one_left = adj_row_one - crossed_one - rest_one
        trail_block = jnp.where(
            here_one,
            tail_rows.astype(jnp.float32),
            jnp.where(here_two, solved_two.astype(jnp.float32), trail_left[:, last:]),
        )
        grad_trail = jnp.concatenate([trail_left[:, :last], trail_block], 1).astype(jnp.bfloat16)
        zero_block = jnp.zeros((band, panel), jnp.float32)
        one_block = jnp.where(here_one | here_two, zero_block, one_left[:, last:])
        grad_row_one = jnp.concatenate([one_left[:, :last], one_block], 1)
        two_block = jnp.where(
            here_one, head_rows.astype(jnp.float32), jnp.where(here_two, zero_block, two_left[:, last:])
        )
        grad_row_two = jnp.concatenate([two_left[:, :last], two_block], 1)
        return (grad_trail, grad_row_one, grad_row_two, grad_diag_one, grad_diag_two)

    return per_device


def solution(mesh):
    in_specs = (
        P("row", "col"),
        P("row", "col"),
        P("row", "col"),
        P(),
        P(),
        P("row", "col"),
        P("row", "col"),
        P("row", "col"),
        P(),
        P(),
    )
    out_specs = (P("row", "col"), P("row", "col"), P("row", "col"), P(), P())
    return jax.shard_map(
        make_per_device(mesh.shape["row"], mesh.shape["col"]),
        mesh=mesh,
        in_specs=in_specs,
        out_specs=out_specs,
        check_vma=False,
    )
```

time: 565 us -> 208 us (0.37)
  the two profiles are of different devices: /device:TPU:1 before, /device:TPU:2 now
where the time goes in v1:
time: 208 us
  waiting for transfers between devices  124 us (60%)
  starting transfers between devices  27.7 us (13%)
  other arithmetic  25.6 us (12%)
  matrix products  24.4 us (12%)
  local copies, waits for them, and re-layouts  4.11 us (2%)
    ppermute x16, waiting for transfers between devices, tree_broadcast(): arrived = lax.ppermute(value, axis, pairs)  96.7 us
    another operation x4, other arithmetic, inverse_lower(): return lax.linalg.triangular_solve(block, ident, left_side=True, lower=True)  20.5 us
    ppermute x6, waiting for transfers between devices, butterfly_sum(): value = value + lax.ppermute(value, axis, pairs)  15 us
    ppermute x16, starting transfers between devices, tree_broadcast(): arrived = lax.ppermute(value, axis, pairs)  13.3 us
    ppermute x6, waiting for transfers between devices, halving_scatter(): blocks = keep + lax.ppermute(send, axis, pairs)  7.87 us
    ppermute x6, starting transfers between devices, butterfly_sum(): value = value + lax.ppermute(value, axis, pairs)  4.94 us
    ppermute x6, starting transfers between devices, halving_scatter(): blocks = keep + lax.ppermute(send, axis, pairs)  4.92 us
    ppermute x6, waiting for transfers between devices, doubling_gather(): other = lax.ppermute(value, axis, pairs)  4.72 us
  transfers between devices with their start and end apart: 34, of which 12 were waited for; matrix products, arithmetic and copies ran while one was open for 17% of the time, Pallas kernels for 0%

profile of v1, /device:TPU:2, one launch (start us, length us, event | category | flops | bytes accessed | tf_op | source)
XLA Modules:
  0.0 207.7 jit_solution(7525783582080233361)
XLA Ops:
  0.7 0.9 select_bitcast_fusion.1
  1.5 9.8 %custom-call.4 = f32[1,128,128]{1,2,0:T(8,128)S(1)} custom-call(f32[1,128,128]{2,1,0:T(8,128)S(1)} %select_bitcast_fusion.1), custom_call_target="InvertDiagBlocksLowerTriangular" | custom-call | tf_op jit(solution)/shard_map/triangular_solve/custom-call.1 | solution.py:72
  11.4 0.3 fusion.19
  11.6 2.2 %fusion = bf16[2048,128]{1,0:T(8,128)(2,1)S(1)} fusion(f32[128,128]{1,0:T(8,128)S(1)} %fusion.19, f32[2048,1024]{1,0:T(8,128)} %param.17), kind=kOutput, calls=%fused_computation.6 | convolution fusion | flops 402915328 | bytes 1638400 | tf_op jit(solution)/shard_map/dot_general | solution.py:111
  13.8 0.7 collective-permute-start
  14.6 0.7 collective-permute-start.1
  15.4 0.7 collective-permute-start.2
  16.3 1.3 collective-permute-start.3
  17.6 9.8 %custom-call.5 = f32[1,128,128]{1,2,0:T(8,128)S(1)} custom-call(f32[1,128,128]{2,1,0:T(8,128)S(1)} %select_bitcast_fusion), custom_call_target="InvertDiagBlocksLowerTriangular" | custom-call | tf_op jit(solution)/shard_map/triangular_solve/custom-call.1 | solution.py:72
  27.5 0.3 fusion.17
  27.9 0.5 collective-permute-start.5
  28.4 44.6 %collective-permute-done.3 = bf16[2048,128]{1,0:T(8,128)(2,1)S(1)} collective-permute-done((bf16[2048,128]{1,0:T(8,128)(2,1)S(1)}, bf16[2048,128]{1,0:T(8,128)(2,1)S(1)}, u32[]{:S(2)}, u32[]{:S(2)}) %collective-permute-start.3) | collective-permute-done | bytes 524320 | tf_op jit(solution)/shard_map/ppermute | solution.py:14
  73.0 1.4 fusion.11
  74.6 2.2 %collective-permute-start.6 = (bf16[64,1024]{1,0:T(8,128)(2,1)S(1)}, bf16[64,1024]{1,0:T(8,128)(2,1)S(1)}, u32[]{:S(2)}, u32[]{:S(2)}) collective-permute-start(bf16[64,1024]{1,0:T(8,128)(2,1)S(1)} %maximum_select_fusion.2), channel_id=1, source_target_pairs={{0,64},{16,80},{32,96},{48,112},{64,0},{80,16},{96,32},{112,48},{1... | collective-permute-start | bytes 393224 | tf_op jit(solution)/shard_map/ppermute | solution.py:51
  76.8 1.5 collective-permute-start.11
  78.3 2.9 %fusion.57 = f32[128,1024]{1,0:T(8,128)S(1)} fusion(bf16[2048,128]{1,0:T(8,128)(2,1)S(1)} %broadcast_select_fusion.7, bf16[2048,1024]{1,0:T(8,128)(2,1)} %param.12), kind=kOutput, calls=%fused_computation.114 | convolution fusion | flops 536870912 | bytes 5242880 | tf_op jit(solution)/shard_map/dot_general | solution.py:127
  81.2 2.2 %collective-permute-done.11 = f32[128,128]{1,0:T(8,128)S(1)} collective-permute-done((f32[128,128]{1,0:T(8,128)S(1)}, f32[128,128]{1,0:T(8,128)S(1)}, u32[]{:S(2)}, u32[]{:S(2)}) %collective-permute-start.11) | collective-permute-done | bytes 65568 | tf_op jit(solution)/shard_map/ppermute | solution.py:25
  83.6 3.6 %collective-permute-start.7 = (f32[4,16,1024]{2,1,0:T(8,128)S(1)}, f32[4,16,1024]{2,1,0:T(8,128)S(1)}, u32[]{:S(2)}, u32[]{:S(2)}) collective-permute-start(f32[4,16,1024]{2,1,0:T(8,128)S(1)} %bitcast.55), channel_id=1, source_target_pairs={{0,64},{16,80},{32,96},{48,112},{64,0},{80,16},{96,32},{112,48},{1... | collective-permute-start | bytes 786440 | tf_op jit(solution)/shard_map/ppermute | solution.py:41
  87.2 2.9 %collective-permute-done.12 = f32[128,128]{1,0:T(8,128)S(1)} collective-permute-done((f32[128,128]{1,0:T(8,128)S(1)}, f32[128,128]{1,0:T(8,128)S(1)}, u32[]{:S(2)}, u32[]{:S(2)}) %collective-permute-start.12) | collective-permute-done | bytes 65568 | tf_op jit(solution)/shard_map/ppermute | solution.py:25
  90.1 0.7 collective-permute-start.13
  90.8 4.6 %convolution_subtract_fusion.1 = f32[2048,1024]{1,0:T(8,128)S(1)} fusion(f32[2048,1024]{1,0:T(8,128)} %param.17, bf16[2048,128]{1,0:T(8,128)(2,1)S(1)} %broadcast_select_fusion.7, bf16[64,1024]{1,0:T(8,128)(2,1)S(1)} %maximum_select_fusion.2, bf16[64,1024]{1,0:T(8,128)(2,1)S(1)} %collective-permute-done.6, pred[]{:T(512)S(6)} %eq.62), kind=kOutput, calls=%fused_computation.2 | convolution fusion | flops 540147712 | bytes 17563648 | tf_op jit(solution)/shard_map/dot_general | solution.py:130
  95.4 3.3 %copy-done = f32[2048,1024]{1,0:T(8,128)} copy-done((f32[2048,1024]{1,0:T(8,128)}, f32[2048,1024]{1,0:T(8,128)S(1)}, u32[]{:S(2)}) %copy-start) | copy-done | bytes 8388632
  99.0 0.7 collective-permute-start.14
  99.8 0.7 collective-permute-start.15
  100.4 4.2 %collective-permute-done.8 = f32[2,16,1024]{2,1,0:T(8,128)S(1)} collective-permute-done((f32[2,16,1024]{2,1,0:T(8,128)S(1)}, f32[2,16,1024]{2,1,0:T(8,128)S(1)}, u32[]{:S(2)}, u32[]{:S(2)}) %collective-permute-start.8) | collective-permute-done | bytes 131104 | tf_op jit(solution)/shard_map/ppermute | solution.py:41
  104.8 1.3 collective-permute-start.16
  106.1 0.3 collective-permute-start.9
  106.4 9.1 %collective-permute-done.16 = f32[128,128]{1,0:T(8,128)S(1)} collective-permute-done((f32[128,128]{1,0:T(8,128)S(1)}, f32[128,128]{1,0:T(8,128)S(1)}, u32[]{:S(2)}, u32[]{:S(2)}) %collective-permute-start.16) | collective-permute-done | bytes 65568 | tf_op jit(solution)/shard_map/ppermute | solution.py:14
  115.4 0.3 fusion.2
  115.7 0.3 fusion.58
  116.4 0.3 fusion.23
  116.6 1.0 convolution_convert_fusion
  117.6 0.7 collective-permute-start.17
  118.4 0.7 collective-permute-start.18
  119.2 0.7 collective-permute-start.19
  120.0 1.3 collective-permute-start.20
  121.4 1.2 collective-permute-done.21
  122.6 0.8 collective-permute-start.22
  123.4 3.5 %collective-permute-done.22 = bf16[32,1024]{1,0:T(8,128)(2,1)S(1)} collective-permute-done((bf16[32,1024]{1,0:T(8,128)(2,1)S(1)}, bf16[32,1024]{1,0:T(8,128)(2,1)S(1)}, u32[]{:S(2)}, u32[]{:S(2)}) %collective-permute-start.22) | collective-permute-done | bytes 65568 | tf_op jit(solution)/shard_map/ppermute | solution.py:51
  127.0 0.8 collective-permute-start.23
  127.7 34.2 %collective-permute-done.20 = bf16[2064,128]{1,0:T(8,128)(2,1)S(1)} collective-permute-done((bf16[2064,128]{1,0:T(8,128)(2,1)S(1)}, bf16[2064,128]{1,0:T(8,128)(2,1)S(1)}, u32[]{:S(2)}, u32[]{:S(2)}) %collective-permute-start.20) | collective-permute-done | bytes 528416 | tf_op jit(solution)/shard_map/ppermute | solution.py:14
  162.0 1.4 fusion.9
  163.4 2.9 %fusion.14 = f32[128,1024]{1,0:T(8,128)S(1)} fusion(bf16[2048,1024]{1,0:T(8,128)(2,1)} %param.12, bf16[2064,128]{1,0:T(8,128)(2,1)S(1)} %broadcast_select_fusion.3), kind=kOutput, calls=%fused_computation.34 | convolution fusion | flops 536870912 | bytes 5242880 | tf_op jit(solution)/shard_map/dot_general | solution.py:147
  166.7 0.3 convolution_add_fusion
  166.9 4.6 %convolution_subtract_fusion = bf16[2048,1024]{1,0:T(8,128)(2,1)S(1)} fusion(f32[2048,1024]{1,0:T(8,128)} %copy-done, bf16[2064,128]{1,0:T(8,128)(2,1)S(1)} %broadcast_select_fusion.3, bf16[64,1024]{1,0:T(8,128)(2,1)S(1)} %maximum_select_fusion.3, bf16[64,1024]{1,0:T(8,128)(2,1)S(1)} %collective-permute-done.23, pred[]{:T(512)S(6)} %eq.62), kind=kOutput, calls=%fused_computation.1 | convolution fusion | flops 542244864 | bytes 13369345 | tf_op jit(solution)/shard_map/dot_general | solution.py:144
  171.6 0.2 fusion.7
  171.9 0.4 slice.206
  172.3 0.8 collective-permute-start.24
  173.1 2.1 collective-permute-start.28
  175.2 2.6 %pad_maximum_fusion = bf16[2048,1024]{1,0:T(8,128)(2,1)} fusion(bf16[2048,128]{1,0:T(8,128)(2,1)S(1)} %fusion.7, bf16[2048,896]{1,0:T(8,128)(2,1)S(1)} %slice.206), kind=kLoop, calls=%fused_computation.3 | loop fusion | flops 8388608 | bytes 8388608 | tf_op jit(solution)/shard_map/concatenate | solution.py:157
  177.8 5.3 %collective-permute-done.28 = f32[128,128]{1,0:T(8,128)S(1)} collective-permute-done((f32[128,128]{1,0:T(8,128)S(1)}, f32[128,128]{1,0:T(8,128)S(1)}, u32[]{:S(2)}, u32[]{:S(2)}) %collective-permute-start.28) | collective-permute-done | bytes 65568 | tf_op jit(solution)/shard_map/ppermute | solution.py:25
  183.2 1.1 collective-permute-start.29
  184.4 4.6 %collective-permute-done.29 = f32[128,128]{1,0:T(8,128)S(1)} collective-permute-done((f32[128,128]{1,0:T(8,128)S(1)}, f32[128,128]{1,0:T(8,128)S(1)}, u32[]{:S(2)}, u32[]{:S(2)}) %collective-permute-start.29) | collective-permute-done | bytes 65568 | tf_op jit(solution)/shard_map/ppermute | solution.py:25
  189.0 0.7 collective-permute-start.30
  189.8 0.7 collective-permute-start.31
  190.4 0.6 pad_maximum_fusion.2
  191.1 0.7 collective-permute-start.32
  192.0 1.3 collective-permute-start.33
  193.3 3.6 %collective-permute-done.25 = f32[2,16,1024]{2,1,0:T(8,128)S(1)} collective-permute-done((f32[2,16,1024]{2,1,0:T(8,128)S(1)}, f32[2,16,1024]{2,1,0:T(8,128)S(1)}, u32[]{:S(2)}, u32[]{:S(2)}) %collective-permute-start.25) | collective-permute-done | bytes 131104 | tf_op jit(solution)/shard_map/ppermute | solution.py:41
  197.0 8.8 %collective-permute-done.33 = f32[128,128]{1,0:T(8,128)S(1)} collective-permute-done((f32[128,128]{1,0:T(8,128)S(1)}, f32[128,128]{1,0:T(8,128)S(1)}, u32[]{:S(2)}, u32[]{:S(2)}) %collective-permute-start.33) | collective-permute-done | bytes 65568 | tf_op jit(solution)/shard_map/ppermute | solution.py:14
  205.8 0.3 fusion.1
  206.1 0.3 fusion.59
  206.8 0.3 fusion.21
  207.1 0.6 pad_maximum_fusion.1
  (99 shorter events, 2.9 us)
Async XLA Ops:
  0.6 15.5 %copy-start.3 = (bf16[16,1024]{1,0:T(8,128)(2,1)S(1)}, bf16[16,1024]{1,0:T(8,128)(2,1)}, u32[]{:S(2)}) copy-start(bf16[16,1024]{1,0:T(8,128)(2,1)} %param.14) | copy-start | bytes 98308
  0.6 17.0 %copy-start.2 = (f32[128,128]{1,0:T(8,128)S(1)}, f32[128,128]{1,0:T(8,128)}, u32[]{:S(2)}) copy-start(f32[128,128]{1,0:T(8,128)} %param.15) | copy-start | bytes 196612
  13.8 0.7 collective-permute-start
  14.6 0.7 collective-permute-start.1
  15.4 0.8 collective-permute-start.2
  16.1 11.7 %collective-permute-start.4 = (bf16[16,1024]{1,0:T(8,128)(2,1)S(1)}, bf16[16,1024]{1,0:T(8,128)(2,1)S(1)}, u32[]{:S(2)}, u32[]{:S(2)}) collective-permute-start(bf16[16,1024]{1,0:T(8,128)(2,1)S(1)} %copy-done.3), channel_id=1, source_target_pairs={{0,16},{16,0},{32,48},{48,32},{64,80},{80,64},{96,112},{112,96},{1... | collective-permute-start | bytes 98312 | tf_op jit(solution)/shard_map/ppermute | solution.py:51
  16.3 56.7 %collective-permute-start.3 = (bf16[2048,128]{1,0:T(8,128)(2,1)S(1)}, bf16[2048,128]{1,0:T(8,128)(2,1)S(1)}, u32[]{:S(2)}, u32[]{:S(2)}) collective-permute-start(bf16[2048,128]{1,0:T(8,128)(2,1)S(1)} %broadcast_select_fusion.6), channel_id=1, source_target_pairs={{15,7},{14,6},{13,5},{12,4},{11,3},{10,2},{9,1},{8,0},{31,23},{30,... | collective-permute-start | bytes 1572872 | tf_op jit(solution)/shard_map/ppermute | solution.py:14
  27.9 46.6 %collective-permute-start.5 = (bf16[32,1024]{1,0:T(8,128)(2,1)S(1)}, bf16[32,1024]{1,0:T(8,128)(2,1)S(1)}, u32[]{:S(2)}, u32[]{:S(2)}) collective-permute-start(bf16[32,1024]{1,0:T(8,128)(2,1)S(1)} %maximum_select_fusion.4), channel_id=1, source_target_pairs={{0,32},{16,48},{32,0},{48,16},{64,96},{80,112},{96,64},{112,80},{1... | collective-permute-start | bytes 196616 | tf_op jit(solution)/shard_map/ppermute | solution.py:51
  74.4 2.3 %collective-permute-start.10 = (f32[128,128]{1,0:T(8,128)S(1)}, f32[128,128]{1,0:T(8,128)S(1)}, u32[]{:S(2)}, u32[]{:S(2)}) collective-permute-start(f32[128,128]{1,0:T(8,128)S(1)} %fusion.11), channel_id=1, source_target_pairs={{0,16},{16,0},{32,48},{48,32},{64,80},{80,64},{96,112},{112,96},{1... | collective-permute-start | bytes 196616 | tf_op jit(solution)/shard_map/ppermute | solution.py:25
  74.6 16.2 %collective-permute-start.6 = (bf16[64,1024]{1,0:T(8,128)(2,1)S(1)}, bf16[64,1024]{1,0:T(8,128)(2,1)S(1)}, u32[]{:S(2)}, u32[]{:S(2)}) collective-permute-start(bf16[64,1024]{1,0:T(8,128)(2,1)S(1)} %maximum_select_fusion.2), channel_id=1, source_target_pairs={{0,64},{16,80},{32,96},{48,112},{64,0},{80,16},{96,32},{112,48},{1... | collective-permute-start | bytes 393224 | tf_op jit(solution)/shard_map/ppermute | solution.py:51
  76.8 6.7 %collective-permute-start.11 = (f32[128,128]{1,0:T(8,128)S(1)}, f32[128,128]{1,0:T(8,128)S(1)}, u32[]{:S(2)}, u32[]{:S(2)}) collective-permute-start(f32[128,128]{1,0:T(8,128)S(1)} %add.81), channel_id=1, source_target_pairs={{0,32},{16,48},{32,0},{48,16},{64,96},{80,112},{96,64},{112,80},{1... | collective-permute-start | bytes 196616 | tf_op jit(solution)/shard_map/ppermute | solution.py:25
  83.5 6.6 %collective-permute-start.12 = (f32[128,128]{1,0:T(8,128)S(1)}, f32[128,128]{1,0:T(8,128)S(1)}, u32[]{:S(2)}, u32[]{:S(2)}) collective-permute-start(f32[128,128]{1,0:T(8,128)S(1)} %add.82), channel_id=1, source_target_pairs={{0,64},{16,80},{32,96},{48,112},{64,0},{80,16},{96,32},{112,48},{1... | collective-permute-start | bytes 196616 | tf_op jit(solution)/shard_map/ppermute | solution.py:25
  83.6 15.2 %collective-permute-start.7 = (f32[4,16,1024]{2,1,0:T(8,128)S(1)}, f32[4,16,1024]{2,1,0:T(8,128)S(1)}, u32[]{:S(2)}, u32[]{:S(2)}) collective-permute-start(f32[4,16,1024]{2,1,0:T(8,128)S(1)} %bitcast.55), channel_id=1, source_target_pairs={{0,64},{16,80},{32,96},{48,112},{64,0},{80,16},{96,32},{112,48},{1... | collective-permute-start | bytes 786440 | tf_op jit(solution)/shard_map/ppermute | solution.py:41
  90.1 8.8 %collective-permute-start.13 = (f32[128,128]{1,0:T(8,128)S(1)}, f32[128,128]{1,0:T(8,128)S(1)}, u32[]{:S(2)}, u32[]{:S(2)}) collective-permute-start(f32[128,128]{1,0:T(8,128)S(1)} %add.83), channel_id=1, source_target_pairs={{15,14},{31,30},{47,46},{63,62},{79,78},{95,94},{111,110},{127,126}} | collective-permute-start | bytes 196616 | tf_op jit(solution)/shard_map/ppermute | solution.py:14
  95.4 3.3 %copy-start = (f32[2048,1024]{1,0:T(8,128)}, f32[2048,1024]{1,0:T(8,128)S(1)}, u32[]{:S(2)}) copy-start(f32[2048,1024]{1,0:T(8,128)S(1)} %convolution_subtract_fusion.1) | copy-start | bytes 25165828
  98.7 16.7 %copy-start.1 = (f32[128,128]{1,0:T(8,128)S(1)}, f32[128,128]{1,0:T(8,128)}, u32[]{:S(2)}) copy-start(f32[128,128]{1,0:T(8,128)} %param.16) | copy-start | bytes 196612
  98.7 16.7 %copy-start.4 = (f32[128,128]{1,0:T(8,128)S(1)}, f32[128,128]{1,0:T(8,128)}, u32[]{:S(2)}) copy-start(f32[128,128]{1,0:T(8,128)} %param.21) | copy-start | bytes 196612
  98.7 17.6 %copy-start.9 = (f32[16,1024]{1,0:T(8,128)S(1)}, f32[16,1024]{1,0:T(8,128)}, u32[]{:S(2)}) copy-start(f32[16,1024]{1,0:T(8,128)} %param.19) | copy-start | bytes 196612
  99.0 0.8 collective-permute-start.14
  99.6 5.0 %collective-permute-start.8 = (f32[2,16,1024]{2,1,0:T(8,128)S(1)}, f32[2,16,1024]{2,1,0:T(8,128)S(1)}, u32[]{:S(2)}, u32[]{:S(2)}) collective-permute-start(f32[2,16,1024]{2,1,0:T(8,128)S(1)} %slice_select_fusion.6), channel_id=1, source_target_pairs={{0,32},{16,48},{32,0},{48,16},{64,96},{80,112},{96,64},{112,80},{1... | collective-permute-start | bytes 393224 | tf_op jit(solution)/shard_map/ppermute | solution.py:41
  99.8 5.0 %collective-permute-start.15 = (f32[128,128]{1,0:T(8,128)S(1)}, f32[128,128]{1,0:T(8,128)S(1)}, u32[]{:S(2)}, u32[]{:S(2)}) collective-permute-start(f32[128,128]{1,0:T(8,128)S(1)} %broadcast_select_fusion.12), channel_id=1, source_target_pairs={{15,11},{14,10},{13,9},{12,8},{31,27},{30,26},{29,25},{28,24},{47,... | collective-permute-start | bytes 196616 | tf_op jit(solution)/shard_map/ppermute | solution.py:14
  104.8 10.7 %collective-permute-start.16 = (f32[128,128]{1,0:T(8,128)S(1)}, f32[128,128]{1,0:T(8,128)S(1)}, u32[]{:S(2)}, u32[]{:S(2)}) collective-permute-start(f32[128,128]{1,0:T(8,128)S(1)} %broadcast_select_fusion.13), channel_id=1, source_target_pairs={{15,7},{14,6},{13,5},{12,4},{11,3},{10,2},{9,1},{8,0},{31,23},{30,... | collective-permute-start | bytes 196616 | tf_op jit(solution)/shard_map/ppermute | solution.py:14
  106.1 15.2 %copy-start.8 = (bf16[16,1024]{1,0:T(8,128)(2,1)S(1)}, bf16[16,1024]{1,0:T(8,128)(2,1)}, u32[]{:S(2)}) copy-start(bf16[16,1024]{1,0:T(8,128)(2,1)} %param.13) | copy-start | bytes 98308
  106.1 10.2 %collective-permute-start.9 = (f32[1,16,1024]{2,1,0:T(8,128)S(1)}, f32[1,16,1024]{2,1,0:T(8,128)S(1)}, u32[]{:S(2)}, u32[]{:S(2)}) collective-permute-start(f32[1,16,1024]{2,1,0:T(8,128)S(1)} %slice_select_fusion.8), channel_id=1, source_target_pairs={{0,16},{16,0},{32,48},{48,32},{64,80},{80,64},{96,112},{112,96},{1... | collective-permute-start | bytes 196616 | tf_op jit(solution)/shard_map/ppermute | solution.py:41
  116.2 45.8 %copy-start.6 = (f32[128,128]{1,0:T(8,128)}, f32[128,128]{1,0:T(8,128)S(1)}, u32[]{:S(2)}) copy-start(f32[128,128]{1,0:T(8,128)S(1)} %get-tuple-element.25) | copy-start | bytes 196612
  117.6 0.7 collective-permute-start.17
  118.4 0.7 collective-permute-start.18
  119.2 0.7 collective-permute-start.19
  120.0 42.0 %collective-permute-start.20 = (bf16[2064,128]{1,0:T(8,128)(2,1)S(1)}, bf16[2064,128]{1,0:T(8,128)(2,1)S(1)}, u32[]{:S(2)}, u32[]{:S(2)}) collective-permute-start(bf16[2064,128]{1,0:T(8,128)(2,1)S(1)} %broadcast_select_fusion.2), channel_id=1, source_target_pairs={{14,6},{15,7},{12,4},{13,5},{10,2},{11,3},{8,0},{9,1},{30,22},{31,... | collective-permute-start | bytes 1585160 | tf_op jit(solution)/shard_map/ppermute | solution.py:14
  121.3 1.3 collective-permute-start.21
  122.6 4.3 %collective-permute-start.22 = (bf16[32,1024]{1,0:T(8,128)(2,1)S(1)}, bf16[32,1024]{1,0:T(8,128)(2,1)S(1)}, u32[]{:S(2)}, u32[]{:S(2)}) collective-permute-start(bf16[32,1024]{1,0:T(8,128)(2,1)S(1)} %maximum_select_fusion.5), channel_id=1, source_target_pairs={{0,32},{16,48},{32,0},{48,16},{64,96},{80,112},{96,64},{112,80},{1... | collective-permute-start | bytes 196616 | tf_op jit(solution)/shard_map/ppermute | solution.py:51
  127.0 40.0 %collective-permute-start.23 = (bf16[64,1024]{1,0:T(8,128)(2,1)S(1)}, bf16[64,1024]{1,0:T(8,128)(2,1)S(1)}, u32[]{:S(2)}, u32[]{:S(2)}) collective-permute-start(bf16[64,1024]{1,0:T(8,128)(2,1)S(1)} %maximum_select_fusion.3), channel_id=1, source_target_pairs={{0,64},{16,80},{32,96},{48,112},{64,0},{80,16},{96,32},{112,48},{1... | collective-permute-start | bytes 393224 | tf_op jit(solution)/shard_map/ppermute | solution.py:51
  166.6 6.5 %collective-permute-start.27 = (f32[128,128]{1,0:T(8,128)S(1)}, f32[128,128]{1,0:T(8,128)S(1)}, u32[]{:S(2)}, u32[]{:S(2)}) collective-permute-start(f32[128,128]{1,0:T(8,128)S(1)} %convolution_add_fusion.1), channel_id=1, source_target_pairs={{0,16},{16,0},{32,48},{48,32},{64,80},{80,64},{96,112},{112,96},{1... | collective-permute-start | bytes 196616 | tf_op jit(solution)/shard_map/ppermute | solution.py:25
  172.3 18.8 %collective-permute-start.24 = (f32[4,16,1024]{2,1,0:T(8,128)S(1)}, f32[4,16,1024]{2,1,0:T(8,128)S(1)}, u32[]{:S(2)}, u32[]{:S(2)}) collective-permute-start(f32[4,16,1024]{2,1,0:T(8,128)S(1)} %bitcast.54), channel_id=1, source_target_pairs={{0,64},{16,80},{32,96},{48,112},{64,0},{80,16},{96,32},{112,48},{1... | collective-permute-start | bytes 786440 | tf_op jit(solution)/shard_map/ppermute | solution.py:41
  173.1 32.7 %copy-start.5 = (f32[128,128]{1,0:T(8,128)S(1)}, f32[128,128]{1,0:T(8,128)}, u32[]{:S(2)}) copy-start(f32[128,128]{1,0:T(8,128)} %param.20) | copy-start | bytes 196612
  173.1 10.0 %collective-permute-start.28 = (f32[128,128]{1,0:T(8,128)S(1)}, f32[128,128]{1,0:T(8,128)S(1)}, u32[]{:S(2)}, u32[]{:S(2)}) collective-permute-start(f32[128,128]{1,0:T(8,128)S(1)} %add.91), channel_id=1, source_target_pairs={{0,32},{16,48},{32,0},{48,16},{64,96},{80,112},{96,64},{112,80},{1... | collective-permute-start | bytes 196616 | tf_op jit(solution)/shard_map/ppermute | solution.py:25
  177.8 29.0 %copy-start.10 = (f32[16,1024]{1,0:T(8,128)S(1)}, f32[16,1024]{1,0:T(8,128)}, u32[]{:S(2)}) copy-start(f32[16,1024]{1,0:T(8,128)} %param.18) | copy-start | bytes 196612
  183.2 5.8 %collective-permute-start.29 = (f32[128,128]{1,0:T(8,128)S(1)}, f32[128,128]{1,0:T(8,128)S(1)}, u32[]{:S(2)}, u32[]{:S(2)}) collective-permute-start(f32[128,128]{1,0:T(8,128)S(1)} %add.92), channel_id=1, source_target_pairs={{0,64},{16,80},{32,96},{48,112},{64,0},{80,16},{96,32},{112,48},{1... | collective-permute-start | bytes 196616 | tf_op jit(solution)/shard_map/ppermute | solution.py:25
  189.0 0.7 collective-permute-start.30
  189.8 1.4 collective-permute-start.31
  191.1 0.8 collective-permute-start.32
  191.8 5.0 %collective-permute-start.25 = (f32[2,16,1024]{2,1,0:T(8,128)S(1)}, f32[2,16,1024]{2,1,0:T(8,128)S(1)}, u32[]{:S(2)}, u32[]{:S(2)}) collective-permute-start(f32[2,16,1024]{2,1,0:T(8,128)S(1)} %slice_select_fusion.5), channel_id=1, source_target_pairs={{0,32},{16,48},{32,0},{48,16},{64,96},{80,112},{96,64},{112,80},{1... | collective-permute-start | bytes 393224 | tf_op jit(solution)/shard_map/ppermute | solution.py:41
  192.0 13.9 %collective-permute-start.33 = (f32[128,128]{1,0:T(8,128)S(1)}, f32[128,128]{1,0:T(8,128)S(1)}, u32[]{:S(2)}, u32[]{:S(2)}) collective-permute-start(f32[128,128]{1,0:T(8,128)S(1)} %broadcast_select_fusion.10), channel_id=1, source_target_pairs={{14,6},{15,7},{12,4},{13,5},{10,2},{11,3},{8,0},{9,1},{30,22},{31,... | collective-permute-start | bytes 196616 | tf_op jit(solution)/shard_map/ppermute | solution.py:14
  196.9 9.8 %collective-permute-start.26 = (f32[1,16,1024]{2,1,0:T(8,128)S(1)}, f32[1,16,1024]{2,1,0:T(8,128)S(1)}, u32[]{:S(2)}, u32[]{:S(2)}) collective-permute-start(f32[1,16,1024]{2,1,0:T(8,128)S(1)} %slice_select_fusion.7), channel_id=1, source_target_pairs={{0,16},{16,0},{32,48},{48,32},{64,80},{80,64},{96,112},{112,96},{1... | collective-permute-start | bytes 196616 | tf_op jit(solution)/shard_map/ppermute | solution.py:41
  206.6 1.1 copy-start.7

commit v2 on v1

--- a/solution.py
+++ b/solution.py
@@ -16,6 +16,11 @@
         value = jnp.where(take, arrived, value)
         step *= 2
     return value
+
+
+def chunked_broadcast(value, axis, size, root, chunks):
+    parts = jnp.split(value, chunks, 0)
+    return jnp.concatenate([tree_broadcast(p, axis, size, root) for p in parts], 0)
 
 
 def butterfly_sum(value, axis, size):
@@ -109,33 +114,42 @@
 
         def solve_panel(rows, inverse, root):
             local = jnp.dot(rows, inverse, precision=exact_mode).astype(jnp.bfloat16)
-            return tree_broadcast(local, "col", n_col, root)
+            return chunked_broadcast(local, "col", n_col, root, 4)
 
         def summed_block(partial_value, root):
             rows_sum = butterfly_sum(partial_value, "row", n_row)
             return tree_broadcast(rows_sum, "col", n_col, root)
 
         inverse_two = inverse_lower(diag_two)
+        inverse_one = inverse_lower(diag_one)
         solved_two = solve_panel(adj_trail[:, last:], inverse_two, root_two)
+        next_panel = adj_trail[:, last:] - jnp.dot(
+            solved_two, full_two[:, last:], preferred_element_type=jnp.float32
+        )
+        tail_rows = solve_panel(next_panel, inverse_one, root_one)
         partial_two = jnp.dot(solved_two.T, trail[:, last:], preferred_element_type=jnp.float32)
         seed_two = jnp.tril(adj_diag_two - summed_block(partial_two, root_two))
         grad_diag_two = block_adjoint(diag_two, inverse_two, seed_two)
         mirror_two = own_rows(grad_diag_two + grad_diag_two.T)
         rest_two = jnp.dot(mirror_two, full_two.astype(jnp.float32), precision=exact_mode)
-        inverse_one = inverse_lower(diag_one)
         crossed = halving_scatter(
             jnp.dot(solved_two.T, trail, preferred_element_type=jnp.float32), "row", n_row
         )
         adj_two = adj_row_two - crossed - rest_two
         adj_next = adj_trail - jnp.dot(solved_two, full_two, preferred_element_type=jnp.float32)
-        stacked = jnp.concatenate([adj_two[:, last:], adj_next[:, last:]], 0)
-        solved_one = solve_panel(stacked, inverse_one, root_one)
-        head_rows = solved_one[:band]
-        tail_rows = solved_one[band:]
-        partial_one = jnp.dot(
-            head_rows.T, row_two[:, last:], preferred_element_type=jnp.float32
-        ) + jnp.dot(tail_rows.T, trail[:, last:], preferred_element_type=jnp.float32)
-        seed_one = jnp.tril(adj_diag_one - summed_block(partial_one, root_one))
+        head_local = jnp.dot(adj_two[:, last:], inverse_one, precision=exact_mode).astype(
+            jnp.bfloat16
+        )
+        head_rows = tree_broadcast(head_local, "col", n_col, root_one)
+        tail_sum = butterfly_sum(
+            jnp.dot(tail_rows.T, trail[:, last:], preferred_element_type=jnp.float32), "row", n_row
+        )
+        head_sum = butterfly_sum(
+            jnp.dot(head_local.T, row_two[:, last:], preferred_element_type=jnp.float32), "row", n_row
+        )
+        seed_one = jnp.tril(
+            adj_diag_one - tree_broadcast(head_sum + tail_sum, "col", n_col, root_one)
+        )
         grad_diag_one = block_adjoint(diag_one, inverse_one, seed_one)
         mirror_one = own_rows(grad_diag_one + grad_diag_one.T)
         rest_one = jnp.dot(mirror_one, full_one.astype(jnp.float32), precision=exact_mode)

time: 208 us -> 220 us (1.058)
  the two profiles are of different devices: /device:TPU:2 before, /device:TPU:1 now
where the time goes in v2:
time: 220 us; the launch traced here: 217 us
  starting transfers between devices  83.6 us (38%)
  waiting for transfers between devices  65.8 us (30%)
  other arithmetic  26.5 us (12%)
  matrix products  22.2 us (10%)
  local copies, waits for them, and re-layouts  16.4 us (7%)
    ppermute x44, waiting for transfers between devices, tree_broadcast(): arrived = lax.ppermute(value, axis, pairs)  50.8 us
    ppermute x44, starting transfers between devices, tree_broadcast(): arrived = lax.ppermute(value, axis, pairs)  36.3 us
    ppermute x9, starting transfers between devices, butterfly_sum(): value = value + lax.ppermute(value, axis, pairs)  27.1 us
    another operation x4, other arithmetic, inverse_lower(): return lax.linalg.triangular_solve(block, ident, left_side=True, lower=True)  21.3 us
    unnamed x26, local copies, waits for them, and re-layouts  15.7 us
    ppermute x6, starting transfers between devices, halving_scatter(): blocks = keep + lax.ppermute(send, axis, pairs)  13.9 us
    ppermute x9, waiting for transfers between devices, butterfly_sum(): value = value + lax.ppermute(value, axis, pairs)  8.75 us
    dot_general x1, matrix products, per_device(): jnp.dot(tail_rows, full_one, preferred_element_type=jnp.float32)  7.08 us
  transfers between devices with their start and end apart: 65, of which 16 were waited for; matrix products, arithmetic and copies ran while one was open for 30% of the time, Pallas kernels for 0%

profile of v2, /device:TPU:1, one launch (start us, length us, event | category | flops | bytes accessed | tf_op | source)
XLA Modules:
  0.0 216.6 jit_solution(18348065160166694718)
XLA Ops:
  0.6 1.5 collective-permute-start.35
  2.2 0.8 select_bitcast_fusion.1
  3.1 9.8 %custom-call.4 = f32[1,128,128]{1,2,0:T(8,128)S(1)} custom-call(f32[1,128,128]{2,1,0:T(8,128)S(1)} %select_bitcast_fusion.1), custom_call_target="InvertDiagBlocksLowerTriangular" | custom-call | tf_op jit(solution)/shard_map/triangular_solve/custom-call.1 | solution.py:77
  13.2 2.3 %fusion = bf16[2048,128]{0,1:T(8,128)(2,1)S(1)} fusion(f32[128,128]{1,0:T(8,128)S(1)} %fusion.12, f32[2048,1024]{1,0:T(8,128)} %param.17), kind=kOutput, calls=%fused_computation.6 | convolution fusion | flops 402915328 | bytes 1638400 | tf_op jit(solution)/shard_map/dot_general | solution.py:116
  15.5 0.7 collective-permute-start
  16.2 0.9 select_bitcast_fusion
  17.0 9.8 %custom-call.5 = f32[1,128,128]{1,2,0:T(8,128)S(1)} custom-call(f32[1,128,128]{2,1,0:T(8,128)S(1)} %select_bitcast_fusion), custom_call_target="InvertDiagBlocksLowerTriangular" | custom-call | tf_op jit(solution)/shard_map/triangular_solve/custom-call.1 | solution.py:77
  27.3 9.2 %copy.15 = f32[2048,1024]{0,1:T(8,128)} copy(f32[2048,1024]{1,0:T(8,128)} %param.17) | data formatting | bytes 16777216 | tf_op args[5]
  36.5 1.4 collective-permute-start.17
  38.2 1.5 collective-permute-done.17
  39.8 2.9 %collective-permute-start.18 = (bf16[64,1024]{1,0:T(8,128)(2,1)S(1)}, bf16[64,1024]{1,0:T(8,128)(2,1)S(1)}, u32[]{:S(2)}, u32[]{:S(2)}) collective-permute-start(bf16[64,1024]{1,0:T(8,128)(2,1)S(1)} %maximum_select_fusion.2), channel_id=1, source_target_pairs={{0,64},{16,80},{32,96},{48,112},{64,0},{80,16},{96,32},{112,48},{1... | collective-permute-start | bytes 393224 | tf_op jit(solution)/shard_map/ppermute | solution.py:56
  44.1 0.7 collective-permute-start.4
  47.0 0.7 collective-permute-start.9
  47.7 0.7 collective-permute-start.13
  50.5 0.7 collective-permute-start.14
  51.2 1.3 collective-permute-start.3
  52.6 1.3 collective-permute-start.7
  53.9 1.3 collective-permute-start.11
  55.3 1.3 collective-permute-start.15
  56.6 9.5 %collective-permute-done.3 = bf16[512,128]{0,1:T(8,128)(2,1)S(1)} collective-permute-done((bf16[512,128]{0,1:T(8,128)(2,1)S(1)}, bf16[512,128]{0,1:T(8,128)(2,1)S(1)}, u32[]{:S(2)}, u32[]{:S(2)}) %collective-permute-start.3) | collective-permute-done | bytes 131104 | tf_op jit(solution)/shard_map/ppermute | solution.py:14
  66.1 5.9 %collective-permute-done.7 = bf16[512,128]{0,1:T(8,128)(2,1)S(1)} collective-permute-done((bf16[512,128]{0,1:T(8,128)(2,1)S(1)}, bf16[512,128]{0,1:T(8,128)(2,1)S(1)}, u32[]{:S(2)}, u32[]{:S(2)}) %collective-permute-start.7) | collective-permute-done | bytes 131104 | tf_op jit(solution)/shard_map/ppermute | solution.py:14
  72.0 1.4 collective-permute-done.11
  73.4 1.4 collective-permute-done.15
  75.1 0.8 fusion.49
  75.9 11.5 %collective-permute-start.41 = (f32[128,128]{1,0:T(8,128)S(1)}, f32[128,128]{1,0:T(8,128)S(1)}, u32[]{:S(2)}, u32[]{:S(2)}) collective-permute-start(f32[128,128]{1,0:T(8,128)S(1)} %fusion.8), channel_id=1, source_target_pairs={{0,16},{16,0},{32,48},{48,32},{64,80},{80,64},{96,112},{112,96},{1... | collective-permute-start | bytes 196616 | tf_op jit(solution)/shard_map/ppermute | solution.py:30
  87.4 0.9 collective-permute-start.38
  88.3 1.6 convolution_subtract_fusion
  89.9 1.1 convolution_convert_fusion
  91.7 1.7 collective-permute-start.42
  93.4 4.6 %fusion.50 = f32[2048,1024]{0,1:T(8,128)} fusion(bf16[128,1024]{1,0:T(8,128)(2,1)S(1)} %maximum_select_fusion, bf16[512,128]{0,1:T(8,128)(2,1)S(1)} %broadcast_select_fusion.28, bf16[512,128]{0,1:T(8,128)(2,1)S(1)} %broadcast_select_fusion.29, bf16[512,128]{0,1:T(8,128)(2,1)S(1)} %broadcast_select_fusion.30, bf16[512,128]{0,1:T(8,128)(2,1)S(1)} %broadcast_select_fusion.31), kind=kOutput, calls=%fused_computation.138 | convolution fusion | flops 538968064 | bytes 9175040 | tf_op jit(solution)/shard_map/dot_general | solution.py:139
  98.0 1.8 collective-permute-start.43
  100.6 0.7 collective-permute-start.27
  101.3 1.5 collective-permute-done.43
  106.4 0.7 collective-permute-start.28
  107.1 0.7 collective-permute-start.32
  107.8 1.6 collective-permute-done.39
  110.9 1.3 collective-permute-start.47
  112.2 16.7 %collective-permute-done.47 = f32[128,128]{1,0:T(8,128)S(1)} collective-permute-done((f32[128,128]{1,0:T(8,128)S(1)}, f32[128,128]{1,0:T(8,128)S(1)}, u32[]{:S(2)}, u32[]{:S(2)}) %collective-permute-start.47) | collective-permute-done | bytes 65568 | tf_op jit(solution)/shard_map/ppermute | solution.py:14
  128.9 6.3 %collective-permute-start.40 = (f32[1,16,1024]{2,1,0:T(8,128)S(1)}, f32[1,16,1024]{2,1,0:T(8,128)S(1)}, u32[]{:S(2)}, u32[]{:S(2)}) collective-permute-start(f32[1,16,1024]{2,1,0:T(8,128)S(1)} %slice_select_fusion.8), channel_id=1, source_target_pairs={{0,16},{16,0},{32,48},{48,32},{64,80},{80,64},{96,112},{112,96},{1... | collective-permute-start | bytes 196616 | tf_op jit(solution)/shard_map/ppermute | solution.py:46
  136.2 0.8 collective-permute-start.25
  138.1 0.7 collective-permute-start.29
  140.9 1.3 collective-permute-start.51
  142.4 12.4 %collective-permute-done.51 = bf16[16,128]{1,0:T(8,128)(2,1)S(1)} collective-permute-done((bf16[16,128]{1,0:T(8,128)(2,1)S(1)}, bf16[16,128]{1,0:T(8,128)(2,1)S(1)}, u32[]{:S(2)}, u32[]{:S(2)}) %collective-permute-start.51) | collective-permute-done | bytes 4128 | tf_op jit(solution)/shard_map/ppermute | solution.py:14
  154.8 1.3 collective-permute-start.22
  156.1 4.0 %collective-permute-start.55 = (f32[128,128]{1,0:T(8,128)S(1)}, f32[128,128]{1,0:T(8,128)S(1)}, u32[]{:S(2)}, u32[]{:S(2)}) collective-permute-start(f32[128,128]{1,0:T(8,128)S(1)} %fusion.41), channel_id=1, source_target_pairs={{0,16},{16,0},{32,48},{48,32},{64,80},{80,64},{96,112},{112,96},{1... | collective-permute-start | bytes 196616 | tf_op jit(solution)/shard_map/ppermute | solution.py:30
  160.9 1.3 collective-permute-start.26
  162.2 1.3 collective-permute-start.30
  163.6 1.3 collective-permute-start.34
  165.4 3.3 %collective-permute-done.56 = f32[128,128]{1,0:T(8,128)S(1)} collective-permute-done((f32[128,128]{1,0:T(8,128)S(1)}, f32[128,128]{1,0:T(8,128)S(1)}, u32[]{:S(2)}, u32[]{:S(2)}) %collective-permute-start.56) | collective-permute-done | bytes 65568 | tf_op jit(solution)/shard_map/ppermute | solution.py:30
  168.7 3.3 %collective-permute-start.57 = (f32[128,128]{1,0:T(8,128)S(1)}, f32[128,128]{1,0:T(8,128)S(1)}, u32[]{:S(2)}, u32[]{:S(2)}) collective-permute-start(f32[128,128]{1,0:T(8,128)S(1)} %add.100), channel_id=1, source_target_pairs={{0,64},{16,80},{32,96},{48,112},{64,0},{80,16},{96,32},{112,48},{1... | collective-permute-start | bytes 196616 | tf_op jit(solution)/shard_map/ppermute | solution.py:30
  172.0 0.7 collective-permute-done.30
  172.7 2.8 %collective-permute-done.34 = bf16[512,128]{0,1:T(8,128)(2,1)S(1)} collective-permute-done((bf16[512,128]{0,1:T(8,128)(2,1)S(1)}, bf16[512,128]{0,1:T(8,128)(2,1)S(1)}, u32[]{:S(2)}, u32[]{:S(2)}) %collective-permute-start.34) | collective-permute-done | bytes 131104 | tf_op jit(solution)/shard_map/ppermute | solution.py:14
  175.9 0.7 collective-permute-start.58
  176.6 7.1 %subtract_subtract_fusion = bf16[2048,1024]{0,1:T(8,128)(2,1)S(1)} fusion(f32[2048,1024]{0,1:T(8,128)} %copy.15, f32[2048,1024]{0,1:T(8,128)} %fusion.50, bf16[64,1024]{1,0:T(8,128)(2,1)S(1)} %maximum_select_fusion.3, bf16[64,1024]{1,0:T(8,128)(2,1)S(1)} %collective-permute-done.37, pred[]{:T(512)S(6)} %eq.62, ...), kind=kOutput, calls=%fused_computation | convolution fusion | flops 546439168 | bytes 21757952 | tf_op jit(solution)/shard_map/dot_general | solution.py:158
  184.4 0.7 fusion.48
  185.1 2.6 %collective-permute-done.59 = f32[128,128]{1,0:T(8,128)S(1)} collective-permute-done((f32[128,128]{1,0:T(8,128)S(1)}, f32[128,128]{1,0:T(8,128)S(1)}, u32[]{:S(2)}, u32[]{:S(2)}) %collective-permute-start.59) | collective-permute-done | bytes 65568 | tf_op jit(solution)/shard_map/ppermute | solution.py:30
  187.7 3.3 %collective-permute-start.60 = (f32[128,128]{1,0:T(8,128)S(1)}, f32[128,128]{1,0:T(8,128)S(1)}, u32[]{:S(2)}, u32[]{:S(2)}) collective-permute-start(f32[128,128]{1,0:T(8,128)S(1)} %add.103), channel_id=1, source_target_pairs={{0,64},{16,80},{32,96},{48,112},{64,0},{80,16},{96,32},{112,48},{1... | collective-permute-start | bytes 196616 | tf_op jit(solution)/shard_map/ppermute | solution.py:30
  191.2 1.4 collective-permute-done.60
  193.9 3.0 %collective-permute-start.52 = (f32[4,16,1024]{2,1,0:T(8,128)S(1)}, f32[4,16,1024]{2,1,0:T(8,128)S(1)}, u32[]{:S(2)}, u32[]{:S(2)}) collective-permute-start(f32[4,16,1024]{2,1,0:T(8,128)S(1)} %bitcast.59), channel_id=1, source_target_pairs={{0,64},{16,80},{32,96},{48,112},{64,0},{80,16},{96,32},{112,48},{1... | collective-permute-start | bytes 786440 | tf_op jit(solution)/shard_map/ppermute | solution.py:46
  197.6 2.5 %pad_maximum_fusion = bf16[2048,1024]{0,1:T(8,128)(2,1)} fusion(bf16[2048,128]{0,1:T(8,128)(2,1)S(1)} %fusion.4, bf16[2048,896]{0,1:T(8,128)(2,1)S(1)} %slice.188), kind=kLoop, calls=%fused_computation.2 | loop fusion | flops 8388608 | bytes 8388608 | tf_op jit(solution)/shard_map/concatenate | solution.py:171
  200.1 6.4 %copy.19 = bf16[2048,1024]{1,0:T(8,128)(2,1)} copy(bf16[2048,1024]{0,1:T(8,128)(2,1)} %pad_maximum_fusion) | data formatting | bytes 8388608
  207.4 1.3 collective-permute-start.64
  208.7 2.5 %collective-permute-done.53 = f32[2,16,1024]{2,1,0:T(8,128)S(1)} collective-permute-done((f32[2,16,1024]{2,1,0:T(8,128)S(1)}, f32[2,16,1024]{2,1,0:T(8,128)S(1)}, u32[]{:S(2)}, u32[]{:S(2)}) %collective-permute-start.53) | collective-permute-done | bytes 131104 | tf_op jit(solution)/shard_map/ppermute | solution.py:46
  211.3 3.5 %collective-permute-start.54 = (f32[1,16,1024]{2,1,0:T(8,128)S(1)}, f32[1,16,1024]{2,1,0:T(8,128)S(1)}, u32[]{:S(2)}, u32[]{:S(2)}) collective-permute-start(f32[1,16,1024]{2,1,0:T(8,128)S(1)} %slice_select_fusion.7), channel_id=1, source_target_pairs={{0,16},{16,0},{32,48},{48,32},{64,80},{80,64},{96,112},{112,96},{1... | collective-permute-start | bytes 196616 | tf_op jit(solution)/shard_map/ppermute | solution.py:46
  (194 shorter events, 25.2 us)
Async XLA Ops:
  0.6 37.3 %collective-permute-start.35 = (bf16[16,1024]{1,0:T(8,128)(2,1)}, bf16[16,1024]{1,0:T(8,128)(2,1)S(1)}, u32[]{:S(2)}, u32[]{:S(2)}) collective-permute-start(bf16[16,1024]{1,0:T(8,128)(2,1)} %param.13), channel_id=1, source_target_pairs={{0,16},{16,0},{32,48},{48,32},{64,80},{80,64},{96,112},{112,96},{1... | collective-permute-start | bytes 98312 | tf_op jit(solution)/shard_map/ppermute | solution.py:56
  2.1 34.4 %collective-permute-start.16 = (bf16[16,1024]{1,0:T(8,128)(2,1)}, bf16[16,1024]{1,0:T(8,128)(2,1)S(1)}, u32[]{:S(2)}, u32[]{:S(2)}) collective-permute-start(bf16[16,1024]{1,0:T(8,128)(2,1)} %param.14), channel_id=1, source_target_pairs={{0,16},{16,0},{32,48},{48,32},{64,80},{80,64},{96,112},{112,96},{1... | collective-permute-start | bytes 98312 | tf_op jit(solution)/shard_map/ppermute | solution.py:56
  15.5 27.2 %collective-permute-start = (bf16[512,128]{0,1:T(8,128)(2,1)S(1)}, bf16[512,128]{0,1:T(8,128)(2,1)S(1)}, u32[]{:S(2)}, u32[]{:S(2)}) collective-permute-start(bf16[512,128]{0,1:T(8,128)(2,1)S(1)} %split.32), channel_id=1, source_target_pairs={{15,14},{31,30},{47,46},{63,62},{79,78},{95,94},{111,110},{127,126}} | collective-permute-start | bytes 393224 | tf_op jit(solution)/shard_map/ppermute | solution.py:14
  36.5 3.2 %collective-permute-start.17 = (bf16[32,1024]{1,0:T(8,128)(2,1)S(1)}, bf16[32,1024]{1,0:T(8,128)(2,1)S(1)}, u32[]{:S(2)}, u32[]{:S(2)}) collective-permute-start(bf16[32,1024]{1,0:T(8,128)(2,1)S(1)} %maximum_select_fusion.4), channel_id=1, source_target_pairs={{0,32},{16,48},{32,0},{48,16},{64,96},{80,112},{96,64},{112,80},{1... | collective-permute-start | bytes 196616 | tf_op jit(solution)/shard_map/ppermute | solution.py:56
  37.9 6.8 %collective-permute-start.36 = (bf16[32,1024]{1,0:T(8,128)(2,1)S(1)}, bf16[32,1024]{1,0:T(8,128)(2,1)S(1)}, u32[]{:S(2)}, u32[]{:S(2)}) collective-permute-start(bf16[32,1024]{1,0:T(8,128)(2,1)S(1)} %maximum_select_fusion.5), channel_id=1, source_target_pairs={{0,32},{16,48},{32,0},{48,16},{64,96},{80,112},{96,64},{112,80},{1... | collective-permute-start | bytes 196616 | tf_op jit(solution)/shard_map/ppermute | solution.py:56
  39.8 5.8 %collective-permute-start.18 = (bf16[64,1024]{1,0:T(8,128)(2,1)S(1)}, bf16[64,1024]{1,0:T(8,128)(2,1)S(1)}, u32[]{:S(2)}, u32[]{:S(2)}) collective-permute-start(bf16[64,1024]{1,0:T(8,128)(2,1)S(1)} %maximum_select_fusion.2), channel_id=1, source_target_pairs={{0,64},{16,80},{32,96},{48,112},{64,0},{80,16},{96,32},{112,48},{1... | collective-permute-start | bytes 393224 | tf_op jit(solution)/shard_map/ppermute | solution.py:56
  42.7 3.5 %collective-permute-start.12 = (bf16[512,128]{0,1:T(8,128)(2,1)S(1)}, bf16[512,128]{0,1:T(8,128)(2,1)S(1)}, u32[]{:S(2)}, u32[]{:S(2)}) collective-permute-start(bf16[512,128]{0,1:T(8,128)(2,1)S(1)} %get-tuple-element.23), channel_id=1, source_target_pairs={{15,14},{31,30},{47,46},{63,62},{79,78},{95,94},{111,110},{127,126}} | collective-permute-start | bytes 393224 | tf_op jit(solution)/shard_map/ppermute | solution.py:14
  43.4 2.9 %collective-permute-start.8 = (bf16[512,128]{0,1:T(8,128)(2,1)S(1)}, bf16[512,128]{0,1:T(8,128)(2,1)S(1)}, u32[]{:S(2)}, u32[]{:S(2)}) collective-permute-start(bf16[512,128]{0,1:T(8,128)(2,1)S(1)} %get-tuple-element.24), channel_id=1, source_target_pairs={{15,14},{31,30},{47,46},{63,62},{79,78},{95,94},{111,110},{127,126}} | collective-permute-start | bytes 393224 | tf_op jit(solution)/shard_map/ppermute | solution.py:14
  44.1 2.2 %collective-permute-start.4 = (bf16[512,128]{0,1:T(8,128)(2,1)S(1)}, bf16[512,128]{0,1:T(8,128)(2,1)S(1)}, u32[]{:S(2)}, u32[]{:S(2)}) collective-permute-start(bf16[512,128]{0,1:T(8,128)(2,1)S(1)} %get-tuple-element.25), channel_id=1, source_target_pairs={{15,14},{31,30},{47,46},{63,62},{79,78},{95,94},{111,110},{127,126}} | collective-permute-start | bytes 393224 | tf_op jit(solution)/shard_map/ppermute | solution.py:14
  44.8 111.3 %collective-permute-start.37 = (bf16[64,1024]{1,0:T(8,128)(2,1)S(1)}, bf16[64,1024]{1,0:T(8,128)(2,1)S(1)}, u32[]{:S(2)}, u32[]{:S(2)}) collective-permute-start(bf16[64,1024]{1,0:T(8,128)(2,1)S(1)} %maximum_select_fusion.3), channel_id=1, source_target_pairs={{0,64},{16,80},{32,96},{48,112},{64,0},{80,16},{96,32},{112,48},{1... | collective-permute-start | bytes 393224 | tf_op jit(solution)/shard_map/ppermute | solution.py:56
  45.5 2.8 %collective-permute-start.1 = (bf16[512,128]{0,1:T(8,128)(2,1)S(1)}, bf16[512,128]{0,1:T(8,128)(2,1)S(1)}, u32[]{:S(2)}, u32[]{:S(2)}) collective-permute-start(bf16[512,128]{0,1:T(8,128)(2,1)S(1)} %get-tuple-element.22), channel_id=1, source_target_pairs={{15,13},{14,12},{31,29},{30,28},{47,45},{46,44},{63,61},{62,60},{7... | collective-permute-start | bytes 393224 | tf_op jit(solution)/shard_map/ppermute | solution.py:14
  46.3 2.7 %collective-permute-start.5 = (bf16[512,128]{0,1:T(8,128)(2,1)S(1)}, bf16[512,128]{0,1:T(8,128)(2,1)S(1)}, u32[]{:S(2)}, u32[]{:S(2)}) collective-permute-start(bf16[512,128]{0,1:T(8,128)(2,1)S(1)} %get-tuple-element.26), channel_id=1, source_target_pairs={{15,13},{14,12},{31,29},{30,28},{47,45},{46,44},{63,61},{62,60},{7... | collective-permute-start | bytes 393224 | tf_op jit(solution)/shard_map/ppermute | solution.py:14
  47.0 2.8 %collective-permute-start.9 = (bf16[512,128]{0,1:T(8,128)(2,1)S(1)}, bf16[512,128]{0,1:T(8,128)(2,1)S(1)}, u32[]{:S(2)}, u32[]{:S(2)}) collective-permute-start(bf16[512,128]{0,1:T(8,128)(2,1)S(1)} %get-tuple-element.27), channel_id=1, source_target_pairs={{15,13},{14,12},{31,29},{30,28},{47,45},{46,44},{63,61},{62,60},{7... | collective-permute-start | bytes 393224 | tf_op jit(solution)/shard_map/ppermute | solution.py:14
  47.7 2.8 %collective-permute-start.13 = (bf16[512,128]{0,1:T(8,128)(2,1)S(1)}, bf16[512,128]{0,1:T(8,128)(2,1)S(1)}, u32[]{:S(2)}, u32[]{:S(2)}) collective-permute-start(bf16[512,128]{0,1:T(8,128)(2,1)S(1)} %get-tuple-element.28), channel_id=1, source_target_pairs={{15,13},{14,12},{31,29},{30,28},{47,45},{46,44},{63,61},{62,60},{7... | collective-permute-start | bytes 393224 | tf_op jit(solution)/shard_map/ppermute | solution.py:14
  48.4 2.8 %collective-permute-start.2 = (bf16[512,128]{0,1:T(8,128)(2,1)S(1)}, bf16[512,128]{0,1:T(8,128)(2,1)S(1)}, u32[]{:S(2)}, u32[]{:S(2)}) collective-permute-start(bf16[512,128]{0,1:T(8,128)(2,1)S(1)} %broadcast_select_fusion.23), channel_id=1, source_target_pairs={{15,11},{14,10},{13,9},{12,8},{31,27},{30,26},{29,25},{28,24},{47,... | collective-permute-start | bytes 393224 | tf_op jit(solution)/shard_map/ppermute | solution.py:14
  49.1 3.4 %collective-permute-start.6 = (bf16[512,128]{0,1:T(8,128)(2,1)S(1)}, bf16[512,128]{0,1:T(8,128)(2,1)S(1)}, u32[]{:S(2)}, u32[]{:S(2)}) collective-permute-start(bf16[512,128]{0,1:T(8,128)(2,1)S(1)} %broadcast_select_fusion.22), channel_id=1, source_target_pairs={{15,11},{14,10},{13,9},{12,8},{31,27},{30,26},{29,25},{28,24},{47,... | collective-permute-start | bytes 393224 | tf_op jit(solution)/shard_map/ppermute | solution.py:14
  49.8 4.1 %collective-permute-start.10 = (bf16[512,128]{0,1:T(8,128)(2,1)S(1)}, bf16[512,128]{0,1:T(8,128)(2,1)S(1)}, u32[]{:S(2)}, u32[]{:S(2)}) collective-permute-start(bf16[512,128]{0,1:T(8,128)(2,1)S(1)} %broadcast_select_fusion.21), channel_id=1, source_target_pairs={{15,11},{14,10},{13,9},{12,8},{31,27},{30,26},{29,25},{28,24},{47,... | collective-permute-start | bytes 393224 | tf_op jit(solution)/shard_map/ppermute | solution.py:14
  50.5 4.7 %collective-permute-start.14 = (bf16[512,128]{0,1:T(8,128)(2,1)S(1)}, bf16[512,128]{0,1:T(8,128)(2,1)S(1)}, u32[]{:S(2)}, u32[]{:S(2)}) collective-permute-start(bf16[512,128]{0,1:T(8,128)(2,1)S(1)} %broadcast_select_fusion.20), channel_id=1, source_target_pairs={{15,11},{14,10},{13,9},{12,8},{31,27},{30,26},{29,25},{28,24},{47,... | collective-permute-start | bytes 393224 | tf_op jit(solution)/shard_map/ppermute | solution.py:14
  51.2 14.8 %collective-permute-start.3 = (bf16[512,128]{0,1:T(8,128)(2,1)S(1)}, bf16[512,128]{0,1:T(8,128)(2,1)S(1)}, u32[]{:S(2)}, u32[]{:S(2)}) collective-permute-start(bf16[512,128]{0,1:T(8,128)(2,1)S(1)} %broadcast_select_fusion.27), channel_id=1, source_target_pairs={{15,7},{14,6},{13,5},{12,4},{11,3},{10,2},{9,1},{8,0},{31,23},{30,... | collective-permute-start | bytes 393224 | tf_op jit(solution)/shard_map/ppermute | solution.py:14
  52.6 19.3 %collective-permute-start.7 = (bf16[512,128]{0,1:T(8,128)(2,1)S(1)}, bf16[512,128]{0,1:T(8,128)(2,1)S(1)}, u32[]{:S(2)}, u32[]{:S(2)}) collective-permute-start(bf16[512,128]{0,1:T(8,128)(2,1)S(1)} %broadcast_select_fusion.26), channel_id=1, source_target_pairs={{15,7},{14,6},{13,5},{12,4},{11,3},{10,2},{9,1},{8,0},{31,23},{30,... | collective-permute-start | bytes 393224 | tf_op jit(solution)/shard_map/ppermute | solution.py:14
  53.9 19.4 %collective-permute-start.11 = (bf16[512,128]{0,1:T(8,128)(2,1)S(1)}, bf16[512,128]{0,1:T(8,128)(2,1)S(1)}, u32[]{:S(2)}, u32[]{:S(2)}) collective-permute-start(bf16[512,128]{0,1:T(8,128)(2,1)S(1)} %broadcast_select_fusion.25), channel_id=1, source_target_pairs={{15,7},{14,6},{13,5},{12,4},{11,3},{10,2},{9,1},{8,0},{31,23},{30,... | collective-permute-start | bytes 393224 | tf_op jit(solution)/shard_map/ppermute | solution.py:14
  55.3 19.5 %collective-permute-start.15 = (bf16[512,128]{0,1:T(8,128)(2,1)S(1)}, bf16[512,128]{0,1:T(8,128)(2,1)S(1)}, u32[]{:S(2)}, u32[]{:S(2)}) collective-permute-start(bf16[512,128]{0,1:T(8,128)(2,1)S(1)} %broadcast_select_fusion.24), channel_id=1, source_target_pairs={{15,7},{14,6},{13,5},{12,4},{11,3},{10,2},{9,1},{8,0},{31,23},{30,... | collective-permute-start | bytes 393224 | tf_op jit(solution)/shard_map/ppermute | solution.py:14
  75.9 15.8 %collective-permute-start.41 = (f32[128,128]{1,0:T(8,128)S(1)}, f32[128,128]{1,0:T(8,128)S(1)}, u32[]{:S(2)}, u32[]{:S(2)}) collective-permute-start(f32[128,128]{1,0:T(8,128)S(1)} %fusion.8), channel_id=1, source_target_pairs={{0,16},{16,0},{32,48},{48,32},{64,80},{80,64},{96,112},{112,96},{1... | collective-permute-start | bytes 196616 | tf_op jit(solution)/shard_map/ppermute | solution.py:30
  87.4 16.0 %collective-permute-start.38 = (f32[4,16,1024]{2,1,0:T(8,128)S(1)}, f32[4,16,1024]{2,1,0:T(8,128)S(1)}, u32[]{:S(2)}, u32[]{:S(2)}) collective-permute-start(f32[4,16,1024]{2,1,0:T(8,128)S(1)} %bitcast.58), channel_id=1, source_target_pairs={{0,64},{16,80},{32,96},{48,112},{64,0},{80,16},{96,32},{112,48},{1... | collective-permute-start | bytes 786440 | tf_op jit(solution)/shard_map/ppermute | solution.py:46
  91.0 8.9 %collective-permute-start.19 = (bf16[512,128]{0,1:T(8,128)(2,1)S(1)}, bf16[512,128]{0,1:T(8,128)(2,1)S(1)}, u32[]{:S(2)}, u32[]{:S(2)}) collective-permute-start(bf16[512,128]{0,1:T(8,128)(2,1)S(1)} %split.36), channel_id=1, source_target_pairs={{14,15},{30,31},{46,47},{62,63},{78,79},{94,95},{110,111},{126,127}} | collective-permute-start | bytes 393224 | tf_op jit(solution)/shard_map/ppermute | solution.py:14
  91.7 6.3 %collective-permute-start.42 = (f32[128,128]{1,0:T(8,128)S(1)}, f32[128,128]{1,0:T(8,128)S(1)}, u32[]{:S(2)}, u32[]{:S(2)}) collective-permute-start(f32[128,128]{1,0:T(8,128)S(1)} %add.90), channel_id=1, source_target_pairs={{0,32},{16,48},{32,0},{48,16},{64,96},{80,112},{96,64},{112,80},{1... | collective-permute-start | bytes 196616 | tf_op jit(solution)/shard_map/ppermute | solution.py:30
  98.0 4.7 %collective-permute-start.43 = (f32[128,128]{1,0:T(8,128)S(1)}, f32[128,128]{1,0:T(8,128)S(1)}, u32[]{:S(2)}, u32[]{:S(2)}) collective-permute-start(f32[128,128]{1,0:T(8,128)S(1)} %add.91), channel_id=1, source_target_pairs={{0,64},{16,80},{32,96},{48,112},{64,0},{80,16},{96,32},{112,48},{1... | collective-permute-start | bytes 196616 | tf_op jit(solution)/shard_map/ppermute | solution.py:30
  99.9 5.0 %collective-permute-start.31 = (bf16[512,128]{0,1:T(8,128)(2,1)S(1)}, bf16[512,128]{0,1:T(8,128)(2,1)S(1)}, u32[]{:S(2)}, u32[]{:S(2)}) collective-permute-start(bf16[512,128]{0,1:T(8,128)(2,1)S(1)} %get-tuple-element.16), channel_id=1, source_target_pairs={{14,15},{30,31},{46,47},{62,63},{78,79},{94,95},{110,111},{126,127}} | collective-permute-start | bytes 393224 | tf_op jit(solution)/shard_map/ppermute | solution.py:14
  100.6 5.0 %collective-permute-start.27 = (bf16[512,128]{0,1:T(8,128)(2,1)S(1)}, bf16[512,128]{0,1:T(8,128)(2,1)S(1)}, u32[]{:S(2)}, u32[]{:S(2)}) collective-permute-start(bf16[512,128]{0,1:T(8,128)(2,1)S(1)} %get-tuple-element.17), channel_id=1, source_target_pairs={{14,15},{30,31},{46,47},{62,63},{78,79},{94,95},{110,111},{126,127}} | collective-permute-start | bytes 393224 | tf_op jit(solution)/shard_map/ppermute | solution.py:14
  102.7 2.9 %collective-permute-start.23 = (bf16[512,128]{0,1:T(8,128)(2,1)S(1)}, bf16[512,128]{0,1:T(8,128)(2,1)S(1)}, u32[]{:S(2)}, u32[]{:S(2)}) collective-permute-start(bf16[512,128]{0,1:T(8,128)(2,1)S(1)} %get-tuple-element.18), channel_id=1, source_target_pairs={{14,15},{30,31},{46,47},{62,63},{78,79},{94,95},{110,111},{126,127}} | collective-permute-start | bytes 393224 | tf_op jit(solution)/shard_map/ppermute | solution.py:14
  103.4 0.7 collective-permute-start.44
  104.2 2.2 %collective-permute-start.20 = (bf16[512,128]{0,1:T(8,128)(2,1)S(1)}, bf16[512,128]{0,1:T(8,128)(2,1)S(1)}, u32[]{:S(2)}, u32[]{:S(2)}) collective-permute-start(bf16[512,128]{0,1:T(8,128)(2,1)S(1)} %get-tuple-element.15), channel_id=1, source_target_pairs={{14,12},{15,13},{30,28},{31,29},{46,44},{47,45},{62,60},{63,61},{7... | collective-permute-start | bytes 393224 | tf_op jit(solution)/shard_map/ppermute | solution.py:14
  104.9 2.2 %collective-permute-start.45 = (f32[128,128]{1,0:T(8,128)S(1)}, f32[128,128]{1,0:T(8,128)S(1)}, u32[]{:S(2)}, u32[]{:S(2)}) collective-permute-start(f32[128,128]{1,0:T(8,128)S(1)} %broadcast_select_fusion.35), channel_id=1, source_target_pairs={{15,13},{14,12},{31,29},{30,28},{47,45},{46,44},{63,61},{62,60},{7... | collective-permute-start | bytes 196616 | tf_op jit(solution)/shard_map/ppermute | solution.py:14
  105.6 3.9 %collective-permute-start.39 = (f32[2,16,1024]{2,1,0:T(8,128)S(1)}, f32[2,16,1024]{2,1,0:T(8,128)S(1)}, u32[]{:S(2)}, u32[]{:S(2)}) collective-permute-start(f32[2,16,1024]{2,1,0:T(8,128)S(1)} %slice_select_fusion.6), channel_id=1, source_target_pairs={{0,32},{16,48},{32,0},{48,16},{64,96},{80,112},{96,64},{112,80},{1... | collective-permute-start | bytes 393224 | tf_op jit(solution)/shard_map/ppermute | solution.py:46
  105.7 4.4 %collective-permute-start.24 = (bf16[512,128]{0,1:T(8,128)(2,1)S(1)}, bf16[512,128]{0,1:T(8,128)(2,1)S(1)}, u32[]{:S(2)}, u32[]{:S(2)}) collective-permute-start(bf16[512,128]{0,1:T(8,128)(2,1)S(1)} %get-tuple-element.19), channel_id=1, source_target_pairs={{14,12},{15,13},{30,28},{31,29},{46,44},{47,45},{62,60},{63,61},{7... | collective-permute-start | bytes 393224 | tf_op jit(solution)/shard_map/ppermute | solution.py:14
  106.4 31.0 %collective-permute-start.28 = (bf16[512,128]{0,1:T(8,128)(2,1)S(1)}, bf16[512,128]{0,1:T(8,128)(2,1)S(1)}, u32[]{:S(2)}, u32[]{:S(2)}) collective-permute-start(bf16[512,128]{0,1:T(8,128)(2,1)S(1)} %get-tuple-element.20), channel_id=1, source_target_pairs={{14,12},{15,13},{30,28},{31,29},{46,44},{47,45},{62,60},{63,61},{7... | collective-permute-start | bytes 393224 | tf_op jit(solution)/shard_map/ppermute | solution.py:14
  107.1 31.7 %collective-permute-start.32 = (bf16[512,128]{0,1:T(8,128)(2,1)S(1)}, bf16[512,128]{0,1:T(8,128)(2,1)S(1)}, u32[]{:S(2)}, u32[]{:S(2)}) collective-permute-start(bf16[512,128]{0,1:T(8,128)(2,1)S(1)} %get-tuple-element.21), channel_id=1, source_target_pairs={{14,12},{15,13},{30,28},{31,29},{46,44},{47,45},{62,60},{63,61},{7... | collective-permute-start | bytes 393224 | tf_op jit(solution)/shard_map/ppermute | solution.py:14
  109.5 30.7 %collective-permute-start.21 = (bf16[512,128]{0,1:T(8,128)(2,1)S(1)}, bf16[512,128]{0,1:T(8,128)(2,1)S(1)}, u32[]{:S(2)}, u32[]{:S(2)}) collective-permute-start(bf16[512,128]{0,1:T(8,128)(2,1)S(1)} %broadcast_select_fusion.7), channel_id=1, source_target_pairs={{14,10},{15,11},{12,8},{13,9},{30,26},{31,27},{28,24},{29,25},{46,... | collective-permute-start | bytes 393224 | tf_op jit(solution)/shard_map/ppermute | solution.py:14
  110.2 0.7 collective-permute-start.46
  110.9 18.0 %collective-permute-start.47 = (f32[128,128]{1,0:T(8,128)S(1)}, f32[128,128]{1,0:T(8,128)S(1)}, u32[]{:S(2)}, u32[]{:S(2)}) collective-permute-start(f32[128,128]{1,0:T(8,128)S(1)} %broadcast_select_fusion.37), channel_id=1, source_target_pairs={{15,7},{14,6},{13,5},{12,4},{11,3},{10,2},{9,1},{8,0},{31,23},{30,... | collective-permute-start | bytes 196616 | tf_op jit(solution)/shard_map/ppermute | solution.py:14
  128.9 7.2 %collective-permute-start.40 = (f32[1,16,1024]{2,1,0:T(8,128)S(1)}, f32[1,16,1024]{2,1,0:T(8,128)S(1)}, u32[]{:S(2)}, u32[]{:S(2)}) collective-permute-start(f32[1,16,1024]{2,1,0:T(8,128)S(1)} %slice_select_fusion.8), channel_id=1, source_target_pairs={{0,16},{16,0},{32,48},{48,32},{64,80},{80,64},{96,112},{112,96},{1... | collective-permute-start | bytes 196616 | tf_op jit(solution)/shard_map/ppermute | solution.py:46
  136.2 24.7 %collective-permute-start.25 = (bf16[512,128]{0,1:T(8,128)(2,1)S(1)}, bf16[512,128]{0,1:T(8,128)(2,1)S(1)}, u32[]{:S(2)}, u32[]{:S(2)}) collective-permute-start(bf16[512,128]{0,1:T(8,128)(2,1)S(1)} %broadcast_select_fusion.6), channel_id=1, source_target_pairs={{14,10},{15,11},{12,8},{13,9},{30,26},{31,27},{28,24},{29,25},{46,... | collective-permute-start | bytes 393224 | tf_op jit(solution)/shard_map/ppermute | solution.py:14
  137.4 0.7 collective-permute-start.48
  138.1 24.1 %collective-permute-start.29 = (bf16[512,128]{0,1:T(8,128)(2,1)S(1)}, bf16[512,128]{0,1:T(8,128)(2,1)S(1)}, u32[]{:S(2)}, u32[]{:S(2)}) collective-permute-start(bf16[512,128]{0,1:T(8,128)(2,1)S(1)} %broadcast_select_fusion.5), channel_id=1, source_target_pairs={{14,10},{15,11},{12,8},{13,9},{30,26},{31,27},{28,24},{29,25},{46,... | collective-permute-start | bytes 393224 | tf_op jit(solution)/shard_map/ppermute | solution.py:14
  138.8 0.7 collective-permute-start.49
  139.5 24.0 %collective-permute-start.33 = (bf16[512,128]{0,1:T(8,128)(2,1)S(1)}, bf16[512,128]{0,1:T(8,128)(2,1)S(1)}, u32[]{:S(2)}, u32[]{:S(2)}) collective-permute-start(bf16[512,128]{0,1:T(8,128)(2,1)S(1)} %broadcast_select_fusion.4), channel_id=1, source_target_pairs={{14,10},{15,11},{12,8},{13,9},{30,26},{31,27},{28,24},{29,25},{46,... | collective-permute-start | bytes 393224 | tf_op jit(solution)/shard_map/ppermute | solution.py:14
  140.9 13.8 %collective-permute-start.51 = (bf16[16,128]{1,0:T(8,128)(2,1)S(1)}, bf16[16,128]{1,0:T(8,128)(2,1)S(1)}, u32[]{:S(2)}, u32[]{:S(2)}) collective-permute-start(bf16[16,128]{1,0:T(8,128)(2,1)S(1)} %broadcast_select_fusion.40), channel_id=1, source_target_pairs={{14,6},{15,7},{12,4},{13,5},{10,2},{11,3},{8,0},{9,1},{30,22},{31,... | collective-permute-start | bytes 12296 | tf_op jit(solution)/shard_map/ppermute | solution.py:14
  154.8 10.6 %collective-permute-start.22 = (bf16[512,128]{0,1:T(8,128)(2,1)S(1)}, bf16[512,128]{0,1:T(8,128)(2,1)S(1)}, u32[]{:S(2)}, u32[]{:S(2)}) collective-permute-start(bf16[512,128]{0,1:T(8,128)(2,1)S(1)} %broadcast_select_fusion.11), channel_id=1, source_target_pairs={{14,6},{15,7},{12,4},{13,5},{10,2},{11,3},{8,0},{9,1},{30,22},{31,... | collective-permute-start | bytes 393224 | tf_op jit(solution)/shard_map/ppermute | solution.py:14
  156.1 8.8 %collective-permute-start.55 = (f32[128,128]{1,0:T(8,128)S(1)}, f32[128,128]{1,0:T(8,128)S(1)}, u32[]{:S(2)}, u32[]{:S(2)}) collective-permute-start(f32[128,128]{1,0:T(8,128)S(1)} %fusion.41), channel_id=1, source_target_pairs={{0,16},{16,0},{32,48},{48,32},{64,80},{80,64},{96,112},{112,96},{1... | collective-permute-start | bytes 196616 | tf_op jit(solution)/shard_map/ppermute | solution.py:30
  160.9 11.1 %collective-permute-start.26 = (bf16[512,128]{0,1:T(8,128)(2,1)S(1)}, bf16[512,128]{0,1:T(8,128)(2,1)S(1)}, u32[]{:S(2)}, u32[]{:S(2)}) collective-permute-start(bf16[512,128]{0,1:T(8,128)(2,1)S(1)} %broadcast_select_fusion.10), channel_id=1, source_target_pairs={{14,6},{15,7},{12,4},{13,5},{10,2},{11,3},{8,0},{9,1},{30,22},{31,... | collective-permute-start | bytes 393224 | tf_op jit(solution)/shard_map/ppermute | solution.py:14
  162.2 10.5 %collective-permute-start.30 = (bf16[512,128]{0,1:T(8,128)(2,1)S(1)}, bf16[512,128]{0,1:T(8,128)(2,1)S(1)}, u32[]{:S(2)}, u32[]{:S(2)}) collective-permute-start(bf16[512,128]{0,1:T(8,128)(2,1)S(1)} %broadcast_select_fusion.9), channel_id=1, source_target_pairs={{14,6},{15,7},{12,4},{13,5},{10,2},{11,3},{8,0},{9,1},{30,22},{31,... | collective-permute-start | bytes 393224 | tf_op jit(solution)/shard_map/ppermute | solution.py:14
  163.6 12.0 %collective-permute-start.34 = (bf16[512,128]{0,1:T(8,128)(2,1)S(1)}, bf16[512,128]{0,1:T(8,128)(2,1)S(1)}, u32[]{:S(2)}, u32[]{:S(2)}) collective-permute-start(bf16[512,128]{0,1:T(8,128)(2,1)S(1)} %broadcast_select_fusion.8), channel_id=1, source_target_pairs={{14,6},{15,7},{12,4},{13,5},{10,2},{11,3},{8,0},{9,1},{30,22},{31,... | collective-permute-start | bytes 393224 | tf_op jit(solution)/shard_map/ppermute | solution.py:14
  164.9 3.8 %collective-permute-start.56 = (f32[128,128]{1,0:T(8,128)S(1)}, f32[128,128]{1,0:T(8,128)S(1)}, u32[]{:S(2)}, u32[]{:S(2)}) collective-permute-start(f32[128,128]{1,0:T(8,128)S(1)} %add.99), channel_id=1, source_target_pairs={{0,32},{16,48},{32,0},{48,16},{64,96},{80,112},{96,64},{112,80},{1... | collective-permute-start | bytes 196616 | tf_op jit(solution)/shard_map/ppermute | solution.py:30
  168.7 22.5 %collective-permute-start.57 = (f32[128,128]{1,0:T(8,128)S(1)}, f32[128,128]{1,0:T(8,128)S(1)}, u32[]{:S(2)}, u32[]{:S(2)}) collective-permute-start(f32[128,128]{1,0:T(8,128)S(1)} %add.100), channel_id=1, source_target_pairs={{0,64},{16,80},{32,96},{48,112},{64,0},{80,16},{96,32},{112,48},{1... | collective-permute-start | bytes 196616 | tf_op jit(solution)/shard_map/ppermute | solution.py:30
  175.9 8.0 %collective-permute-start.58 = (f32[128,128]{1,0:T(8,128)S(1)}, f32[128,128]{1,0:T(8,128)S(1)}, u32[]{:S(2)}, u32[]{:S(2)}) collective-permute-start(f32[128,128]{1,0:T(8,128)S(1)} %fusion.6), channel_id=1, source_target_pairs={{0,16},{16,0},{32,48},{48,32},{64,80},{80,64},{96,112},{112,96},{1... | collective-permute-start | bytes 196616 | tf_op jit(solution)/shard_map/ppermute | solution.py:30
  183.9 3.8 %collective-permute-start.59 = (f32[128,128]{1,0:T(8,128)S(1)}, f32[128,128]{1,0:T(8,128)S(1)}, u32[]{:S(2)}, u32[]{:S(2)}) collective-permute-start(f32[128,128]{1,0:T(8,128)S(1)} %add.102), channel_id=1, source_target_pairs={{0,32},{16,48},{32,0},{48,16},{64,96},{80,112},{96,64},{112,80},{1... | collective-permute-start | bytes 196616 | tf_op jit(solution)/shard_map/ppermute | solution.py:30
  187.7 4.9 %collective-permute-start.60 = (f32[128,128]{1,0:T(8,128)S(1)}, f32[128,128]{1,0:T(8,128)S(1)}, u32[]{:S(2)}, u32[]{:S(2)}) collective-permute-start(f32[128,128]{1,0:T(8,128)S(1)} %add.103), channel_id=1, source_target_pairs={{0,64},{16,80},{32,96},{48,112},{64,0},{80,16},{96,32},{112,48},{1... | collective-permute-start | bytes 196616 | tf_op jit(solution)/shard_map/ppermute | solution.py:30
  192.6 4.3 %collective-permute-start.61 = (f32[128,128]{1,0:T(8,128)S(1)}, f32[128,128]{1,0:T(8,128)S(1)}, u32[]{:S(2)}, u32[]{:S(2)}) collective-permute-start(f32[128,128]{1,0:T(8,128)S(1)} %add_add_fusion), channel_id=1, source_target_pairs={{14,15},{30,31},{46,47},{62,63},{78,79},{94,95},{110,111},{126,127}} | collective-permute-start | bytes 196616 | tf_op jit(solution)/shard_map/ppermute | solution.py:14
  193.9 12.7 %collective-permute-start.52 = (f32[4,16,1024]{2,1,0:T(8,128)S(1)}, f32[4,16,1024]{2,1,0:T(8,128)S(1)}, u32[]{:S(2)}, u32[]{:S(2)}) collective-permute-start(f32[4,16,1024]{2,1,0:T(8,128)S(1)} %bitcast.59), channel_id=1, source_target_pairs={{0,64},{16,80},{32,96},{48,112},{64,0},{80,16},{96,32},{112,48},{1... | collective-permute-start | bytes 786440 | tf_op jit(solution)/shard_map/ppermute | solution.py:46
  196.9 9.7 %collective-permute-start.62 = (f32[128,128]{1,0:T(8,128)S(1)}, f32[128,128]{1,0:T(8,128)S(1)}, u32[]{:S(2)}, u32[]{:S(2)}) collective-permute-start(f32[128,128]{1,0:T(8,128)S(1)} %broadcast_select_fusion.32), channel_id=1, source_target_pairs={{14,12},{15,13},{30,28},{31,29},{46,44},{47,45},{62,60},{63,61},{7... | collective-permute-start | bytes 196616 | tf_op jit(solution)/shard_map/ppermute | solution.py:14
  206.6 0.8 collective-permute-start.63
  207.3 3.9 %collective-permute-start.53 = (f32[2,16,1024]{2,1,0:T(8,128)S(1)}, f32[2,16,1024]{2,1,0:T(8,128)S(1)}, u32[]{:S(2)}, u32[]{:S(2)}) collective-permute-start(f32[2,16,1024]{2,1,0:T(8,128)S(1)} %slice_select_fusion.5), channel_id=1, source_target_pairs={{0,32},{16,48},{32,0},{48,16},{64,96},{80,112},{96,64},{112,80},{1... | collective-permute-start | bytes 393224 | tf_op jit(solution)/shard_map/ppermute | solution.py:46
  207.4 7.3 %collective-permute-start.64 = (f32[128,128]{1,0:T(8,128)S(1)}, f32[128,128]{1,0:T(8,128)S(1)}, u32[]{:S(2)}, u32[]{:S(2)}) collective-permute-start(f32[128,128]{1,0:T(8,128)S(1)} %broadcast_select_fusion.34), channel_id=1, source_target_pairs={{14,6},{15,7},{12,4},{13,5},{10,2},{11,3},{8,0},{9,1},{30,22},{31,... | collective-permute-start | bytes 196616 | tf_op jit(solution)/shard_map/ppermute | solution.py:14
  211.3 4.4 %collective-permute-start.54 = (f32[1,16,1024]{2,1,0:T(8,128)S(1)}, f32[1,16,1024]{2,1,0:T(8,128)S(1)}, u32[]{:S(2)}, u32[]{:S(2)}) collective-permute-start(f32[1,16,1024]{2,1,0:T(8,128)S(1)} %slice_select_fusion.7), channel_id=1, source_target_pairs={{0,16},{16,0},{32,48},{48,32},{64,80},{80,64},{96,112},{112,96},{1... | collective-permute-start | bytes 196616 | tf_op jit(solution)/shard_map/ppermute | solution.py:46
  (13 other events, 297.3 us)

commit v3 on v1

--- a/solution.py
+++ b/solution.py
@@ -1,9 +1,88 @@
+import functools
+
 import jax
 import jax.numpy as jnp
 from jax import lax
+from jax.experimental import pallas as pl
+from jax.experimental.pallas import tpu as pltpu
 from jax.sharding import PartitionSpec as P
 
 exact_mode = lax.Precision.HIGHEST
+
+
+def broadcast_kernel(root, size, chunks, x_ref, y_ref, buf, recv_sem, send_sem):
+    bits = size.bit_length() - 1
+    me = lax.axis_index("col")
+    row = lax.axis_index("row")
+    rel_bits = []
+    for j in range(bits):
+        b = (me // (1 << j)) % 2
+        rel_bits.append(1 - b if (root >> j) & 1 else b)
+    is_root = sum(rel_bits) == 0
+    sends = []
+    for j in range(bits):
+        above = sum(rel_bits[j:]) if j < bits else 0
+        sends.append(above == 0)
+    rows = x_ref.shape[0] // chunks
+
+    def child(j):
+        b = (me // (1 << j)) % 2
+        return me + (1 - 2 * b) * (1 << j)
+
+    def copy(c, j, src):
+        part = pl.ds(c * rows, rows)
+        return pltpu.make_async_remote_copy(
+            src_ref=src.at[part],
+            dst_ref=buf.at[part],
+            send_sem=send_sem.at[c, j],
+            recv_sem=recv_sem.at[c],
+            device_id=(row, child(j)),
+            device_id_type=pl.DeviceIdType.MESH,
+        )
+
+    for c in range(chunks):
+        @pl.when(jnp.logical_not(is_root))
+        def _():
+            copy(c, 0, buf).wait_recv()
+
+        for j in range(bits):
+            @pl.when(sends[j] & is_root)
+            def _():
+                copy(c, j, x_ref).start()
+
+            @pl.when(sends[j] & jnp.logical_not(is_root))
+            def _():
+                copy(c, j, buf).start()
+
+    for c in range(chunks):
+        for j in range(bits):
+            @pl.when(sends[j])
+            def _():
+                copy(c, j, buf).wait_send()
+
+    @pl.when(is_root)
+    def _():
+        y_ref[...] = x_ref[...]
+
+    @pl.when(jnp.logical_not(is_root))
+    def _():
+        y_ref[...] = buf[...]
+
+
+def panel_broadcast(value, size, root, chunks):
+    bits = size.bit_length() - 1
+    return pl.pallas_call(
+        functools.partial(broadcast_kernel, root, size, chunks),
+        out_shape=jax.ShapeDtypeStruct(value.shape, value.dtype),
+        in_specs=[pl.BlockSpec(memory_space=pltpu.VMEM)],
+        out_specs=pl.BlockSpec(memory_space=pltpu.VMEM),
+        scratch_shapes=[
+            pltpu.VMEM(value.shape, value.dtype),
+            pltpu.SemaphoreType.DMA((chunks,)),
+            pltpu.SemaphoreType.DMA((chunks, bits)),
+        ],
+        compiler_params=pltpu.CompilerParams(has_side_effects=True),
+    )(value)
 
 
 def tree_broadcast(value, axis, size, root):
@@ -109,7 +188,8 @@
 
         def solve_panel(rows, inverse, root):
             local = jnp.dot(rows, inverse, precision=exact_mode).astype(jnp.bfloat16)
-            return tree_broadcast(local, "col", n_col, root)
+            chunks = 4 if local.shape[0] % 64 == 0 else 3
+            return panel_broadcast(local, n_col, root, chunks)
 
         def summed_block(partial_value, root):
             rows_sum = butterfly_sum(partial_value, "row", n_row)

time: 208 us -> 214 us (1.029)
  the two profiles are of different devices: /device:TPU:2 before, /device:TPU:1 now
where the time goes in v3:
time: 214 us; the launch traced here: 211 us
  Pallas kernels  93.8 us (44%)
  starting transfers between devices  38.3 us (18%)
  matrix products  27.9 us (13%)
  other arithmetic  25.1 us (12%)
  waiting for transfers between devices  20.1 us (9%)
  local copies, waits for them, and re-layouts  4.11 us (2%)
    pallas_call x2, Pallas kernels, panel_broadcast(): pl.pallas_call(functools.partial(broadcast_kernel, root, size, chunks), o...  93.8 us
    another operation x4, other arithmetic, inverse_lower(): return lax.linalg.triangular_solve(block, ident, left_side=True, lower=True)  20.5 us
    ppermute x6, starting transfers between devices, halving_scatter(): blocks = keep + lax.ppermute(send, axis, pairs)  14.6 us
    ppermute x6, waiting for transfers between devices, butterfly_sum(): value = value + lax.ppermute(value, axis, pairs)  12 us
    ppermute x6, starting transfers between devices, butterfly_sum(): value = value + lax.ppermute(value, axis, pairs)  11 us
    ppermute x8, starting transfers between devices, tree_broadcast(): arrived = lax.ppermute(value, axis, pairs)  6.75 us
    ppermute x6, starting transfers between devices, doubling_gather(): other = lax.ppermute(value, axis, pairs)  5.96 us
    dot_general x2, matrix products, solve_panel(): local = jnp.dot(rows, inverse, precision=exact_mode).astype(jnp.bfloat16)  4.76 us
  transfers between devices with their start and end apart: 26, of which 9 were waited for; matrix products, arithmetic and copies ran while one was open for 18% of the time, Pallas kernels for 22%

profile of v3, /device:TPU:1, one launch (start us, length us, event | category | flops | bytes accessed | tf_op | source)
XLA Modules:
  0.0 210.7 jit_solution(5887754296107939076)
XLA Ops:
  0.6 0.9 select_bitcast_fusion.1
  1.5 9.8 %custom-call.4 = f32[1,128,128]{1,2,0:T(8,128)S(1)} custom-call(f32[1,128,128]{2,1,0:T(8,128)S(1)} %select_bitcast_fusion.1), custom_call_target="InvertDiagBlocksLowerTriangular" | custom-call | tf_op jit(solution)/shard_map/triangular_solve/custom-call.1 | solution.py:151
  11.3 0.3 fusion.17
  11.6 3.0 %fusion.x_ref = bf16[2048,128]{1,0:T(8,128)(2,1)} fusion(f32[128,128]{1,0:T(8,128)S(1)} %fusion.17, f32[2048,1024]{1,0:T(8,128)} %param.17), kind=kOutput, calls=%fused_computation.6 | convolution fusion | flops 402915328 | bytes 1638400 | tf_op jit(solution)/shard_map/dot_general | solution.py:190
  14.6 48.4 %shard_map.137 = bf16[2048,128]{1,0:T(8,128)(2,1)} custom-call(bf16[2048,128]{1,0:T(8,128)(2,1)} %fusion.x_ref), custom_call_target="tpu_custom_call" | custom-call | tf_op jit(solution)/shard_map/pallas_call | solution.py:74
  63.0 1.5 fusion.10
  64.5 4.5 %collective-permute-start.6 = (f32[128,128]{1,0:T(8,128)S(1)}, f32[128,128]{1,0:T(8,128)S(1)}, u32[]{:S(2)}, u32[]{:S(2)}) collective-permute-start(f32[128,128]{1,0:T(8,128)S(1)} %fusion.10), channel_id=1, source_target_pairs={{0,16},{16,0},{32,48},{48,32},{64,80},{80,64},{96,112},{112,96},{1... | collective-permute-start | bytes 196616 | tf_op jit(solution)/shard_map/ppermute | solution.py:104
  69.0 3.1 %fusion.57 = f32[128,1024]{1,0:T(8,128)S(1)} fusion(bf16[2048,128]{1,0:T(8,128)(2,1)} %shard_map.137, bf16[2048,1024]{1,0:T(8,128)(2,1)} %param.12), kind=kOutput, calls=%fused_computation.106 | convolution fusion | flops 536870912 | bytes 5242880 | tf_op jit(solution)/shard_map/dot_general | solution.py:207
  72.1 2.8 %collective-permute-start.3 = (f32[4,16,1024]{2,1,0:T(8,128)S(1)}, f32[4,16,1024]{2,1,0:T(8,128)S(1)}, u32[]{:S(2)}, u32[]{:S(2)}) collective-permute-start(f32[4,16,1024]{2,1,0:T(8,128)S(1)} %bitcast.54), channel_id=1, source_target_pairs={{0,64},{16,80},{32,96},{48,112},{64,0},{80,16},{96,32},{112,48},{1... | collective-permute-start | bytes 786440 | tf_op jit(solution)/shard_map/ppermute | solution.py:120
  74.9 0.4 collective-permute-start
  75.5 9.8 %custom-call.5 = f32[1,128,128]{1,2,0:T(8,128)S(1)} custom-call(f32[1,128,128]{2,1,0:T(8,128)S(1)} %select_bitcast_fusion), custom_call_target="InvertDiagBlocksLowerTriangular" | custom-call | tf_op jit(solution)/shard_map/triangular_solve/custom-call.1 | solution.py:151
  85.3 0.3 fusion.15
  85.6 0.4 collective-permute-start.1
  86.0 1.2 collective-permute-start.14
  87.3 0.4 collective-permute-start.7
  87.7 1.2 collective-permute-done.1
  88.9 1.2 collective-permute-start.2
  90.1 1.7 collective-permute-done.7
  91.9 0.5 collective-permute-start.8
  92.4 2.6 %collective-permute-start.15 = (bf16[64,1024]{1,0:T(8,128)(2,1)S(1)}, bf16[64,1024]{1,0:T(8,128)(2,1)S(1)}, u32[]{:S(2)}, u32[]{:S(2)}) collective-permute-start(bf16[64,1024]{1,0:T(8,128)(2,1)S(1)} %maximum_select_fusion.3), channel_id=1, source_target_pairs={{0,64},{16,80},{32,96},{48,112},{64,0},{80,16},{96,32},{112,48},{1... | collective-permute-start | bytes 393224 | tf_op jit(solution)/shard_map/ppermute | solution.py:130
  95.0 2.4 %collective-permute-done.8 = f32[128,128]{1,0:T(8,128)S(1)} collective-permute-done((f32[128,128]{1,0:T(8,128)S(1)}, f32[128,128]{1,0:T(8,128)S(1)}, u32[]{:S(2)}, u32[]{:S(2)}) %collective-permute-start.8) | collective-permute-done | bytes 65568 | tf_op jit(solution)/shard_map/ppermute | solution.py:104
  97.5 0.7 collective-permute-start.9
  98.2 4.6 %convolution_subtract_fusion.1 = f32[2048,1024]{1,0:T(8,128)S(1)} fusion(f32[2048,1024]{1,0:T(8,128)} %param.17, bf16[2048,128]{1,0:T(8,128)(2,1)S(1)} %copy-done.1, bf16[64,1024]{1,0:T(8,128)(2,1)S(1)} %maximum_select_fusion.2, bf16[64,1024]{1,0:T(8,128)(2,1)S(1)} %collective-permute-done.2, pred[]{:T(512)S(6)} %eq.62), kind=kOutput, calls=%fused_computation.2 | convolution fusion | flops 540147712 | bytes 17563648 | tf_op jit(solution)/shard_map/dot_general | solution.py:210
  102.8 3.3 %copy-done = f32[2048,1024]{1,0:T(8,128)} copy-done((f32[2048,1024]{1,0:T(8,128)}, f32[2048,1024]{1,0:T(8,128)S(1)}, u32[]{:S(2)}) %copy-start) | copy-done | bytes 8388632
  106.3 0.8 collective-permute-start.10
  107.2 0.4 collective-permute-start.4
  107.7 0.7 collective-permute-start.11
  108.3 2.8 %collective-permute-done.4 = f32[2,16,1024]{2,1,0:T(8,128)S(1)} collective-permute-done((f32[2,16,1024]{2,1,0:T(8,128)S(1)}, f32[2,16,1024]{2,1,0:T(8,128)S(1)}, u32[]{:S(2)}, u32[]{:S(2)}) %collective-permute-start.4) | collective-permute-done | bytes 131104 | tf_op jit(solution)/shard_map/ppermute | solution.py:120
  111.2 1.3 collective-permute-start.12
  112.5 4.1 %collective-permute-start.5 = (f32[1,16,1024]{2,1,0:T(8,128)S(1)}, f32[1,16,1024]{2,1,0:T(8,128)S(1)}, u32[]{:S(2)}, u32[]{:S(2)}) collective-permute-start(f32[1,16,1024]{2,1,0:T(8,128)S(1)} %slice_select_fusion.8), channel_id=1, source_target_pairs={{0,16},{16,0},{32,48},{48,32},{64,80},{80,64},{96,112},{112,96},{1... | collective-permute-start | bytes 196616 | tf_op jit(solution)/shard_map/ppermute | solution.py:120
  116.7 1.0 collective-permute-done.12
  117.7 0.3 fusion.2
  118.0 0.3 fusion.58
  118.3 0.2 fusion.32
  118.6 0.3 fusion.21
  118.9 1.8 convolution_convert_fusion.x_ref
  120.7 45.4 %shard_map.138 = bf16[2064,128]{1,0:T(8,128)(2,1)} custom-call(bf16[2064,128]{1,0:T(8,128)(2,1)} %convolution_convert_fusion.x_ref), custom_call_target="tpu_custom_call" | custom-call | tf_op jit(solution)/shard_map/pallas_call | solution.py:74
  166.1 0.9 fusion.44
  167.0 0.9 fusion.48
  167.9 1.5 convolution_add_fusion.1
  169.5 3.5 %collective-permute-start.19 = (f32[128,128]{1,0:T(8,128)S(1)}, f32[128,128]{1,0:T(8,128)S(1)}, u32[]{:S(2)}, u32[]{:S(2)}) collective-permute-start(f32[128,128]{1,0:T(8,128)S(1)} %convolution_add_fusion.1), channel_id=1, source_target_pairs={{0,16},{16,0},{32,48},{48,32},{64,80},{80,64},{96,112},{112,96},{1... | collective-permute-start | bytes 196616 | tf_op jit(solution)/shard_map/ppermute | solution.py:104
  173.0 3.1 %convolution_add_fusion = f32[128,1024]{1,0:T(8,128)S(1)} fusion(f32[128,1024]{1,0:T(8,128)S(1)} %fusion.48, bf16[2048,1024]{1,0:T(8,128)(2,1)} %param.12, bf16[2064,128]{1,0:T(8,128)(2,1)} %shard_map.138), kind=kOutput, calls=%fused_computation.7 | convolution fusion | flops 537001984 | bytes 5767168 | tf_op jit(solution)/shard_map/dot_general | solution.py:227
  176.1 4.6 %convolution_subtract_fusion = bf16[2048,1024]{1,0:T(8,128)(2,1)S(1)} fusion(f32[2048,1024]{1,0:T(8,128)} %copy-done, bf16[2064,128]{1,0:T(8,128)(2,1)S(1)} %copy-done.2, bf16[64,1024]{1,0:T(8,128)(2,1)S(1)} %maximum_select_fusion.3, bf16[64,1024]{1,0:T(8,128)(2,1)S(1)} %collective-permute-done.15, pred[]{:T(512)S(6)} %eq.62), kind=kOutput, calls=%fused_computation.1 | convolution fusion | flops 542244864 | bytes 13369345 | tf_op jit(solution)/shard_map/dot_general | solution.py:224
  180.7 0.2 fusion.7
  181.0 0.4 slice.204
  181.4 2.8 %collective-permute-start.16 = (f32[4,16,1024]{2,1,0:T(8,128)S(1)}, f32[4,16,1024]{2,1,0:T(8,128)S(1)}, u32[]{:S(2)}, u32[]{:S(2)}) collective-permute-start(f32[4,16,1024]{2,1,0:T(8,128)S(1)} %bitcast.55), channel_id=1, source_target_pairs={{0,64},{16,80},{32,96},{48,112},{64,0},{80,16},{96,32},{112,48},{1... | collective-permute-start | bytes 786440 | tf_op jit(solution)/shard_map/ppermute | solution.py:120
  184.3 0.4 collective-permute-start.20
  184.7 2.6 %pad_maximum_fusion = bf16[2048,1024]{1,0:T(8,128)(2,1)} fusion(bf16[2048,128]{1,0:T(8,128)(2,1)S(1)} %fusion.7, bf16[2048,896]{1,0:T(8,128)(2,1)S(1)} %slice.204), kind=kLoop, calls=%fused_computation.3 | loop fusion | flops 8388608 | bytes 8388608 | tf_op jit(solution)/shard_map/concatenate | solution.py:237
  187.3 5.1 %collective-permute-done.20 = f32[128,128]{1,0:T(8,128)S(1)} collective-permute-done((f32[128,128]{1,0:T(8,128)S(1)}, f32[128,128]{1,0:T(8,128)S(1)}, u32[]{:S(2)}, u32[]{:S(2)}) %collective-permute-start.20) | collective-permute-done | bytes 65568 | tf_op jit(solution)/shard_map/ppermute | solution.py:104
  192.4 1.8 collective-permute-start.21
  194.4 2.7 %collective-permute-done.21 = f32[128,128]{1,0:T(8,128)S(1)} collective-permute-done((f32[128,128]{1,0:T(8,128)S(1)}, f32[128,128]{1,0:T(8,128)S(1)}, u32[]{:S(2)}, u32[]{:S(2)}) %collective-permute-start.21) | collective-permute-done | bytes 65568 | tf_op jit(solution)/shard_map/ppermute | solution.py:104
  197.1 0.7 collective-permute-start.22
  197.9 0.7 collective-permute-start.23
  198.5 0.6 pad_maximum_fusion.2
  199.2 0.7 collective-permute-start.24
  199.9 1.2 collective-permute-start.17
  201.2 1.3 collective-permute-start.25
  202.5 1.3 collective-permute-done.17
  203.9 3.2 %collective-permute-start.18 = (f32[1,16,1024]{2,1,0:T(8,128)S(1)}, f32[1,16,1024]{2,1,0:T(8,128)S(1)}, u32[]{:S(2)}, u32[]{:S(2)}) collective-permute-start(f32[1,16,1024]{2,1,0:T(8,128)S(1)} %slice_select_fusion.7), channel_id=1, source_target_pairs={{0,16},{16,0},{32,48},{48,32},{64,80},{80,64},{96,112},{112,96},{1... | collective-permute-start | bytes 196616 | tf_op jit(solution)/shard_map/ppermute | solution.py:120
  207.1 1.8 collective-permute-done.25
  208.9 0.3 fusion.1
  209.2 0.3 fusion.59
  209.8 0.3 fusion.19
  210.1 0.6 pad_maximum_fusion.1
  (81 shorter events, 1.5 us)
Async XLA Ops:
  14.6 60.3 %copy-start.5 = (bf16[16,1024]{1,0:T(8,128)(2,1)S(1)}, bf16[16,1024]{1,0:T(8,128)(2,1)}, u32[]{:S(2)}) copy-start(bf16[16,1024]{1,0:T(8,128)(2,1)} %param.14) | copy-start | bytes 98308
  14.6 60.7 %copy-start.10 = (bf16[16,1024]{1,0:T(8,128)(2,1)S(1)}, bf16[16,1024]{1,0:T(8,128)(2,1)}, u32[]{:S(2)}) copy-start(bf16[16,1024]{1,0:T(8,128)(2,1)} %param.13) | copy-start | bytes 98308
  14.6 60.9 %copy-start.4 = (f32[128,128]{1,0:T(8,128)S(1)}, f32[128,128]{1,0:T(8,128)}, u32[]{:S(2)}) copy-start(f32[128,128]{1,0:T(8,128)} %param.15) | copy-start | bytes 196612
  64.5 33.7 %copy-start.1 = (bf16[2048,128]{1,0:T(8,128)(2,1)S(1)}, bf16[2048,128]{1,0:T(8,128)(2,1)}, u32[]{:S(2)}) copy-start(bf16[2048,128]{1,0:T(8,128)(2,1)} %shard_map.137) | copy-start | bytes 1572868
  64.5 22.8 %collective-permute-start.6 = (f32[128,128]{1,0:T(8,128)S(1)}, f32[128,128]{1,0:T(8,128)S(1)}, u32[]{:S(2)}, u32[]{:S(2)}) collective-permute-start(f32[128,128]{1,0:T(8,128)S(1)} %fusion.10), channel_id=1, source_target_pairs={{0,16},{16,0},{32,48},{48,32},{64,80},{80,64},{96,112},{112,96},{1... | collective-permute-start | bytes 196616 | tf_op jit(solution)/shard_map/ppermute | solution.py:104
  72.1 35.0 %collective-permute-start.3 = (f32[4,16,1024]{2,1,0:T(8,128)S(1)}, f32[4,16,1024]{2,1,0:T(8,128)S(1)}, u32[]{:S(2)}, u32[]{:S(2)}) collective-permute-start(f32[4,16,1024]{2,1,0:T(8,128)S(1)} %bitcast.54), channel_id=1, source_target_pairs={{0,64},{16,80},{32,96},{48,112},{64,0},{80,16},{96,32},{112,48},{1... | collective-permute-start | bytes 786440 | tf_op jit(solution)/shard_map/ppermute | solution.py:120
  74.9 10.7 %collective-permute-start = (bf16[16,1024]{1,0:T(8,128)(2,1)S(1)}, bf16[16,1024]{1,0:T(8,128)(2,1)S(1)}, u32[]{:S(2)}, u32[]{:S(2)}) collective-permute-start(bf16[16,1024]{1,0:T(8,128)(2,1)S(1)} %copy-done.5), channel_id=1, source_target_pairs={{0,16},{16,0},{32,48},{48,32},{64,80},{80,64},{96,112},{112,96},{1... | collective-permute-start | bytes 98312 | tf_op jit(solution)/shard_map/ppermute | solution.py:130
  75.3 10.7 %collective-permute-start.13 = (bf16[16,1024]{1,0:T(8,128)(2,1)S(1)}, bf16[16,1024]{1,0:T(8,128)(2,1)S(1)}, u32[]{:S(2)}, u32[]{:S(2)}) collective-permute-start(bf16[16,1024]{1,0:T(8,128)(2,1)S(1)} %copy-done.10), channel_id=1, source_target_pairs={{0,16},{16,0},{32,48},{48,32},{64,80},{80,64},{96,112},{112,96},{1... | collective-permute-start | bytes 98312 | tf_op jit(solution)/shard_map/ppermute | solution.py:130
  85.6 3.2 %collective-permute-start.1 = (bf16[32,1024]{1,0:T(8,128)(2,1)S(1)}, bf16[32,1024]{1,0:T(8,128)(2,1)S(1)}, u32[]{:S(2)}, u32[]{:S(2)}) collective-permute-start(bf16[32,1024]{1,0:T(8,128)(2,1)S(1)} %maximum_select_fusion.4), channel_id=1, source_target_pairs={{0,32},{16,48},{32,0},{48,16},{64,96},{80,112},{96,64},{112,80},{1... | collective-permute-start | bytes 196616 | tf_op jit(solution)/shard_map/ppermute | solution.py:130
  86.0 6.3 %collective-permute-start.14 = (bf16[32,1024]{1,0:T(8,128)(2,1)S(1)}, bf16[32,1024]{1,0:T(8,128)(2,1)S(1)}, u32[]{:S(2)}, u32[]{:S(2)}) collective-permute-start(bf16[32,1024]{1,0:T(8,128)(2,1)S(1)} %maximum_select_fusion.5), channel_id=1, source_target_pairs={{0,32},{16,48},{32,0},{48,16},{64,96},{80,112},{96,64},{112,80},{1... | collective-permute-start | bytes 196616 | tf_op jit(solution)/shard_map/ppermute | solution.py:130
  87.3 4.6 %collective-permute-start.7 = (f32[128,128]{1,0:T(8,128)S(1)}, f32[128,128]{1,0:T(8,128)S(1)}, u32[]{:S(2)}, u32[]{:S(2)}) collective-permute-start(f32[128,128]{1,0:T(8,128)S(1)} %add.81), channel_id=1, source_target_pairs={{0,32},{16,48},{32,0},{48,16},{64,96},{80,112},{96,64},{112,80},{1... | collective-permute-start | bytes 196616 | tf_op jit(solution)/shard_map/ppermute | solution.py:104
  88.9 9.3 %collective-permute-start.2 = (bf16[64,1024]{1,0:T(8,128)(2,1)S(1)}, bf16[64,1024]{1,0:T(8,128)(2,1)S(1)}, u32[]{:S(2)}, u32[]{:S(2)}) collective-permute-start(bf16[64,1024]{1,0:T(8,128)(2,1)S(1)} %maximum_select_fusion.2), channel_id=1, source_target_pairs={{0,64},{16,80},{32,96},{48,112},{64,0},{80,16},{96,32},{112,48},{1... | collective-permute-start | bytes 393224 | tf_op jit(solution)/shard_map/ppermute | solution.py:130
  91.9 5.6 %collective-permute-start.8 = (f32[128,128]{1,0:T(8,128)S(1)}, f32[128,128]{1,0:T(8,128)S(1)}, u32[]{:S(2)}, u32[]{:S(2)}) collective-permute-start(f32[128,128]{1,0:T(8,128)S(1)} %add.82), channel_id=1, source_target_pairs={{0,64},{16,80},{32,96},{48,112},{64,0},{80,16},{96,32},{112,48},{1... | collective-permute-start | bytes 196616 | tf_op jit(solution)/shard_map/ppermute | solution.py:104
  92.4 83.7 %collective-permute-start.15 = (bf16[64,1024]{1,0:T(8,128)(2,1)S(1)}, bf16[64,1024]{1,0:T(8,128)(2,1)S(1)}, u32[]{:S(2)}, u32[]{:S(2)}) collective-permute-start(bf16[64,1024]{1,0:T(8,128)(2,1)S(1)} %maximum_select_fusion.3), channel_id=1, source_target_pairs={{0,64},{16,80},{32,96},{48,112},{64,0},{80,16},{96,32},{112,48},{1... | collective-permute-start | bytes 393224 | tf_op jit(solution)/shard_map/ppermute | solution.py:130
  97.5 8.8 %collective-permute-start.9 = (f32[128,128]{1,0:T(8,128)S(1)}, f32[128,128]{1,0:T(8,128)S(1)}, u32[]{:S(2)}, u32[]{:S(2)}) collective-permute-start(f32[128,128]{1,0:T(8,128)S(1)} %add.83), channel_id=1, source_target_pairs={{15,14},{31,30},{47,46},{63,62},{79,78},{95,94},{111,110},{127,126}} | collective-permute-start | bytes 196616 | tf_op jit(solution)/shard_map/ppermute | solution.py:93
  102.8 3.3 %copy-start = (f32[2048,1024]{1,0:T(8,128)}, f32[2048,1024]{1,0:T(8,128)S(1)}, u32[]{:S(2)}) copy-start(f32[2048,1024]{1,0:T(8,128)S(1)} %convolution_subtract_fusion.1) | copy-start | bytes 25165828
  106.1 11.6 %copy-start.3 = (f32[128,128]{1,0:T(8,128)S(1)}, f32[128,128]{1,0:T(8,128)}, u32[]{:S(2)}) copy-start(f32[128,128]{1,0:T(8,128)} %param.16) | copy-start | bytes 196612
  106.1 11.6 %copy-start.6 = (f32[128,128]{1,0:T(8,128)S(1)}, f32[128,128]{1,0:T(8,128)}, u32[]{:S(2)}) copy-start(f32[128,128]{1,0:T(8,128)} %param.21) | copy-start | bytes 196612
  106.1 12.5 %copy-start.11 = (f32[16,1024]{1,0:T(8,128)S(1)}, f32[16,1024]{1,0:T(8,128)}, u32[]{:S(2)}) copy-start(f32[16,1024]{1,0:T(8,128)} %param.19) | copy-start | bytes 196612
  106.3 1.4 collective-permute-start.10
  107.2 3.9 %collective-permute-start.4 = (f32[2,16,1024]{2,1,0:T(8,128)S(1)}, f32[2,16,1024]{2,1,0:T(8,128)S(1)}, u32[]{:S(2)}, u32[]{:S(2)}) collective-permute-start(f32[2,16,1024]{2,1,0:T(8,128)S(1)} %slice_select_fusion.6), channel_id=1, source_target_pairs={{0,32},{16,48},{32,0},{48,16},{64,96},{80,112},{96,64},{112,80},{1... | collective-permute-start | bytes 393224 | tf_op jit(solution)/shard_map/ppermute | solution.py:120
  107.7 3.5 %collective-permute-start.11 = (f32[128,128]{1,0:T(8,128)S(1)}, f32[128,128]{1,0:T(8,128)S(1)}, u32[]{:S(2)}, u32[]{:S(2)}) collective-permute-start(f32[128,128]{1,0:T(8,128)S(1)} %broadcast_select_fusion.4), channel_id=1, source_target_pairs={{15,11},{14,10},{13,9},{12,8},{31,27},{30,26},{29,25},{28,24},{47,... | collective-permute-start | bytes 196616 | tf_op jit(solution)/shard_map/ppermute | solution.py:93
  111.2 6.5 %collective-permute-start.12 = (f32[128,128]{1,0:T(8,128)S(1)}, f32[128,128]{1,0:T(8,128)S(1)}, u32[]{:S(2)}, u32[]{:S(2)}) collective-permute-start(f32[128,128]{1,0:T(8,128)S(1)} %broadcast_select_fusion.5), channel_id=1, source_target_pairs={{15,7},{14,6},{13,5},{12,4},{11,3},{10,2},{9,1},{8,0},{31,23},{30,... | collective-permute-start | bytes 196616 | tf_op jit(solution)/shard_map/ppermute | solution.py:93
  112.5 6.1 %collective-permute-start.5 = (f32[1,16,1024]{2,1,0:T(8,128)S(1)}, f32[1,16,1024]{2,1,0:T(8,128)S(1)}, u32[]{:S(2)}, u32[]{:S(2)}) collective-permute-start(f32[1,16,1024]{2,1,0:T(8,128)S(1)} %slice_select_fusion.8), channel_id=1, source_target_pairs={{0,16},{16,0},{32,48},{48,32},{64,80},{80,64},{96,112},{112,96},{1... | collective-permute-start | bytes 196616 | tf_op jit(solution)/shard_map/ppermute | solution.py:120
  118.5 57.6 %copy-start.8 = (f32[128,128]{1,0:T(8,128)}, f32[128,128]{1,0:T(8,128)S(1)}, u32[]{:S(2)}) copy-start(f32[128,128]{1,0:T(8,128)S(1)} %get-tuple-element.10) | copy-start | bytes 196612
  166.1 10.0 %copy-start.2 = (bf16[2064,128]{1,0:T(8,128)(2,1)S(1)}, bf16[2064,128]{1,0:T(8,128)(2,1)}, u32[]{:S(2)}) copy-start(bf16[2064,128]{1,0:T(8,128)(2,1)} %shard_map.138) | copy-start | bytes 1585156
  169.5 14.8 %collective-permute-start.19 = (f32[128,128]{1,0:T(8,128)S(1)}, f32[128,128]{1,0:T(8,128)S(1)}, u32[]{:S(2)}, u32[]{:S(2)}) collective-permute-start(f32[128,128]{1,0:T(8,128)S(1)} %convolution_add_fusion.1), channel_id=1, source_target_pairs={{0,16},{16,0},{32,48},{48,32},{64,80},{80,64},{96,112},{112,96},{1... | collective-permute-start | bytes 196616 | tf_op jit(solution)/shard_map/ppermute | solution.py:104
  181.4 17.7 %collective-permute-start.16 = (f32[4,16,1024]{2,1,0:T(8,128)S(1)}, f32[4,16,1024]{2,1,0:T(8,128)S(1)}, u32[]{:S(2)}, u32[]{:S(2)}) collective-permute-start(f32[4,16,1024]{2,1,0:T(8,128)S(1)} %bitcast.55), channel_id=1, source_target_pairs={{0,64},{16,80},{32,96},{48,112},{64,0},{80,16},{96,32},{112,48},{1... | collective-permute-start | bytes 786440 | tf_op jit(solution)/shard_map/ppermute | solution.py:120
  184.3 24.6 %copy-start.7 = (f32[128,128]{1,0:T(8,128)S(1)}, f32[128,128]{1,0:T(8,128)}, u32[]{:S(2)}) copy-start(f32[128,128]{1,0:T(8,128)} %param.20) | copy-start | bytes 196612
  184.3 8.1 %collective-permute-start.20 = (f32[128,128]{1,0:T(8,128)S(1)}, f32[128,128]{1,0:T(8,128)S(1)}, u32[]{:S(2)}, u32[]{:S(2)}) collective-permute-start(f32[128,128]{1,0:T(8,128)S(1)} %add.91), channel_id=1, source_target_pairs={{0,32},{16,48},{32,0},{48,16},{64,96},{80,112},{96,64},{112,80},{1... | collective-permute-start | bytes 196616 | tf_op jit(solution)/shard_map/ppermute | solution.py:104
  187.3 22.5 %copy-start.12 = (f32[16,1024]{1,0:T(8,128)S(1)}, f32[16,1024]{1,0:T(8,128)}, u32[]{:S(2)}) copy-start(f32[16,1024]{1,0:T(8,128)} %param.18) | copy-start | bytes 196612
  192.4 4.7 %collective-permute-start.21 = (f32[128,128]{1,0:T(8,128)S(1)}, f32[128,128]{1,0:T(8,128)S(1)}, u32[]{:S(2)}, u32[]{:S(2)}) collective-permute-start(f32[128,128]{1,0:T(8,128)S(1)} %add.92), channel_id=1, source_target_pairs={{0,64},{16,80},{32,96},{48,112},{64,0},{80,16},{96,32},{112,48},{1... | collective-permute-start | bytes 196616 | tf_op jit(solution)/shard_map/ppermute | solution.py:104
  197.1 0.7 collective-permute-start.22
  197.9 1.3 collective-permute-start.23
  199.2 1.9 collective-permute-start.24
  199.9 3.9 %collective-permute-start.17 = (f32[2,16,1024]{2,1,0:T(8,128)S(1)}, f32[2,16,1024]{2,1,0:T(8,128)S(1)}, u32[]{:S(2)}, u32[]{:S(2)}) collective-permute-start(f32[2,16,1024]{2,1,0:T(8,128)S(1)} %slice_select_fusion.5), channel_id=1, source_target_pairs={{0,32},{16,48},{32,0},{48,16},{64,96},{80,112},{96,64},{112,80},{1... | collective-permute-start | bytes 393224 | tf_op jit(solution)/shard_map/ppermute | solution.py:120
  201.2 7.6 %collective-permute-start.25 = (f32[128,128]{1,0:T(8,128)S(1)}, f32[128,128]{1,0:T(8,128)S(1)}, u32[]{:S(2)}, u32[]{:S(2)}) collective-permute-start(f32[128,128]{1,0:T(8,128)S(1)} %broadcast_select_fusion.2), channel_id=1, source_target_pairs={{14,6},{15,7},{12,4},{13,5},{10,2},{11,3},{8,0},{9,1},{30,22},{31,... | collective-permute-start | bytes 196616 | tf_op jit(solution)/shard_map/ppermute | solution.py:93
  203.9 5.9 %collective-permute-start.18 = (f32[1,16,1024]{2,1,0:T(8,128)S(1)}, f32[1,16,1024]{2,1,0:T(8,128)S(1)}, u32[]{:S(2)}, u32[]{:S(2)}) collective-permute-start(f32[1,16,1024]{2,1,0:T(8,128)S(1)} %slice_select_fusion.7), channel_id=1, source_target_pairs={{0,16},{16,0},{32,48},{48,32},{64,80},{80,64},{96,112},{112,96},{1... | collective-permute-start | bytes 196616 | tf_op jit(solution)/shard_map/ppermute | solution.py:120
  209.7 1.1 copy-start.9

commit v4 on v1

--- a/solution.py
+++ b/solution.py
@@ -1,9 +1,82 @@
+import functools
+
 import jax
 import jax.numpy as jnp
 from jax import lax
+from jax.experimental import pallas as pl
+from jax.experimental.pallas import tpu as pltpu
 from jax.sharding import PartitionSpec as P
 
 exact_mode = lax.Precision.HIGHEST
+
+
+def spread_kernel(root, size, x_ref, y_ref, buf, recv_sem, send_sem):
+    me = lax.axis_index("col")
+    row = lax.axis_index("row")
+    rows = x_ref.shape[0] // size
+    is_root = me == root
+
+    def piece(p):
+        return pl.ds(p * rows, rows)
+
+    def copy(p, dest, src, phase):
+        return pltpu.make_async_remote_copy(
+            src_ref=src.at[piece(p)],
+            dst_ref=buf.at[piece(p)],
+            send_sem=send_sem.at[phase, dest],
+            recv_sem=recv_sem.at[p],
+            device_id=(row, dest),
+            device_id_type=pl.DeviceIdType.MESH,
+        )
+
+    @pl.when(is_root)
+    def _():
+        for dest in range(size):
+            if dest != root:
+                copy(dest, dest, x_ref, 0).start()
+        for dest in range(size):
+            if dest != root:
+                copy(root, dest, x_ref, 1).start()
+        for dest in range(size):
+            if dest != root:
+                copy(dest, dest, x_ref, 0).wait_send()
+                copy(root, dest, x_ref, 1).wait_send()
+        y_ref[...] = x_ref[...]
+
+    @pl.when(jnp.logical_not(is_root))
+    def _():
+        for own in range(size):
+            if own == root:
+                continue
+
+            @pl.when(me == own)
+            def _():
+                copy(own, own, buf, 0).wait_recv()
+                for dest in range(size):
+                    if dest != root and dest != own:
+                        copy(own, dest, buf, 1).start()
+                for p in range(size):
+                    if p != own:
+                        copy(p, own, buf, 1).wait_recv()
+                for dest in range(size):
+                    if dest != root and dest != own:
+                        copy(own, dest, buf, 1).wait_send()
+        y_ref[...] = buf[...]
+
+
+def panel_broadcast(value, size, root):
+    return pl.pallas_call(
+        functools.partial(spread_kernel, root, size),
+        out_shape=jax.ShapeDtypeStruct(value.shape, value.dtype),
+        in_specs=[pl.BlockSpec(memory_space=pltpu.VMEM)],
+        out_specs=pl.BlockSpec(memory_space=pltpu.VMEM),
+        scratch_shapes=[
+            pltpu.VMEM(value.shape, value.dtype),
+            pltpu.SemaphoreType.DMA((size,)),
+            pltpu.SemaphoreType.DMA((2, size)),
+        ],
+        compiler_params=pltpu.CompilerParams(has_side_effects=True),
+    )(value)
 
 
 def tree_broadcast(value, axis, size, root):
@@ -109,7 +182,11 @@
 
         def solve_panel(rows, inverse, root):
             local = jnp.dot(rows, inverse, precision=exact_mode).astype(jnp.bfloat16)
-            return tree_broadcast(local, "col", n_col, root)
+            head = local.shape[0] % (16 * n_col)
+            tail = panel_broadcast(local[head:], n_col, root)
+            if head == 0:
+                return tail
+            return jnp.concatenate([tree_broadcast(local[:head], "col", n_col, root), tail], 0)
 
         def summed_block(partial_value, root):
             rows_sum = butterfly_sum(partial_value, "row", n_row)

time: 208 us -> 184 us (0.88)
  the two profiles are of different devices: /device:TPU:2 before, /device:TPU:0 now
where the time goes in v4:
time: 184 us; the launch traced here: 183 us
  Pallas kernels  50.2 us (27%)
  waiting for transfers between devices  48.7 us (26%)
  starting transfers between devices  30.4 us (17%)
  other arithmetic  25.1 us (14%)
  matrix products  22.5 us (12%)
  local copies, waits for them, and re-layouts  4.94 us (3%)
    pallas_call x2, Pallas kernels, panel_broadcast(): pl.pallas_call(functools.partial(spread_kernel, root, size), out_shape=ja...  50.2 us
    ppermute x12, waiting for transfers between devices, tree_broadcast(): arrived = lax.ppermute(value, axis, pairs)  25.1 us
    another operation x4, other arithmetic, inverse_lower(): return lax.linalg.triangular_solve(block, ident, left_side=True, lower=True)  20.5 us
    ppermute x6, waiting for transfers between devices, butterfly_sum(): value = value + lax.ppermute(value, axis, pairs)  11.7 us
    ppermute x12, starting transfers between devices, tree_broadcast(): arrived = lax.ppermute(value, axis, pairs)  10.1 us
    ppermute x6, waiting for transfers between devices, halving_scatter(): blocks = keep + lax.ppermute(send, axis, pairs)  9.85 us
    ppermute x6, starting transfers between devices, halving_scatter(): blocks = keep + lax.ppermute(send, axis, pairs)  8.13 us
    ppermute x6, starting transfers between devices, butterfly_sum(): value = value + lax.ppermute(value, axis, pairs)  6.47 us
  transfers between devices with their start and end apart: 30, of which 12 were waited for; matrix products, arithmetic and copies ran while one was open for 18% of the time, Pallas kernels for 12%

profile of v4, /device:TPU:0, one launch (start us, length us, event | category | flops | bytes accessed | tf_op | source)
XLA Modules:
  0.0 183.4 jit_solution(5446876907165652264)
XLA Ops:
  0.6 0.9 select_bitcast_fusion.1
  1.5 9.8 %custom-call.4 = f32[1,128,128]{1,2,0:T(8,128)S(1)} custom-call(f32[1,128,128]{2,1,0:T(8,128)S(1)} %select_bitcast_fusion.1), custom_call_target="InvertDiagBlocksLowerTriangular" | custom-call | tf_op jit(solution)/shard_map/triangular_solve/custom-call.1 | solution.py:145
  11.3 0.3 fusion.15
  11.6 3.0 %fusion.x_ref = bf16[2048,128]{1,0:T(8,128)(2,1)} fusion(f32[128,128]{1,0:T(8,128)S(1)} %fusion.15, f32[2048,1024]{1,0:T(8,128)} %param.17), kind=kOutput, calls=%fused_computation.6 | convolution fusion | flops 402915328 | bytes 1638400 | tf_op jit(solution)/shard_map/dot_general | solution.py:184
  14.6 29.1 %shard_map.137 = bf16[2048,128]{1,0:T(8,128)(2,1)} custom-call(bf16[2048,128]{1,0:T(8,128)(2,1)} %fusion.x_ref), custom_call_target="tpu_custom_call" | custom-call | tf_op jit(solution)/shard_map/pallas_call | solution.py:68
  43.7 1.5 fusion.11
  45.4 3.1 %fusion.50 = f32[128,1024]{1,0:T(8,128)S(1)} fusion(bf16[2048,128]{1,0:T(8,128)(2,1)} %shard_map.137, bf16[2048,1024]{1,0:T(8,128)(2,1)} %param.12), kind=kOutput, calls=%fused_computation.103 | convolution fusion | flops 536870912 | bytes 5242880 | tf_op jit(solution)/shard_map/dot_general | solution.py:204
  48.6 3.1 %collective-permute-start.3 = (f32[4,16,1024]{2,1,0:T(8,128)S(1)}, f32[4,16,1024]{2,1,0:T(8,128)S(1)}, u32[]{:S(2)}, u32[]{:S(2)}) collective-permute-start(f32[4,16,1024]{2,1,0:T(8,128)S(1)} %bitcast.60), channel_id=1, source_target_pairs={{0,64},{16,80},{32,96},{48,112},{64,0},{80,16},{96,32},{112,48},{1... | collective-permute-start | bytes 786440 | tf_op jit(solution)/shard_map/ppermute | solution.py:114
  51.8 0.3 collective-permute-start.13
  52.2 9.8 %custom-call.5 = f32[1,128,128]{1,2,0:T(8,128)S(1)} custom-call(f32[1,128,128]{2,1,0:T(8,128)S(1)} %select_bitcast_fusion), custom_call_target="InvertDiagBlocksLowerTriangular" | custom-call | tf_op jit(solution)/shard_map/triangular_solve/custom-call.1 | solution.py:145
  62.0 0.3 fusion.13
  62.3 0.7 collective-permute-start.1
  63.0 1.5 collective-permute-start.14
  64.6 0.7 collective-permute-start.7
  65.2 2.1 %collective-permute-done.1 = bf16[32,1024]{1,0:T(8,128)(2,1)S(1)} collective-permute-done((bf16[32,1024]{1,0:T(8,128)(2,1)S(1)}, bf16[32,1024]{1,0:T(8,128)(2,1)S(1)}, u32[]{:S(2)}, u32[]{:S(2)}) %collective-permute-start.1) | collective-permute-done | bytes 65568 | tf_op jit(solution)/shard_map/ppermute | solution.py:124
  67.7 2.5 %collective-permute-done.7 = f32[128,128]{1,0:T(8,128)S(1)} collective-permute-done((f32[128,128]{1,0:T(8,128)S(1)}, f32[128,128]{1,0:T(8,128)S(1)}, u32[]{:S(2)}, u32[]{:S(2)}) %collective-permute-start.7) | collective-permute-done | bytes 65568 | tf_op jit(solution)/shard_map/ppermute | solution.py:98
  70.2 1.0 collective-permute-start.8
  71.2 2.7 %collective-permute-start.15 = (bf16[64,1024]{1,0:T(8,128)(2,1)S(1)}, bf16[64,1024]{1,0:T(8,128)(2,1)S(1)}, u32[]{:S(2)}, u32[]{:S(2)}) collective-permute-start(bf16[64,1024]{1,0:T(8,128)(2,1)S(1)} %maximum_select_fusion.3), channel_id=1, source_target_pairs={{0,64},{16,80},{32,96},{48,112},{64,0},{80,16},{96,32},{112,48},{1... | collective-permute-start | bytes 393224 | tf_op jit(solution)/shard_map/ppermute | solution.py:124
  73.9 2.8 %collective-permute-done.8 = f32[128,128]{1,0:T(8,128)S(1)} collective-permute-done((f32[128,128]{1,0:T(8,128)S(1)}, f32[128,128]{1,0:T(8,128)S(1)}, u32[]{:S(2)}, u32[]{:S(2)}) %collective-permute-start.8) | collective-permute-done | bytes 65568 | tf_op jit(solution)/shard_map/ppermute | solution.py:98
  76.8 0.8 collective-permute-start.9
  77.6 4.6 %convolution_subtract_fusion.1 = f32[2048,1024]{1,0:T(8,128)S(1)} fusion(f32[2048,1024]{1,0:T(8,128)} %param.17, bf16[2048,128]{1,0:T(8,128)(2,1)S(1)} %copy-done.2, bf16[64,1024]{1,0:T(8,128)(2,1)S(1)} %maximum_select_fusion.2, bf16[64,1024]{1,0:T(8,128)(2,1)S(1)} %collective-permute-done.2, pred[]{:T(512)S(6)} %eq.62), kind=kOutput, calls=%fused_computation.2 | convolution fusion | flops 540147712 | bytes 17563648 | tf_op jit(solution)/shard_map/dot_general | solution.py:207
  82.3 3.3 %copy-done = f32[2048,1024]{1,0:T(8,128)} copy-done((f32[2048,1024]{1,0:T(8,128)}, f32[2048,1024]{1,0:T(8,128)S(1)}, u32[]{:S(2)}) %copy-start) | copy-done | bytes 8388632
  85.7 0.7 collective-permute-start.10
  86.5 0.2 collective-permute-start.4
  86.8 0.7 collective-permute-start.11
  87.4 4.1 %collective-permute-done.4 = f32[2,16,1024]{2,1,0:T(8,128)S(1)} collective-permute-done((f32[2,16,1024]{2,1,0:T(8,128)S(1)}, f32[2,16,1024]{2,1,0:T(8,128)S(1)}, u32[]{:S(2)}, u32[]{:S(2)}) %collective-permute-start.4) | collective-permute-done | bytes 131104 | tf_op jit(solution)/shard_map/ppermute | solution.py:114
  91.6 1.3 collective-permute-start.12
  93.0 11.0 %collective-permute-done.12 = f32[128,128]{1,0:T(8,128)S(1)} collective-permute-done((f32[128,128]{1,0:T(8,128)S(1)}, f32[128,128]{1,0:T(8,128)S(1)}, u32[]{:S(2)}, u32[]{:S(2)}) %collective-permute-start.12) | collective-permute-done | bytes 65568 | tf_op jit(solution)/shard_map/ppermute | solution.py:87
  104.0 0.3 fusion.2
  104.3 0.3 fusion.51
  104.9 0.3 fusion.19
  105.2 1.0 convolution_convert_fusion
  106.2 0.8 slice.136.x_ref
  107.0 0.6 collective-permute-start.16
  107.7 21.1 %shard_map.138 = bf16[2048,128]{1,0:T(8,128)(2,1)} custom-call(bf16[2048,128]{1,0:T(8,128)(2,1)} %slice.136.x_ref), custom_call_target="tpu_custom_call" | custom-call | tf_op jit(solution)/shard_map/pallas_call | solution.py:68
  128.8 4.9 %convolution_subtract_fusion = bf16[2048,1024]{1,0:T(8,128)(2,1)S(1)} fusion(f32[2048,1024]{1,0:T(8,128)} %copy-done, bf16[2048,128]{1,0:T(8,128)(2,1)} %shard_map.138, bf16[64,1024]{1,0:T(8,128)(2,1)S(1)} %maximum_select_fusion.3, bf16[64,1024]{1,0:T(8,128)(2,1)S(1)} %collective-permute-done.15, pred[]{:T(512)S(6)} %eq.62), kind=kOutput, calls=%fused_computation.1 | convolution fusion | flops 542244864 | bytes 13369345 | tf_op jit(solution)/shard_map/dot_general | solution.py:221
  134.1 0.7 collective-permute-start.17
  134.7 0.7 fusion.52
  135.5 0.4 slice.193
  135.9 0.7 collective-permute-start.18
  136.6 2.6 %pad_maximum_fusion = bf16[2048,1024]{1,0:T(8,128)(2,1)} fusion(bf16[2048,128]{1,0:T(8,128)(2,1)S(1)} %fusion.7, bf16[2048,896]{1,0:T(8,128)(2,1)S(1)} %slice.193), kind=kLoop, calls=%fused_computation.3 | loop fusion | flops 8388608 | bytes 8388608 | tf_op jit(solution)/shard_map/concatenate | solution.py:234
  139.3 1.4 collective-permute-start.19
  140.7 0.3 fusion.9
  141.1 9.2 %collective-permute-done.19 = bf16[16,128]{1,0:T(8,128)(2,1)S(1)} collective-permute-done((bf16[16,128]{1,0:T(8,128)(2,1)S(1)}, bf16[16,128]{1,0:T(8,128)(2,1)S(1)}, u32[]{:S(2)}, u32[]{:S(2)}) %collective-permute-start.19) | collective-permute-done | bytes 4128 | tf_op jit(solution)/shard_map/ppermute | solution.py:87
  150.6 0.2 convolution_add_fusion
  150.8 1.0 collective-permute-done.23
  151.8 1.6 collective-permute-start.24
  153.4 2.7 %collective-permute-done.24 = f32[128,128]{1,0:T(8,128)S(1)} collective-permute-done((f32[128,128]{1,0:T(8,128)S(1)}, f32[128,128]{1,0:T(8,128)S(1)}, u32[]{:S(2)}, u32[]{:S(2)}) %collective-permute-start.24) | collective-permute-done | bytes 65568 | tf_op jit(solution)/shard_map/ppermute | solution.py:98
  156.2 3.1 %collective-permute-start.25 = (f32[128,128]{1,0:T(8,128)S(1)}, f32[128,128]{1,0:T(8,128)S(1)}, u32[]{:S(2)}, u32[]{:S(2)}) collective-permute-start(f32[128,128]{1,0:T(8,128)S(1)} %add.92), channel_id=1, source_target_pairs={{0,64},{16,80},{32,96},{48,112},{64,0},{80,16},{96,32},{112,48},{1... | collective-permute-start | bytes 196616 | tf_op jit(solution)/shard_map/ppermute | solution.py:98
  159.4 2.6 %collective-permute-done.25 = f32[128,128]{1,0:T(8,128)S(1)} collective-permute-done((f32[128,128]{1,0:T(8,128)S(1)}, f32[128,128]{1,0:T(8,128)S(1)}, u32[]{:S(2)}, u32[]{:S(2)}) %collective-permute-start.25) | collective-permute-done | bytes 65568 | tf_op jit(solution)/shard_map/ppermute | solution.py:98
  162.0 0.7 collective-permute-start.26
  162.7 3.1 %collective-permute-start.20 = (f32[4,16,1024]{2,1,0:T(8,128)S(1)}, f32[4,16,1024]{2,1,0:T(8,128)S(1)}, u32[]{:S(2)}, u32[]{:S(2)}) collective-permute-start(f32[4,16,1024]{2,1,0:T(8,128)S(1)} %bitcast.61), channel_id=1, source_target_pairs={{0,64},{16,80},{32,96},{48,112},{64,0},{80,16},{96,32},{112,48},{1... | collective-permute-start | bytes 786440 | tf_op jit(solution)/shard_map/ppermute | solution.py:114
  165.8 0.7 collective-permute-start.27
  166.5 0.6 pad_maximum_fusion.2
  167.2 3.5 %collective-permute-done.20 = f32[4,16,1024]{2,1,0:T(8,128)S(1)} collective-permute-done((f32[4,16,1024]{2,1,0:T(8,128)S(1)}, f32[4,16,1024]{2,1,0:T(8,128)S(1)}, u32[]{:S(2)}, u32[]{:S(2)}) %collective-permute-start.20) | collective-permute-done | bytes 262176 | tf_op jit(solution)/shard_map/ppermute | solution.py:114
  170.8 0.7 collective-permute-start.28
  171.5 1.6 collective-permute-start.21
  173.1 1.3 collective-permute-start.29
  174.4 2.2 %collective-permute-done.21 = f32[2,16,1024]{2,1,0:T(8,128)S(1)} collective-permute-done((f32[2,16,1024]{2,1,0:T(8,128)S(1)}, f32[2,16,1024]{2,1,0:T(8,128)S(1)}, u32[]{:S(2)}, u32[]{:S(2)}) %collective-permute-start.21) | collective-permute-done | bytes 131104 | tf_op jit(solution)/shard_map/ppermute | solution.py:114
  176.7 4.8 %collective-permute-done.29 = f32[128,128]{1,0:T(8,128)S(1)} collective-permute-done((f32[128,128]{1,0:T(8,128)S(1)}, f32[128,128]{1,0:T(8,128)S(1)}, u32[]{:S(2)}, u32[]{:S(2)}) %collective-permute-start.29) | collective-permute-done | bytes 65568 | tf_op jit(solution)/shard_map/ppermute | solution.py:87
  181.5 0.3 fusion.1
  181.8 0.3 fusion.53
  182.4 0.3 fusion.17
  182.7 0.6 pad_maximum_fusion.1
  (97 shorter events, 2.7 us)
Async XLA Ops:
  14.6 37.0 %copy-start.6 = (bf16[16,1024]{1,0:T(8,128)(2,1)S(1)}, bf16[16,1024]{1,0:T(8,128)(2,1)}, u32[]{:S(2)}) copy-start(bf16[16,1024]{1,0:T(8,128)(2,1)} %param.14) | copy-start | bytes 98308
  14.6 37.2 %copy-start.11 = (bf16[16,1024]{1,0:T(8,128)(2,1)S(1)}, bf16[16,1024]{1,0:T(8,128)(2,1)}, u32[]{:S(2)}) copy-start(bf16[16,1024]{1,0:T(8,128)(2,1)} %param.13) | copy-start | bytes 98308
  14.6 37.6 %copy-start.5 = (f32[128,128]{1,0:T(8,128)S(1)}, f32[128,128]{1,0:T(8,128)}, u32[]{:S(2)}) copy-start(f32[128,128]{1,0:T(8,128)} %param.15) | copy-start | bytes 196612
  45.2 32.4 %copy-start.2 = (bf16[2048,128]{1,0:T(8,128)(2,1)S(1)}, bf16[2048,128]{1,0:T(8,128)(2,1)}, u32[]{:S(2)}) copy-start(bf16[2048,128]{1,0:T(8,128)(2,1)} %shard_map.137) | copy-start | bytes 1572868
  45.2 19.3 %collective-permute-start.6 = (f32[128,128]{1,0:T(8,128)S(1)}, f32[128,128]{1,0:T(8,128)S(1)}, u32[]{:S(2)}, u32[]{:S(2)}) collective-permute-start(f32[128,128]{1,0:T(8,128)S(1)} %fusion.11), channel_id=1, source_target_pairs={{0,16},{16,0},{32,48},{48,32},{64,80},{80,64},{96,112},{112,96},{1... | collective-permute-start | bytes 196616 | tf_op jit(solution)/shard_map/ppermute | solution.py:98
  48.6 37.9 %collective-permute-start.3 = (f32[4,16,1024]{2,1,0:T(8,128)S(1)}, f32[4,16,1024]{2,1,0:T(8,128)S(1)}, u32[]{:S(2)}, u32[]{:S(2)}) collective-permute-start(f32[4,16,1024]{2,1,0:T(8,128)S(1)} %bitcast.60), channel_id=1, source_target_pairs={{0,64},{16,80},{32,96},{48,112},{64,0},{80,16},{96,32},{112,48},{1... | collective-permute-start | bytes 786440 | tf_op jit(solution)/shard_map/ppermute | solution.py:114
  51.6 10.7 %collective-permute-start = (bf16[16,1024]{1,0:T(8,128)(2,1)S(1)}, bf16[16,1024]{1,0:T(8,128)(2,1)S(1)}, u32[]{:S(2)}, u32[]{:S(2)}) collective-permute-start(bf16[16,1024]{1,0:T(8,128)(2,1)S(1)} %copy-done.6), channel_id=1, source_target_pairs={{0,16},{16,0},{32,48},{48,32},{64,80},{80,64},{96,112},{112,96},{1... | collective-permute-start | bytes 98312 | tf_op jit(solution)/shard_map/ppermute | solution.py:124
  51.8 11.2 %collective-permute-start.13 = (bf16[16,1024]{1,0:T(8,128)(2,1)S(1)}, bf16[16,1024]{1,0:T(8,128)(2,1)S(1)}, u32[]{:S(2)}, u32[]{:S(2)}) collective-permute-start(bf16[16,1024]{1,0:T(8,128)(2,1)S(1)} %copy-done.11), channel_id=1, source_target_pairs={{0,16},{16,0},{32,48},{48,32},{64,80},{80,64},{96,112},{112,96},{1... | collective-permute-start | bytes 98312 | tf_op jit(solution)/shard_map/ppermute | solution.py:124
  62.3 5.0 %collective-permute-start.1 = (bf16[32,1024]{1,0:T(8,128)(2,1)S(1)}, bf16[32,1024]{1,0:T(8,128)(2,1)S(1)}, u32[]{:S(2)}, u32[]{:S(2)}) collective-permute-start(bf16[32,1024]{1,0:T(8,128)(2,1)S(1)} %maximum_select_fusion.4), channel_id=1, source_target_pairs={{0,32},{16,48},{32,0},{48,16},{64,96},{80,112},{96,64},{112,80},{1... | collective-permute-start | bytes 196616 | tf_op jit(solution)/shard_map/ppermute | solution.py:124
  63.0 8.2 %collective-permute-start.14 = (bf16[32,1024]{1,0:T(8,128)(2,1)S(1)}, bf16[32,1024]{1,0:T(8,128)(2,1)S(1)}, u32[]{:S(2)}, u32[]{:S(2)}) collective-permute-start(bf16[32,1024]{1,0:T(8,128)(2,1)S(1)} %maximum_select_fusion.5), channel_id=1, source_target_pairs={{0,32},{16,48},{32,0},{48,16},{64,96},{80,112},{96,64},{112,80},{1... | collective-permute-start | bytes 196616 | tf_op jit(solution)/shard_map/ppermute | solution.py:124
  64.6 5.6 %collective-permute-start.7 = (f32[128,128]{1,0:T(8,128)S(1)}, f32[128,128]{1,0:T(8,128)S(1)}, u32[]{:S(2)}, u32[]{:S(2)}) collective-permute-start(f32[128,128]{1,0:T(8,128)S(1)} %add.81), channel_id=1, source_target_pairs={{0,32},{16,48},{32,0},{48,16},{64,96},{80,112},{96,64},{112,80},{1... | collective-permute-start | bytes 196616 | tf_op jit(solution)/shard_map/ppermute | solution.py:98
  67.4 10.2 %collective-permute-start.2 = (bf16[64,1024]{1,0:T(8,128)(2,1)S(1)}, bf16[64,1024]{1,0:T(8,128)(2,1)S(1)}, u32[]{:S(2)}, u32[]{:S(2)}) collective-permute-start(bf16[64,1024]{1,0:T(8,128)(2,1)S(1)} %maximum_select_fusion.2), channel_id=1, source_target_pairs={{0,64},{16,80},{32,96},{48,112},{64,0},{80,16},{96,32},{112,48},{1... | collective-permute-start | bytes 393224 | tf_op jit(solution)/shard_map/ppermute | solution.py:124
  70.2 6.6 %collective-permute-start.8 = (f32[128,128]{1,0:T(8,128)S(1)}, f32[128,128]{1,0:T(8,128)S(1)}, u32[]{:S(2)}, u32[]{:S(2)}) collective-permute-start(f32[128,128]{1,0:T(8,128)S(1)} %add.82), channel_id=1, source_target_pairs={{0,64},{16,80},{32,96},{48,112},{64,0},{80,16},{96,32},{112,48},{1... | collective-permute-start | bytes 196616 | tf_op jit(solution)/shard_map/ppermute | solution.py:98
  71.2 57.6 %collective-permute-start.15 = (bf16[64,1024]{1,0:T(8,128)(2,1)S(1)}, bf16[64,1024]{1,0:T(8,128)(2,1)S(1)}, u32[]{:S(2)}, u32[]{:S(2)}) collective-permute-start(bf16[64,1024]{1,0:T(8,128)(2,1)S(1)} %maximum_select_fusion.3), channel_id=1, source_target_pairs={{0,64},{16,80},{32,96},{48,112},{64,0},{80,16},{96,32},{112,48},{1... | collective-permute-start | bytes 393224 | tf_op jit(solution)/shard_map/ppermute | solution.py:124
  76.8 9.0 %collective-permute-start.9 = (f32[128,128]{1,0:T(8,128)S(1)}, f32[128,128]{1,0:T(8,128)S(1)}, u32[]{:S(2)}, u32[]{:S(2)}) collective-permute-start(f32[128,128]{1,0:T(8,128)S(1)} %add.83), channel_id=1, source_target_pairs={{15,14},{31,30},{47,46},{63,62},{79,78},{95,94},{111,110},{127,126}} | collective-permute-start | bytes 196616 | tf_op jit(solution)/shard_map/ppermute | solution.py:87
  82.3 3.3 %copy-start = (f32[2048,1024]{1,0:T(8,128)}, f32[2048,1024]{1,0:T(8,128)S(1)}, u32[]{:S(2)}) copy-start(f32[2048,1024]{1,0:T(8,128)S(1)} %convolution_subtract_fusion.1) | copy-start | bytes 25165828
  85.6 18.4 %copy-start.4 = (f32[128,128]{1,0:T(8,128)S(1)}, f32[128,128]{1,0:T(8,128)}, u32[]{:S(2)}) copy-start(f32[128,128]{1,0:T(8,128)} %param.16) | copy-start | bytes 196612
  85.6 18.4 %copy-start.7 = (f32[128,128]{1,0:T(8,128)S(1)}, f32[128,128]{1,0:T(8,128)}, u32[]{:S(2)}) copy-start(f32[128,128]{1,0:T(8,128)} %param.21) | copy-start | bytes 196612
  85.6 19.4 %copy-start.12 = (f32[16,1024]{1,0:T(8,128)S(1)}, f32[16,1024]{1,0:T(8,128)}, u32[]{:S(2)}) copy-start(f32[16,1024]{1,0:T(8,128)} %param.19) | copy-start | bytes 196612
  85.7 1.0 collective-permute-start.10
  86.5 5.0 %collective-permute-start.4 = (f32[2,16,1024]{2,1,0:T(8,128)S(1)}, f32[2,16,1024]{2,1,0:T(8,128)S(1)}, u32[]{:S(2)}, u32[]{:S(2)}) collective-permute-start(f32[2,16,1024]{2,1,0:T(8,128)S(1)} %slice_select_fusion.6), channel_id=1, source_target_pairs={{0,32},{16,48},{32,0},{48,16},{64,96},{80,112},{96,64},{112,80},{1... | collective-permute-start | bytes 393224 | tf_op jit(solution)/shard_map/ppermute | solution.py:114
  86.8 4.8 %collective-permute-start.11 = (f32[128,128]{1,0:T(8,128)S(1)}, f32[128,128]{1,0:T(8,128)S(1)}, u32[]{:S(2)}, u32[]{:S(2)}) collective-permute-start(f32[128,128]{1,0:T(8,128)S(1)} %broadcast_select_fusion.4), channel_id=1, source_target_pairs={{15,11},{14,10},{13,9},{12,8},{31,27},{30,26},{29,25},{28,24},{47,... | collective-permute-start | bytes 196616 | tf_op jit(solution)/shard_map/ppermute | solution.py:87
  91.6 12.4 %collective-permute-start.12 = (f32[128,128]{1,0:T(8,128)S(1)}, f32[128,128]{1,0:T(8,128)S(1)}, u32[]{:S(2)}, u32[]{:S(2)}) collective-permute-start(f32[128,128]{1,0:T(8,128)S(1)} %broadcast_select_fusion.5), channel_id=1, source_target_pairs={{15,7},{14,6},{13,5},{12,4},{11,3},{10,2},{9,1},{8,0},{31,23},{30,... | collective-permute-start | bytes 196616 | tf_op jit(solution)/shard_map/ppermute | solution.py:87
  92.9 12.0 %collective-permute-start.5 = (f32[1,16,1024]{2,1,0:T(8,128)S(1)}, f32[1,16,1024]{2,1,0:T(8,128)S(1)}, u32[]{:S(2)}, u32[]{:S(2)}) collective-permute-start(f32[1,16,1024]{2,1,0:T(8,128)S(1)} %slice_select_fusion.8), channel_id=1, source_target_pairs={{0,16},{16,0},{32,48},{48,32},{64,80},{80,64},{96,112},{112,96},{1... | collective-permute-start | bytes 196616 | tf_op jit(solution)/shard_map/ppermute | solution.py:114
  104.8 29.0 %copy-start.9 = (f32[128,128]{1,0:T(8,128)}, f32[128,128]{1,0:T(8,128)S(1)}, u32[]{:S(2)}) copy-start(f32[128,128]{1,0:T(8,128)S(1)} %get-tuple-element.10) | copy-start | bytes 196612
  107.0 27.0 %collective-permute-start.16 = (bf16[16,128]{1,0:T(8,128)(2,1)S(1)}, bf16[16,128]{1,0:T(8,128)(2,1)S(1)}, u32[]{:S(2)}, u32[]{:S(2)}) collective-permute-start(bf16[16,128]{1,0:T(8,128)(2,1)S(1)} %slice.139), channel_id=1, source_target_pairs={{14,15},{30,31},{46,47},{62,63},{78,79},{94,95},{110,111},{126,127}} | collective-permute-start | bytes 12296 | tf_op jit(solution)/shard_map/ppermute | solution.py:87
  128.8 5.0 %copy-start.3 = (bf16[2048,128]{1,0:T(8,128)(2,1)S(1)}, bf16[2048,128]{1,0:T(8,128)(2,1)}, u32[]{:S(2)}) copy-start(bf16[2048,128]{1,0:T(8,128)(2,1)} %shard_map.138) | copy-start | bytes 1572868
  128.8 5.9 %copy-start.1 = (bf16[2048,1024]{1,0:T(8,128)(2,1)S(1)}, bf16[2048,1024]{1,0:T(8,128)(2,1)}, u32[]{:S(2)}) copy-start(bf16[2048,1024]{1,0:T(8,128)(2,1)} %param.12) | copy-start | bytes 12582916
  134.1 1.9 %collective-permute-start.17 = (bf16[16,128]{1,0:T(8,128)(2,1)S(1)}, bf16[16,128]{1,0:T(8,128)(2,1)S(1)}, u32[]{:S(2)}, u32[]{:S(2)}) collective-permute-start(bf16[16,128]{1,0:T(8,128)(2,1)S(1)} %broadcast_select_fusion.6), channel_id=1, source_target_pairs={{14,12},{15,13},{30,28},{31,29},{46,44},{47,45},{62,60},{63,61},{7... | collective-permute-start | bytes 12296 | tf_op jit(solution)/shard_map/ppermute | solution.py:87
  135.9 3.3 %collective-permute-start.18 = (bf16[16,128]{1,0:T(8,128)(2,1)S(1)}, bf16[16,128]{1,0:T(8,128)(2,1)S(1)}, u32[]{:S(2)}, u32[]{:S(2)}) collective-permute-start(bf16[16,128]{1,0:T(8,128)(2,1)S(1)} %broadcast_select_fusion.7), channel_id=1, source_target_pairs={{14,10},{15,11},{12,8},{13,9},{30,26},{31,27},{28,24},{29,25},{46,... | collective-permute-start | bytes 12296 | tf_op jit(solution)/shard_map/ppermute | solution.py:87
  139.3 42.3 %copy-start.8 = (f32[128,128]{1,0:T(8,128)S(1)}, f32[128,128]{1,0:T(8,128)}, u32[]{:S(2)}) copy-start(f32[128,128]{1,0:T(8,128)} %param.20) | copy-start | bytes 196612
  139.3 43.2 %copy-start.13 = (f32[16,1024]{1,0:T(8,128)S(1)}, f32[16,1024]{1,0:T(8,128)}, u32[]{:S(2)}) copy-start(f32[16,1024]{1,0:T(8,128)} %param.18) | copy-start | bytes 196612
  139.3 11.0 %collective-permute-start.19 = (bf16[16,128]{1,0:T(8,128)(2,1)S(1)}, bf16[16,128]{1,0:T(8,128)(2,1)S(1)}, u32[]{:S(2)}, u32[]{:S(2)}) collective-permute-start(bf16[16,128]{1,0:T(8,128)(2,1)S(1)} %broadcast_select_fusion.8), channel_id=1, source_target_pairs={{14,6},{15,7},{12,4},{13,5},{10,2},{11,3},{8,0},{9,1},{30,22},{31,... | collective-permute-start | bytes 12296 | tf_op jit(solution)/shard_map/ppermute | solution.py:87
  150.5 1.3 collective-permute-start.23
  151.8 4.3 %collective-permute-start.24 = (f32[128,128]{1,0:T(8,128)S(1)}, f32[128,128]{1,0:T(8,128)S(1)}, u32[]{:S(2)}, u32[]{:S(2)}) collective-permute-start(f32[128,128]{1,0:T(8,128)S(1)} %add.91), channel_id=1, source_target_pairs={{0,32},{16,48},{32,0},{48,16},{64,96},{80,112},{96,64},{112,80},{1... | collective-permute-start | bytes 196616 | tf_op jit(solution)/shard_map/ppermute | solution.py:98
  156.2 5.8 %collective-permute-start.25 = (f32[128,128]{1,0:T(8,128)S(1)}, f32[128,128]{1,0:T(8,128)S(1)}, u32[]{:S(2)}, u32[]{:S(2)}) collective-permute-start(f32[128,128]{1,0:T(8,128)S(1)} %add.92), channel_id=1, source_target_pairs={{0,64},{16,80},{32,96},{48,112},{64,0},{80,16},{96,32},{112,48},{1... | collective-permute-start | bytes 196616 | tf_op jit(solution)/shard_map/ppermute | solution.py:98
  162.0 3.8 %collective-permute-start.26 = (f32[128,128]{1,0:T(8,128)S(1)}, f32[128,128]{1,0:T(8,128)S(1)}, u32[]{:S(2)}, u32[]{:S(2)}) collective-permute-start(f32[128,128]{1,0:T(8,128)S(1)} %add.93), channel_id=1, source_target_pairs={{14,15},{30,31},{46,47},{62,63},{78,79},{94,95},{110,111},{126,127}} | collective-permute-start | bytes 196616 | tf_op jit(solution)/shard_map/ppermute | solution.py:87
  162.7 8.0 %collective-permute-start.20 = (f32[4,16,1024]{2,1,0:T(8,128)S(1)}, f32[4,16,1024]{2,1,0:T(8,128)S(1)}, u32[]{:S(2)}, u32[]{:S(2)}) collective-permute-start(f32[4,16,1024]{2,1,0:T(8,128)S(1)} %bitcast.61), channel_id=1, source_target_pairs={{0,64},{16,80},{32,96},{48,112},{64,0},{80,16},{96,32},{112,48},{1... | collective-permute-start | bytes 786440 | tf_op jit(solution)/shard_map/ppermute | solution.py:114
  165.8 4.9 %collective-permute-start.27 = (f32[128,128]{1,0:T(8,128)S(1)}, f32[128,128]{1,0:T(8,128)S(1)}, u32[]{:S(2)}, u32[]{:S(2)}) collective-permute-start(f32[128,128]{1,0:T(8,128)S(1)} %broadcast_select_fusion), channel_id=1, source_target_pairs={{14,12},{15,13},{30,28},{31,29},{46,44},{47,45},{62,60},{63,61},{7... | collective-permute-start | bytes 196616 | tf_op jit(solution)/shard_map/ppermute | solution.py:87
  170.8 2.3 %collective-permute-start.28 = (f32[128,128]{1,0:T(8,128)S(1)}, f32[128,128]{1,0:T(8,128)S(1)}, u32[]{:S(2)}, u32[]{:S(2)}) collective-permute-start(f32[128,128]{1,0:T(8,128)S(1)} %broadcast_select_fusion.1), channel_id=1, source_target_pairs={{14,10},{15,11},{12,8},{13,9},{30,26},{31,27},{28,24},{29,25},{46,... | collective-permute-start | bytes 196616 | tf_op jit(solution)/shard_map/ppermute | solution.py:87
  171.5 5.0 %collective-permute-start.21 = (f32[2,16,1024]{2,1,0:T(8,128)S(1)}, f32[2,16,1024]{2,1,0:T(8,128)S(1)}, u32[]{:S(2)}, u32[]{:S(2)}) collective-permute-start(f32[2,16,1024]{2,1,0:T(8,128)S(1)} %slice_select_fusion.5), channel_id=1, source_target_pairs={{0,32},{16,48},{32,0},{48,16},{64,96},{80,112},{96,64},{112,80},{1... | collective-permute-start | bytes 393224 | tf_op jit(solution)/shard_map/ppermute | solution.py:114
  173.1 8.5 %collective-permute-start.29 = (f32[128,128]{1,0:T(8,128)S(1)}, f32[128,128]{1,0:T(8,128)S(1)}, u32[]{:S(2)}, u32[]{:S(2)}) collective-permute-start(f32[128,128]{1,0:T(8,128)S(1)} %broadcast_select_fusion.2), channel_id=1, source_target_pairs={{14,6},{15,7},{12,4},{13,5},{10,2},{11,3},{8,0},{9,1},{30,22},{31,... | collective-permute-start | bytes 196616 | tf_op jit(solution)/shard_map/ppermute | solution.py:87
  176.6 5.9 %collective-permute-start.22 = (f32[1,16,1024]{2,1,0:T(8,128)S(1)}, f32[1,16,1024]{2,1,0:T(8,128)S(1)}, u32[]{:S(2)}, u32[]{:S(2)}) collective-permute-start(f32[1,16,1024]{2,1,0:T(8,128)S(1)} %slice_select_fusion.7), channel_id=1, source_target_pairs={{0,16},{16,0},{32,48},{48,32},{64,80},{80,64},{96,112},{112,96},{1... | collective-permute-start | bytes 196616 | tf_op jit(solution)/shard_map/ppermute | solution.py:114
  182.3 1.1 copy-start.10

commit v5 on v4

--- a/solution.py
+++ b/solution.py
@@ -141,7 +141,7 @@
 
 
 def inverse_lower(block):
-    ident = jnp.eye(block.shape[0], dtype=block.dtype)
+    ident = jnp.broadcast_to(jnp.eye(block.shape[-1], dtype=block.dtype), block.shape)
     return lax.linalg.triangular_solve(block, ident, left_side=True, lower=True)
 
 
@@ -192,14 +192,15 @@
             rows_sum = butterfly_sum(partial_value, "row", n_row)
             return tree_broadcast(rows_sum, "col", n_col, root)
 
-        inverse_two = inverse_lower(diag_two)
+        both = inverse_lower(jnp.stack([diag_two, diag_one]))
+        inverse_two = both[0]
+        inverse_one = both[1]
         solved_two = solve_panel(adj_trail[:, last:], inverse_two, root_two)
         partial_two = jnp.dot(solved_two.T, trail[:, last:], preferred_element_type=jnp.float32)
         seed_two = jnp.tril(adj_diag_two - summed_block(partial_two, root_two))
         grad_diag_two = block_adjoint(diag_two, inverse_two, seed_two)
         mirror_two = own_rows(grad_diag_two + grad_diag_two.T)
         rest_two = jnp.dot(mirror_two, full_two.astype(jnp.float32), precision=exact_mode)
-        inverse_one = inverse_lower(diag_one)
         crossed = halving_scatter(
             jnp.dot(solved_two.T, trail, preferred_element_type=jnp.float32), "row", n_row
         )

time: 184 us -> 189 us (1.027)
  starting transfers between devices: 30.4 us -> 33.3 us
    ppermute x6, waiting for transfers between devices: 2.14 us -> 6.21 us  [doubling_gather(): other = lax.ppermute(value, axis, pairs)]
    ppermute x6, waiting for transfers between devices: 11.7 us -> 9.7 us  [butterfly_sum(): value = value + lax.ppermute(value, axis, pairs)]
    another operation x4 -> x3, other arithmetic: 20.5 us -> 20.6 us  [inverse_lower(): return lax.linalg.triangular_solve(block, ident, left_side=True, lower=True)]
  transfers between devices with their start and end apart: 30 -> 30, of which waited for: 12 -> 13; matrix products, arithmetic and copies ran while one was open for 18% -> 12% of each run, Pallas kernels for 12% -> 12%
where the time goes in v5:
time: 189 us; the launch traced here: 188 us
  Pallas kernels  51.2 us (27%)
  waiting for transfers between devices  49.5 us (26%)
  starting transfers between devices  33.3 us (18%)
  other arithmetic  25.2 us (13%)
  matrix products  22.3 us (12%)
  local copies, waits for them, and re-layouts  4.94 us (3%)
    pallas_call x2, Pallas kernels, panel_broadcast(): pl.pallas_call(functools.partial(spread_kernel, root, size), out_shape=ja...  51.2 us
    ppermute x12, waiting for transfers between devices, tree_broadcast(): arrived = lax.ppermute(value, axis, pairs)  24.9 us
    another operation x3, other arithmetic, inverse_lower(): return lax.linalg.triangular_solve(block, ident, left_side=True, lower=True)  20.6 us
    ppermute x12, starting transfers between devices, tree_broadcast(): arrived = lax.ppermute(value, axis, pairs)  9.97 us
    ppermute x6, waiting for transfers between devices, butterfly_sum(): value = value + lax.ppermute(value, axis, pairs)  9.7 us
    ppermute x6, starting transfers between devices, halving_scatter(): blocks = keep + lax.ppermute(send, axis, pairs)  9.43 us
    ppermute x6, waiting for transfers between devices, halving_scatter(): blocks = keep + lax.ppermute(send, axis, pairs)  8.73 us
    ppermute x6, starting transfers between devices, butterfly_sum(): value = value + lax.ppermute(value, axis, pairs)  7.25 us
  transfers between devices with their start and end apart: 30, of which 13 were waited for; matrix products, arithmetic and copies ran while one was open for 12% of the time, Pallas kernels for 12%

profile of v5, /device:TPU:0, one launch (start us, length us, event | category | flops | bytes accessed | tf_op | source)
XLA Modules:
  0.0 188.0 jit_solution(2661689223250479026)
XLA Ops:
  0.7 0.9 maximum_select_fusion.2
  1.6 19.7 %custom-call.3 = f32[2,1,128,128]{2,3,1,0:T(8,128)S(1)} custom-call(f32[2,1,128,128]{3,2,1,0:T(8,128)S(1)} %maximum_select_fusion.2), custom_call_target="InvertDiagBlocksLowerTriangular" | custom-call | tf_op jit(solution)/shard_map/triangular_solve | solution.py:145
  21.3 0.4 fusion.13
  21.6 3.0 %fusion.x_ref = bf16[2048,128]{1,0:T(8,128)(2,1)} fusion(f32[2048,1024]{1,0:T(8,128)} %param.15, f32[2,128,128]{2,1,0:T(8,128)S(1)} %fusion.13), kind=kOutput, calls=%fused_computation.6 | convolution fusion | flops 402915328 | bytes 1638400 | tf_op jit(solution)/shard_map/dot_general | solution.py:184
  24.6 29.1 %shard_map.137 = bf16[2048,128]{1,0:T(8,128)(2,1)} custom-call(bf16[2048,128]{1,0:T(8,128)(2,1)} %fusion.x_ref), custom_call_target="tpu_custom_call" | custom-call | tf_op jit(solution)/shard_map/pallas_call | solution.py:68
  53.7 1.5 fusion.11
  55.4 0.5 collective-permute-start
  55.9 3.1 %fusion.48 = f32[128,1024]{1,0:T(8,128)S(1)} fusion(bf16[2048,128]{1,0:T(8,128)(2,1)} %shard_map.137, bf16[2048,1024]{1,0:T(8,128)(2,1)} %param.10), kind=kOutput, calls=%fused_computation.105 | convolution fusion | flops 536870912 | bytes 5242880 | tf_op jit(solution)/shard_map/dot_general | solution.py:205
  59.0 3.1 %collective-permute-start.3 = (f32[4,16,1024]{2,1,0:T(8,128)S(1)}, f32[4,16,1024]{2,1,0:T(8,128)S(1)}, u32[]{:S(2)}, u32[]{:S(2)}) collective-permute-start(f32[4,16,1024]{2,1,0:T(8,128)S(1)} %bitcast.65), channel_id=1, source_target_pairs={{0,64},{16,80},{32,96},{48,112},{64,0},{80,16},{96,32},{112,48},{1... | collective-permute-start | bytes 786440 | tf_op jit(solution)/shard_map/ppermute | solution.py:114
  62.2 0.7 collective-permute-start.1
  62.8 0.5 collective-permute-done.13
  63.4 1.0 collective-permute-start.14
  64.4 1.2 collective-permute-start.7
  65.6 5.7 %collective-permute-done.1 = bf16[32,1024]{1,0:T(8,128)(2,1)S(1)} collective-permute-done((bf16[32,1024]{1,0:T(8,128)(2,1)S(1)}, bf16[32,1024]{1,0:T(8,128)(2,1)S(1)}, u32[]{:S(2)}, u32[]{:S(2)}) %collective-permute-start.1) | collective-permute-done | bytes 65568 | tf_op jit(solution)/shard_map/ppermute | solution.py:124
  71.3 2.1 %collective-permute-start.2 = (bf16[64,1024]{1,0:T(8,128)(2,1)S(1)}, bf16[64,1024]{1,0:T(8,128)(2,1)S(1)}, u32[]{:S(2)}, u32[]{:S(2)}) collective-permute-start(bf16[64,1024]{1,0:T(8,128)(2,1)S(1)} %maximum_select_fusion.3), channel_id=1, source_target_pairs={{0,64},{16,80},{32,96},{48,112},{64,0},{80,16},{96,32},{112,48},{1... | collective-permute-start | bytes 393224 | tf_op jit(solution)/shard_map/ppermute | solution.py:124
  73.4 0.6 collective-permute-done.7
  74.1 1.3 collective-permute-start.8
  75.4 2.4 %collective-permute-start.15 = (bf16[64,1024]{1,0:T(8,128)(2,1)S(1)}, bf16[64,1024]{1,0:T(8,128)(2,1)S(1)}, u32[]{:S(2)}, u32[]{:S(2)}) collective-permute-start(bf16[64,1024]{1,0:T(8,128)(2,1)S(1)} %maximum_select_fusion.4), channel_id=1, source_target_pairs={{0,64},{16,80},{32,96},{48,112},{64,0},{80,16},{96,32},{112,48},{1... | collective-permute-start | bytes 393224 | tf_op jit(solution)/shard_map/ppermute | solution.py:124
  77.8 2.8 %collective-permute-done.8 = f32[128,128]{1,0:T(8,128)S(1)} collective-permute-done((f32[128,128]{1,0:T(8,128)S(1)}, f32[128,128]{1,0:T(8,128)S(1)}, u32[]{:S(2)}, u32[]{:S(2)}) %collective-permute-start.8) | collective-permute-done | bytes 65568 | tf_op jit(solution)/shard_map/ppermute | solution.py:98
  80.6 0.7 collective-permute-start.9
  81.3 4.6 %convolution_subtract_fusion.1 = f32[2048,1024]{1,0:T(8,128)S(1)} fusion(f32[2048,1024]{1,0:T(8,128)} %param.15, bf16[2048,128]{1,0:T(8,128)(2,1)S(1)} %copy-done.2, bf16[64,1024]{1,0:T(8,128)(2,1)S(1)} %maximum_select_fusion.3, bf16[64,1024]{1,0:T(8,128)(2,1)S(1)} %collective-permute-done.2, pred[]{:T(512)S(6)} %eq.59), kind=kOutput, calls=%fused_computation.2 | convolution fusion | flops 540147712 | bytes 17563648 | tf_op jit(solution)/shard_map/dot_general | solution.py:208
  85.9 3.3 %copy-done = f32[2048,1024]{1,0:T(8,128)} copy-done((f32[2048,1024]{1,0:T(8,128)}, f32[2048,1024]{1,0:T(8,128)S(1)}, u32[]{:S(2)}) %copy-start) | copy-done | bytes 8388632
  89.4 0.7 collective-permute-start.10
  90.1 1.4 collective-permute-start.4
  91.5 0.7 collective-permute-start.11
  92.2 3.0 %collective-permute-done.4 = f32[2,16,1024]{2,1,0:T(8,128)S(1)} collective-permute-done((f32[2,16,1024]{2,1,0:T(8,128)S(1)}, f32[2,16,1024]{2,1,0:T(8,128)S(1)}, u32[]{:S(2)}, u32[]{:S(2)}) %collective-permute-start.4) | collective-permute-done | bytes 131104 | tf_op jit(solution)/shard_map/ppermute | solution.py:114
  95.2 1.3 collective-permute-start.12
  96.6 0.3 collective-permute-start.5
  96.8 10.8 %collective-permute-done.12 = f32[128,128]{1,0:T(8,128)S(1)} collective-permute-done((f32[128,128]{1,0:T(8,128)S(1)}, f32[128,128]{1,0:T(8,128)S(1)}, u32[]{:S(2)}, u32[]{:S(2)}) %collective-permute-start.12) | collective-permute-done | bytes 65568 | tf_op jit(solution)/shard_map/ppermute | solution.py:87
  107.6 0.3 fusion.2
  107.9 0.3 fusion.28
  108.6 0.3 fusion.16
  108.8 1.0 convolution_convert_fusion
  109.8 0.8 slice.148.x_ref
  110.7 0.6 collective-permute-start.16
  111.3 22.1 %shard_map.138 = bf16[2048,128]{1,0:T(8,128)(2,1)} custom-call(bf16[2048,128]{1,0:T(8,128)(2,1)} %slice.148.x_ref), custom_call_target="tpu_custom_call" | custom-call | tf_op jit(solution)/shard_map/pallas_call | solution.py:68
  133.4 4.9 %convolution_subtract_fusion = bf16[2048,1024]{1,0:T(8,128)(2,1)S(1)} fusion(f32[2048,1024]{1,0:T(8,128)} %copy-done, bf16[2048,128]{1,0:T(8,128)(2,1)} %shard_map.138, bf16[64,1024]{1,0:T(8,128)(2,1)S(1)} %maximum_select_fusion.4, bf16[64,1024]{1,0:T(8,128)(2,1)S(1)} %collective-permute-done.15, pred[]{:T(512)S(6)} %eq.59), kind=kOutput, calls=%fused_computation.1 | convolution fusion | flops 542244864 | bytes 13369345 | tf_op jit(solution)/shard_map/dot_general | solution.py:222
  138.7 0.7 collective-permute-start.17
  139.3 0.7 fusion.49
  140.1 0.4 slice.213
  140.5 0.7 collective-permute-start.18
  141.2 2.6 %pad_maximum_fusion = bf16[2048,1024]{1,0:T(8,128)(2,1)} fusion(bf16[2048,128]{1,0:T(8,128)(2,1)S(1)} %fusion.7, bf16[2048,896]{1,0:T(8,128)(2,1)S(1)} %slice.213), kind=kLoop, calls=%fused_computation.3 | loop fusion | flops 8388608 | bytes 8388608 | tf_op jit(solution)/shard_map/concatenate | solution.py:235
  143.9 1.4 collective-permute-start.19
  145.3 0.3 fusion.9
  145.7 9.2 %collective-permute-done.19 = bf16[16,128]{1,0:T(8,128)(2,1)S(1)} collective-permute-done((bf16[16,128]{1,0:T(8,128)(2,1)S(1)}, bf16[16,128]{1,0:T(8,128)(2,1)S(1)}, u32[]{:S(2)}, u32[]{:S(2)}) %collective-permute-start.19) | collective-permute-done | bytes 4128 | tf_op jit(solution)/shard_map/ppermute | solution.py:87
  155.4 1.0 collective-permute-done.23
  156.4 1.6 collective-permute-start.24
  158.0 2.7 %collective-permute-done.24 = f32[128,128]{1,0:T(8,128)S(1)} collective-permute-done((f32[128,128]{1,0:T(8,128)S(1)}, f32[128,128]{1,0:T(8,128)S(1)}, u32[]{:S(2)}, u32[]{:S(2)}) %collective-permute-start.24) | collective-permute-done | bytes 65568 | tf_op jit(solution)/shard_map/ppermute | solution.py:98
  160.8 3.1 %collective-permute-start.25 = (f32[128,128]{1,0:T(8,128)S(1)}, f32[128,128]{1,0:T(8,128)S(1)}, u32[]{:S(2)}, u32[]{:S(2)}) collective-permute-start(f32[128,128]{1,0:T(8,128)S(1)} %add.93), channel_id=1, source_target_pairs={{0,64},{16,80},{32,96},{48,112},{64,0},{80,16},{96,32},{112,48},{1... | collective-permute-start | bytes 196616 | tf_op jit(solution)/shard_map/ppermute | solution.py:98
  164.0 2.6 %collective-permute-done.25 = f32[128,128]{1,0:T(8,128)S(1)} collective-permute-done((f32[128,128]{1,0:T(8,128)S(1)}, f32[128,128]{1,0:T(8,128)S(1)}, u32[]{:S(2)}, u32[]{:S(2)}) %collective-permute-start.25) | collective-permute-done | bytes 65568 | tf_op jit(solution)/shard_map/ppermute | solution.py:98
  166.6 0.7 collective-permute-start.26
  167.3 3.1 %collective-permute-start.20 = (f32[4,16,1024]{2,1,0:T(8,128)S(1)}, f32[4,16,1024]{2,1,0:T(8,128)S(1)}, u32[]{:S(2)}, u32[]{:S(2)}) collective-permute-start(f32[4,16,1024]{2,1,0:T(8,128)S(1)} %bitcast.66), channel_id=1, source_target_pairs={{0,64},{16,80},{32,96},{48,112},{64,0},{80,16},{96,32},{112,48},{1... | collective-permute-start | bytes 786440 | tf_op jit(solution)/shard_map/ppermute | solution.py:114
  170.4 0.7 collective-permute-start.27
  171.1 0.6 pad_maximum_fusion.2
  171.8 3.5 %collective-permute-done.20 = f32[4,16,1024]{2,1,0:T(8,128)S(1)} collective-permute-done((f32[4,16,1024]{2,1,0:T(8,128)S(1)}, f32[4,16,1024]{2,1,0:T(8,128)S(1)}, u32[]{:S(2)}, u32[]{:S(2)}) %collective-permute-start.20) | collective-permute-done | bytes 262176 | tf_op jit(solution)/shard_map/ppermute | solution.py:114
  175.4 0.7 collective-permute-start.28
  176.1 1.6 collective-permute-start.21
  177.7 1.3 collective-permute-start.29
  178.9 2.2 %collective-permute-done.21 = f32[2,16,1024]{2,1,0:T(8,128)S(1)} collective-permute-done((f32[2,16,1024]{2,1,0:T(8,128)S(1)}, f32[2,16,1024]{2,1,0:T(8,128)S(1)}, u32[]{:S(2)}, u32[]{:S(2)}) %collective-permute-start.21) | collective-permute-done | bytes 131104 | tf_op jit(solution)/shard_map/ppermute | solution.py:114
  181.3 4.9 %collective-permute-done.29 = f32[128,128]{1,0:T(8,128)S(1)} collective-permute-done((f32[128,128]{1,0:T(8,128)S(1)}, f32[128,128]{1,0:T(8,128)S(1)}, u32[]{:S(2)}, u32[]{:S(2)}) %collective-permute-start.29) | collective-permute-done | bytes 65568 | tf_op jit(solution)/shard_map/ppermute | solution.py:87
  186.1 0.3 fusion.1
  186.4 0.3 fusion.30
  187.1 0.3 fusion.15
  187.3 0.6 pad_maximum_fusion.1
  (96 shorter events, 2.5 us)
Async XLA Ops:
  0.6 54.8 %copy-start.6 = (bf16[16,1024]{1,0:T(8,128)(2,1)S(1)}, bf16[16,1024]{1,0:T(8,128)(2,1)}, u32[]{:S(2)}) copy-start(bf16[16,1024]{1,0:T(8,128)(2,1)} %param.12) | copy-start | bytes 98308
  24.6 37.5 %copy-start.11 = (bf16[16,1024]{1,0:T(8,128)(2,1)S(1)}, bf16[16,1024]{1,0:T(8,128)(2,1)}, u32[]{:S(2)}) copy-start(bf16[16,1024]{1,0:T(8,128)(2,1)} %param.11) | copy-start | bytes 98308
  55.3 26.0 %copy-start.2 = (bf16[2048,128]{1,0:T(8,128)(2,1)S(1)}, bf16[2048,128]{1,0:T(8,128)(2,1)}, u32[]{:S(2)}) copy-start(bf16[2048,128]{1,0:T(8,128)(2,1)} %shard_map.137) | copy-start | bytes 1572868
  55.3 9.1 %collective-permute-start.6 = (f32[128,128]{1,0:T(8,128)S(1)}, f32[128,128]{1,0:T(8,128)S(1)}, u32[]{:S(2)}, u32[]{:S(2)}) collective-permute-start(f32[128,128]{1,0:T(8,128)S(1)} %fusion.11), channel_id=1, source_target_pairs={{0,16},{16,0},{32,48},{48,32},{64,80},{80,64},{96,112},{112,96},{1... | collective-permute-start | bytes 196616 | tf_op jit(solution)/shard_map/ppermute | solution.py:98
  55.4 6.7 %collective-permute-start = (bf16[16,1024]{1,0:T(8,128)(2,1)S(1)}, bf16[16,1024]{1,0:T(8,128)(2,1)S(1)}, u32[]{:S(2)}, u32[]{:S(2)}) collective-permute-start(bf16[16,1024]{1,0:T(8,128)(2,1)S(1)} %copy-done.6), channel_id=1, source_target_pairs={{0,16},{16,0},{32,48},{48,32},{64,80},{80,64},{96,112},{112,96},{1... | collective-permute-start | bytes 98312 | tf_op jit(solution)/shard_map/ppermute | solution.py:124
  59.0 31.0 %collective-permute-start.3 = (f32[4,16,1024]{2,1,0:T(8,128)S(1)}, f32[4,16,1024]{2,1,0:T(8,128)S(1)}, u32[]{:S(2)}, u32[]{:S(2)}) collective-permute-start(f32[4,16,1024]{2,1,0:T(8,128)S(1)} %bitcast.65), channel_id=1, source_target_pairs={{0,64},{16,80},{32,96},{48,112},{64,0},{80,16},{96,32},{112,48},{1... | collective-permute-start | bytes 786440 | tf_op jit(solution)/shard_map/ppermute | solution.py:114
  62.1 1.2 collective-permute-start.13
  62.2 9.1 %collective-permute-start.1 = (bf16[32,1024]{1,0:T(8,128)(2,1)S(1)}, bf16[32,1024]{1,0:T(8,128)(2,1)S(1)}, u32[]{:S(2)}, u32[]{:S(2)}) collective-permute-start(bf16[32,1024]{1,0:T(8,128)(2,1)S(1)} %maximum_select_fusion.5), channel_id=1, source_target_pairs={{0,32},{16,48},{32,0},{48,16},{64,96},{80,112},{96,64},{112,80},{1... | collective-permute-start | bytes 196616 | tf_op jit(solution)/shard_map/ppermute | solution.py:124
  63.4 12.0 %collective-permute-start.14 = (bf16[32,1024]{1,0:T(8,128)(2,1)S(1)}, bf16[32,1024]{1,0:T(8,128)(2,1)S(1)}, u32[]{:S(2)}, u32[]{:S(2)}) collective-permute-start(bf16[32,1024]{1,0:T(8,128)(2,1)S(1)} %maximum_select_fusion.6), channel_id=1, source_target_pairs={{0,32},{16,48},{32,0},{48,16},{64,96},{80,112},{96,64},{112,80},{1... | collective-permute-start | bytes 196616 | tf_op jit(solution)/shard_map/ppermute | solution.py:124
  64.4 9.7 %collective-permute-start.7 = (f32[128,128]{1,0:T(8,128)S(1)}, f32[128,128]{1,0:T(8,128)S(1)}, u32[]{:S(2)}, u32[]{:S(2)}) collective-permute-start(f32[128,128]{1,0:T(8,128)S(1)} %add.82), channel_id=1, source_target_pairs={{0,32},{16,48},{32,0},{48,16},{64,96},{80,112},{96,64},{112,80},{1... | collective-permute-start | bytes 196616 | tf_op jit(solution)/shard_map/ppermute | solution.py:98
  71.3 10.0 %collective-permute-start.2 = (bf16[64,1024]{1,0:T(8,128)(2,1)S(1)}, bf16[64,1024]{1,0:T(8,128)(2,1)S(1)}, u32[]{:S(2)}, u32[]{:S(2)}) collective-permute-start(bf16[64,1024]{1,0:T(8,128)(2,1)S(1)} %maximum_select_fusion.3), channel_id=1, source_target_pairs={{0,64},{16,80},{32,96},{48,112},{64,0},{80,16},{96,32},{112,48},{1... | collective-permute-start | bytes 393224 | tf_op jit(solution)/shard_map/ppermute | solution.py:124
  74.1 6.5 %collective-permute-start.8 = (f32[128,128]{1,0:T(8,128)S(1)}, f32[128,128]{1,0:T(8,128)S(1)}, u32[]{:S(2)}, u32[]{:S(2)}) collective-permute-start(f32[128,128]{1,0:T(8,128)S(1)} %add.83), channel_id=1, source_target_pairs={{0,64},{16,80},{32,96},{48,112},{64,0},{80,16},{96,32},{112,48},{1... | collective-permute-start | bytes 196616 | tf_op jit(solution)/shard_map/ppermute | solution.py:98
  75.4 58.1 %collective-permute-start.15 = (bf16[64,1024]{1,0:T(8,128)(2,1)S(1)}, bf16[64,1024]{1,0:T(8,128)(2,1)S(1)}, u32[]{:S(2)}, u32[]{:S(2)}) collective-permute-start(bf16[64,1024]{1,0:T(8,128)(2,1)S(1)} %maximum_select_fusion.4), channel_id=1, source_target_pairs={{0,64},{16,80},{32,96},{48,112},{64,0},{80,16},{96,32},{112,48},{1... | collective-permute-start | bytes 393224 | tf_op jit(solution)/shard_map/ppermute | solution.py:124
  80.6 8.8 %collective-permute-start.9 = (f32[128,128]{1,0:T(8,128)S(1)}, f32[128,128]{1,0:T(8,128)S(1)}, u32[]{:S(2)}, u32[]{:S(2)}) collective-permute-start(f32[128,128]{1,0:T(8,128)S(1)} %add.84), channel_id=1, source_target_pairs={{15,14},{31,30},{47,46},{63,62},{79,78},{95,94},{111,110},{127,126}} | collective-permute-start | bytes 196616 | tf_op jit(solution)/shard_map/ppermute | solution.py:87
  85.9 3.3 %copy-start = (f32[2048,1024]{1,0:T(8,128)}, f32[2048,1024]{1,0:T(8,128)S(1)}, u32[]{:S(2)}) copy-start(f32[2048,1024]{1,0:T(8,128)S(1)} %convolution_subtract_fusion.1) | copy-start | bytes 25165828
  89.2 18.4 %copy-start.4 = (f32[128,128]{1,0:T(8,128)S(1)}, f32[128,128]{1,0:T(8,128)}, u32[]{:S(2)}) copy-start(f32[128,128]{1,0:T(8,128)} %param.14) | copy-start | bytes 196612
  89.2 18.4 %copy-start.7 = (f32[128,128]{1,0:T(8,128)S(1)}, f32[128,128]{1,0:T(8,128)}, u32[]{:S(2)}) copy-start(f32[128,128]{1,0:T(8,128)} %param.19) | copy-start | bytes 196612
  89.2 19.4 %copy-start.12 = (f32[16,1024]{1,0:T(8,128)S(1)}, f32[16,1024]{1,0:T(8,128)}, u32[]{:S(2)}) copy-start(f32[16,1024]{1,0:T(8,128)} %param.17) | copy-start | bytes 196612
  89.4 2.1 %collective-permute-start.10 = (f32[128,128]{1,0:T(8,128)S(1)}, f32[128,128]{1,0:T(8,128)S(1)}, u32[]{:S(2)}, u32[]{:S(2)}) collective-permute-start(f32[128,128]{1,0:T(8,128)S(1)} %broadcast_select_fusion.3), channel_id=1, source_target_pairs={{15,13},{14,12},{31,29},{30,28},{47,45},{46,44},{63,61},{62,60},{7... | collective-permute-start | bytes 196616 | tf_op jit(solution)/shard_map/ppermute | solution.py:87
  90.1 5.0 %collective-permute-start.4 = (f32[2,16,1024]{2,1,0:T(8,128)S(1)}, f32[2,16,1024]{2,1,0:T(8,128)S(1)}, u32[]{:S(2)}, u32[]{:S(2)}) collective-permute-start(f32[2,16,1024]{2,1,0:T(8,128)S(1)} %slice_select_fusion.6), channel_id=1, source_target_pairs={{0,32},{16,48},{32,0},{48,16},{64,96},{80,112},{96,64},{112,80},{1... | collective-permute-start | bytes 393224 | tf_op jit(solution)/shard_map/ppermute | solution.py:114
  91.5 3.7 %collective-permute-start.11 = (f32[128,128]{1,0:T(8,128)S(1)}, f32[128,128]{1,0:T(8,128)S(1)}, u32[]{:S(2)}, u32[]{:S(2)}) collective-permute-start(f32[128,128]{1,0:T(8,128)S(1)} %broadcast_select_fusion.4), channel_id=1, source_target_pairs={{15,11},{14,10},{13,9},{12,8},{31,27},{30,26},{29,25},{28,24},{47,... | collective-permute-start | bytes 196616 | tf_op jit(solution)/shard_map/ppermute | solution.py:87
  95.2 12.4 %collective-permute-start.12 = (f32[128,128]{1,0:T(8,128)S(1)}, f32[128,128]{1,0:T(8,128)S(1)}, u32[]{:S(2)}, u32[]{:S(2)}) collective-permute-start(f32[128,128]{1,0:T(8,128)S(1)} %broadcast_select_fusion.5), channel_id=1, source_target_pairs={{15,7},{14,6},{13,5},{12,4},{11,3},{10,2},{9,1},{8,0},{31,23},{30,... | collective-permute-start | bytes 196616 | tf_op jit(solution)/shard_map/ppermute | solution.py:87
  96.6 12.0 %collective-permute-start.5 = (f32[1,16,1024]{2,1,0:T(8,128)S(1)}, f32[1,16,1024]{2,1,0:T(8,128)S(1)}, u32[]{:S(2)}, u32[]{:S(2)}) collective-permute-start(f32[1,16,1024]{2,1,0:T(8,128)S(1)} %slice_select_fusion.8), channel_id=1, source_target_pairs={{0,16},{16,0},{32,48},{48,32},{64,80},{80,64},{96,112},{112,96},{1... | collective-permute-start | bytes 196616 | tf_op jit(solution)/shard_map/ppermute | solution.py:114
  108.4 30.0 %copy-start.9 = (f32[128,128]{1,0:T(8,128)}, f32[128,128]{1,0:T(8,128)S(1)}, u32[]{:S(2)}) copy-start(f32[128,128]{1,0:T(8,128)S(1)} %get-tuple-element.9) | copy-start | bytes 196612
  110.7 28.0 %collective-permute-start.16 = (bf16[16,128]{1,0:T(8,128)(2,1)S(1)}, bf16[16,128]{1,0:T(8,128)(2,1)S(1)}, u32[]{:S(2)}, u32[]{:S(2)}) collective-permute-start(bf16[16,128]{1,0:T(8,128)(2,1)S(1)} %slice.151), channel_id=1, source_target_pairs={{14,15},{30,31},{46,47},{62,63},{78,79},{94,95},{110,111},{126,127}} | collective-permute-start | bytes 12296 | tf_op jit(solution)/shard_map/ppermute | solution.py:87
  133.4 5.0 %copy-start.3 = (bf16[2048,128]{1,0:T(8,128)(2,1)S(1)}, bf16[2048,128]{1,0:T(8,128)(2,1)}, u32[]{:S(2)}) copy-start(bf16[2048,128]{1,0:T(8,128)(2,1)} %shard_map.138) | copy-start | bytes 1572868
  133.4 5.9 %copy-start.1 = (bf16[2048,1024]{1,0:T(8,128)(2,1)S(1)}, bf16[2048,1024]{1,0:T(8,128)(2,1)}, u32[]{:S(2)}) copy-start(bf16[2048,1024]{1,0:T(8,128)(2,1)} %param.10) | copy-start | bytes 12582916
  138.7 1.9 collective-permute-start.17
  140.5 3.3 %collective-permute-start.18 = (bf16[16,128]{1,0:T(8,128)(2,1)S(1)}, bf16[16,128]{1,0:T(8,128)(2,1)S(1)}, u32[]{:S(2)}, u32[]{:S(2)}) collective-permute-start(bf16[16,128]{1,0:T(8,128)(2,1)S(1)} %broadcast_select_fusion.7), channel_id=1, source_target_pairs={{14,10},{15,11},{12,8},{13,9},{30,26},{31,27},{28,24},{29,25},{46,... | collective-permute-start | bytes 12296 | tf_op jit(solution)/shard_map/ppermute | solution.py:87
  143.9 42.3 %copy-start.5 = (f32[128,128]{1,0:T(8,128)S(1)}, f32[128,128]{1,0:T(8,128)}, u32[]{:S(2)}) copy-start(f32[128,128]{1,0:T(8,128)} %param.13) | copy-start | bytes 196612
  143.9 42.3 %copy-start.8 = (f32[128,128]{1,0:T(8,128)S(1)}, f32[128,128]{1,0:T(8,128)}, u32[]{:S(2)}) copy-start(f32[128,128]{1,0:T(8,128)} %param.18) | copy-start | bytes 196612
  143.9 43.2 %copy-start.13 = (f32[16,1024]{1,0:T(8,128)S(1)}, f32[16,1024]{1,0:T(8,128)}, u32[]{:S(2)}) copy-start(f32[16,1024]{1,0:T(8,128)} %param.16) | copy-start | bytes 196612
  143.9 11.0 %collective-permute-start.19 = (bf16[16,128]{1,0:T(8,128)(2,1)S(1)}, bf16[16,128]{1,0:T(8,128)(2,1)S(1)}, u32[]{:S(2)}, u32[]{:S(2)}) collective-permute-start(bf16[16,128]{1,0:T(8,128)(2,1)S(1)} %broadcast_select_fusion.8), channel_id=1, source_target_pairs={{14,6},{15,7},{12,4},{13,5},{10,2},{11,3},{8,0},{9,1},{30,22},{31,... | collective-permute-start | bytes 12296 | tf_op jit(solution)/shard_map/ppermute | solution.py:87
  155.1 1.3 collective-permute-start.23
  156.4 4.3 %collective-permute-start.24 = (f32[128,128]{1,0:T(8,128)S(1)}, f32[128,128]{1,0:T(8,128)S(1)}, u32[]{:S(2)}, u32[]{:S(2)}) collective-permute-start(f32[128,128]{1,0:T(8,128)S(1)} %add.92), channel_id=1, source_target_pairs={{0,32},{16,48},{32,0},{48,16},{64,96},{80,112},{96,64},{112,80},{1... | collective-permute-start | bytes 196616 | tf_op jit(solution)/shard_map/ppermute | solution.py:98
  160.8 5.8 %collective-permute-start.25 = (f32[128,128]{1,0:T(8,128)S(1)}, f32[128,128]{1,0:T(8,128)S(1)}, u32[]{:S(2)}, u32[]{:S(2)}) collective-permute-start(f32[128,128]{1,0:T(8,128)S(1)} %add.93), channel_id=1, source_target_pairs={{0,64},{16,80},{32,96},{48,112},{64,0},{80,16},{96,32},{112,48},{1... | collective-permute-start | bytes 196616 | tf_op jit(solution)/shard_map/ppermute | solution.py:98
  166.6 3.8 %collective-permute-start.26 = (f32[128,128]{1,0:T(8,128)S(1)}, f32[128,128]{1,0:T(8,128)S(1)}, u32[]{:S(2)}, u32[]{:S(2)}) collective-permute-start(f32[128,128]{1,0:T(8,128)S(1)} %add.94), channel_id=1, source_target_pairs={{14,15},{30,31},{46,47},{62,63},{78,79},{94,95},{110,111},{126,127}} | collective-permute-start | bytes 196616 | tf_op jit(solution)/shard_map/ppermute | solution.py:87
  167.3 8.0 %collective-permute-start.20 = (f32[4,16,1024]{2,1,0:T(8,128)S(1)}, f32[4,16,1024]{2,1,0:T(8,128)S(1)}, u32[]{:S(2)}, u32[]{:S(2)}) collective-permute-start(f32[4,16,1024]{2,1,0:T(8,128)S(1)} %bitcast.66), channel_id=1, source_target_pairs={{0,64},{16,80},{32,96},{48,112},{64,0},{80,16},{96,32},{112,48},{1... | collective-permute-start | bytes 786440 | tf_op jit(solution)/shard_map/ppermute | solution.py:114
  170.4 4.9 %collective-permute-start.27 = (f32[128,128]{1,0:T(8,128)S(1)}, f32[128,128]{1,0:T(8,128)S(1)}, u32[]{:S(2)}, u32[]{:S(2)}) collective-permute-start(f32[128,128]{1,0:T(8,128)S(1)} %broadcast_select_fusion), channel_id=1, source_target_pairs={{14,12},{15,13},{30,28},{31,29},{46,44},{47,45},{62,60},{63,61},{7... | collective-permute-start | bytes 196616 | tf_op jit(solution)/shard_map/ppermute | solution.py:87
  175.4 2.3 %collective-permute-start.28 = (f32[128,128]{1,0:T(8,128)S(1)}, f32[128,128]{1,0:T(8,128)S(1)}, u32[]{:S(2)}, u32[]{:S(2)}) collective-permute-start(f32[128,128]{1,0:T(8,128)S(1)} %broadcast_select_fusion.1), channel_id=1, source_target_pairs={{14,10},{15,11},{12,8},{13,9},{30,26},{31,27},{28,24},{29,25},{46,... | collective-permute-start | bytes 196616 | tf_op jit(solution)/shard_map/ppermute | solution.py:87
  176.1 5.0 %collective-permute-start.21 = (f32[2,16,1024]{2,1,0:T(8,128)S(1)}, f32[2,16,1024]{2,1,0:T(8,128)S(1)}, u32[]{:S(2)}, u32[]{:S(2)}) collective-permute-start(f32[2,16,1024]{2,1,0:T(8,128)S(1)} %slice_select_fusion.5), channel_id=1, source_target_pairs={{0,32},{16,48},{32,0},{48,16},{64,96},{80,112},{96,64},{112,80},{1... | collective-permute-start | bytes 393224 | tf_op jit(solution)/shard_map/ppermute | solution.py:114
  177.7 8.5 %collective-permute-start.29 = (f32[128,128]{1,0:T(8,128)S(1)}, f32[128,128]{1,0:T(8,128)S(1)}, u32[]{:S(2)}, u32[]{:S(2)}) collective-permute-start(f32[128,128]{1,0:T(8,128)S(1)} %broadcast_select_fusion.2), channel_id=1, source_target_pairs={{14,6},{15,7},{12,4},{13,5},{10,2},{11,3},{8,0},{9,1},{30,22},{31,... | collective-permute-start | bytes 196616 | tf_op jit(solution)/shard_map/ppermute | solution.py:87
  181.2 5.9 %collective-permute-start.22 = (f32[1,16,1024]{2,1,0:T(8,128)S(1)}, f32[1,16,1024]{2,1,0:T(8,128)S(1)}, u32[]{:S(2)}, u32[]{:S(2)}) collective-permute-start(f32[1,16,1024]{2,1,0:T(8,128)S(1)} %slice_select_fusion.7), channel_id=1, source_target_pairs={{0,16},{16,0},{32,48},{48,32},{64,80},{80,64},{96,112},{112,96},{1... | collective-permute-start | bytes 196616 | tf_op jit(solution)/shard_map/ppermute | solution.py:114
  186.9 1.1 copy-start.10

commit v6 on v4

--- a/solution.py
+++ b/solution.py
@@ -190,7 +190,7 @@
 
         def summed_block(partial_value, root):
             rows_sum = butterfly_sum(partial_value, "row", n_row)
-            return tree_broadcast(rows_sum, "col", n_col, root)
+            return panel_broadcast(rows_sum, n_col, root)
 
         inverse_two = inverse_lower(diag_two)
         solved_two = solve_panel(adj_trail[:, last:], inverse_two, root_two)

time: 184 us -> 202 us (1.098)
  the two profiles are of different devices: /device:TPU:0 before, /device:TPU:1 now
where the time goes in v6:
time: 202 us
  Pallas kernels  84 us (42%)
  starting transfers between devices  37.5 us (19%)
  other arithmetic  26.3 us (13%)
  matrix products  24.1 us (12%)
  waiting for transfers between devices  23.5 us (12%)
  local copies, waits for them, and re-layouts  4.95 us (2%)
    pallas_call x4, Pallas kernels, panel_broadcast(): pl.pallas_call(functools.partial(spread_kernel, root, size), out_shape=ja...  84 us
    another operation x4, other arithmetic, inverse_lower(): return lax.linalg.triangular_solve(block, ident, left_side=True, lower=True)  20.5 us
    ppermute x6, starting transfers between devices, halving_scatter(): blocks = keep + lax.ppermute(send, axis, pairs)  14.7 us
    ppermute x6, starting transfers between devices, butterfly_sum(): value = value + lax.ppermute(value, axis, pairs)  10.5 us
    ppermute x6, waiting for transfers between devices, butterfly_sum(): value = value + lax.ppermute(value, axis, pairs)  10.1 us
    ppermute x6, starting transfers between devices, doubling_gather(): other = lax.ppermute(value, axis, pairs)  8.96 us
    ppermute x4, waiting for transfers between devices, tree_broadcast(): arrived = lax.ppermute(value, axis, pairs)  6.5 us
    ppermute x6, waiting for transfers between devices, halving_scatter(): blocks = keep + lax.ppermute(send, axis, pairs)  5.22 us
  transfers between devices with their start and end apart: 22, of which 9 were waited for; matrix products, arithmetic and copies ran while one was open for 17% of the time, Pallas kernels for 28%

profile of v6, /device:TPU:1, one launch (start us, length us, event | category | flops | bytes accessed | tf_op | source)
XLA Modules:
  0.0 201.7 jit_solution(15658715905316594772)
XLA Ops:
  0.7 0.9 select_bitcast_fusion.1
  1.5 9.8 %custom-call.4 = f32[1,128,128]{1,2,0:T(8,128)S(1)} custom-call(f32[1,128,128]{2,1,0:T(8,128)S(1)} %select_bitcast_fusion.1), custom_call_target="InvertDiagBlocksLowerTriangular" | custom-call | tf_op jit(solution)/shard_map/triangular_solve/custom-call.1 | solution.py:145
  11.3 0.3 fusion.15
  11.6 3.0 %fusion.x_ref = bf16[2048,128]{1,0:T(8,128)(2,1)} fusion(f32[128,128]{1,0:T(8,128)S(1)} %fusion.15, f32[2048,1024]{1,0:T(8,128)} %param.17), kind=kOutput, calls=%fused_computation.6 | convolution fusion | flops 402915328 | bytes 1638400 | tf_op jit(solution)/shard_map/dot_general | solution.py:184
  14.6 27.6 %shard_map.137 = bf16[2048,128]{1,0:T(8,128)(2,1)} custom-call(bf16[2048,128]{1,0:T(8,128)(2,1)} %fusion.x_ref), custom_call_target="tpu_custom_call" | custom-call | tf_op jit(solution)/shard_map/pallas_call | solution.py:68
  42.3 3.1 %fusion.46 = f32[128,1024]{1,0:T(8,128)S(1)} fusion(bf16[2048,128]{1,0:T(8,128)(2,1)} %shard_map.137, bf16[2048,1024]{1,0:T(8,128)(2,1)} %param.12), kind=kOutput, calls=%fused_computation.93 | convolution fusion | flops 536870912 | bytes 5242880 | tf_op jit(solution)/shard_map/dot_general | solution.py:204
  45.5 2.8 %collective-permute-start.3 = (f32[4,16,1024]{2,1,0:T(8,128)S(1)}, f32[4,16,1024]{2,1,0:T(8,128)S(1)}, u32[]{:S(2)}, u32[]{:S(2)}) collective-permute-start(f32[4,16,1024]{2,1,0:T(8,128)S(1)} %bitcast.60), channel_id=1, source_target_pairs={{0,64},{16,80},{32,96},{48,112},{64,0},{80,16},{96,32},{112,48},{1... | collective-permute-start | bytes 786440 | tf_op jit(solution)/shard_map/ppermute | solution.py:114
  48.3 3.2 %collective-permute-start = (bf16[16,1024]{1,0:T(8,128)(2,1)S(1)}, bf16[16,1024]{1,0:T(8,128)(2,1)S(1)}, u32[]{:S(2)}, u32[]{:S(2)}) collective-permute-start(bf16[16,1024]{1,0:T(8,128)(2,1)S(1)} %copy-done.6), channel_id=1, source_target_pairs={{0,16},{16,0},{32,48},{48,32},{64,80},{80,64},{96,112},{112,96},{1... | collective-permute-start | bytes 98312 | tf_op jit(solution)/shard_map/ppermute | solution.py:124
  51.5 1.4 fusion.11
  53.0 0.5 collective-permute-start.9
  53.5 9.8 %custom-call.5 = f32[1,128,128]{1,2,0:T(8,128)S(1)} custom-call(f32[1,128,128]{2,1,0:T(8,128)S(1)} %select_bitcast_fusion), custom_call_target="InvertDiagBlocksLowerTriangular" | custom-call | tf_op jit(solution)/shard_map/triangular_solve/custom-call.1 | solution.py:145
  63.3 0.3 fusion.13
  63.7 0.4 collective-permute-start.1
  64.1 1.2 collective-permute-start.10
  65.4 0.4 collective-permute-start.7
  65.8 1.7 collective-permute-done.1
  67.5 0.8 collective-permute-start.2
  68.3 1.9 collective-permute-done.7
  70.3 0.5 collective-permute-start.8
  70.8 2.8 %collective-permute-start.11 = (bf16[64,1024]{1,0:T(8,128)(2,1)S(1)}, bf16[64,1024]{1,0:T(8,128)(2,1)S(1)}, u32[]{:S(2)}, u32[]{:S(2)}) collective-permute-start(bf16[64,1024]{1,0:T(8,128)(2,1)S(1)} %maximum_select_fusion.3), channel_id=1, source_target_pairs={{0,64},{16,80},{32,96},{48,112},{64,0},{80,16},{96,32},{112,48},{1... | collective-permute-start | bytes 393224 | tf_op jit(solution)/shard_map/ppermute | solution.py:124
  73.6 1.8 collective-permute-done.8
  75.4 0.6 add.83.x_ref
  76.0 18.0 %shard_map.138 = f32[128,128]{1,0:T(8,128)} custom-call(f32[128,128]{1,0:T(8,128)} %add.83.x_ref), custom_call_target="tpu_custom_call" | custom-call | tf_op jit(solution)/shard_map/pallas_call | solution.py:68
  94.0 1.1 fusion.2
  95.2 0.3 fusion.47
  95.5 1.3 collective-permute-start.4
  96.8 0.2 fusion.29
  97.1 2.3 %collective-permute-done.4 = f32[2,16,1024]{2,1,0:T(8,128)S(1)} collective-permute-done((f32[2,16,1024]{2,1,0:T(8,128)S(1)}, f32[2,16,1024]{2,1,0:T(8,128)S(1)}, u32[]{:S(2)}, u32[]{:S(2)}) %collective-permute-start.4) | collective-permute-done | bytes 131104 | tf_op jit(solution)/shard_map/ppermute | solution.py:114
  99.5 3.5 %collective-permute-start.5 = (f32[1,16,1024]{2,1,0:T(8,128)S(1)}, f32[1,16,1024]{2,1,0:T(8,128)S(1)}, u32[]{:S(2)}, u32[]{:S(2)}) collective-permute-start(f32[1,16,1024]{2,1,0:T(8,128)S(1)} %slice_select_fusion.8), channel_id=1, source_target_pairs={{0,16},{16,0},{32,48},{48,32},{64,80},{80,64},{96,112},{112,96},{1... | collective-permute-start | bytes 196616 | tf_op jit(solution)/shard_map/ppermute | solution.py:114
  103.0 4.6 %convolution_subtract_fusion.1 = f32[2048,1024]{1,0:T(8,128)S(1)} fusion(f32[2048,1024]{1,0:T(8,128)} %param.17, bf16[2048,128]{1,0:T(8,128)(2,1)S(1)} %copy-done.2, bf16[64,1024]{1,0:T(8,128)(2,1)S(1)} %maximum_select_fusion.2, bf16[64,1024]{1,0:T(8,128)(2,1)S(1)} %collective-permute-done.2, pred[]{:T(512)S(6)} %eq.62), kind=kOutput, calls=%fused_computation.2 | convolution fusion | flops 540147712 | bytes 17563648 | tf_op jit(solution)/shard_map/dot_general | solution.py:207
  107.6 3.3 %copy-done = f32[2048,1024]{1,0:T(8,128)} copy-done((f32[2048,1024]{1,0:T(8,128)}, f32[2048,1024]{1,0:T(8,128)S(1)}, u32[]{:S(2)}) %copy-start) | copy-done | bytes 8388632
  111.1 0.3 fusion.19
  111.4 1.0 convolution_convert_fusion
  112.4 0.8 slice.136.x_ref
  113.2 0.6 collective-permute-start.12
  113.8 23.4 %shard_map.139 = bf16[2048,128]{1,0:T(8,128)(2,1)} custom-call(bf16[2048,128]{1,0:T(8,128)(2,1)} %slice.136.x_ref), custom_call_target="tpu_custom_call" | custom-call | tf_op jit(solution)/shard_map/pallas_call | solution.py:68
  137.2 4.9 %convolution_subtract_fusion = bf16[2048,1024]{1,0:T(8,128)(2,1)S(1)} fusion(f32[2048,1024]{1,0:T(8,128)} %copy-done, bf16[2048,128]{1,0:T(8,128)(2,1)} %shard_map.139, bf16[64,1024]{1,0:T(8,128)(2,1)S(1)} %maximum_select_fusion.3, bf16[64,1024]{1,0:T(8,128)(2,1)S(1)} %collective-permute-done.11, pred[]{:T(512)S(6)} %eq.62), kind=kOutput, calls=%fused_computation.1 | convolution fusion | flops 542244864 | bytes 13369345 | tf_op jit(solution)/shard_map/dot_general | solution.py:221
  142.2 0.2 fusion.7
  142.4 0.7 collective-permute-start.13
  143.1 0.7 fusion.48
  143.9 0.4 slice.193
  144.3 0.7 collective-permute-start.14
  145.0 2.6 %pad_maximum_fusion = bf16[2048,1024]{1,0:T(8,128)(2,1)} fusion(bf16[2048,128]{1,0:T(8,128)(2,1)S(1)} %fusion.7, bf16[2048,896]{1,0:T(8,128)(2,1)S(1)} %slice.193), kind=kLoop, calls=%fused_computation.3 | loop fusion | flops 8388608 | bytes 8388608 | tf_op jit(solution)/shard_map/concatenate | solution.py:234
  147.7 1.4 collective-permute-start.15
  149.1 0.3 fusion.9
  149.4 6.5 %collective-permute-done.15 = bf16[16,128]{1,0:T(8,128)(2,1)S(1)} collective-permute-done((bf16[16,128]{1,0:T(8,128)(2,1)S(1)}, bf16[16,128]{1,0:T(8,128)(2,1)S(1)}, u32[]{:S(2)}, u32[]{:S(2)}) %collective-permute-start.15) | collective-permute-done | bytes 4128 | tf_op jit(solution)/shard_map/ppermute | solution.py:87
  156.1 5.8 %collective-permute-start.19 = (f32[128,128]{1,0:T(8,128)S(1)}, f32[128,128]{1,0:T(8,128)S(1)}, u32[]{:S(2)}, u32[]{:S(2)}) collective-permute-start(f32[128,128]{1,0:T(8,128)S(1)} %convolution_add_fusion.1), channel_id=1, source_target_pairs={{0,16},{16,0},{32,48},{48,32},{64,80},{80,64},{96,112},{112,96},{1... | collective-permute-start | bytes 196616 | tf_op jit(solution)/shard_map/ppermute | solution.py:98
  162.0 0.2 convolution_add_fusion
  162.4 0.4 collective-permute-done.19
  162.9 1.5 collective-permute-start.20
  164.4 2.5 %collective-permute-start.16 = (f32[4,16,1024]{2,1,0:T(8,128)S(1)}, f32[4,16,1024]{2,1,0:T(8,128)S(1)}, u32[]{:S(2)}, u32[]{:S(2)}) collective-permute-start(f32[4,16,1024]{2,1,0:T(8,128)S(1)} %bitcast.61), channel_id=1, source_target_pairs={{0,64},{16,80},{32,96},{48,112},{64,0},{80,16},{96,32},{112,48},{1... | collective-permute-start | bytes 786440 | tf_op jit(solution)/shard_map/ppermute | solution.py:114
  166.9 2.2 %collective-permute-start.21 = (f32[128,128]{1,0:T(8,128)S(1)}, f32[128,128]{1,0:T(8,128)S(1)}, u32[]{:S(2)}, u32[]{:S(2)}) collective-permute-start(f32[128,128]{1,0:T(8,128)S(1)} %add.92), channel_id=1, source_target_pairs={{0,64},{16,80},{32,96},{48,112},{64,0},{80,16},{96,32},{112,48},{1... | collective-permute-start | bytes 196616 | tf_op jit(solution)/shard_map/ppermute | solution.py:98
  169.1 0.6 pad_maximum_fusion.2
  169.7 5.9 %collective-permute-done.21 = f32[128,128]{1,0:T(8,128)S(1)} collective-permute-done((f32[128,128]{1,0:T(8,128)S(1)}, f32[128,128]{1,0:T(8,128)S(1)}, u32[]{:S(2)}, u32[]{:S(2)}) %collective-permute-start.21) | collective-permute-done | bytes 65568 | tf_op jit(solution)/shard_map/ppermute | solution.py:98
  175.7 0.6 add.93.x_ref
  176.3 15.0 %shard_map.140 = f32[128,128]{1,0:T(8,128)} custom-call(f32[128,128]{1,0:T(8,128)} %add.93.x_ref), custom_call_target="tpu_custom_call" | custom-call | tf_op jit(solution)/shard_map/pallas_call | solution.py:68
  191.4 1.1 fusion.1
  192.6 1.3 collective-permute-start.17
  193.9 0.3 fusion.49
  194.2 2.3 %collective-permute-done.17 = f32[2,16,1024]{2,1,0:T(8,128)S(1)} collective-permute-done((f32[2,16,1024]{2,1,0:T(8,128)S(1)}, f32[2,16,1024]{2,1,0:T(8,128)S(1)}, u32[]{:S(2)}, u32[]{:S(2)}) %collective-permute-start.17) | collective-permute-done | bytes 131104 | tf_op jit(solution)/shard_map/ppermute | solution.py:114
  196.5 3.3 %collective-permute-start.18 = (f32[1,16,1024]{2,1,0:T(8,128)S(1)}, f32[1,16,1024]{2,1,0:T(8,128)S(1)}, u32[]{:S(2)}, u32[]{:S(2)}) collective-permute-start(f32[1,16,1024]{2,1,0:T(8,128)S(1)} %slice_select_fusion.7), channel_id=1, source_target_pairs={{0,16},{16,0},{32,48},{48,32},{64,80},{80,64},{96,112},{112,96},{1... | collective-permute-start | bytes 196616 | tf_op jit(solution)/shard_map/ppermute | solution.py:114
  200.2 0.6 collective-permute-done.18
  200.8 0.2 fusion.17
  201.0 0.6 pad_maximum_fusion.1
  (77 shorter events, 1.5 us)
Async XLA Ops:
  11.6 36.7 %copy-start.6 = (bf16[16,1024]{1,0:T(8,128)(2,1)S(1)}, bf16[16,1024]{1,0:T(8,128)(2,1)}, u32[]{:S(2)}) copy-start(bf16[16,1024]{1,0:T(8,128)(2,1)} %param.14) | copy-start | bytes 98308
  14.6 38.3 %copy-start.11 = (bf16[16,1024]{1,0:T(8,128)(2,1)S(1)}, bf16[16,1024]{1,0:T(8,128)(2,1)}, u32[]{:S(2)}) copy-start(bf16[16,1024]{1,0:T(8,128)(2,1)} %param.13) | copy-start | bytes 98308
  14.6 38.8 %copy-start.5 = (f32[128,128]{1,0:T(8,128)S(1)}, f32[128,128]{1,0:T(8,128)}, u32[]{:S(2)}) copy-start(f32[128,128]{1,0:T(8,128)} %param.15) | copy-start | bytes 196612
  42.3 9.2 %copy-start.2 = (bf16[2048,128]{1,0:T(8,128)(2,1)S(1)}, bf16[2048,128]{1,0:T(8,128)(2,1)}, u32[]{:S(2)}) copy-start(bf16[2048,128]{1,0:T(8,128)(2,1)} %shard_map.137) | copy-start | bytes 1572868
  42.3 51.7 %copy-start.4 = (f32[128,128]{1,0:T(8,128)S(1)}, f32[128,128]{1,0:T(8,128)}, u32[]{:S(2)}) copy-start(f32[128,128]{1,0:T(8,128)} %param.16) | copy-start | bytes 196612
  42.3 51.7 %copy-start.7 = (f32[128,128]{1,0:T(8,128)S(1)}, f32[128,128]{1,0:T(8,128)}, u32[]{:S(2)}) copy-start(f32[128,128]{1,0:T(8,128)} %param.21) | copy-start | bytes 196612
  45.5 50.0 %collective-permute-start.3 = (f32[4,16,1024]{2,1,0:T(8,128)S(1)}, f32[4,16,1024]{2,1,0:T(8,128)S(1)}, u32[]{:S(2)}, u32[]{:S(2)}) collective-permute-start(f32[4,16,1024]{2,1,0:T(8,128)S(1)} %bitcast.60), channel_id=1, source_target_pairs={{0,64},{16,80},{32,96},{48,112},{64,0},{80,16},{96,32},{112,48},{1... | collective-permute-start | bytes 786440 | tf_op jit(solution)/shard_map/ppermute | solution.py:114
  48.3 15.4 %collective-permute-start = (bf16[16,1024]{1,0:T(8,128)(2,1)S(1)}, bf16[16,1024]{1,0:T(8,128)(2,1)S(1)}, u32[]{:S(2)}, u32[]{:S(2)}) collective-permute-start(bf16[16,1024]{1,0:T(8,128)(2,1)S(1)} %copy-done.6), channel_id=1, source_target_pairs={{0,16},{16,0},{32,48},{48,32},{64,80},{80,64},{96,112},{112,96},{1... | collective-permute-start | bytes 98312 | tf_op jit(solution)/shard_map/ppermute | solution.py:124
  52.9 12.5 %collective-permute-start.6 = (f32[128,128]{1,0:T(8,128)S(1)}, f32[128,128]{1,0:T(8,128)S(1)}, u32[]{:S(2)}, u32[]{:S(2)}) collective-permute-start(f32[128,128]{1,0:T(8,128)S(1)} %fusion.11), channel_id=1, source_target_pairs={{0,16},{16,0},{32,48},{48,32},{64,80},{80,64},{96,112},{112,96},{1... | collective-permute-start | bytes 196616 | tf_op jit(solution)/shard_map/ppermute | solution.py:98
  53.0 11.1 %collective-permute-start.9 = (bf16[16,1024]{1,0:T(8,128)(2,1)S(1)}, bf16[16,1024]{1,0:T(8,128)(2,1)S(1)}, u32[]{:S(2)}, u32[]{:S(2)}) collective-permute-start(bf16[16,1024]{1,0:T(8,128)(2,1)S(1)} %copy-done.11), channel_id=1, source_target_pairs={{0,16},{16,0},{32,48},{48,32},{64,80},{80,64},{96,112},{112,96},{1... | collective-permute-start | bytes 98312 | tf_op jit(solution)/shard_map/ppermute | solution.py:124
  63.7 3.7 %collective-permute-start.1 = (bf16[32,1024]{1,0:T(8,128)(2,1)S(1)}, bf16[32,1024]{1,0:T(8,128)(2,1)S(1)}, u32[]{:S(2)}, u32[]{:S(2)}) collective-permute-start(bf16[32,1024]{1,0:T(8,128)(2,1)S(1)} %maximum_select_fusion.4), channel_id=1, source_target_pairs={{0,32},{16,48},{32,0},{48,16},{64,96},{80,112},{96,64},{112,80},{1... | collective-permute-start | bytes 196616 | tf_op jit(solution)/shard_map/ppermute | solution.py:124
  64.1 6.6 %collective-permute-start.10 = (bf16[32,1024]{1,0:T(8,128)(2,1)S(1)}, bf16[32,1024]{1,0:T(8,128)(2,1)S(1)}, u32[]{:S(2)}, u32[]{:S(2)}) collective-permute-start(bf16[32,1024]{1,0:T(8,128)(2,1)S(1)} %maximum_select_fusion.5), channel_id=1, source_target_pairs={{0,32},{16,48},{32,0},{48,16},{64,96},{80,112},{96,64},{112,80},{1... | collective-permute-start | bytes 196616 | tf_op jit(solution)/shard_map/ppermute | solution.py:124
  65.4 4.9 %collective-permute-start.7 = (f32[128,128]{1,0:T(8,128)S(1)}, f32[128,128]{1,0:T(8,128)S(1)}, u32[]{:S(2)}, u32[]{:S(2)}) collective-permute-start(f32[128,128]{1,0:T(8,128)S(1)} %add.81), channel_id=1, source_target_pairs={{0,32},{16,48},{32,0},{48,16},{64,96},{80,112},{96,64},{112,80},{1... | collective-permute-start | bytes 196616 | tf_op jit(solution)/shard_map/ppermute | solution.py:98
  67.5 35.5 %collective-permute-start.2 = (bf16[64,1024]{1,0:T(8,128)(2,1)S(1)}, bf16[64,1024]{1,0:T(8,128)(2,1)S(1)}, u32[]{:S(2)}, u32[]{:S(2)}) collective-permute-start(bf16[64,1024]{1,0:T(8,128)(2,1)S(1)} %maximum_select_fusion.2), channel_id=1, source_target_pairs={{0,64},{16,80},{32,96},{48,112},{64,0},{80,16},{96,32},{112,48},{1... | collective-permute-start | bytes 393224 | tf_op jit(solution)/shard_map/ppermute | solution.py:124
  70.3 5.1 %collective-permute-start.8 = (f32[128,128]{1,0:T(8,128)S(1)}, f32[128,128]{1,0:T(8,128)S(1)}, u32[]{:S(2)}, u32[]{:S(2)}) collective-permute-start(f32[128,128]{1,0:T(8,128)S(1)} %add.82), channel_id=1, source_target_pairs={{0,64},{16,80},{32,96},{48,112},{64,0},{80,16},{96,32},{112,48},{1... | collective-permute-start | bytes 196616 | tf_op jit(solution)/shard_map/ppermute | solution.py:98
  70.8 66.4 %collective-permute-start.11 = (bf16[64,1024]{1,0:T(8,128)(2,1)S(1)}, bf16[64,1024]{1,0:T(8,128)(2,1)S(1)}, u32[]{:S(2)}, u32[]{:S(2)}) collective-permute-start(bf16[64,1024]{1,0:T(8,128)(2,1)S(1)} %maximum_select_fusion.3), channel_id=1, source_target_pairs={{0,64},{16,80},{32,96},{48,112},{64,0},{80,16},{96,32},{112,48},{1... | collective-permute-start | bytes 393224 | tf_op jit(solution)/shard_map/ppermute | solution.py:124
  95.5 3.9 %collective-permute-start.4 = (f32[2,16,1024]{2,1,0:T(8,128)S(1)}, f32[2,16,1024]{2,1,0:T(8,128)S(1)}, u32[]{:S(2)}, u32[]{:S(2)}) collective-permute-start(f32[2,16,1024]{2,1,0:T(8,128)S(1)} %slice_select_fusion.6), channel_id=1, source_target_pairs={{0,32},{16,48},{32,0},{48,16},{64,96},{80,112},{96,64},{112,80},{1... | collective-permute-start | bytes 393224 | tf_op jit(solution)/shard_map/ppermute | solution.py:114
  97.0 14.1 %copy-start.9 = (f32[128,128]{1,0:T(8,128)}, f32[128,128]{1,0:T(8,128)S(1)}, u32[]{:S(2)}) copy-start(f32[128,128]{1,0:T(8,128)S(1)} %get-tuple-element.10) | copy-start | bytes 196612
  99.5 11.6 %copy-start.12 = (f32[16,1024]{1,0:T(8,128)S(1)}, f32[16,1024]{1,0:T(8,128)}, u32[]{:S(2)}) copy-start(f32[16,1024]{1,0:T(8,128)} %param.19) | copy-start | bytes 196612
  99.5 11.6 %collective-permute-start.5 = (f32[1,16,1024]{2,1,0:T(8,128)S(1)}, f32[1,16,1024]{2,1,0:T(8,128)S(1)}, u32[]{:S(2)}, u32[]{:S(2)}) collective-permute-start(f32[1,16,1024]{2,1,0:T(8,128)S(1)} %slice_select_fusion.8), channel_id=1, source_target_pairs={{0,16},{16,0},{32,48},{48,32},{64,80},{80,64},{96,112},{112,96},{1... | collective-permute-start | bytes 196616 | tf_op jit(solution)/shard_map/ppermute | solution.py:114
  107.6 3.3 %copy-start = (f32[2048,1024]{1,0:T(8,128)}, f32[2048,1024]{1,0:T(8,128)S(1)}, u32[]{:S(2)}) copy-start(f32[2048,1024]{1,0:T(8,128)S(1)} %convolution_subtract_fusion.1) | copy-start | bytes 25165828
  113.2 29.2 %collective-permute-start.12 = (bf16[16,128]{1,0:T(8,128)(2,1)S(1)}, bf16[16,128]{1,0:T(8,128)(2,1)S(1)}, u32[]{:S(2)}, u32[]{:S(2)}) collective-permute-start(bf16[16,128]{1,0:T(8,128)(2,1)S(1)} %slice.139), channel_id=1, source_target_pairs={{14,15},{30,31},{46,47},{62,63},{78,79},{94,95},{110,111},{126,127}} | collective-permute-start | bytes 12296 | tf_op jit(solution)/shard_map/ppermute | solution.py:87
  137.2 5.0 %copy-start.3 = (bf16[2048,128]{1,0:T(8,128)(2,1)S(1)}, bf16[2048,128]{1,0:T(8,128)(2,1)}, u32[]{:S(2)}) copy-start(bf16[2048,128]{1,0:T(8,128)(2,1)} %shard_map.139) | copy-start | bytes 1572868
  137.2 5.9 %copy-start.1 = (bf16[2048,1024]{1,0:T(8,128)(2,1)S(1)}, bf16[2048,1024]{1,0:T(8,128)(2,1)}, u32[]{:S(2)}) copy-start(bf16[2048,1024]{1,0:T(8,128)(2,1)} %param.12) | copy-start | bytes 12582916
  142.4 1.9 collective-permute-start.13
  144.3 3.3 %collective-permute-start.14 = (bf16[16,128]{1,0:T(8,128)(2,1)S(1)}, bf16[16,128]{1,0:T(8,128)(2,1)S(1)}, u32[]{:S(2)}, u32[]{:S(2)}) collective-permute-start(bf16[16,128]{1,0:T(8,128)(2,1)S(1)} %broadcast_select_fusion.1), channel_id=1, source_target_pairs={{14,10},{15,11},{12,8},{13,9},{30,26},{31,27},{28,24},{29,25},{46,... | collective-permute-start | bytes 12296 | tf_op jit(solution)/shard_map/ppermute | solution.py:87
  147.7 43.7 %copy-start.8 = (f32[128,128]{1,0:T(8,128)S(1)}, f32[128,128]{1,0:T(8,128)}, u32[]{:S(2)}) copy-start(f32[128,128]{1,0:T(8,128)} %param.20) | copy-start | bytes 196612
  147.7 53.1 %copy-start.13 = (f32[16,1024]{1,0:T(8,128)S(1)}, f32[16,1024]{1,0:T(8,128)}, u32[]{:S(2)}) copy-start(f32[16,1024]{1,0:T(8,128)} %param.18) | copy-start | bytes 196612
  147.7 8.3 %collective-permute-start.15 = (bf16[16,128]{1,0:T(8,128)(2,1)S(1)}, bf16[16,128]{1,0:T(8,128)(2,1)S(1)}, u32[]{:S(2)}, u32[]{:S(2)}) collective-permute-start(bf16[16,128]{1,0:T(8,128)(2,1)S(1)} %broadcast_select_fusion.2), channel_id=1, source_target_pairs={{14,6},{15,7},{12,4},{13,5},{10,2},{11,3},{8,0},{9,1},{30,22},{31,... | collective-permute-start | bytes 12296 | tf_op jit(solution)/shard_map/ppermute | solution.py:87
  156.1 6.7 %collective-permute-start.19 = (f32[128,128]{1,0:T(8,128)S(1)}, f32[128,128]{1,0:T(8,128)S(1)}, u32[]{:S(2)}, u32[]{:S(2)}) collective-permute-start(f32[128,128]{1,0:T(8,128)S(1)} %convolution_add_fusion.1), channel_id=1, source_target_pairs={{0,16},{16,0},{32,48},{48,32},{64,80},{80,64},{96,112},{112,96},{1... | collective-permute-start | bytes 196616 | tf_op jit(solution)/shard_map/ppermute | solution.py:98
  162.9 4.0 %collective-permute-start.20 = (f32[128,128]{1,0:T(8,128)S(1)}, f32[128,128]{1,0:T(8,128)S(1)}, u32[]{:S(2)}, u32[]{:S(2)}) collective-permute-start(f32[128,128]{1,0:T(8,128)S(1)} %add.91), channel_id=1, source_target_pairs={{0,32},{16,48},{32,0},{48,16},{64,96},{80,112},{96,64},{112,80},{1... | collective-permute-start | bytes 196616 | tf_op jit(solution)/shard_map/ppermute | solution.py:98
  164.4 28.1 %collective-permute-start.16 = (f32[4,16,1024]{2,1,0:T(8,128)S(1)}, f32[4,16,1024]{2,1,0:T(8,128)S(1)}, u32[]{:S(2)}, u32[]{:S(2)}) collective-permute-start(f32[4,16,1024]{2,1,0:T(8,128)S(1)} %bitcast.61), channel_id=1, source_target_pairs={{0,64},{16,80},{32,96},{48,112},{64,0},{80,16},{96,32},{112,48},{1... | collective-permute-start | bytes 786440 | tf_op jit(solution)/shard_map/ppermute | solution.py:114
  166.9 8.8 %collective-permute-start.21 = (f32[128,128]{1,0:T(8,128)S(1)}, f32[128,128]{1,0:T(8,128)S(1)}, u32[]{:S(2)}, u32[]{:S(2)}) collective-permute-start(f32[128,128]{1,0:T(8,128)S(1)} %add.92), channel_id=1, source_target_pairs={{0,64},{16,80},{32,96},{48,112},{64,0},{80,16},{96,32},{112,48},{1... | collective-permute-start | bytes 196616 | tf_op jit(solution)/shard_map/ppermute | solution.py:98
  192.6 3.9 %collective-permute-start.17 = (f32[2,16,1024]{2,1,0:T(8,128)S(1)}, f32[2,16,1024]{2,1,0:T(8,128)S(1)}, u32[]{:S(2)}, u32[]{:S(2)}) collective-permute-start(f32[2,16,1024]{2,1,0:T(8,128)S(1)} %slice_select_fusion.5), channel_id=1, source_target_pairs={{0,32},{16,48},{32,0},{48,16},{64,96},{80,112},{96,64},{112,80},{1... | collective-permute-start | bytes 393224 | tf_op jit(solution)/shard_map/ppermute | solution.py:114
  196.5 4.2 %collective-permute-start.18 = (f32[1,16,1024]{2,1,0:T(8,128)S(1)}, f32[1,16,1024]{2,1,0:T(8,128)S(1)}, u32[]{:S(2)}, u32[]{:S(2)}) collective-permute-start(f32[1,16,1024]{2,1,0:T(8,128)S(1)} %slice_select_fusion.7), channel_id=1, source_target_pairs={{0,16},{16,0},{32,48},{48,32},{64,80},{80,64},{96,112},{112,96},{1... | collective-permute-start | bytes 196616 | tf_op jit(solution)/shard_map/ppermute | solution.py:114
  200.1 1.6 copy-start.10

commit v7 on v4

--- a/solution.py
+++ b/solution.py
@@ -13,6 +13,15 @@
 def spread_kernel(root, size, x_ref, y_ref, buf, recv_sem, send_sem):
     me = lax.axis_index("col")
     row = lax.axis_index("row")
+    barrier = pltpu.get_barrier_semaphore()
+    for step in range(1, size):
+        pl.semaphore_signal(
+            barrier,
+            inc=1,
+            device_id=(row, lax.rem(me + step, size)),
+            device_id_type=pl.DeviceIdType.MESH,
+        )
+    pl.semaphore_wait(barrier, size - 1)
     rows = x_ref.shape[0] // size
     is_root = me == root
 
@@ -64,7 +73,7 @@
         y_ref[...] = buf[...]
 
 
-def panel_broadcast(value, size, root):
+def panel_broadcast(value, size, root, call_id):
     return pl.pallas_call(
         functools.partial(spread_kernel, root, size),
         out_shape=jax.ShapeDtypeStruct(value.shape, value.dtype),
@@ -75,7 +84,7 @@
             pltpu.SemaphoreType.DMA((size,)),
             pltpu.SemaphoreType.DMA((2, size)),
         ],
-        compiler_params=pltpu.CompilerParams(has_side_effects=True),
+        compiler_params=pltpu.CompilerParams(collective_id=call_id, has_side_effects=True),
     )(value)
 
 
@@ -183,7 +192,7 @@
         def solve_panel(rows, inverse, root):
             local = jnp.dot(rows, inverse, precision=exact_mode).astype(jnp.bfloat16)
             head = local.shape[0] % (16 * n_col)
-            tail = panel_broadcast(local[head:], n_col, root)
+            tail = panel_broadcast(local[head:], n_col, root, n_col - 1 - root)
             if head == 0:
                 return tail
             return jnp.concatenate([tree_broadcast(local[:head], "col", n_col, root), tail], 0)

time: 184 us -> 170 us (0.924)
  the two profiles are of different devices: /device:TPU:0 before, /device:TPU:1 now
where the time goes in v7:
time: 170 us; the launch traced here: 168 us
  starting transfers between devices  44.5 us (26%)
  waiting for transfers between devices  35.1 us (21%)
  Pallas kernels  34.1 us (20%)
  other arithmetic  25.1 us (15%)
  matrix products  22.5 us (13%)
  local copies, waits for them, and re-layouts  4.94 us (3%)
    pallas_call x2, Pallas kernels, panel_broadcast(): pl.pallas_call(functools.partial(spread_kernel, root, size), out_shape=ja...  34.1 us
    another operation x4, other arithmetic, inverse_lower(): return lax.linalg.triangular_solve(block, ident, left_side=True, lower=True)  20.5 us
    ppermute x6, starting transfers between devices, butterfly_sum(): value = value + lax.ppermute(value, axis, pairs)  15.1 us
    ppermute x6, starting transfers between devices, halving_scatter(): blocks = keep + lax.ppermute(send, axis, pairs)  13.3 us
    ppermute x12, waiting for transfers between devices, tree_broadcast(): arrived = lax.ppermute(value, axis, pairs)  12.2 us
    ppermute x6, waiting for transfers between devices, butterfly_sum(): value = value + lax.ppermute(value, axis, pairs)  11.7 us
    ppermute x12, starting transfers between devices, tree_broadcast(): arrived = lax.ppermute(value, axis, pairs)  10.1 us
    ppermute x6, waiting for transfers between devices, halving_scatter(): blocks = keep + lax.ppermute(send, axis, pairs)  10 us
  transfers between devices with their start and end apart: 30, of which 11 were waited for; matrix products, arithmetic and copies ran while one was open for 19% of the time, Pallas kernels for 9%

profile of v7, /device:TPU:1, one launch (start us, length us, event | category | flops | bytes accessed | tf_op | source)
XLA Modules:
  0.0 167.7 jit_solution(13452570386048196768)
XLA Ops:
  0.6 0.9 select_bitcast_fusion.1
  1.5 9.8 %custom-call.4 = f32[1,128,128]{1,2,0:T(8,128)S(1)} custom-call(f32[1,128,128]{2,1,0:T(8,128)S(1)} %select_bitcast_fusion.1), custom_call_target="InvertDiagBlocksLowerTriangular" | custom-call | tf_op jit(solution)/shard_map/triangular_solve/custom-call.1 | solution.py:154
  11.3 0.3 fusion.15
  11.6 3.0 %fusion.x_ref = bf16[2048,128]{1,0:T(8,128)(2,1)} fusion(f32[128,128]{1,0:T(8,128)S(1)} %fusion.15, f32[2048,1024]{1,0:T(8,128)} %param.17), kind=kOutput, calls=%fused_computation.6 | convolution fusion | flops 402915328 | bytes 1638400 | tf_op jit(solution)/shard_map/dot_general | solution.py:193
  14.6 19.2 %shard_map.137 = bf16[2048,128]{1,0:T(8,128)(2,1)} custom-call(bf16[2048,128]{1,0:T(8,128)(2,1)} %fusion.x_ref), custom_call_target="tpu_custom_call" | custom-call | tf_op jit(solution)/shard_map/pallas_call | solution.py:77
  33.8 1.5 fusion.11
  35.4 3.4 %collective-permute-start.6 = (f32[128,128]{1,0:T(8,128)S(1)}, f32[128,128]{1,0:T(8,128)S(1)}, u32[]{:S(2)}, u32[]{:S(2)}) collective-permute-start(f32[128,128]{1,0:T(8,128)S(1)} %fusion.11), channel_id=1, source_target_pairs={{0,16},{16,0},{32,48},{48,32},{64,80},{80,64},{96,112},{112,96},{1... | collective-permute-start | bytes 196616 | tf_op jit(solution)/shard_map/ppermute | solution.py:107
  38.8 3.1 %fusion.50 = f32[128,1024]{1,0:T(8,128)S(1)} fusion(bf16[2048,128]{1,0:T(8,128)(2,1)} %shard_map.137, bf16[2048,1024]{1,0:T(8,128)(2,1)} %param.12), kind=kOutput, calls=%fused_computation.103 | convolution fusion | flops 536870912 | bytes 5242880 | tf_op jit(solution)/shard_map/dot_general | solution.py:213
  41.9 2.8 %collective-permute-start.3 = (f32[4,16,1024]{2,1,0:T(8,128)S(1)}, f32[4,16,1024]{2,1,0:T(8,128)S(1)}, u32[]{:S(2)}, u32[]{:S(2)}) collective-permute-start(f32[4,16,1024]{2,1,0:T(8,128)S(1)} %bitcast.60), channel_id=1, source_target_pairs={{0,64},{16,80},{32,96},{48,112},{64,0},{80,16},{96,32},{112,48},{1... | collective-permute-start | bytes 786440 | tf_op jit(solution)/shard_map/ppermute | solution.py:123
  44.7 0.3 collective-permute-start
  45.3 9.8 %custom-call.5 = f32[1,128,128]{1,2,0:T(8,128)S(1)} custom-call(f32[1,128,128]{2,1,0:T(8,128)S(1)} %select_bitcast_fusion), custom_call_target="InvertDiagBlocksLowerTriangular" | custom-call | tf_op jit(solution)/shard_map/triangular_solve/custom-call.1 | solution.py:154
  55.1 0.3 fusion.13
  55.4 0.4 collective-permute-start.1
  55.9 1.2 collective-permute-start.14
  57.1 0.4 collective-permute-start.7
  57.5 1.1 collective-permute-done.1
  58.7 1.2 collective-permute-start.2
  59.9 1.7 %collective-permute-done.7 = f32[128,128]{1,0:T(8,128)S(1)} collective-permute-done((f32[128,128]{1,0:T(8,128)S(1)}, f32[128,128]{1,0:T(8,128)S(1)}, u32[]{:S(2)}, u32[]{:S(2)}) %collective-permute-start.7) | collective-permute-done | bytes 65568 | tf_op jit(solution)/shard_map/ppermute | solution.py:107
  61.7 0.5 collective-permute-start.8
  62.2 2.6 %collective-permute-start.15 = (bf16[64,1024]{1,0:T(8,128)(2,1)S(1)}, bf16[64,1024]{1,0:T(8,128)(2,1)S(1)}, u32[]{:S(2)}, u32[]{:S(2)}) collective-permute-start(bf16[64,1024]{1,0:T(8,128)(2,1)S(1)} %maximum_select_fusion.3), channel_id=1, source_target_pairs={{0,64},{16,80},{32,96},{48,112},{64,0},{80,16},{96,32},{112,48},{1... | collective-permute-start | bytes 393224 | tf_op jit(solution)/shard_map/ppermute | solution.py:133
  64.8 2.4 %collective-permute-done.8 = f32[128,128]{1,0:T(8,128)S(1)} collective-permute-done((f32[128,128]{1,0:T(8,128)S(1)}, f32[128,128]{1,0:T(8,128)S(1)}, u32[]{:S(2)}, u32[]{:S(2)}) %collective-permute-start.8) | collective-permute-done | bytes 65568 | tf_op jit(solution)/shard_map/ppermute | solution.py:107
  67.3 0.8 collective-permute-start.9
  68.2 4.6 %convolution_subtract_fusion.1 = f32[2048,1024]{1,0:T(8,128)S(1)} fusion(f32[2048,1024]{1,0:T(8,128)} %param.17, bf16[2048,128]{1,0:T(8,128)(2,1)S(1)} %copy-done.2, bf16[64,1024]{1,0:T(8,128)(2,1)S(1)} %maximum_select_fusion.2, bf16[64,1024]{1,0:T(8,128)(2,1)S(1)} %collective-permute-done.2, pred[]{:T(512)S(6)} %eq.62), kind=kOutput, calls=%fused_computation.2 | convolution fusion | flops 540147712 | bytes 17563648 | tf_op jit(solution)/shard_map/dot_general | solution.py:216
  72.8 3.3 %copy-done = f32[2048,1024]{1,0:T(8,128)} copy-done((f32[2048,1024]{1,0:T(8,128)}, f32[2048,1024]{1,0:T(8,128)S(1)}, u32[]{:S(2)}) %copy-start) | copy-done | bytes 8388632
  76.3 0.7 collective-permute-start.10
  77.0 0.5 collective-permute-start.4
  77.5 0.7 collective-permute-start.11
  78.2 2.7 %collective-permute-done.4 = f32[2,16,1024]{2,1,0:T(8,128)S(1)} collective-permute-done((f32[2,16,1024]{2,1,0:T(8,128)S(1)}, f32[2,16,1024]{2,1,0:T(8,128)S(1)}, u32[]{:S(2)}, u32[]{:S(2)}) %collective-permute-start.4) | collective-permute-done | bytes 131104 | tf_op jit(solution)/shard_map/ppermute | solution.py:123
  81.0 1.3 collective-permute-start.12
  82.3 4.1 %collective-permute-start.5 = (f32[1,16,1024]{2,1,0:T(8,128)S(1)}, f32[1,16,1024]{2,1,0:T(8,128)S(1)}, u32[]{:S(2)}, u32[]{:S(2)}) collective-permute-start(f32[1,16,1024]{2,1,0:T(8,128)S(1)} %slice_select_fusion.8), channel_id=1, source_target_pairs={{0,16},{16,0},{32,48},{48,32},{64,80},{80,64},{96,112},{112,96},{1... | collective-permute-start | bytes 196616 | tf_op jit(solution)/shard_map/ppermute | solution.py:123
  86.5 5.0 %collective-permute-done.12 = f32[128,128]{1,0:T(8,128)S(1)} collective-permute-done((f32[128,128]{1,0:T(8,128)S(1)}, f32[128,128]{1,0:T(8,128)S(1)}, u32[]{:S(2)}, u32[]{:S(2)}) %collective-permute-start.12) | collective-permute-done | bytes 65568 | tf_op jit(solution)/shard_map/ppermute | solution.py:96
  91.5 0.3 fusion.2
  91.8 0.3 fusion.51
  92.4 0.3 fusion.19
  92.7 1.0 convolution_convert_fusion
  93.7 0.8 slice.136.x_ref
  94.5 0.6 collective-permute-start.16
  95.2 14.8 %shard_map.138 = bf16[2048,128]{1,0:T(8,128)(2,1)} custom-call(bf16[2048,128]{1,0:T(8,128)(2,1)} %slice.136.x_ref), custom_call_target="tpu_custom_call" | custom-call | tf_op jit(solution)/shard_map/pallas_call | solution.py:77
  110.0 4.9 %convolution_subtract_fusion = bf16[2048,1024]{1,0:T(8,128)(2,1)S(1)} fusion(f32[2048,1024]{1,0:T(8,128)} %copy-done, bf16[2048,128]{1,0:T(8,128)(2,1)} %shard_map.138, bf16[64,1024]{1,0:T(8,128)(2,1)S(1)} %maximum_select_fusion.3, bf16[64,1024]{1,0:T(8,128)(2,1)S(1)} %collective-permute-done.15, pred[]{:T(512)S(6)} %eq.62), kind=kOutput, calls=%fused_computation.1 | convolution fusion | flops 542244864 | bytes 13369345 | tf_op jit(solution)/shard_map/dot_general | solution.py:230
  115.3 0.7 collective-permute-start.17
  115.9 0.7 fusion.52
  116.7 0.4 slice.193
  117.2 0.7 collective-permute-start.18
  117.8 2.6 %pad_maximum_fusion = bf16[2048,1024]{1,0:T(8,128)(2,1)} fusion(bf16[2048,128]{1,0:T(8,128)(2,1)S(1)} %fusion.7, bf16[2048,896]{1,0:T(8,128)(2,1)S(1)} %slice.193), kind=kLoop, calls=%fused_computation.3 | loop fusion | flops 8388608 | bytes 8388608 | tf_op jit(solution)/shard_map/concatenate | solution.py:243
  120.5 1.4 collective-permute-start.19
  121.9 0.3 fusion.9
  122.3 7.1 %collective-permute-done.19 = bf16[16,128]{1,0:T(8,128)(2,1)S(1)} collective-permute-done((bf16[16,128]{1,0:T(8,128)(2,1)S(1)}, bf16[16,128]{1,0:T(8,128)(2,1)S(1)}, u32[]{:S(2)}, u32[]{:S(2)}) %collective-permute-start.19) | collective-permute-done | bytes 4128 | tf_op jit(solution)/shard_map/ppermute | solution.py:96
  129.6 10.0 %collective-permute-start.23 = (f32[128,128]{1,0:T(8,128)S(1)}, f32[128,128]{1,0:T(8,128)S(1)}, u32[]{:S(2)}, u32[]{:S(2)}) collective-permute-start(f32[128,128]{1,0:T(8,128)S(1)} %convolution_add_fusion.1), channel_id=1, source_target_pairs={{0,16},{16,0},{32,48},{48,32},{64,80},{80,64},{96,112},{112,96},{1... | collective-permute-start | bytes 196616 | tf_op jit(solution)/shard_map/ppermute | solution.py:107
  139.9 0.7 collective-permute-done.23
  140.7 3.1 %collective-permute-done.24 = f32[128,128]{1,0:T(8,128)S(1)} collective-permute-done((f32[128,128]{1,0:T(8,128)S(1)}, f32[128,128]{1,0:T(8,128)S(1)}, u32[]{:S(2)}, u32[]{:S(2)}) %collective-permute-start.24) | collective-permute-done | bytes 65568 | tf_op jit(solution)/shard_map/ppermute | solution.py:107
  143.8 0.7 collective-permute-start.25
  144.6 3.9 %collective-permute-done.25 = f32[128,128]{1,0:T(8,128)S(1)} collective-permute-done((f32[128,128]{1,0:T(8,128)S(1)}, f32[128,128]{1,0:T(8,128)S(1)}, u32[]{:S(2)}, u32[]{:S(2)}) %collective-permute-start.25) | collective-permute-done | bytes 65568 | tf_op jit(solution)/shard_map/ppermute | solution.py:107
  148.5 0.7 collective-permute-start.26
  149.2 0.7 collective-permute-start.20
  149.9 0.7 collective-permute-start.27
  150.5 0.6 pad_maximum_fusion.2
  151.2 4.8 %collective-permute-done.20 = f32[4,16,1024]{2,1,0:T(8,128)S(1)} collective-permute-done((f32[4,16,1024]{2,1,0:T(8,128)S(1)}, f32[4,16,1024]{2,1,0:T(8,128)S(1)}, u32[]{:S(2)}, u32[]{:S(2)}) %collective-permute-start.20) | collective-permute-done | bytes 262176 | tf_op jit(solution)/shard_map/ppermute | solution.py:123
  156.1 0.7 collective-permute-start.28
  156.9 1.3 collective-permute-start.29
  158.2 2.5 %collective-permute-done.21 = f32[2,16,1024]{2,1,0:T(8,128)S(1)} collective-permute-done((f32[2,16,1024]{2,1,0:T(8,128)S(1)}, f32[2,16,1024]{2,1,0:T(8,128)S(1)}, u32[]{:S(2)}, u32[]{:S(2)}) %collective-permute-start.21) | collective-permute-done | bytes 131104 | tf_op jit(solution)/shard_map/ppermute | solution.py:123
  160.7 5.1 %collective-permute-start.22 = (f32[1,16,1024]{2,1,0:T(8,128)S(1)}, f32[1,16,1024]{2,1,0:T(8,128)S(1)}, u32[]{:S(2)}, u32[]{:S(2)}) collective-permute-start(f32[1,16,1024]{2,1,0:T(8,128)S(1)} %slice_select_fusion.7), channel_id=1, source_target_pairs={{0,16},{16,0},{32,48},{48,32},{64,80},{80,64},{96,112},{112,96},{1... | collective-permute-start | bytes 196616 | tf_op jit(solution)/shard_map/ppermute | solution.py:123
  165.8 0.3 fusion.1
  166.1 0.3 fusion.53
  167.1 0.6 pad_maximum_fusion.1
  (97 shorter events, 2.8 us)
Async XLA Ops:
  14.6 30.2 %copy-start.6 = (bf16[16,1024]{1,0:T(8,128)(2,1)S(1)}, bf16[16,1024]{1,0:T(8,128)(2,1)}, u32[]{:S(2)}) copy-start(bf16[16,1024]{1,0:T(8,128)(2,1)} %param.14) | copy-start | bytes 98308
  14.6 30.5 %copy-start.11 = (bf16[16,1024]{1,0:T(8,128)(2,1)S(1)}, bf16[16,1024]{1,0:T(8,128)(2,1)}, u32[]{:S(2)}) copy-start(bf16[16,1024]{1,0:T(8,128)(2,1)} %param.13) | copy-start | bytes 98308
  14.6 30.7 %copy-start.5 = (f32[128,128]{1,0:T(8,128)S(1)}, f32[128,128]{1,0:T(8,128)}, u32[]{:S(2)}) copy-start(f32[128,128]{1,0:T(8,128)} %param.15) | copy-start | bytes 196612
  35.4 32.8 %copy-start.2 = (bf16[2048,128]{1,0:T(8,128)(2,1)S(1)}, bf16[2048,128]{1,0:T(8,128)(2,1)}, u32[]{:S(2)}) copy-start(bf16[2048,128]{1,0:T(8,128)(2,1)} %shard_map.137) | copy-start | bytes 1572868
  35.4 21.7 %collective-permute-start.6 = (f32[128,128]{1,0:T(8,128)S(1)}, f32[128,128]{1,0:T(8,128)S(1)}, u32[]{:S(2)}, u32[]{:S(2)}) collective-permute-start(f32[128,128]{1,0:T(8,128)S(1)} %fusion.11), channel_id=1, source_target_pairs={{0,16},{16,0},{32,48},{48,32},{64,80},{80,64},{96,112},{112,96},{1... | collective-permute-start | bytes 196616 | tf_op jit(solution)/shard_map/ppermute | solution.py:107
  41.9 35.0 %collective-permute-start.3 = (f32[4,16,1024]{2,1,0:T(8,128)S(1)}, f32[4,16,1024]{2,1,0:T(8,128)S(1)}, u32[]{:S(2)}, u32[]{:S(2)}) collective-permute-start(f32[4,16,1024]{2,1,0:T(8,128)S(1)} %bitcast.60), channel_id=1, source_target_pairs={{0,64},{16,80},{32,96},{48,112},{64,0},{80,16},{96,32},{112,48},{1... | collective-permute-start | bytes 786440 | tf_op jit(solution)/shard_map/ppermute | solution.py:123
  44.7 10.7 %collective-permute-start = (bf16[16,1024]{1,0:T(8,128)(2,1)S(1)}, bf16[16,1024]{1,0:T(8,128)(2,1)S(1)}, u32[]{:S(2)}, u32[]{:S(2)}) collective-permute-start(bf16[16,1024]{1,0:T(8,128)(2,1)S(1)} %copy-done.6), channel_id=1, source_target_pairs={{0,16},{16,0},{32,48},{48,32},{64,80},{80,64},{96,112},{112,96},{1... | collective-permute-start | bytes 98312 | tf_op jit(solution)/shard_map/ppermute | solution.py:133
  45.1 10.8 %collective-permute-start.13 = (bf16[16,1024]{1,0:T(8,128)(2,1)S(1)}, bf16[16,1024]{1,0:T(8,128)(2,1)S(1)}, u32[]{:S(2)}, u32[]{:S(2)}) collective-permute-start(bf16[16,1024]{1,0:T(8,128)(2,1)S(1)} %copy-done.11), channel_id=1, source_target_pairs={{0,16},{16,0},{32,48},{48,32},{64,80},{80,64},{96,112},{112,96},{1... | collective-permute-start | bytes 98312 | tf_op jit(solution)/shard_map/ppermute | solution.py:133
  55.4 3.2 %collective-permute-start.1 = (bf16[32,1024]{1,0:T(8,128)(2,1)S(1)}, bf16[32,1024]{1,0:T(8,128)(2,1)S(1)}, u32[]{:S(2)}, u32[]{:S(2)}) collective-permute-start(bf16[32,1024]{1,0:T(8,128)(2,1)S(1)} %maximum_select_fusion.4), channel_id=1, source_target_pairs={{0,32},{16,48},{32,0},{48,16},{64,96},{80,112},{96,64},{112,80},{1... | collective-permute-start | bytes 196616 | tf_op jit(solution)/shard_map/ppermute | solution.py:133
  55.9 6.3 %collective-permute-start.14 = (bf16[32,1024]{1,0:T(8,128)(2,1)S(1)}, bf16[32,1024]{1,0:T(8,128)(2,1)S(1)}, u32[]{:S(2)}, u32[]{:S(2)}) collective-permute-start(bf16[32,1024]{1,0:T(8,128)(2,1)S(1)} %maximum_select_fusion.5), channel_id=1, source_target_pairs={{0,32},{16,48},{32,0},{48,16},{64,96},{80,112},{96,64},{112,80},{1... | collective-permute-start | bytes 196616 | tf_op jit(solution)/shard_map/ppermute | solution.py:133
  57.1 4.6 %collective-permute-start.7 = (f32[128,128]{1,0:T(8,128)S(1)}, f32[128,128]{1,0:T(8,128)S(1)}, u32[]{:S(2)}, u32[]{:S(2)}) collective-permute-start(f32[128,128]{1,0:T(8,128)S(1)} %add.81), channel_id=1, source_target_pairs={{0,32},{16,48},{32,0},{48,16},{64,96},{80,112},{96,64},{112,80},{1... | collective-permute-start | bytes 196616 | tf_op jit(solution)/shard_map/ppermute | solution.py:107
  58.7 9.5 %collective-permute-start.2 = (bf16[64,1024]{1,0:T(8,128)(2,1)S(1)}, bf16[64,1024]{1,0:T(8,128)(2,1)S(1)}, u32[]{:S(2)}, u32[]{:S(2)}) collective-permute-start(bf16[64,1024]{1,0:T(8,128)(2,1)S(1)} %maximum_select_fusion.2), channel_id=1, source_target_pairs={{0,64},{16,80},{32,96},{48,112},{64,0},{80,16},{96,32},{112,48},{1... | collective-permute-start | bytes 393224 | tf_op jit(solution)/shard_map/ppermute | solution.py:133
  61.7 5.6 %collective-permute-start.8 = (f32[128,128]{1,0:T(8,128)S(1)}, f32[128,128]{1,0:T(8,128)S(1)}, u32[]{:S(2)}, u32[]{:S(2)}) collective-permute-start(f32[128,128]{1,0:T(8,128)S(1)} %add.82), channel_id=1, source_target_pairs={{0,64},{16,80},{32,96},{48,112},{64,0},{80,16},{96,32},{112,48},{1... | collective-permute-start | bytes 196616 | tf_op jit(solution)/shard_map/ppermute | solution.py:107
  62.2 47.8 %collective-permute-start.15 = (bf16[64,1024]{1,0:T(8,128)(2,1)S(1)}, bf16[64,1024]{1,0:T(8,128)(2,1)S(1)}, u32[]{:S(2)}, u32[]{:S(2)}) collective-permute-start(bf16[64,1024]{1,0:T(8,128)(2,1)S(1)} %maximum_select_fusion.3), channel_id=1, source_target_pairs={{0,64},{16,80},{32,96},{48,112},{64,0},{80,16},{96,32},{112,48},{1... | collective-permute-start | bytes 393224 | tf_op jit(solution)/shard_map/ppermute | solution.py:133
  67.3 9.0 %collective-permute-start.9 = (f32[128,128]{1,0:T(8,128)S(1)}, f32[128,128]{1,0:T(8,128)S(1)}, u32[]{:S(2)}, u32[]{:S(2)}) collective-permute-start(f32[128,128]{1,0:T(8,128)S(1)} %add.83), channel_id=1, source_target_pairs={{15,14},{31,30},{47,46},{63,62},{79,78},{95,94},{111,110},{127,126}} | collective-permute-start | bytes 196616 | tf_op jit(solution)/shard_map/ppermute | solution.py:96
  72.8 3.3 %copy-start = (f32[2048,1024]{1,0:T(8,128)}, f32[2048,1024]{1,0:T(8,128)S(1)}, u32[]{:S(2)}) copy-start(f32[2048,1024]{1,0:T(8,128)S(1)} %convolution_subtract_fusion.1) | copy-start | bytes 25165828
  76.1 15.4 %copy-start.4 = (f32[128,128]{1,0:T(8,128)S(1)}, f32[128,128]{1,0:T(8,128)}, u32[]{:S(2)}) copy-start(f32[128,128]{1,0:T(8,128)} %param.16) | copy-start | bytes 196612
  76.1 15.4 %copy-start.7 = (f32[128,128]{1,0:T(8,128)S(1)}, f32[128,128]{1,0:T(8,128)}, u32[]{:S(2)}) copy-start(f32[128,128]{1,0:T(8,128)} %param.21) | copy-start | bytes 196612
  76.1 16.3 %copy-start.12 = (f32[16,1024]{1,0:T(8,128)S(1)}, f32[16,1024]{1,0:T(8,128)}, u32[]{:S(2)}) copy-start(f32[16,1024]{1,0:T(8,128)} %param.19) | copy-start | bytes 196612
  76.3 1.2 collective-permute-start.10
  77.0 3.9 %collective-permute-start.4 = (f32[2,16,1024]{2,1,0:T(8,128)S(1)}, f32[2,16,1024]{2,1,0:T(8,128)S(1)}, u32[]{:S(2)}, u32[]{:S(2)}) collective-permute-start(f32[2,16,1024]{2,1,0:T(8,128)S(1)} %slice_select_fusion.6), channel_id=1, source_target_pairs={{0,32},{16,48},{32,0},{48,16},{64,96},{80,112},{96,64},{112,80},{1... | collective-permute-start | bytes 393224 | tf_op jit(solution)/shard_map/ppermute | solution.py:123
  77.5 3.4 %collective-permute-start.11 = (f32[128,128]{1,0:T(8,128)S(1)}, f32[128,128]{1,0:T(8,128)S(1)}, u32[]{:S(2)}, u32[]{:S(2)}) collective-permute-start(f32[128,128]{1,0:T(8,128)S(1)} %broadcast_select_fusion.4), channel_id=1, source_target_pairs={{15,11},{14,10},{13,9},{12,8},{31,27},{30,26},{29,25},{28,24},{47,... | collective-permute-start | bytes 196616 | tf_op jit(solution)/shard_map/ppermute | solution.py:96
  81.0 10.5 %collective-permute-start.12 = (f32[128,128]{1,0:T(8,128)S(1)}, f32[128,128]{1,0:T(8,128)S(1)}, u32[]{:S(2)}, u32[]{:S(2)}) collective-permute-start(f32[128,128]{1,0:T(8,128)S(1)} %broadcast_select_fusion.5), channel_id=1, source_target_pairs={{15,7},{14,6},{13,5},{12,4},{11,3},{10,2},{9,1},{8,0},{31,23},{30,... | collective-permute-start | bytes 196616 | tf_op jit(solution)/shard_map/ppermute | solution.py:96
  82.3 10.1 %collective-permute-start.5 = (f32[1,16,1024]{2,1,0:T(8,128)S(1)}, f32[1,16,1024]{2,1,0:T(8,128)S(1)}, u32[]{:S(2)}, u32[]{:S(2)}) collective-permute-start(f32[1,16,1024]{2,1,0:T(8,128)S(1)} %slice_select_fusion.8), channel_id=1, source_target_pairs={{0,16},{16,0},{32,48},{48,32},{64,80},{80,64},{96,112},{112,96},{1... | collective-permute-start | bytes 196616 | tf_op jit(solution)/shard_map/ppermute | solution.py:123
  92.3 22.7 %copy-start.9 = (f32[128,128]{1,0:T(8,128)}, f32[128,128]{1,0:T(8,128)S(1)}, u32[]{:S(2)}) copy-start(f32[128,128]{1,0:T(8,128)S(1)} %get-tuple-element.10) | copy-start | bytes 196612
  94.5 20.7 %collective-permute-start.16 = (bf16[16,128]{1,0:T(8,128)(2,1)S(1)}, bf16[16,128]{1,0:T(8,128)(2,1)S(1)}, u32[]{:S(2)}, u32[]{:S(2)}) collective-permute-start(bf16[16,128]{1,0:T(8,128)(2,1)S(1)} %slice.139), channel_id=1, source_target_pairs={{14,15},{30,31},{46,47},{62,63},{78,79},{94,95},{110,111},{126,127}} | collective-permute-start | bytes 12296 | tf_op jit(solution)/shard_map/ppermute | solution.py:96
  110.0 5.0 %copy-start.3 = (bf16[2048,128]{1,0:T(8,128)(2,1)S(1)}, bf16[2048,128]{1,0:T(8,128)(2,1)}, u32[]{:S(2)}) copy-start(bf16[2048,128]{1,0:T(8,128)(2,1)} %shard_map.138) | copy-start | bytes 1572868
  110.0 5.9 %copy-start.1 = (bf16[2048,1024]{1,0:T(8,128)(2,1)S(1)}, bf16[2048,1024]{1,0:T(8,128)(2,1)}, u32[]{:S(2)}) copy-start(bf16[2048,1024]{1,0:T(8,128)(2,1)} %param.12) | copy-start | bytes 12582916
  115.3 1.9 %collective-permute-start.17 = (bf16[16,128]{1,0:T(8,128)(2,1)S(1)}, bf16[16,128]{1,0:T(8,128)(2,1)S(1)}, u32[]{:S(2)}, u32[]{:S(2)}) collective-permute-start(bf16[16,128]{1,0:T(8,128)(2,1)S(1)} %broadcast_select_fusion.6), channel_id=1, source_target_pairs={{14,12},{15,13},{30,28},{31,29},{46,44},{47,45},{62,60},{63,61},{7... | collective-permute-start | bytes 12296 | tf_op jit(solution)/shard_map/ppermute | solution.py:96
  117.2 3.3 %collective-permute-start.18 = (bf16[16,128]{1,0:T(8,128)(2,1)S(1)}, bf16[16,128]{1,0:T(8,128)(2,1)S(1)}, u32[]{:S(2)}, u32[]{:S(2)}) collective-permute-start(bf16[16,128]{1,0:T(8,128)(2,1)S(1)} %broadcast_select_fusion.7), channel_id=1, source_target_pairs={{14,10},{15,11},{12,8},{13,9},{30,26},{31,27},{28,24},{29,25},{46,... | collective-permute-start | bytes 12296 | tf_op jit(solution)/shard_map/ppermute | solution.py:96
  120.5 45.4 %copy-start.8 = (f32[128,128]{1,0:T(8,128)S(1)}, f32[128,128]{1,0:T(8,128)}, u32[]{:S(2)}) copy-start(f32[128,128]{1,0:T(8,128)} %param.20) | copy-start | bytes 196612
  120.5 46.3 %copy-start.13 = (f32[16,1024]{1,0:T(8,128)S(1)}, f32[16,1024]{1,0:T(8,128)}, u32[]{:S(2)}) copy-start(f32[16,1024]{1,0:T(8,128)} %param.18) | copy-start | bytes 196612
  120.5 8.9 %collective-permute-start.19 = (bf16[16,128]{1,0:T(8,128)(2,1)S(1)}, bf16[16,128]{1,0:T(8,128)(2,1)S(1)}, u32[]{:S(2)}, u32[]{:S(2)}) collective-permute-start(bf16[16,128]{1,0:T(8,128)(2,1)S(1)} %broadcast_select_fusion.8), channel_id=1, source_target_pairs={{14,6},{15,7},{12,4},{13,5},{10,2},{11,3},{8,0},{9,1},{30,22},{31,... | collective-permute-start | bytes 12296 | tf_op jit(solution)/shard_map/ppermute | solution.py:96
  129.6 10.9 %collective-permute-start.23 = (f32[128,128]{1,0:T(8,128)S(1)}, f32[128,128]{1,0:T(8,128)S(1)}, u32[]{:S(2)}, u32[]{:S(2)}) collective-permute-start(f32[128,128]{1,0:T(8,128)S(1)} %convolution_add_fusion.1), channel_id=1, source_target_pairs={{0,16},{16,0},{32,48},{48,32},{64,80},{80,64},{96,112},{112,96},{1... | collective-permute-start | bytes 196616 | tf_op jit(solution)/shard_map/ppermute | solution.py:107
  140.6 3.2 %collective-permute-start.24 = (f32[128,128]{1,0:T(8,128)S(1)}, f32[128,128]{1,0:T(8,128)S(1)}, u32[]{:S(2)}, u32[]{:S(2)}) collective-permute-start(f32[128,128]{1,0:T(8,128)S(1)} %add.91), channel_id=1, source_target_pairs={{0,32},{16,48},{32,0},{48,16},{64,96},{80,112},{96,64},{112,80},{1... | collective-permute-start | bytes 196616 | tf_op jit(solution)/shard_map/ppermute | solution.py:107
  143.8 4.7 %collective-permute-start.25 = (f32[128,128]{1,0:T(8,128)S(1)}, f32[128,128]{1,0:T(8,128)S(1)}, u32[]{:S(2)}, u32[]{:S(2)}) collective-permute-start(f32[128,128]{1,0:T(8,128)S(1)} %add.92), channel_id=1, source_target_pairs={{0,64},{16,80},{32,96},{48,112},{64,0},{80,16},{96,32},{112,48},{1... | collective-permute-start | bytes 196616 | tf_op jit(solution)/shard_map/ppermute | solution.py:107
  148.5 1.4 collective-permute-start.26
  149.2 6.8 %collective-permute-start.20 = (f32[4,16,1024]{2,1,0:T(8,128)S(1)}, f32[4,16,1024]{2,1,0:T(8,128)S(1)}, u32[]{:S(2)}, u32[]{:S(2)}) collective-permute-start(f32[4,16,1024]{2,1,0:T(8,128)S(1)} %bitcast.61), channel_id=1, source_target_pairs={{0,64},{16,80},{32,96},{48,112},{64,0},{80,16},{96,32},{112,48},{1... | collective-permute-start | bytes 786440 | tf_op jit(solution)/shard_map/ppermute | solution.py:123
  149.9 6.2 %collective-permute-start.27 = (f32[128,128]{1,0:T(8,128)S(1)}, f32[128,128]{1,0:T(8,128)S(1)}, u32[]{:S(2)}, u32[]{:S(2)}) collective-permute-start(f32[128,128]{1,0:T(8,128)S(1)} %broadcast_select_fusion), channel_id=1, source_target_pairs={{14,12},{15,13},{30,28},{31,29},{46,44},{47,45},{62,60},{63,61},{7... | collective-permute-start | bytes 196616 | tf_op jit(solution)/shard_map/ppermute | solution.py:96
  156.1 0.8 collective-permute-start.28
  156.8 3.9 %collective-permute-start.21 = (f32[2,16,1024]{2,1,0:T(8,128)S(1)}, f32[2,16,1024]{2,1,0:T(8,128)S(1)}, u32[]{:S(2)}, u32[]{:S(2)}) collective-permute-start(f32[2,16,1024]{2,1,0:T(8,128)S(1)} %slice_select_fusion.5), channel_id=1, source_target_pairs={{0,32},{16,48},{32,0},{48,16},{64,96},{80,112},{96,64},{112,80},{1... | collective-permute-start | bytes 393224 | tf_op jit(solution)/shard_map/ppermute | solution.py:123
  156.9 9.0 %collective-permute-start.29 = (f32[128,128]{1,0:T(8,128)S(1)}, f32[128,128]{1,0:T(8,128)S(1)}, u32[]{:S(2)}, u32[]{:S(2)}) collective-permute-start(f32[128,128]{1,0:T(8,128)S(1)} %broadcast_select_fusion.2), channel_id=1, source_target_pairs={{14,6},{15,7},{12,4},{13,5},{10,2},{11,3},{8,0},{9,1},{30,22},{31,... | collective-permute-start | bytes 196616 | tf_op jit(solution)/shard_map/ppermute | solution.py:96
  160.7 6.1 %collective-permute-start.22 = (f32[1,16,1024]{2,1,0:T(8,128)S(1)}, f32[1,16,1024]{2,1,0:T(8,128)S(1)}, u32[]{:S(2)}, u32[]{:S(2)}) collective-permute-start(f32[1,16,1024]{2,1,0:T(8,128)S(1)} %slice_select_fusion.7), channel_id=1, source_target_pairs={{0,16},{16,0},{32,48},{48,32},{64,80},{80,64},{96,112},{112,96},{1... | collective-permute-start | bytes 196616 | tf_op jit(solution)/shard_map/ppermute | solution.py:123
  166.6 1.1 copy-start.10

commit v8 on v7

--- a/solution.py
+++ b/solution.py
@@ -204,11 +204,13 @@
         inverse_two = inverse_lower(diag_two)
         solved_two = solve_panel(adj_trail[:, last:], inverse_two, root_two)
         partial_two = jnp.dot(solved_two.T, trail[:, last:], preferred_element_type=jnp.float32)
-        seed_two = jnp.tril(adj_diag_two - summed_block(partial_two, root_two))
+        rows_two = butterfly_sum(partial_two, "row", n_row)
+        diag_one_late, rows_two = lax.optimization_barrier((diag_one, rows_two))
+        inverse_one = inverse_lower(diag_one_late)
+        seed_two = jnp.tril(adj_diag_two - tree_broadcast(rows_two, "col", n_col, root_two))
         grad_diag_two = block_adjoint(diag_two, inverse_two, seed_two)
         mirror_two = own_rows(grad_diag_two + grad_diag_two.T)
         rest_two = jnp.dot(mirror_two, full_two.astype(jnp.float32), precision=exact_mode)
-        inverse_one = inverse_lower(diag_one)
         crossed = halving_scatter(
             jnp.dot(solved_two.T, trail, preferred_element_type=jnp.float32), "row", n_row
         )

time: 170 us -> 174 us (1.024)
  starting transfers between devices: 44.5 us -> 48.7 us
    ppermute x6, waiting for transfers between devices: 1.14 us -> 5.42 us  [doubling_gather(): other = lax.ppermute(value, axis, pairs)]
    ppermute x6, starting transfers between devices: 15.1 us -> 17.8 us  [butterfly_sum(): value = value + lax.ppermute(value, axis, pairs)]
    ppermute x6, waiting for transfers between devices: 11.7 us -> 9.03 us  [butterfly_sum(): value = value + lax.ppermute(value, axis, pairs)]
    ppermute x6, waiting for transfers between devices: 10 us -> 7.84 us  [halving_scatter(): blocks = keep + lax.ppermute(send, axis, pairs)]
    ppermute x6, starting transfers between devices: 13.3 us -> 15.2 us  [halving_scatter(): blocks = keep + lax.ppermute(send, axis, pairs)]
  transfers between devices with their start and end apart: 30 -> 30, of which waited for: 11 -> 12; matrix products, arithmetic and copies ran while one was open for 19% -> 19% of each run, Pallas kernels for 9% -> 9%
where the time goes in v8:
time: 174 us; the launch traced here: 171 us
  starting transfers between devices  48.7 us (28%)
  waiting for transfers between devices  34.5 us (20%)
  Pallas kernels  33.9 us (19%)
  other arithmetic  25.1 us (14%)
  matrix products  22.5 us (13%)
  local copies, waits for them, and re-layouts  4.94 us (3%)
    pallas_call x2, Pallas kernels, panel_broadcast(): pl.pallas_call(functools.partial(spread_kernel, root, size), out_shape=ja...  33.9 us
    another operation x4, other arithmetic, inverse_lower(): return lax.linalg.triangular_solve(block, ident, left_side=True, lower=True)  20.5 us
    ppermute x6, starting transfers between devices, butterfly_sum(): value = value + lax.ppermute(value, axis, pairs)  17.8 us
    ppermute x6, starting transfers between devices, halving_scatter(): blocks = keep + lax.ppermute(send, axis, pairs)  15.2 us
    ppermute x12, waiting for transfers between devices, tree_broadcast(): arrived = lax.ppermute(value, axis, pairs)  12.2 us
    ppermute x12, starting transfers between devices, tree_broadcast(): arrived = lax.ppermute(value, axis, pairs)  10.4 us
    ppermute x6, waiting for transfers between devices, butterfly_sum(): value = value + lax.ppermute(value, axis, pairs)  9.03 us
    ppermute x6, waiting for transfers between devices, halving_scatter(): blocks = keep + lax.ppermute(send, axis, pairs)  7.84 us
  transfers between devices with their start and end apart: 30, of which 12 were waited for; matrix products, arithmetic and copies ran while one was open for 19% of the time, Pallas kernels for 9%

profile of v8, /device:TPU:1, one launch (start us, length us, event | category | flops | bytes accessed | tf_op | source)
XLA Modules:
  0.0 171.0 jit_solution(8343950834428976578)
XLA Ops:
  0.6 0.9 select_bitcast_fusion.1
  1.5 9.8 %custom-call.4 = f32[1,128,128]{1,2,0:T(8,128)S(1)} custom-call(f32[1,128,128]{2,1,0:T(8,128)S(1)} %select_bitcast_fusion.1), custom_call_target="InvertDiagBlocksLowerTriangular" | custom-call | tf_op jit(solution)/shard_map/triangular_solve/custom-call.1 | solution.py:154
  11.3 0.3 fusion.15
  11.6 3.0 %fusion.x_ref = bf16[2048,128]{1,0:T(8,128)(2,1)} fusion(f32[128,128]{1,0:T(8,128)S(1)} %fusion.15, f32[2048,1024]{1,0:T(8,128)} %param.17), kind=kOutput, calls=%fused_computation.6 | convolution fusion | flops 402915328 | bytes 1638400 | tf_op jit(solution)/shard_map/dot_general | solution.py:193
  14.6 19.2 %shard_map.137 = bf16[2048,128]{1,0:T(8,128)(2,1)} custom-call(bf16[2048,128]{1,0:T(8,128)(2,1)} %fusion.x_ref), custom_call_target="tpu_custom_call" | custom-call | tf_op jit(solution)/shard_map/pallas_call | solution.py:77
  33.8 1.5 fusion.11
  35.4 3.4 %collective-permute-start.6 = (f32[128,128]{1,0:T(8,128)S(1)}, f32[128,128]{1,0:T(8,128)S(1)}, u32[]{:S(2)}, u32[]{:S(2)}) collective-permute-start(f32[128,128]{1,0:T(8,128)S(1)} %fusion.11), channel_id=1, source_target_pairs={{0,16},{16,0},{32,48},{48,32},{64,80},{80,64},{96,112},{112,96},{1... | collective-permute-start | bytes 196616 | tf_op jit(solution)/shard_map/ppermute | solution.py:107
  38.7 3.1 %fusion.50 = f32[128,1024]{1,0:T(8,128)S(1)} fusion(bf16[2048,128]{1,0:T(8,128)(2,1)} %shard_map.137, bf16[2048,1024]{1,0:T(8,128)(2,1)} %param.12), kind=kOutput, calls=%fused_computation.103 | convolution fusion | flops 536870912 | bytes 5242880 | tf_op jit(solution)/shard_map/dot_general | solution.py:215
  41.9 2.8 %collective-permute-start.3 = (f32[4,16,1024]{2,1,0:T(8,128)S(1)}, f32[4,16,1024]{2,1,0:T(8,128)S(1)}, u32[]{:S(2)}, u32[]{:S(2)}) collective-permute-start(f32[4,16,1024]{2,1,0:T(8,128)S(1)} %bitcast.60), channel_id=1, source_target_pairs={{0,64},{16,80},{32,96},{48,112},{64,0},{80,16},{96,32},{112,48},{1... | collective-permute-start | bytes 786440 | tf_op jit(solution)/shard_map/ppermute | solution.py:123
  44.7 0.3 collective-permute-start
  45.4 0.6 collective-permute-done
  46.0 0.4 collective-permute-start.1
  46.4 1.2 collective-permute-start.14
  47.6 0.4 collective-permute-start.7
  48.0 4.8 %collective-permute-done.1 = bf16[32,1024]{1,0:T(8,128)(2,1)S(1)} collective-permute-done((bf16[32,1024]{1,0:T(8,128)(2,1)S(1)}, bf16[32,1024]{1,0:T(8,128)(2,1)S(1)}, u32[]{:S(2)}, u32[]{:S(2)}) %collective-permute-start.1) | collective-permute-done | bytes 65568 | tf_op jit(solution)/shard_map/ppermute | solution.py:133
  52.9 1.8 %collective-permute-start.2 = (bf16[64,1024]{1,0:T(8,128)(2,1)S(1)}, bf16[64,1024]{1,0:T(8,128)(2,1)S(1)}, u32[]{:S(2)}, u32[]{:S(2)}) collective-permute-start(bf16[64,1024]{1,0:T(8,128)(2,1)S(1)} %maximum_select_fusion.2), channel_id=1, source_target_pairs={{0,64},{16,80},{32,96},{48,112},{64,0},{80,16},{96,32},{112,48},{1... | collective-permute-start | bytes 393224 | tf_op jit(solution)/shard_map/ppermute | solution.py:133
  54.7 1.0 collective-permute-done.7
  55.7 1.8 %collective-permute-start.8 = (f32[128,128]{1,0:T(8,128)S(1)}, f32[128,128]{1,0:T(8,128)S(1)}, u32[]{:S(2)}, u32[]{:S(2)}) collective-permute-start(f32[128,128]{1,0:T(8,128)S(1)} %add.82), channel_id=1, source_target_pairs={{0,64},{16,80},{32,96},{48,112},{64,0},{80,16},{96,32},{112,48},{1... | collective-permute-start | bytes 196616 | tf_op jit(solution)/shard_map/ppermute | solution.py:107
  57.5 1.3 collective-permute-start.15
  58.8 1.9 %collective-permute-done.8 = f32[128,128]{1,0:T(8,128)S(1)} collective-permute-done((f32[128,128]{1,0:T(8,128)S(1)}, f32[128,128]{1,0:T(8,128)S(1)}, u32[]{:S(2)}, u32[]{:S(2)}) %collective-permute-start.8) | collective-permute-done | bytes 65568 | tf_op jit(solution)/shard_map/ppermute | solution.py:107
  60.8 0.8 collective-permute-start.9
  61.7 9.8 %custom-call.5 = f32[1,128,128]{1,2,0:T(8,128)S(1)} custom-call(f32[1,128,128]{2,1,0:T(8,128)S(1)} %select_bitcast_fusion), custom_call_target="InvertDiagBlocksLowerTriangular" | custom-call | tf_op jit(solution)/shard_map/triangular_solve/custom-call.1 | solution.py:154
  71.5 0.3 fusion.13
  71.8 4.6 %convolution_subtract_fusion.1 = f32[2048,1024]{1,0:T(8,128)S(1)} fusion(f32[2048,1024]{1,0:T(8,128)} %param.17, bf16[2048,128]{1,0:T(8,128)(2,1)S(1)} %copy-done.2, bf16[64,1024]{1,0:T(8,128)(2,1)S(1)} %maximum_select_fusion.2, bf16[64,1024]{1,0:T(8,128)(2,1)S(1)} %collective-permute-done.2, pred[]{:T(512)S(6)} %eq.62), kind=kOutput, calls=%fused_computation.2 | convolution fusion | flops 540147712 | bytes 17563648 | tf_op jit(solution)/shard_map/dot_general | solution.py:218
  76.4 3.3 %copy-done = f32[2048,1024]{1,0:T(8,128)} copy-done((f32[2048,1024]{1,0:T(8,128)}, f32[2048,1024]{1,0:T(8,128)S(1)}, u32[]{:S(2)}) %copy-start) | copy-done | bytes 8388632
  79.9 0.7 collective-permute-start.10
  80.7 1.2 collective-permute-start.4
  81.9 0.7 collective-permute-start.11
  82.6 2.0 %collective-permute-done.4 = f32[2,16,1024]{2,1,0:T(8,128)S(1)} collective-permute-done((f32[2,16,1024]{2,1,0:T(8,128)S(1)}, f32[2,16,1024]{2,1,0:T(8,128)S(1)}, u32[]{:S(2)}, u32[]{:S(2)}) %collective-permute-start.4) | collective-permute-done | bytes 131104 | tf_op jit(solution)/shard_map/ppermute | solution.py:123
  84.6 1.3 collective-permute-start.12
  85.9 3.9 %collective-permute-start.5 = (f32[1,16,1024]{2,1,0:T(8,128)S(1)}, f32[1,16,1024]{2,1,0:T(8,128)S(1)}, u32[]{:S(2)}, u32[]{:S(2)}) collective-permute-start(f32[1,16,1024]{2,1,0:T(8,128)S(1)} %slice_select_fusion.8), channel_id=1, source_target_pairs={{0,16},{16,0},{32,48},{48,32},{64,80},{80,64},{96,112},{112,96},{1... | collective-permute-start | bytes 196616 | tf_op jit(solution)/shard_map/ppermute | solution.py:123
  89.9 5.2 %collective-permute-done.12 = f32[128,128]{1,0:T(8,128)S(1)} collective-permute-done((f32[128,128]{1,0:T(8,128)S(1)}, f32[128,128]{1,0:T(8,128)S(1)}, u32[]{:S(2)}, u32[]{:S(2)}) %collective-permute-start.12) | collective-permute-done | bytes 65568 | tf_op jit(solution)/shard_map/ppermute | solution.py:96
  95.1 0.3 fusion.2
  96.3 1.0 convolution_convert_fusion
  97.3 0.8 slice.136.x_ref
  98.1 0.6 collective-permute-start.16
  98.8 14.6 %shard_map.138 = bf16[2048,128]{1,0:T(8,128)(2,1)} custom-call(bf16[2048,128]{1,0:T(8,128)(2,1)} %slice.136.x_ref), custom_call_target="tpu_custom_call" | custom-call | tf_op jit(solution)/shard_map/pallas_call | solution.py:77
  113.5 4.9 %convolution_subtract_fusion = bf16[2048,1024]{1,0:T(8,128)(2,1)S(1)} fusion(f32[2048,1024]{1,0:T(8,128)} %copy-done, bf16[2048,128]{1,0:T(8,128)(2,1)} %shard_map.138, bf16[64,1024]{1,0:T(8,128)(2,1)S(1)} %maximum_select_fusion.3, bf16[64,1024]{1,0:T(8,128)(2,1)S(1)} %collective-permute-done.15, pred[]{:T(512)S(6)} %eq.62), kind=kOutput, calls=%fused_computation.1 | convolution fusion | flops 542244864 | bytes 13369345 | tf_op jit(solution)/shard_map/dot_general | solution.py:232
  118.7 0.7 collective-permute-start.17
  119.4 0.7 fusion.52
  120.1 0.4 slice.193
  120.6 0.7 collective-permute-start.18
  121.2 2.6 %pad_maximum_fusion = bf16[2048,1024]{1,0:T(8,128)(2,1)} fusion(bf16[2048,128]{1,0:T(8,128)(2,1)S(1)} %fusion.7, bf16[2048,896]{1,0:T(8,128)(2,1)S(1)} %slice.193), kind=kLoop, calls=%fused_computation.3 | loop fusion | flops 8388608 | bytes 8388608 | tf_op jit(solution)/shard_map/concatenate | solution.py:245
  123.9 1.6 collective-permute-start.19
  125.6 0.3 fusion.9
  125.9 6.9 %collective-permute-done.19 = bf16[16,128]{1,0:T(8,128)(2,1)S(1)} collective-permute-done((bf16[16,128]{1,0:T(8,128)(2,1)S(1)}, bf16[16,128]{1,0:T(8,128)(2,1)S(1)}, u32[]{:S(2)}, u32[]{:S(2)}) %collective-permute-start.19) | collective-permute-done | bytes 4128 | tf_op jit(solution)/shard_map/ppermute | solution.py:96
  133.0 10.0 %collective-permute-start.23 = (f32[128,128]{1,0:T(8,128)S(1)}, f32[128,128]{1,0:T(8,128)S(1)}, u32[]{:S(2)}, u32[]{:S(2)}) collective-permute-start(f32[128,128]{1,0:T(8,128)S(1)} %convolution_add_fusion.1), channel_id=1, source_target_pairs={{0,16},{16,0},{32,48},{48,32},{64,80},{80,64},{96,112},{112,96},{1... | collective-permute-start | bytes 196616 | tf_op jit(solution)/shard_map/ppermute | solution.py:107
  143.3 0.7 collective-permute-done.23
  144.0 0.9 collective-permute-start.24
  144.9 2.3 %collective-permute-done.24 = f32[128,128]{1,0:T(8,128)S(1)} collective-permute-done((f32[128,128]{1,0:T(8,128)S(1)}, f32[128,128]{1,0:T(8,128)S(1)}, u32[]{:S(2)}, u32[]{:S(2)}) %collective-permute-start.24) | collective-permute-done | bytes 65568 | tf_op jit(solution)/shard_map/ppermute | solution.py:107
  147.2 1.4 collective-permute-start.25
  148.7 3.2 %collective-permute-done.25 = f32[128,128]{1,0:T(8,128)S(1)} collective-permute-done((f32[128,128]{1,0:T(8,128)S(1)}, f32[128,128]{1,0:T(8,128)S(1)}, u32[]{:S(2)}, u32[]{:S(2)}) %collective-permute-start.25) | collective-permute-done | bytes 65568 | tf_op jit(solution)/shard_map/ppermute | solution.py:107
  151.9 0.7 collective-permute-start.26
  152.6 1.4 collective-permute-start.20
  154.0 0.7 collective-permute-start.27
  154.7 0.6 pad_maximum_fusion.2
  155.3 4.1 %collective-permute-done.20 = f32[4,16,1024]{2,1,0:T(8,128)S(1)} collective-permute-done((f32[4,16,1024]{2,1,0:T(8,128)S(1)}, f32[4,16,1024]{2,1,0:T(8,128)S(1)}, u32[]{:S(2)}, u32[]{:S(2)}) %collective-permute-start.20) | collective-permute-done | bytes 262176 | tf_op jit(solution)/shard_map/ppermute | solution.py:123
  159.5 0.7 collective-permute-start.28
  160.2 0.9 collective-permute-start.21
  161.1 1.3 collective-permute-start.29
  162.4 1.7 %collective-permute-done.21 = f32[2,16,1024]{2,1,0:T(8,128)S(1)} collective-permute-done((f32[2,16,1024]{2,1,0:T(8,128)S(1)}, f32[2,16,1024]{2,1,0:T(8,128)S(1)}, u32[]{:S(2)}, u32[]{:S(2)}) %collective-permute-start.21) | collective-permute-done | bytes 131104 | tf_op jit(solution)/shard_map/ppermute | solution.py:123
  164.1 5.0 %collective-permute-start.22 = (f32[1,16,1024]{2,1,0:T(8,128)S(1)}, f32[1,16,1024]{2,1,0:T(8,128)S(1)}, u32[]{:S(2)}, u32[]{:S(2)}) collective-permute-start(f32[1,16,1024]{2,1,0:T(8,128)S(1)} %slice_select_fusion.7), channel_id=1, source_target_pairs={{0,16},{16,0},{32,48},{48,32},{64,80},{80,64},{96,112},{112,96},{1... | collective-permute-start | bytes 196616 | tf_op jit(solution)/shard_map/ppermute | solution.py:123
  169.2 0.3 fusion.1
  170.4 0.6 pad_maximum_fusion.1
  (97 shorter events, 3.5 us)
Async XLA Ops:
  14.6 30.2 %copy-start.6 = (bf16[16,1024]{1,0:T(8,128)(2,1)S(1)}, bf16[16,1024]{1,0:T(8,128)(2,1)}, u32[]{:S(2)}) copy-start(bf16[16,1024]{1,0:T(8,128)(2,1)} %param.14) | copy-start | bytes 98308
  14.6 30.5 %copy-start.11 = (bf16[16,1024]{1,0:T(8,128)(2,1)S(1)}, bf16[16,1024]{1,0:T(8,128)(2,1)}, u32[]{:S(2)}) copy-start(bf16[16,1024]{1,0:T(8,128)(2,1)} %param.13) | copy-start | bytes 98308
  35.4 26.3 %copy-start.5 = (f32[128,128]{1,0:T(8,128)S(1)}, f32[128,128]{1,0:T(8,128)}, u32[]{:S(2)}) copy-start(f32[128,128]{1,0:T(8,128)} %param.15) | copy-start | bytes 196612
  35.4 36.4 %copy-start.2 = (bf16[2048,128]{1,0:T(8,128)(2,1)S(1)}, bf16[2048,128]{1,0:T(8,128)(2,1)}, u32[]{:S(2)}) copy-start(bf16[2048,128]{1,0:T(8,128)(2,1)} %shard_map.137) | copy-start | bytes 1572868
  35.4 12.2 %collective-permute-start.6 = (f32[128,128]{1,0:T(8,128)S(1)}, f32[128,128]{1,0:T(8,128)S(1)}, u32[]{:S(2)}, u32[]{:S(2)}) collective-permute-start(f32[128,128]{1,0:T(8,128)S(1)} %fusion.11), channel_id=1, source_target_pairs={{0,16},{16,0},{32,48},{48,32},{64,80},{80,64},{96,112},{112,96},{1... | collective-permute-start | bytes 196616 | tf_op jit(solution)/shard_map/ppermute | solution.py:107
  41.9 38.7 %collective-permute-start.3 = (f32[4,16,1024]{2,1,0:T(8,128)S(1)}, f32[4,16,1024]{2,1,0:T(8,128)S(1)}, u32[]{:S(2)}, u32[]{:S(2)}) collective-permute-start(f32[4,16,1024]{2,1,0:T(8,128)S(1)} %bitcast.60), channel_id=1, source_target_pairs={{0,64},{16,80},{32,96},{48,112},{64,0},{80,16},{96,32},{112,48},{1... | collective-permute-start | bytes 786440 | tf_op jit(solution)/shard_map/ppermute | solution.py:123
  44.7 1.2 collective-permute-start
  45.1 1.3 collective-permute-start.13
  46.0 6.9 %collective-permute-start.1 = (bf16[32,1024]{1,0:T(8,128)(2,1)S(1)}, bf16[32,1024]{1,0:T(8,128)(2,1)S(1)}, u32[]{:S(2)}, u32[]{:S(2)}) collective-permute-start(bf16[32,1024]{1,0:T(8,128)(2,1)S(1)} %maximum_select_fusion.4), channel_id=1, source_target_pairs={{0,32},{16,48},{32,0},{48,16},{64,96},{80,112},{96,64},{112,80},{1... | collective-permute-start | bytes 196616 | tf_op jit(solution)/shard_map/ppermute | solution.py:133
  46.4 11.1 %collective-permute-start.14 = (bf16[32,1024]{1,0:T(8,128)(2,1)S(1)}, bf16[32,1024]{1,0:T(8,128)(2,1)S(1)}, u32[]{:S(2)}, u32[]{:S(2)}) collective-permute-start(bf16[32,1024]{1,0:T(8,128)(2,1)S(1)} %maximum_select_fusion.5), channel_id=1, source_target_pairs={{0,32},{16,48},{32,0},{48,16},{64,96},{80,112},{96,64},{112,80},{1... | collective-permute-start | bytes 196616 | tf_op jit(solution)/shard_map/ppermute | solution.py:133
  47.6 8.0 %collective-permute-start.7 = (f32[128,128]{1,0:T(8,128)S(1)}, f32[128,128]{1,0:T(8,128)S(1)}, u32[]{:S(2)}, u32[]{:S(2)}) collective-permute-start(f32[128,128]{1,0:T(8,128)S(1)} %add.81), channel_id=1, source_target_pairs={{0,32},{16,48},{32,0},{48,16},{64,96},{80,112},{96,64},{112,80},{1... | collective-permute-start | bytes 196616 | tf_op jit(solution)/shard_map/ppermute | solution.py:107
  52.9 18.9 %collective-permute-start.2 = (bf16[64,1024]{1,0:T(8,128)(2,1)S(1)}, bf16[64,1024]{1,0:T(8,128)(2,1)S(1)}, u32[]{:S(2)}, u32[]{:S(2)}) collective-permute-start(bf16[64,1024]{1,0:T(8,128)(2,1)S(1)} %maximum_select_fusion.2), channel_id=1, source_target_pairs={{0,64},{16,80},{32,96},{48,112},{64,0},{80,16},{96,32},{112,48},{1... | collective-permute-start | bytes 393224 | tf_op jit(solution)/shard_map/ppermute | solution.py:133
  55.7 5.1 %collective-permute-start.8 = (f32[128,128]{1,0:T(8,128)S(1)}, f32[128,128]{1,0:T(8,128)S(1)}, u32[]{:S(2)}, u32[]{:S(2)}) collective-permute-start(f32[128,128]{1,0:T(8,128)S(1)} %add.82), channel_id=1, source_target_pairs={{0,64},{16,80},{32,96},{48,112},{64,0},{80,16},{96,32},{112,48},{1... | collective-permute-start | bytes 196616 | tf_op jit(solution)/shard_map/ppermute | solution.py:107
  57.5 56.0 %collective-permute-start.15 = (bf16[64,1024]{1,0:T(8,128)(2,1)S(1)}, bf16[64,1024]{1,0:T(8,128)(2,1)S(1)}, u32[]{:S(2)}, u32[]{:S(2)}) collective-permute-start(bf16[64,1024]{1,0:T(8,128)(2,1)S(1)} %maximum_select_fusion.3), channel_id=1, source_target_pairs={{0,64},{16,80},{32,96},{48,112},{64,0},{80,16},{96,32},{112,48},{1... | collective-permute-start | bytes 393224 | tf_op jit(solution)/shard_map/ppermute | solution.py:133
  60.8 19.1 %collective-permute-start.9 = (f32[128,128]{1,0:T(8,128)S(1)}, f32[128,128]{1,0:T(8,128)S(1)}, u32[]{:S(2)}, u32[]{:S(2)}) collective-permute-start(f32[128,128]{1,0:T(8,128)S(1)} %add.83), channel_id=1, source_target_pairs={{15,14},{31,30},{47,46},{63,62},{79,78},{95,94},{111,110},{127,126}} | collective-permute-start | bytes 196616 | tf_op jit(solution)/shard_map/ppermute | solution.py:96
  76.4 3.3 %copy-start = (f32[2048,1024]{1,0:T(8,128)}, f32[2048,1024]{1,0:T(8,128)S(1)}, u32[]{:S(2)}) copy-start(f32[2048,1024]{1,0:T(8,128)S(1)} %convolution_subtract_fusion.1) | copy-start | bytes 25165828
  79.7 15.4 %copy-start.4 = (f32[128,128]{1,0:T(8,128)S(1)}, f32[128,128]{1,0:T(8,128)}, u32[]{:S(2)}) copy-start(f32[128,128]{1,0:T(8,128)} %param.16) | copy-start | bytes 196612
  79.7 15.4 %copy-start.7 = (f32[128,128]{1,0:T(8,128)S(1)}, f32[128,128]{1,0:T(8,128)}, u32[]{:S(2)}) copy-start(f32[128,128]{1,0:T(8,128)} %param.21) | copy-start | bytes 196612
  79.7 16.3 %copy-start.12 = (f32[16,1024]{1,0:T(8,128)S(1)}, f32[16,1024]{1,0:T(8,128)}, u32[]{:S(2)}) copy-start(f32[16,1024]{1,0:T(8,128)} %param.19) | copy-start | bytes 196612
  79.9 2.0 %collective-permute-start.10 = (f32[128,128]{1,0:T(8,128)S(1)}, f32[128,128]{1,0:T(8,128)S(1)}, u32[]{:S(2)}, u32[]{:S(2)}) collective-permute-start(f32[128,128]{1,0:T(8,128)S(1)} %broadcast_select_fusion.3), channel_id=1, source_target_pairs={{15,13},{14,12},{31,29},{30,28},{47,45},{46,44},{63,61},{62,60},{7... | collective-permute-start | bytes 196616 | tf_op jit(solution)/shard_map/ppermute | solution.py:96
  80.7 3.9 %collective-permute-start.4 = (f32[2,16,1024]{2,1,0:T(8,128)S(1)}, f32[2,16,1024]{2,1,0:T(8,128)S(1)}, u32[]{:S(2)}, u32[]{:S(2)}) collective-permute-start(f32[2,16,1024]{2,1,0:T(8,128)S(1)} %slice_select_fusion.6), channel_id=1, source_target_pairs={{0,32},{16,48},{32,0},{48,16},{64,96},{80,112},{96,64},{112,80},{1... | collective-permute-start | bytes 393224 | tf_op jit(solution)/shard_map/ppermute | solution.py:123
  81.9 2.7 %collective-permute-start.11 = (f32[128,128]{1,0:T(8,128)S(1)}, f32[128,128]{1,0:T(8,128)S(1)}, u32[]{:S(2)}, u32[]{:S(2)}) collective-permute-start(f32[128,128]{1,0:T(8,128)S(1)} %broadcast_select_fusion.4), channel_id=1, source_target_pairs={{15,11},{14,10},{13,9},{12,8},{31,27},{30,26},{29,25},{28,24},{47,... | collective-permute-start | bytes 196616 | tf_op jit(solution)/shard_map/ppermute | solution.py:96
  84.6 10.5 %collective-permute-start.12 = (f32[128,128]{1,0:T(8,128)S(1)}, f32[128,128]{1,0:T(8,128)S(1)}, u32[]{:S(2)}, u32[]{:S(2)}) collective-permute-start(f32[128,128]{1,0:T(8,128)S(1)} %broadcast_select_fusion.5), channel_id=1, source_target_pairs={{15,7},{14,6},{13,5},{12,4},{11,3},{10,2},{9,1},{8,0},{31,23},{30,... | collective-permute-start | bytes 196616 | tf_op jit(solution)/shard_map/ppermute | solution.py:96
  85.9 10.1 %collective-permute-start.5 = (f32[1,16,1024]{2,1,0:T(8,128)S(1)}, f32[1,16,1024]{2,1,0:T(8,128)S(1)}, u32[]{:S(2)}, u32[]{:S(2)}) collective-permute-start(f32[1,16,1024]{2,1,0:T(8,128)S(1)} %slice_select_fusion.8), channel_id=1, source_target_pairs={{0,16},{16,0},{32,48},{48,32},{64,80},{80,64},{96,112},{112,96},{1... | collective-permute-start | bytes 196616 | tf_op jit(solution)/shard_map/ppermute | solution.py:123
  95.9 22.5 %copy-start.9 = (f32[128,128]{1,0:T(8,128)}, f32[128,128]{1,0:T(8,128)S(1)}, u32[]{:S(2)}) copy-start(f32[128,128]{1,0:T(8,128)S(1)} %get-tuple-element.14) | copy-start | bytes 196612
  98.1 20.5 %collective-permute-start.16 = (bf16[16,128]{1,0:T(8,128)(2,1)S(1)}, bf16[16,128]{1,0:T(8,128)(2,1)S(1)}, u32[]{:S(2)}, u32[]{:S(2)}) collective-permute-start(bf16[16,128]{1,0:T(8,128)(2,1)S(1)} %slice.139), channel_id=1, source_target_pairs={{14,15},{30,31},{46,47},{62,63},{78,79},{94,95},{110,111},{126,127}} | collective-permute-start | bytes 12296 | tf_op jit(solution)/shard_map/ppermute | solution.py:96
  113.4 5.0 %copy-start.3 = (bf16[2048,128]{1,0:T(8,128)(2,1)S(1)}, bf16[2048,128]{1,0:T(8,128)(2,1)}, u32[]{:S(2)}) copy-start(bf16[2048,128]{1,0:T(8,128)(2,1)} %shard_map.138) | copy-start | bytes 1572868
  113.5 5.9 %copy-start.1 = (bf16[2048,1024]{1,0:T(8,128)(2,1)S(1)}, bf16[2048,1024]{1,0:T(8,128)(2,1)}, u32[]{:S(2)}) copy-start(bf16[2048,1024]{1,0:T(8,128)(2,1)} %param.12) | copy-start | bytes 12582916
  118.7 1.9 %collective-permute-start.17 = (bf16[16,128]{1,0:T(8,128)(2,1)S(1)}, bf16[16,128]{1,0:T(8,128)(2,1)S(1)}, u32[]{:S(2)}, u32[]{:S(2)}) collective-permute-start(bf16[16,128]{1,0:T(8,128)(2,1)S(1)} %broadcast_select_fusion.6), channel_id=1, source_target_pairs={{14,12},{15,13},{30,28},{31,29},{46,44},{47,45},{62,60},{63,61},{7... | collective-permute-start | bytes 12296 | tf_op jit(solution)/shard_map/ppermute | solution.py:96
  120.6 3.3 %collective-permute-start.18 = (bf16[16,128]{1,0:T(8,128)(2,1)S(1)}, bf16[16,128]{1,0:T(8,128)(2,1)S(1)}, u32[]{:S(2)}, u32[]{:S(2)}) collective-permute-start(bf16[16,128]{1,0:T(8,128)(2,1)S(1)} %broadcast_select_fusion.7), channel_id=1, source_target_pairs={{14,10},{15,11},{12,8},{13,9},{30,26},{31,27},{28,24},{29,25},{46,... | collective-permute-start | bytes 12296 | tf_op jit(solution)/shard_map/ppermute | solution.py:96
  123.9 45.3 %copy-start.8 = (f32[128,128]{1,0:T(8,128)S(1)}, f32[128,128]{1,0:T(8,128)}, u32[]{:S(2)}) copy-start(f32[128,128]{1,0:T(8,128)} %param.20) | copy-start | bytes 196612
  123.9 46.2 %copy-start.13 = (f32[16,1024]{1,0:T(8,128)S(1)}, f32[16,1024]{1,0:T(8,128)}, u32[]{:S(2)}) copy-start(f32[16,1024]{1,0:T(8,128)} %param.18) | copy-start | bytes 196612
  123.9 8.9 %collective-permute-start.19 = (bf16[16,128]{1,0:T(8,128)(2,1)S(1)}, bf16[16,128]{1,0:T(8,128)(2,1)S(1)}, u32[]{:S(2)}, u32[]{:S(2)}) collective-permute-start(bf16[16,128]{1,0:T(8,128)(2,1)S(1)} %broadcast_select_fusion.8), channel_id=1, source_target_pairs={{14,6},{15,7},{12,4},{13,5},{10,2},{11,3},{8,0},{9,1},{30,22},{31,... | collective-permute-start | bytes 12296 | tf_op jit(solution)/shard_map/ppermute | solution.py:96
  133.0 10.9 %collective-permute-start.23 = (f32[128,128]{1,0:T(8,128)S(1)}, f32[128,128]{1,0:T(8,128)S(1)}, u32[]{:S(2)}, u32[]{:S(2)}) collective-permute-start(f32[128,128]{1,0:T(8,128)S(1)} %convolution_add_fusion.1), channel_id=1, source_target_pairs={{0,16},{16,0},{32,48},{48,32},{64,80},{80,64},{96,112},{112,96},{1... | collective-permute-start | bytes 196616 | tf_op jit(solution)/shard_map/ppermute | solution.py:107
  144.0 3.2 %collective-permute-start.24 = (f32[128,128]{1,0:T(8,128)S(1)}, f32[128,128]{1,0:T(8,128)S(1)}, u32[]{:S(2)}, u32[]{:S(2)}) collective-permute-start(f32[128,128]{1,0:T(8,128)S(1)} %add.91), channel_id=1, source_target_pairs={{0,32},{16,48},{32,0},{48,16},{64,96},{80,112},{96,64},{112,80},{1... | collective-permute-start | bytes 196616 | tf_op jit(solution)/shard_map/ppermute | solution.py:107
  147.2 4.7 %collective-permute-start.25 = (f32[128,128]{1,0:T(8,128)S(1)}, f32[128,128]{1,0:T(8,128)S(1)}, u32[]{:S(2)}, u32[]{:S(2)}) collective-permute-start(f32[128,128]{1,0:T(8,128)S(1)} %add.92), channel_id=1, source_target_pairs={{0,64},{16,80},{32,96},{48,112},{64,0},{80,16},{96,32},{112,48},{1... | collective-permute-start | bytes 196616 | tf_op jit(solution)/shard_map/ppermute | solution.py:107
  151.9 2.1 %collective-permute-start.26 = (f32[128,128]{1,0:T(8,128)S(1)}, f32[128,128]{1,0:T(8,128)S(1)}, u32[]{:S(2)}, u32[]{:S(2)}) collective-permute-start(f32[128,128]{1,0:T(8,128)S(1)} %add.93), channel_id=1, source_target_pairs={{14,15},{30,31},{46,47},{62,63},{78,79},{94,95},{110,111},{126,127}} | collective-permute-start | bytes 196616 | tf_op jit(solution)/shard_map/ppermute | solution.py:96
  152.6 6.8 %collective-permute-start.20 = (f32[4,16,1024]{2,1,0:T(8,128)S(1)}, f32[4,16,1024]{2,1,0:T(8,128)S(1)}, u32[]{:S(2)}, u32[]{:S(2)}) collective-permute-start(f32[4,16,1024]{2,1,0:T(8,128)S(1)} %bitcast.61), channel_id=1, source_target_pairs={{0,64},{16,80},{32,96},{48,112},{64,0},{80,16},{96,32},{112,48},{1... | collective-permute-start | bytes 786440 | tf_op jit(solution)/shard_map/ppermute | solution.py:123
  154.0 5.5 %collective-permute-start.27 = (f32[128,128]{1,0:T(8,128)S(1)}, f32[128,128]{1,0:T(8,128)S(1)}, u32[]{:S(2)}, u32[]{:S(2)}) collective-permute-start(f32[128,128]{1,0:T(8,128)S(1)} %broadcast_select_fusion), channel_id=1, source_target_pairs={{14,12},{15,13},{30,28},{31,29},{46,44},{47,45},{62,60},{63,61},{7... | collective-permute-start | bytes 196616 | tf_op jit(solution)/shard_map/ppermute | solution.py:96
  159.5 1.6 collective-permute-start.28
  160.2 3.9 %collective-permute-start.21 = (f32[2,16,1024]{2,1,0:T(8,128)S(1)}, f32[2,16,1024]{2,1,0:T(8,128)S(1)}, u32[]{:S(2)}, u32[]{:S(2)}) collective-permute-start(f32[2,16,1024]{2,1,0:T(8,128)S(1)} %slice_select_fusion.5), channel_id=1, source_target_pairs={{0,32},{16,48},{32,0},{48,16},{64,96},{80,112},{96,64},{112,80},{1... | collective-permute-start | bytes 393224 | tf_op jit(solution)/shard_map/ppermute | solution.py:123
  161.1 8.1 %collective-permute-start.29 = (f32[128,128]{1,0:T(8,128)S(1)}, f32[128,128]{1,0:T(8,128)S(1)}, u32[]{:S(2)}, u32[]{:S(2)}) collective-permute-start(f32[128,128]{1,0:T(8,128)S(1)} %broadcast_select_fusion.2), channel_id=1, source_target_pairs={{14,6},{15,7},{12,4},{13,5},{10,2},{11,3},{8,0},{9,1},{30,22},{31,... | collective-permute-start | bytes 196616 | tf_op jit(solution)/shard_map/ppermute | solution.py:96
  164.1 6.0 %collective-permute-start.22 = (f32[1,16,1024]{2,1,0:T(8,128)S(1)}, f32[1,16,1024]{2,1,0:T(8,128)S(1)}, u32[]{:S(2)}, u32[]{:S(2)}) collective-permute-start(f32[1,16,1024]{2,1,0:T(8,128)S(1)} %slice_select_fusion.7), channel_id=1, source_target_pairs={{0,16},{16,0},{32,48},{48,32},{64,80},{80,64},{96,112},{112,96},{1... | collective-permute-start | bytes 196616 | tf_op jit(solution)/shard_map/ppermute | solution.py:123
  170.0 1.1 copy-start.10

commit v9 on v7

--- a/solution.py
+++ b/solution.py
@@ -199,7 +199,7 @@
 
         def summed_block(partial_value, root):
             rows_sum = butterfly_sum(partial_value, "row", n_row)
-            return tree_broadcast(rows_sum, "col", n_col, root)
+            return panel_broadcast(rows_sum, n_col, root, n_col + 1 - root)
 
         inverse_two = inverse_lower(diag_two)
         solved_two = solve_panel(adj_trail[:, last:], inverse_two, root_two)

time: 170 us -> 178 us (1.047)
  Pallas kernels: 34.1 us -> 57.7 us
  starting transfers between devices: 44.5 us -> 35.6 us
  waiting for transfers between devices: 35.1 us -> 27.5 us
    pallas_call x2 -> x4, Pallas kernels: 34.1 us -> 57.7 us  [panel_broadcast(): pl.pallas_call(functools.partial(spread_kernel, root, size), out_shape=ja...]
    ppermute x6, starting transfers between devices: 15.1 us -> 7.19 us  [butterfly_sum(): value = value + lax.ppermute(value, axis, pairs)]
    ppermute x12 -> x4, starting transfers between devices: 10.1 us -> 3.4 us  [tree_broadcast(): arrived = lax.ppermute(value, axis, pairs)]
    ppermute x12 -> x4, waiting for transfers between devices: 12.2 us -> 6.51 us  [tree_broadcast(): arrived = lax.ppermute(value, axis, pairs)]
    ppermute x6, waiting for transfers between devices: 10 us -> 6.46 us  [halving_scatter(): blocks = keep + lax.ppermute(send, axis, pairs)]
    ppermute x6, starting transfers between devices: 5.96 us -> 9.34 us  [doubling_gather(): other = lax.ppermute(value, axis, pairs)]
    ppermute x6, starting transfers between devices: 13.3 us -> 15.7 us  [halving_scatter(): blocks = keep + lax.ppermute(send, axis, pairs)]
  transfers between devices with their start and end apart: 30 -> 22, of which waited for: 11 -> 10; matrix products, arithmetic and copies ran while one was open for 19% -> 19% of each run, Pallas kernels for 9% -> 22%
where the time goes in v9:
time: 178 us; the launch traced here: 177 us
  Pallas kernels  57.7 us (32%)
  starting transfers between devices  35.6 us (20%)
  waiting for transfers between devices  27.5 us (15%)
  other arithmetic  26.3 us (15%)
  matrix products  24.1 us (14%)
  local copies, waits for them, and re-layouts  4.95 us (3%)
    pallas_call x4, Pallas kernels, panel_broadcast(): pl.pallas_call(functools.partial(spread_kernel, root, size), out_shape=ja...  57.7 us
    another operation x4, other arithmetic, inverse_lower(): return lax.linalg.triangular_solve(block, ident, left_side=True, lower=True)  20.5 us
    ppermute x6, starting transfers between devices, halving_scatter(): blocks = keep + lax.ppermute(send, axis, pairs)  15.7 us
    ppermute x6, waiting for transfers between devices, butterfly_sum(): value = value + lax.ppermute(value, axis, pairs)  12.9 us
    ppermute x6, starting transfers between devices, doubling_gather(): other = lax.ppermute(value, axis, pairs)  9.34 us
    ppermute x6, starting transfers between devices, butterfly_sum(): value = value + lax.ppermute(value, axis, pairs)  7.19 us
    ppermute x4, waiting for transfers between devices, tree_broadcast(): arrived = lax.ppermute(value, axis, pairs)  6.51 us
    ppermute x6, waiting for transfers between devices, halving_scatter(): blocks = keep + lax.ppermute(send, axis, pairs)  6.46 us
  transfers between devices with their start and end apart: 22, of which 10 were waited for; matrix products, arithmetic and copies ran while one was open for 19% of the time, Pallas kernels for 22%

profile of v9, /device:TPU:1, one launch (start us, length us, event | category | flops | bytes accessed | tf_op | source)
XLA Modules:
  0.0 177.5 jit_solution(17406749060265384709)
XLA Ops:
  0.7 0.9 select_bitcast_fusion.1
  1.5 9.8 %custom-call.4 = f32[1,128,128]{1,2,0:T(8,128)S(1)} custom-call(f32[1,128,128]{2,1,0:T(8,128)S(1)} %select_bitcast_fusion.1), custom_call_target="InvertDiagBlocksLowerTriangular" | custom-call | tf_op jit(solution)/shard_map/triangular_solve/custom-call.1 | solution.py:154
  11.3 0.3 fusion.15
  11.6 3.0 %fusion.x_ref = bf16[2048,128]{1,0:T(8,128)(2,1)} fusion(f32[128,128]{1,0:T(8,128)S(1)} %fusion.15, f32[2048,1024]{1,0:T(8,128)} %param.17), kind=kOutput, calls=%fused_computation.6 | convolution fusion | flops 402915328 | bytes 1638400 | tf_op jit(solution)/shard_map/dot_general | solution.py:193
  14.6 19.2 %shard_map.137 = bf16[2048,128]{1,0:T(8,128)(2,1)} custom-call(bf16[2048,128]{1,0:T(8,128)(2,1)} %fusion.x_ref), custom_call_target="tpu_custom_call" | custom-call | tf_op jit(solution)/shard_map/pallas_call | solution.py:77
  33.9 3.1 %fusion.46 = f32[128,1024]{1,0:T(8,128)S(1)} fusion(bf16[2048,128]{1,0:T(8,128)(2,1)} %shard_map.137, bf16[2048,1024]{1,0:T(8,128)(2,1)} %param.12), kind=kOutput, calls=%fused_computation.93 | convolution fusion | flops 536870912 | bytes 5242880 | tf_op jit(solution)/shard_map/dot_general | solution.py:213
  37.1 2.8 %collective-permute-start.3 = (f32[4,16,1024]{2,1,0:T(8,128)S(1)}, f32[4,16,1024]{2,1,0:T(8,128)S(1)}, u32[]{:S(2)}, u32[]{:S(2)}) collective-permute-start(f32[4,16,1024]{2,1,0:T(8,128)S(1)} %bitcast.60), channel_id=1, source_target_pairs={{0,64},{16,80},{32,96},{48,112},{64,0},{80,16},{96,32},{112,48},{1... | collective-permute-start | bytes 786440 | tf_op jit(solution)/shard_map/ppermute | solution.py:123
  39.9 3.6 %collective-permute-start = (bf16[16,1024]{1,0:T(8,128)(2,1)S(1)}, bf16[16,1024]{1,0:T(8,128)(2,1)S(1)}, u32[]{:S(2)}, u32[]{:S(2)}) collective-permute-start(bf16[16,1024]{1,0:T(8,128)(2,1)S(1)} %copy-done.6), channel_id=1, source_target_pairs={{0,16},{16,0},{32,48},{48,32},{64,80},{80,64},{96,112},{112,96},{1... | collective-permute-start | bytes 98312 | tf_op jit(solution)/shard_map/ppermute | solution.py:133
  43.5 1.4 fusion.11
  45.0 0.5 collective-permute-start.9
  45.5 9.8 %custom-call.5 = f32[1,128,128]{1,2,0:T(8,128)S(1)} custom-call(f32[1,128,128]{2,1,0:T(8,128)S(1)} %select_bitcast_fusion), custom_call_target="InvertDiagBlocksLowerTriangular" | custom-call | tf_op jit(solution)/shard_map/triangular_solve/custom-call.1 | solution.py:154
  55.3 0.3 fusion.13
  55.7 0.4 collective-permute-start.1
  56.2 1.2 collective-permute-start.10
  57.4 0.4 collective-permute-start.7
  57.8 1.7 collective-permute-done.1
  59.5 0.8 collective-permute-start.2
  60.3 1.9 %collective-permute-done.7 = f32[128,128]{1,0:T(8,128)S(1)} collective-permute-done((f32[128,128]{1,0:T(8,128)S(1)}, f32[128,128]{1,0:T(8,128)S(1)}, u32[]{:S(2)}, u32[]{:S(2)}) %collective-permute-start.7) | collective-permute-done | bytes 65568 | tf_op jit(solution)/shard_map/ppermute | solution.py:107
  62.3 0.5 collective-permute-start.8
  62.8 2.8 %collective-permute-start.11 = (bf16[64,1024]{1,0:T(8,128)(2,1)S(1)}, bf16[64,1024]{1,0:T(8,128)(2,1)S(1)}, u32[]{:S(2)}, u32[]{:S(2)}) collective-permute-start(bf16[64,1024]{1,0:T(8,128)(2,1)S(1)} %maximum_select_fusion.3), channel_id=1, source_target_pairs={{0,64},{16,80},{32,96},{48,112},{64,0},{80,16},{96,32},{112,48},{1... | collective-permute-start | bytes 393224 | tf_op jit(solution)/shard_map/ppermute | solution.py:133
  65.6 1.8 %collective-permute-done.8 = f32[128,128]{1,0:T(8,128)S(1)} collective-permute-done((f32[128,128]{1,0:T(8,128)S(1)}, f32[128,128]{1,0:T(8,128)S(1)}, u32[]{:S(2)}, u32[]{:S(2)}) %collective-permute-start.8) | collective-permute-done | bytes 65568 | tf_op jit(solution)/shard_map/ppermute | solution.py:107
  67.4 0.6 add.83.x_ref
  68.0 11.4 %shard_map.138 = f32[128,128]{1,0:T(8,128)} custom-call(f32[128,128]{1,0:T(8,128)} %add.83.x_ref), custom_call_target="tpu_custom_call" | custom-call | tf_op jit(solution)/shard_map/pallas_call | solution.py:77
  79.5 1.1 fusion.2
  80.6 0.3 fusion.47
  81.1 0.2 fusion.29
  81.4 3.5 %collective-permute-done.4 = f32[2,16,1024]{2,1,0:T(8,128)S(1)} collective-permute-done((f32[2,16,1024]{2,1,0:T(8,128)S(1)}, f32[2,16,1024]{2,1,0:T(8,128)S(1)}, u32[]{:S(2)}, u32[]{:S(2)}) %collective-permute-start.4) | collective-permute-done | bytes 131104 | tf_op jit(solution)/shard_map/ppermute | solution.py:123
  84.9 6.0 %collective-permute-start.5 = (f32[1,16,1024]{2,1,0:T(8,128)S(1)}, f32[1,16,1024]{2,1,0:T(8,128)S(1)}, u32[]{:S(2)}, u32[]{:S(2)}) collective-permute-start(f32[1,16,1024]{2,1,0:T(8,128)S(1)} %slice_select_fusion.8), channel_id=1, source_target_pairs={{0,16},{16,0},{32,48},{48,32},{64,80},{80,64},{96,112},{112,96},{1... | collective-permute-start | bytes 196616 | tf_op jit(solution)/shard_map/ppermute | solution.py:123
  91.0 4.6 %convolution_subtract_fusion.1 = f32[2048,1024]{1,0:T(8,128)S(1)} fusion(f32[2048,1024]{1,0:T(8,128)} %param.17, bf16[2048,128]{1,0:T(8,128)(2,1)S(1)} %copy-done.2, bf16[64,1024]{1,0:T(8,128)(2,1)S(1)} %maximum_select_fusion.2, bf16[64,1024]{1,0:T(8,128)(2,1)S(1)} %collective-permute-done.2, pred[]{:T(512)S(6)} %eq.62), kind=kOutput, calls=%fused_computation.2 | convolution fusion | flops 540147712 | bytes 17563648 | tf_op jit(solution)/shard_map/dot_general | solution.py:216
  95.6 3.3 %copy-done = f32[2048,1024]{1,0:T(8,128)} copy-done((f32[2048,1024]{1,0:T(8,128)}, f32[2048,1024]{1,0:T(8,128)S(1)}, u32[]{:S(2)}) %copy-start) | copy-done | bytes 8388632
  99.1 0.3 fusion.19
  99.3 1.0 convolution_convert_fusion
  100.3 0.8 slice.136.x_ref
  101.2 0.6 collective-permute-start.12
  101.8 16.4 %shard_map.139 = bf16[2048,128]{1,0:T(8,128)(2,1)} custom-call(bf16[2048,128]{1,0:T(8,128)(2,1)} %slice.136.x_ref), custom_call_target="tpu_custom_call" | custom-call | tf_op jit(solution)/shard_map/pallas_call | solution.py:77
  118.3 4.9 %convolution_subtract_fusion = bf16[2048,1024]{1,0:T(8,128)(2,1)S(1)} fusion(f32[2048,1024]{1,0:T(8,128)} %copy-done, bf16[2048,128]{1,0:T(8,128)(2,1)} %shard_map.139, bf16[64,1024]{1,0:T(8,128)(2,1)S(1)} %maximum_select_fusion.3, bf16[64,1024]{1,0:T(8,128)(2,1)S(1)} %collective-permute-done.11, pred[]{:T(512)S(6)} %eq.62), kind=kOutput, calls=%fused_computation.1 | convolution fusion | flops 542244864 | bytes 13369345 | tf_op jit(solution)/shard_map/dot_general | solution.py:230
  123.3 0.2 fusion.7
  123.5 0.7 collective-permute-start.13
  124.2 0.7 fusion.48
  124.9 0.4 slice.193
  125.4 0.7 collective-permute-start.14
  126.1 2.6 %pad_maximum_fusion = bf16[2048,1024]{1,0:T(8,128)(2,1)} fusion(bf16[2048,128]{1,0:T(8,128)(2,1)S(1)} %fusion.7, bf16[2048,896]{1,0:T(8,128)(2,1)S(1)} %slice.193), kind=kLoop, calls=%fused_computation.3 | loop fusion | flops 8388608 | bytes 8388608 | tf_op jit(solution)/shard_map/concatenate | solution.py:243
  128.7 1.4 collective-permute-start.15
  130.2 0.3 fusion.9
  130.5 6.5 %collective-permute-done.15 = bf16[16,128]{1,0:T(8,128)(2,1)S(1)} collective-permute-done((bf16[16,128]{1,0:T(8,128)(2,1)S(1)}, bf16[16,128]{1,0:T(8,128)(2,1)S(1)}, u32[]{:S(2)}, u32[]{:S(2)}) %collective-permute-start.15) | collective-permute-done | bytes 4128 | tf_op jit(solution)/shard_map/ppermute | solution.py:96
  137.2 5.8 %collective-permute-start.19 = (f32[128,128]{1,0:T(8,128)S(1)}, f32[128,128]{1,0:T(8,128)S(1)}, u32[]{:S(2)}, u32[]{:S(2)}) collective-permute-start(f32[128,128]{1,0:T(8,128)S(1)} %convolution_add_fusion.1), channel_id=1, source_target_pairs={{0,16},{16,0},{32,48},{48,32},{64,80},{80,64},{96,112},{112,96},{1... | collective-permute-start | bytes 196616 | tf_op jit(solution)/shard_map/ppermute | solution.py:107
  143.0 0.2 convolution_add_fusion
  143.5 0.4 collective-permute-done.19
  143.9 0.3 collective-permute-start.20
  144.3 1.0 collective-permute-start.16
  145.3 2.0 %collective-permute-done.20 = f32[128,128]{1,0:T(8,128)S(1)} collective-permute-done((f32[128,128]{1,0:T(8,128)S(1)}, f32[128,128]{1,0:T(8,128)S(1)}, u32[]{:S(2)}, u32[]{:S(2)}) %collective-permute-start.20) | collective-permute-done | bytes 65568 | tf_op jit(solution)/shard_map/ppermute | solution.py:107
  147.5 0.6 pad_maximum_fusion.2
  148.1 6.7 %collective-permute-done.21 = f32[128,128]{1,0:T(8,128)S(1)} collective-permute-done((f32[128,128]{1,0:T(8,128)S(1)}, f32[128,128]{1,0:T(8,128)S(1)}, u32[]{:S(2)}, u32[]{:S(2)}) %collective-permute-start.21) | collective-permute-done | bytes 65568 | tf_op jit(solution)/shard_map/ppermute | solution.py:107
  154.8 0.6 add.93.x_ref
  155.4 10.6 %shard_map.140 = f32[128,128]{1,0:T(8,128)} custom-call(f32[128,128]{1,0:T(8,128)} %add.93.x_ref), custom_call_target="tpu_custom_call" | custom-call | tf_op jit(solution)/shard_map/pallas_call | solution.py:77
  166.0 1.1 fusion.1
  167.3 1.2 collective-permute-start.17
  168.5 0.3 fusion.49
  168.8 2.4 %collective-permute-done.17 = f32[2,16,1024]{2,1,0:T(8,128)S(1)} collective-permute-done((f32[2,16,1024]{2,1,0:T(8,128)S(1)}, f32[2,16,1024]{2,1,0:T(8,128)S(1)}, u32[]{:S(2)}, u32[]{:S(2)}) %collective-permute-start.17) | collective-permute-done | bytes 131104 | tf_op jit(solution)/shard_map/ppermute | solution.py:123
  171.2 4.4 %collective-permute-start.18 = (f32[1,16,1024]{2,1,0:T(8,128)S(1)}, f32[1,16,1024]{2,1,0:T(8,128)S(1)}, u32[]{:S(2)}, u32[]{:S(2)}) collective-permute-start(f32[1,16,1024]{2,1,0:T(8,128)S(1)} %slice_select_fusion.7), channel_id=1, source_target_pairs={{0,16},{16,0},{32,48},{48,32},{64,80},{80,64},{96,112},{112,96},{1... | collective-permute-start | bytes 196616 | tf_op jit(solution)/shard_map/ppermute | solution.py:123
  175.6 0.2 fusion.28
  176.0 0.6 collective-permute-done.18
  176.6 0.2 fusion.17
  176.8 0.6 pad_maximum_fusion.1
  (77 shorter events, 1.5 us)
Async XLA Ops:
  11.6 28.3 %copy-start.6 = (bf16[16,1024]{1,0:T(8,128)(2,1)S(1)}, bf16[16,1024]{1,0:T(8,128)(2,1)}, u32[]{:S(2)}) copy-start(bf16[16,1024]{1,0:T(8,128)(2,1)} %param.14) | copy-start | bytes 98308
  14.6 30.3 %copy-start.11 = (bf16[16,1024]{1,0:T(8,128)(2,1)S(1)}, bf16[16,1024]{1,0:T(8,128)(2,1)}, u32[]{:S(2)}) copy-start(bf16[16,1024]{1,0:T(8,128)(2,1)} %param.13) | copy-start | bytes 98308
  14.6 30.8 %copy-start.5 = (f32[128,128]{1,0:T(8,128)S(1)}, f32[128,128]{1,0:T(8,128)}, u32[]{:S(2)}) copy-start(f32[128,128]{1,0:T(8,128)} %param.15) | copy-start | bytes 196612
  33.9 9.6 %copy-start.2 = (bf16[2048,128]{1,0:T(8,128)(2,1)S(1)}, bf16[2048,128]{1,0:T(8,128)(2,1)}, u32[]{:S(2)}) copy-start(bf16[2048,128]{1,0:T(8,128)(2,1)} %shard_map.137) | copy-start | bytes 1572868
  33.9 45.6 %copy-start.4 = (f32[128,128]{1,0:T(8,128)S(1)}, f32[128,128]{1,0:T(8,128)}, u32[]{:S(2)}) copy-start(f32[128,128]{1,0:T(8,128)} %param.16) | copy-start | bytes 196612
  33.9 45.6 %copy-start.7 = (f32[128,128]{1,0:T(8,128)S(1)}, f32[128,128]{1,0:T(8,128)}, u32[]{:S(2)}) copy-start(f32[128,128]{1,0:T(8,128)} %param.21) | copy-start | bytes 196612
  37.1 43.8 %collective-permute-start.3 = (f32[4,16,1024]{2,1,0:T(8,128)S(1)}, f32[4,16,1024]{2,1,0:T(8,128)S(1)}, u32[]{:S(2)}, u32[]{:S(2)}) collective-permute-start(f32[4,16,1024]{2,1,0:T(8,128)S(1)} %bitcast.60), channel_id=1, source_target_pairs={{0,64},{16,80},{32,96},{48,112},{64,0},{80,16},{96,32},{112,48},{1... | collective-permute-start | bytes 786440 | tf_op jit(solution)/shard_map/ppermute | solution.py:123
  39.9 15.8 %collective-permute-start = (bf16[16,1024]{1,0:T(8,128)(2,1)S(1)}, bf16[16,1024]{1,0:T(8,128)(2,1)S(1)}, u32[]{:S(2)}, u32[]{:S(2)}) collective-permute-start(bf16[16,1024]{1,0:T(8,128)(2,1)S(1)} %copy-done.6), channel_id=1, source_target_pairs={{0,16},{16,0},{32,48},{48,32},{64,80},{80,64},{96,112},{112,96},{1... | collective-permute-start | bytes 98312 | tf_op jit(solution)/shard_map/ppermute | solution.py:133
  44.9 12.5 %collective-permute-start.6 = (f32[128,128]{1,0:T(8,128)S(1)}, f32[128,128]{1,0:T(8,128)S(1)}, u32[]{:S(2)}, u32[]{:S(2)}) collective-permute-start(f32[128,128]{1,0:T(8,128)S(1)} %fusion.11), channel_id=1, source_target_pairs={{0,16},{16,0},{32,48},{48,32},{64,80},{80,64},{96,112},{112,96},{1... | collective-permute-start | bytes 196616 | tf_op jit(solution)/shard_map/ppermute | solution.py:107
  45.0 11.2 %collective-permute-start.9 = (bf16[16,1024]{1,0:T(8,128)(2,1)S(1)}, bf16[16,1024]{1,0:T(8,128)(2,1)S(1)}, u32[]{:S(2)}, u32[]{:S(2)}) collective-permute-start(bf16[16,1024]{1,0:T(8,128)(2,1)S(1)} %copy-done.11), channel_id=1, source_target_pairs={{0,16},{16,0},{32,48},{48,32},{64,80},{80,64},{96,112},{112,96},{1... | collective-permute-start | bytes 98312 | tf_op jit(solution)/shard_map/ppermute | solution.py:133
  55.7 3.7 %collective-permute-start.1 = (bf16[32,1024]{1,0:T(8,128)(2,1)S(1)}, bf16[32,1024]{1,0:T(8,128)(2,1)S(1)}, u32[]{:S(2)}, u32[]{:S(2)}) collective-permute-start(bf16[32,1024]{1,0:T(8,128)(2,1)S(1)} %maximum_select_fusion.4), channel_id=1, source_target_pairs={{0,32},{16,48},{32,0},{48,16},{64,96},{80,112},{96,64},{112,80},{1... | collective-permute-start | bytes 196616 | tf_op jit(solution)/shard_map/ppermute | solution.py:133
  56.2 6.6 %collective-permute-start.10 = (bf16[32,1024]{1,0:T(8,128)(2,1)S(1)}, bf16[32,1024]{1,0:T(8,128)(2,1)S(1)}, u32[]{:S(2)}, u32[]{:S(2)}) collective-permute-start(bf16[32,1024]{1,0:T(8,128)(2,1)S(1)} %maximum_select_fusion.5), channel_id=1, source_target_pairs={{0,32},{16,48},{32,0},{48,16},{64,96},{80,112},{96,64},{112,80},{1... | collective-permute-start | bytes 196616 | tf_op jit(solution)/shard_map/ppermute | solution.py:133
  57.4 4.9 %collective-permute-start.7 = (f32[128,128]{1,0:T(8,128)S(1)}, f32[128,128]{1,0:T(8,128)S(1)}, u32[]{:S(2)}, u32[]{:S(2)}) collective-permute-start(f32[128,128]{1,0:T(8,128)S(1)} %add.81), channel_id=1, source_target_pairs={{0,32},{16,48},{32,0},{48,16},{64,96},{80,112},{96,64},{112,80},{1... | collective-permute-start | bytes 196616 | tf_op jit(solution)/shard_map/ppermute | solution.py:107
  59.5 31.5 %collective-permute-start.2 = (bf16[64,1024]{1,0:T(8,128)(2,1)S(1)}, bf16[64,1024]{1,0:T(8,128)(2,1)S(1)}, u32[]{:S(2)}, u32[]{:S(2)}) collective-permute-start(bf16[64,1024]{1,0:T(8,128)(2,1)S(1)} %maximum_select_fusion.2), channel_id=1, source_target_pairs={{0,64},{16,80},{32,96},{48,112},{64,0},{80,16},{96,32},{112,48},{1... | collective-permute-start | bytes 393224 | tf_op jit(solution)/shard_map/ppermute | solution.py:133
  62.3 5.1 %collective-permute-start.8 = (f32[128,128]{1,0:T(8,128)S(1)}, f32[128,128]{1,0:T(8,128)S(1)}, u32[]{:S(2)}, u32[]{:S(2)}) collective-permute-start(f32[128,128]{1,0:T(8,128)S(1)} %add.82), channel_id=1, source_target_pairs={{0,64},{16,80},{32,96},{48,112},{64,0},{80,16},{96,32},{112,48},{1... | collective-permute-start | bytes 196616 | tf_op jit(solution)/shard_map/ppermute | solution.py:107
  62.8 55.5 %collective-permute-start.11 = (bf16[64,1024]{1,0:T(8,128)(2,1)S(1)}, bf16[64,1024]{1,0:T(8,128)(2,1)S(1)}, u32[]{:S(2)}, u32[]{:S(2)}) collective-permute-start(bf16[64,1024]{1,0:T(8,128)(2,1)S(1)} %maximum_select_fusion.3), channel_id=1, source_target_pairs={{0,64},{16,80},{32,96},{48,112},{64,0},{80,16},{96,32},{112,48},{1... | collective-permute-start | bytes 393224 | tf_op jit(solution)/shard_map/ppermute | solution.py:133
  81.0 3.9 %collective-permute-start.4 = (f32[2,16,1024]{2,1,0:T(8,128)S(1)}, f32[2,16,1024]{2,1,0:T(8,128)S(1)}, u32[]{:S(2)}, u32[]{:S(2)}) collective-permute-start(f32[2,16,1024]{2,1,0:T(8,128)S(1)} %slice_select_fusion.6), channel_id=1, source_target_pairs={{0,32},{16,48},{32,0},{48,16},{64,96},{80,112},{96,64},{112,80},{1... | collective-permute-start | bytes 393224 | tf_op jit(solution)/shard_map/ppermute | solution.py:123
  81.3 17.8 %copy-start.9 = (f32[128,128]{1,0:T(8,128)}, f32[128,128]{1,0:T(8,128)S(1)}, u32[]{:S(2)}) copy-start(f32[128,128]{1,0:T(8,128)S(1)} %get-tuple-element.10) | copy-start | bytes 196612
  84.9 14.2 %copy-start.12 = (f32[16,1024]{1,0:T(8,128)S(1)}, f32[16,1024]{1,0:T(8,128)}, u32[]{:S(2)}) copy-start(f32[16,1024]{1,0:T(8,128)} %param.19) | copy-start | bytes 196612
  84.9 14.1 %collective-permute-start.5 = (f32[1,16,1024]{2,1,0:T(8,128)S(1)}, f32[1,16,1024]{2,1,0:T(8,128)S(1)}, u32[]{:S(2)}, u32[]{:S(2)}) collective-permute-start(f32[1,16,1024]{2,1,0:T(8,128)S(1)} %slice_select_fusion.8), channel_id=1, source_target_pairs={{0,16},{16,0},{32,48},{48,32},{64,80},{80,64},{96,112},{112,96},{1... | collective-permute-start | bytes 196616 | tf_op jit(solution)/shard_map/ppermute | solution.py:123
  95.6 3.3 %copy-start = (f32[2048,1024]{1,0:T(8,128)}, f32[2048,1024]{1,0:T(8,128)S(1)}, u32[]{:S(2)}) copy-start(f32[2048,1024]{1,0:T(8,128)S(1)} %convolution_subtract_fusion.1) | copy-start | bytes 25165828
  101.2 22.3 %collective-permute-start.12 = (bf16[16,128]{1,0:T(8,128)(2,1)S(1)}, bf16[16,128]{1,0:T(8,128)(2,1)S(1)}, u32[]{:S(2)}, u32[]{:S(2)}) collective-permute-start(bf16[16,128]{1,0:T(8,128)(2,1)S(1)} %slice.139), channel_id=1, source_target_pairs={{14,15},{30,31},{46,47},{62,63},{78,79},{94,95},{110,111},{126,127}} | collective-permute-start | bytes 12296 | tf_op jit(solution)/shard_map/ppermute | solution.py:96
  118.3 5.0 %copy-start.3 = (bf16[2048,128]{1,0:T(8,128)(2,1)S(1)}, bf16[2048,128]{1,0:T(8,128)(2,1)}, u32[]{:S(2)}) copy-start(bf16[2048,128]{1,0:T(8,128)(2,1)} %shard_map.139) | copy-start | bytes 1572868
  118.3 5.9 %copy-start.1 = (bf16[2048,1024]{1,0:T(8,128)(2,1)S(1)}, bf16[2048,1024]{1,0:T(8,128)(2,1)}, u32[]{:S(2)}) copy-start(bf16[2048,1024]{1,0:T(8,128)(2,1)} %param.12) | copy-start | bytes 12582916
  123.5 1.9 %collective-permute-start.13 = (bf16[16,128]{1,0:T(8,128)(2,1)S(1)}, bf16[16,128]{1,0:T(8,128)(2,1)S(1)}, u32[]{:S(2)}, u32[]{:S(2)}) collective-permute-start(bf16[16,128]{1,0:T(8,128)(2,1)S(1)} %broadcast_select_fusion), channel_id=1, source_target_pairs={{14,12},{15,13},{30,28},{31,29},{46,44},{47,45},{62,60},{63,61},{7... | collective-permute-start | bytes 12296 | tf_op jit(solution)/shard_map/ppermute | solution.py:96
  125.4 3.3 %collective-permute-start.14 = (bf16[16,128]{1,0:T(8,128)(2,1)S(1)}, bf16[16,128]{1,0:T(8,128)(2,1)S(1)}, u32[]{:S(2)}, u32[]{:S(2)}) collective-permute-start(bf16[16,128]{1,0:T(8,128)(2,1)S(1)} %broadcast_select_fusion.1), channel_id=1, source_target_pairs={{14,10},{15,11},{12,8},{13,9},{30,26},{31,27},{28,24},{29,25},{46,... | collective-permute-start | bytes 12296 | tf_op jit(solution)/shard_map/ppermute | solution.py:96
  128.7 37.3 %copy-start.8 = (f32[128,128]{1,0:T(8,128)S(1)}, f32[128,128]{1,0:T(8,128)}, u32[]{:S(2)}) copy-start(f32[128,128]{1,0:T(8,128)} %param.20) | copy-start | bytes 196612
  128.7 47.8 %copy-start.13 = (f32[16,1024]{1,0:T(8,128)S(1)}, f32[16,1024]{1,0:T(8,128)}, u32[]{:S(2)}) copy-start(f32[16,1024]{1,0:T(8,128)} %param.18) | copy-start | bytes 196612
  128.7 8.3 %collective-permute-start.15 = (bf16[16,128]{1,0:T(8,128)(2,1)S(1)}, bf16[16,128]{1,0:T(8,128)(2,1)S(1)}, u32[]{:S(2)}, u32[]{:S(2)}) collective-permute-start(bf16[16,128]{1,0:T(8,128)(2,1)S(1)} %broadcast_select_fusion.2), channel_id=1, source_target_pairs={{14,6},{15,7},{12,4},{13,5},{10,2},{11,3},{8,0},{9,1},{30,22},{31,... | collective-permute-start | bytes 12296 | tf_op jit(solution)/shard_map/ppermute | solution.py:96
  137.2 6.7 %collective-permute-start.19 = (f32[128,128]{1,0:T(8,128)S(1)}, f32[128,128]{1,0:T(8,128)S(1)}, u32[]{:S(2)}, u32[]{:S(2)}) collective-permute-start(f32[128,128]{1,0:T(8,128)S(1)} %convolution_add_fusion.1), channel_id=1, source_target_pairs={{0,16},{16,0},{32,48},{48,32},{64,80},{80,64},{96,112},{112,96},{1... | collective-permute-start | bytes 196616 | tf_op jit(solution)/shard_map/ppermute | solution.py:107
  143.9 3.4 %collective-permute-start.20 = (f32[128,128]{1,0:T(8,128)S(1)}, f32[128,128]{1,0:T(8,128)S(1)}, u32[]{:S(2)}, u32[]{:S(2)}) collective-permute-start(f32[128,128]{1,0:T(8,128)S(1)} %add.91), channel_id=1, source_target_pairs={{0,32},{16,48},{32,0},{48,16},{64,96},{80,112},{96,64},{112,80},{1... | collective-permute-start | bytes 196616 | tf_op jit(solution)/shard_map/ppermute | solution.py:107
  144.3 22.9 %collective-permute-start.16 = (f32[4,16,1024]{2,1,0:T(8,128)S(1)}, f32[4,16,1024]{2,1,0:T(8,128)S(1)}, u32[]{:S(2)}, u32[]{:S(2)}) collective-permute-start(f32[4,16,1024]{2,1,0:T(8,128)S(1)} %bitcast.61), channel_id=1, source_target_pairs={{0,64},{16,80},{32,96},{48,112},{64,0},{80,16},{96,32},{112,48},{1... | collective-permute-start | bytes 786440 | tf_op jit(solution)/shard_map/ppermute | solution.py:123
  147.4 7.4 %collective-permute-start.21 = (f32[128,128]{1,0:T(8,128)S(1)}, f32[128,128]{1,0:T(8,128)S(1)}, u32[]{:S(2)}, u32[]{:S(2)}) collective-permute-start(f32[128,128]{1,0:T(8,128)S(1)} %add.92), channel_id=1, source_target_pairs={{0,64},{16,80},{32,96},{48,112},{64,0},{80,16},{96,32},{112,48},{1... | collective-permute-start | bytes 196616 | tf_op jit(solution)/shard_map/ppermute | solution.py:107
  167.3 3.9 %collective-permute-start.17 = (f32[2,16,1024]{2,1,0:T(8,128)S(1)}, f32[2,16,1024]{2,1,0:T(8,128)S(1)}, u32[]{:S(2)}, u32[]{:S(2)}) collective-permute-start(f32[2,16,1024]{2,1,0:T(8,128)S(1)} %slice_select_fusion.5), channel_id=1, source_target_pairs={{0,32},{16,48},{32,0},{48,16},{64,96},{80,112},{96,64},{112,80},{1... | collective-permute-start | bytes 393224 | tf_op jit(solution)/shard_map/ppermute | solution.py:123
  171.2 5.4 %collective-permute-start.18 = (f32[1,16,1024]{2,1,0:T(8,128)S(1)}, f32[1,16,1024]{2,1,0:T(8,128)S(1)}, u32[]{:S(2)}, u32[]{:S(2)}) collective-permute-start(f32[1,16,1024]{2,1,0:T(8,128)S(1)} %slice_select_fusion.7), channel_id=1, source_target_pairs={{0,16},{16,0},{32,48},{48,32},{64,80},{80,64},{96,112},{112,96},{1... | collective-permute-start | bytes 196616 | tf_op jit(solution)/shard_map/ppermute | solution.py:123
  175.9 1.6 copy-start.10

commit v10 on v7

--- a/solution.py
+++ b/solution.py
@@ -90,13 +90,17 @@
 
 def tree_broadcast(value, axis, size, root):
     here = lax.axis_index(axis) ^ root
-    step = 1
-    while step < size:
-        pairs = [(root ^ d, root ^ (d + step)) for d in range(step)]
-        arrived = lax.ppermute(value, axis, pairs)
-        take = (here >= step) & (here < 2 * step)
+    span = 1
+    while span < size:
+        radix = min(4, size // span)
+        arrived = None
+        for digit in range(1, radix):
+            pairs = [(root ^ d, root ^ (d + digit * span)) for d in range(span)]
+            part = lax.ppermute(value, axis, pairs)
+            arrived = part if arrived is None else arrived + part
+        take = (here >= span) & (here < radix * span)
         value = jnp.where(take, arrived, value)
-        step *= 2
+        span *= radix
     return value
 
 

time: 170 us -> 170 us (level)
  waiting for transfers between devices: 35.1 us -> 27.6 us
  Pallas kernels: 34.1 us -> 40.4 us
  matrix products: 22.5 us -> 25.6 us
    ppermute x6, waiting for transfers between devices: 10 us -> 1.18 us  [halving_scatter(): blocks = keep + lax.ppermute(send, axis, pairs)]
    ppermute x6, starting transfers between devices: 15.1 us -> 8.43 us  [butterfly_sum(): value = value + lax.ppermute(value, axis, pairs)]
    pallas_call x2, Pallas kernels: 34.1 us -> 40.4 us  [panel_broadcast(): pl.pallas_call(functools.partial(spread_kernel, root, size), out_shape=ja...]
    ppermute x12 -> x18, starting transfers between devices: 10.1 us -> 14.3 us  [tree_broadcast(): part = lax.ppermute(value, axis, pairs)]
    ppermute x12 -> x18, waiting for transfers between devices: 12.2 us -> 16 us  [tree_broadcast(): part = lax.ppermute(value, axis, pairs)]
    ppermute x6, waiting for transfers between devices: 11.7 us -> 9.27 us  [butterfly_sum(): value = value + lax.ppermute(value, axis, pairs)]
    dot_general x1, matrix products: 0.73 us -> 3.13 us  [per_device(): jnp.dot(tail_rows.T, trail, preferred_element_type=jnp.float32)]
    ppermute x6, starting transfers between devices: 13.3 us -> 15.5 us  [halving_scatter(): blocks = keep + lax.ppermute(send, axis, pairs)]
  transfers between devices with their start and end apart: 30 -> 36, of which waited for: 11 -> 11; matrix products, arithmetic and copies ran while one was open for 19% -> 21% of each run, Pallas kernels for 9% -> 12%
where the time goes in v10:
time: 170 us; the launch traced here: 169 us
  starting transfers between devices  44.2 us (26%)
  Pallas kernels  40.4 us (24%)
  waiting for transfers between devices  27.6 us (16%)
  matrix products  25.6 us (15%)
  other arithmetic  25.1 us (15%)
  local copies, waits for them, and re-layouts  4.95 us (3%)
    pallas_call x2, Pallas kernels, panel_broadcast(): pl.pallas_call(functools.partial(spread_kernel, root, size), out_shape=ja...  40.4 us
    another operation x4, other arithmetic, inverse_lower(): return lax.linalg.triangular_solve(block, ident, left_side=True, lower=True)  20.5 us
    ppermute x18, waiting for transfers between devices, tree_broadcast(): part = lax.ppermute(value, axis, pairs)  16 us
    ppermute x6, starting transfers between devices, halving_scatter(): blocks = keep + lax.ppermute(send, axis, pairs)  15.5 us
    ppermute x18, starting transfers between devices, tree_broadcast(): part = lax.ppermute(value, axis, pairs)  14.3 us
    ppermute x6, waiting for transfers between devices, butterfly_sum(): value = value + lax.ppermute(value, axis, pairs)  9.27 us
    ppermute x6, starting transfers between devices, butterfly_sum(): value = value + lax.ppermute(value, axis, pairs)  8.43 us
    ppermute x6, starting transfers between devices, doubling_gather(): other = lax.ppermute(value, axis, pairs)  5.97 us
  transfers between devices with their start and end apart: 36, of which 11 were waited for; matrix products, arithmetic and copies ran while one was open for 21% of the time, Pallas kernels for 12%

profile of v10, /device:TPU:1, one launch (start us, length us, event | category | flops | bytes accessed | tf_op | source)
XLA Modules:
  0.0 169.3 jit_solution(14318269600193256852)
XLA Ops:
  0.6 0.9 select_bitcast_fusion.1
  1.5 9.8 %custom-call.4 = f32[1,128,128]{1,2,0:T(8,128)S(1)} custom-call(f32[1,128,128]{2,1,0:T(8,128)S(1)} %select_bitcast_fusion.1), custom_call_target="InvertDiagBlocksLowerTriangular" | custom-call | tf_op jit(solution)/shard_map/triangular_solve/custom-call.1 | solution.py:158
  11.6 3.0 %fusion.x_ref = bf16[2048,128]{1,0:T(8,128)(2,1)} fusion(f32[128,128]{1,0:T(8,128)S(1)} %fusion.15, f32[2048,1024]{1,0:T(8,128)} %param.17), kind=kOutput, calls=%fused_computation.6 | convolution fusion | flops 402915328 | bytes 1638400 | tf_op jit(solution)/shard_map/dot_general | solution.py:197
  14.6 19.2 %shard_map.137 = bf16[2048,128]{1,0:T(8,128)(2,1)} custom-call(bf16[2048,128]{1,0:T(8,128)(2,1)} %fusion.x_ref), custom_call_target="tpu_custom_call" | custom-call | tf_op jit(solution)/shard_map/pallas_call | solution.py:77
  33.8 1.5 fusion.11
  35.4 3.4 %collective-permute-start.6 = (f32[128,128]{1,0:T(8,128)S(1)}, f32[128,128]{1,0:T(8,128)S(1)}, u32[]{:S(2)}, u32[]{:S(2)}) collective-permute-start(f32[128,128]{1,0:T(8,128)S(1)} %fusion.11), channel_id=1, source_target_pairs={{0,16},{16,0},{32,48},{48,32},{64,80},{80,64},{96,112},{112,96},{1... | collective-permute-start | bytes 196616 | tf_op jit(solution)/shard_map/ppermute | solution.py:111
  38.8 3.1 %fusion.54 = f32[128,1024]{1,0:T(8,128)S(1)} fusion(bf16[2048,128]{1,0:T(8,128)(2,1)} %shard_map.137, bf16[2048,1024]{1,0:T(8,128)(2,1)} %param.12), kind=kOutput, calls=%fused_computation.101 | convolution fusion | flops 536870912 | bytes 5242880 | tf_op jit(solution)/shard_map/dot_general | solution.py:217
  41.9 2.8 %collective-permute-start.3 = (f32[4,16,1024]{2,1,0:T(8,128)S(1)}, f32[4,16,1024]{2,1,0:T(8,128)S(1)}, u32[]{:S(2)}, u32[]{:S(2)}) collective-permute-start(f32[4,16,1024]{2,1,0:T(8,128)S(1)} %bitcast.60), channel_id=1, source_target_pairs={{0,64},{16,80},{32,96},{48,112},{64,0},{80,16},{96,32},{112,48},{1... | collective-permute-start | bytes 786440 | tf_op jit(solution)/shard_map/ppermute | solution.py:127
  44.7 0.4 collective-permute-start
  45.3 9.8 %custom-call.5 = f32[1,128,128]{1,2,0:T(8,128)S(1)} custom-call(f32[1,128,128]{2,1,0:T(8,128)S(1)} %select_bitcast_fusion), custom_call_target="InvertDiagBlocksLowerTriangular" | custom-call | tf_op jit(solution)/shard_map/triangular_solve/custom-call.1 | solution.py:158
  55.4 0.4 collective-permute-start.1
  55.9 1.2 collective-permute-start.16
  57.1 0.4 collective-permute-start.7
  57.5 1.1 collective-permute-done.1
  58.7 1.2 collective-permute-start.2
  59.9 1.7 %collective-permute-done.7 = f32[128,128]{1,0:T(8,128)S(1)} collective-permute-done((f32[128,128]{1,0:T(8,128)S(1)}, f32[128,128]{1,0:T(8,128)S(1)}, u32[]{:S(2)}, u32[]{:S(2)}) %collective-permute-start.7) | collective-permute-done | bytes 65568 | tf_op jit(solution)/shard_map/ppermute | solution.py:111
  61.7 0.5 collective-permute-start.8
  62.2 2.6 %collective-permute-start.17 = (bf16[64,1024]{1,0:T(8,128)(2,1)S(1)}, bf16[64,1024]{1,0:T(8,128)(2,1)S(1)}, u32[]{:S(2)}, u32[]{:S(2)}) collective-permute-start(bf16[64,1024]{1,0:T(8,128)(2,1)S(1)} %maximum_select_fusion.3), channel_id=1, source_target_pairs={{0,64},{16,80},{32,96},{48,112},{64,0},{80,16},{96,32},{112,48},{1... | collective-permute-start | bytes 393224 | tf_op jit(solution)/shard_map/ppermute | solution.py:137
  64.8 2.4 %collective-permute-done.8 = f32[128,128]{1,0:T(8,128)S(1)} collective-permute-done((f32[128,128]{1,0:T(8,128)S(1)}, f32[128,128]{1,0:T(8,128)S(1)}, u32[]{:S(2)}, u32[]{:S(2)}) %collective-permute-start.8) | collective-permute-done | bytes 65568 | tf_op jit(solution)/shard_map/ppermute | solution.py:111
  67.3 1.0 collective-permute-start.10
  68.3 0.7 collective-permute-start.11
  69.0 0.7 collective-permute-start.9
  69.7 4.6 %convolution_subtract_fusion.1 = f32[2048,1024]{1,0:T(8,128)S(1)} fusion(f32[2048,1024]{1,0:T(8,128)} %param.17, bf16[2048,128]{1,0:T(8,128)(2,1)S(1)} %copy-done.1, bf16[64,1024]{1,0:T(8,128)(2,1)S(1)} %maximum_select_fusion.2, bf16[64,1024]{1,0:T(8,128)(2,1)S(1)} %collective-permute-done.2, pred[]{:T(512)S(6)} %eq.62), kind=kOutput, calls=%fused_computation.2 | convolution fusion | flops 540147712 | bytes 17563648 | tf_op jit(solution)/shard_map/dot_general | solution.py:220
  74.3 3.3 %copy-done = f32[2048,1024]{1,0:T(8,128)} copy-done((f32[2048,1024]{1,0:T(8,128)}, f32[2048,1024]{1,0:T(8,128)S(1)}, u32[]{:S(2)}) %copy-start) | copy-done | bytes 8388632
  77.8 0.7 collective-permute-start.12
  78.5 0.7 collective-permute-start.13
  79.2 1.3 collective-permute-start.14
  80.5 0.5 collective-permute-start.4
  81.0 4.6 %collective-permute-done.14 = f32[128,128]{1,0:T(8,128)S(1)} collective-permute-done((f32[128,128]{1,0:T(8,128)S(1)}, f32[128,128]{1,0:T(8,128)S(1)}, u32[]{:S(2)}, u32[]{:S(2)}) %collective-permute-start.14) | collective-permute-done | bytes 65568 | tf_op jit(solution)/shard_map/ppermute | solution.py:99
  85.6 0.3 fusion.2
  86.3 4.1 %collective-permute-start.5 = (f32[1,16,1024]{2,1,0:T(8,128)S(1)}, f32[1,16,1024]{2,1,0:T(8,128)S(1)}, u32[]{:S(2)}, u32[]{:S(2)}) collective-permute-start(f32[1,16,1024]{2,1,0:T(8,128)S(1)} %slice_select_fusion.8), channel_id=1, source_target_pairs={{0,16},{16,0},{32,48},{48,32},{64,80},{80,64},{96,112},{112,96},{1... | collective-permute-start | bytes 196616 | tf_op jit(solution)/shard_map/ppermute | solution.py:127
  90.7 0.6 collective-permute-done.5
  91.5 1.0 convolution_convert_fusion
  92.5 0.7 collective-permute-start.18
  93.2 0.7 collective-permute-start.19
  93.9 0.7 collective-permute-start.20
  94.5 0.8 slice.136.x_ref
  95.4 21.2 %shard_map.138 = bf16[2048,128]{1,0:T(8,128)(2,1)} custom-call(bf16[2048,128]{1,0:T(8,128)(2,1)} %slice.136.x_ref), custom_call_target="tpu_custom_call" | custom-call | tf_op jit(solution)/shard_map/pallas_call | solution.py:77
  116.6 3.1 %fusion.56 = f32[128,1024]{1,0:T(8,128)S(1)} fusion(bf16[2048,128]{1,0:T(8,128)(2,1)} %shard_map.138, bf16[2048,1024]{1,0:T(8,128)(2,1)} %param.12), kind=kOutput, calls=%fused_computation.103 | convolution fusion | flops 536870912 | bytes 5242880 | tf_op jit(solution)/shard_map/dot_general | solution.py:237
  119.7 4.6 %convolution_subtract_fusion = bf16[2048,1024]{1,0:T(8,128)(2,1)S(1)} fusion(f32[2048,1024]{1,0:T(8,128)} %copy-done, bf16[2048,128]{1,0:T(8,128)(2,1)S(1)} %copy-done.2, bf16[64,1024]{1,0:T(8,128)(2,1)S(1)} %maximum_select_fusion.3, bf16[64,1024]{1,0:T(8,128)(2,1)S(1)} %collective-permute-done.17, pred[]{:T(512)S(6)} %eq.62), kind=kOutput, calls=%fused_computation.1 | convolution fusion | flops 542244864 | bytes 13369345 | tf_op jit(solution)/shard_map/dot_general | solution.py:234
  124.4 0.4 slice.193
  125.0 2.6 %pad_maximum_fusion = bf16[2048,1024]{1,0:T(8,128)(2,1)} fusion(bf16[2048,128]{1,0:T(8,128)(2,1)S(1)} %fusion.7, bf16[2048,896]{1,0:T(8,128)(2,1)S(1)} %slice.193), kind=kLoop, calls=%fused_computation.3 | loop fusion | flops 8388608 | bytes 8388608 | tf_op jit(solution)/shard_map/concatenate | solution.py:247
  127.7 0.8 collective-permute-start.21
  128.5 0.7 collective-permute-start.22
  129.2 1.3 collective-permute-start.23
  130.5 1.4 fusion.9
  131.9 4.1 %collective-permute-done.23 = bf16[16,128]{1,0:T(8,128)(2,1)S(1)} collective-permute-done((bf16[16,128]{1,0:T(8,128)(2,1)S(1)}, bf16[16,128]{1,0:T(8,128)(2,1)S(1)}, u32[]{:S(2)}, u32[]{:S(2)}) %collective-permute-start.23) | collective-permute-done | bytes 4128 | tf_op jit(solution)/shard_map/ppermute | solution.py:99
  136.2 3.4 %collective-permute-start.27 = (f32[128,128]{1,0:T(8,128)S(1)}, f32[128,128]{1,0:T(8,128)S(1)}, u32[]{:S(2)}, u32[]{:S(2)}) collective-permute-start(f32[128,128]{1,0:T(8,128)S(1)} %convolution_add_fusion.1), channel_id=1, source_target_pairs={{0,16},{16,0},{32,48},{48,32},{64,80},{80,64},{96,112},{112,96},{1... | collective-permute-start | bytes 196616 | tf_op jit(solution)/shard_map/ppermute | solution.py:111
  139.9 0.6 collective-permute-done.27
  140.8 2.9 %collective-permute-done.28 = f32[128,128]{1,0:T(8,128)S(1)} collective-permute-done((f32[128,128]{1,0:T(8,128)S(1)}, f32[128,128]{1,0:T(8,128)S(1)}, u32[]{:S(2)}, u32[]{:S(2)}) %collective-permute-start.28) | collective-permute-done | bytes 65568 | tf_op jit(solution)/shard_map/ppermute | solution.py:111
  143.8 0.6 collective-permute-start.29
  144.4 2.5 %collective-permute-start.24 = (f32[4,16,1024]{2,1,0:T(8,128)S(1)}, f32[4,16,1024]{2,1,0:T(8,128)S(1)}, u32[]{:S(2)}, u32[]{:S(2)}) collective-permute-start(f32[4,16,1024]{2,1,0:T(8,128)S(1)} %bitcast.61), channel_id=1, source_target_pairs={{0,64},{16,80},{32,96},{48,112},{64,0},{80,16},{96,32},{112,48},{1... | collective-permute-start | bytes 786440 | tf_op jit(solution)/shard_map/ppermute | solution.py:127
  146.9 1.6 collective-permute-done.29
  148.5 0.7 collective-permute-start.30
  149.1 0.7 collective-permute-start.31
  149.8 0.7 collective-permute-start.32
  150.5 0.6 pad_maximum_fusion.2
  151.2 0.7 collective-permute-start.33
  151.8 0.7 collective-permute-start.34
  152.5 1.3 collective-permute-start.35
  154.0 7.4 %collective-permute-done.35 = f32[128,128]{1,0:T(8,128)S(1)} collective-permute-done((f32[128,128]{1,0:T(8,128)S(1)}, f32[128,128]{1,0:T(8,128)S(1)}, u32[]{:S(2)}, u32[]{:S(2)}) %collective-permute-start.35) | collective-permute-done | bytes 65568 | tf_op jit(solution)/shard_map/ppermute | solution.py:99
  162.0 5.5 %collective-permute-start.26 = (f32[1,16,1024]{2,1,0:T(8,128)S(1)}, f32[1,16,1024]{2,1,0:T(8,128)S(1)}, u32[]{:S(2)}, u32[]{:S(2)}) collective-permute-start(f32[1,16,1024]{2,1,0:T(8,128)S(1)} %slice_select_fusion.7), channel_id=1, source_target_pairs={{0,16},{16,0},{32,48},{48,32},{64,80},{80,64},{96,112},{112,96},{1... | collective-permute-start | bytes 196616 | tf_op jit(solution)/shard_map/ppermute | solution.py:127
  167.8 0.6 collective-permute-done.26
  168.7 0.6 pad_maximum_fusion.1
  (101 shorter events, 4.5 us)
Async XLA Ops:
  14.6 30.2 %copy-start.5 = (bf16[16,1024]{1,0:T(8,128)(2,1)S(1)}, bf16[16,1024]{1,0:T(8,128)(2,1)}, u32[]{:S(2)}) copy-start(bf16[16,1024]{1,0:T(8,128)(2,1)} %param.14) | copy-start | bytes 98308
  14.6 30.5 %copy-start.10 = (bf16[16,1024]{1,0:T(8,128)(2,1)S(1)}, bf16[16,1024]{1,0:T(8,128)(2,1)}, u32[]{:S(2)}) copy-start(bf16[16,1024]{1,0:T(8,128)(2,1)} %param.13) | copy-start | bytes 98308
  14.6 30.7 %copy-start.4 = (f32[128,128]{1,0:T(8,128)S(1)}, f32[128,128]{1,0:T(8,128)}, u32[]{:S(2)}) copy-start(f32[128,128]{1,0:T(8,128)} %param.15) | copy-start | bytes 196612
  35.4 34.3 %copy-start.1 = (bf16[2048,128]{1,0:T(8,128)(2,1)S(1)}, bf16[2048,128]{1,0:T(8,128)(2,1)}, u32[]{:S(2)}) copy-start(bf16[2048,128]{1,0:T(8,128)(2,1)} %shard_map.137) | copy-start | bytes 1572868
  35.4 21.7 %collective-permute-start.6 = (f32[128,128]{1,0:T(8,128)S(1)}, f32[128,128]{1,0:T(8,128)S(1)}, u32[]{:S(2)}, u32[]{:S(2)}) collective-permute-start(f32[128,128]{1,0:T(8,128)S(1)} %fusion.11), channel_id=1, source_target_pairs={{0,16},{16,0},{32,48},{48,32},{64,80},{80,64},{96,112},{112,96},{1... | collective-permute-start | bytes 196616 | tf_op jit(solution)/shard_map/ppermute | solution.py:111
  41.9 38.6 %collective-permute-start.3 = (f32[4,16,1024]{2,1,0:T(8,128)S(1)}, f32[4,16,1024]{2,1,0:T(8,128)S(1)}, u32[]{:S(2)}, u32[]{:S(2)}) collective-permute-start(f32[4,16,1024]{2,1,0:T(8,128)S(1)} %bitcast.60), channel_id=1, source_target_pairs={{0,64},{16,80},{32,96},{48,112},{64,0},{80,16},{96,32},{112,48},{1... | collective-permute-start | bytes 786440 | tf_op jit(solution)/shard_map/ppermute | solution.py:127
  44.7 10.7 %collective-permute-start = (bf16[16,1024]{1,0:T(8,128)(2,1)S(1)}, bf16[16,1024]{1,0:T(8,128)(2,1)S(1)}, u32[]{:S(2)}, u32[]{:S(2)}) collective-permute-start(bf16[16,1024]{1,0:T(8,128)(2,1)S(1)} %copy-done.5), channel_id=1, source_target_pairs={{0,16},{16,0},{32,48},{48,32},{64,80},{80,64},{96,112},{112,96},{1... | collective-permute-start | bytes 98312 | tf_op jit(solution)/shard_map/ppermute | solution.py:137
  45.1 10.8 %collective-permute-start.15 = (bf16[16,1024]{1,0:T(8,128)(2,1)S(1)}, bf16[16,1024]{1,0:T(8,128)(2,1)S(1)}, u32[]{:S(2)}, u32[]{:S(2)}) collective-permute-start(bf16[16,1024]{1,0:T(8,128)(2,1)S(1)} %copy-done.10), channel_id=1, source_target_pairs={{0,16},{16,0},{32,48},{48,32},{64,80},{80,64},{96,112},{112,96},{1... | collective-permute-start | bytes 98312 | tf_op jit(solution)/shard_map/ppermute | solution.py:137
  55.4 3.2 %collective-permute-start.1 = (bf16[32,1024]{1,0:T(8,128)(2,1)S(1)}, bf16[32,1024]{1,0:T(8,128)(2,1)S(1)}, u32[]{:S(2)}, u32[]{:S(2)}) collective-permute-start(bf16[32,1024]{1,0:T(8,128)(2,1)S(1)} %maximum_select_fusion.4), channel_id=1, source_target_pairs={{0,32},{16,48},{32,0},{48,16},{64,96},{80,112},{96,64},{112,80},{1... | collective-permute-start | bytes 196616 | tf_op jit(solution)/shard_map/ppermute | solution.py:137
  55.9 6.3 %collective-permute-start.16 = (bf16[32,1024]{1,0:T(8,128)(2,1)S(1)}, bf16[32,1024]{1,0:T(8,128)(2,1)S(1)}, u32[]{:S(2)}, u32[]{:S(2)}) collective-permute-start(bf16[32,1024]{1,0:T(8,128)(2,1)S(1)} %maximum_select_fusion.5), channel_id=1, source_target_pairs={{0,32},{16,48},{32,0},{48,16},{64,96},{80,112},{96,64},{112,80},{1... | collective-permute-start | bytes 196616 | tf_op jit(solution)/shard_map/ppermute | solution.py:137
  57.1 4.6 %collective-permute-start.7 = (f32[128,128]{1,0:T(8,128)S(1)}, f32[128,128]{1,0:T(8,128)S(1)}, u32[]{:S(2)}, u32[]{:S(2)}) collective-permute-start(f32[128,128]{1,0:T(8,128)S(1)} %add.117), channel_id=1, source_target_pairs={{0,32},{16,48},{32,0},{48,16},{64,96},{80,112},{96,64},{112,80},{1... | collective-permute-start | bytes 196616 | tf_op jit(solution)/shard_map/ppermute | solution.py:111
  58.7 10.3 %collective-permute-start.2 = (bf16[64,1024]{1,0:T(8,128)(2,1)S(1)}, bf16[64,1024]{1,0:T(8,128)(2,1)S(1)}, u32[]{:S(2)}, u32[]{:S(2)}) collective-permute-start(bf16[64,1024]{1,0:T(8,128)(2,1)S(1)} %maximum_select_fusion.2), channel_id=1, source_target_pairs={{0,64},{16,80},{32,96},{48,112},{64,0},{80,16},{96,32},{112,48},{1... | collective-permute-start | bytes 393224 | tf_op jit(solution)/shard_map/ppermute | solution.py:137
  61.7 5.6 %collective-permute-start.8 = (f32[128,128]{1,0:T(8,128)S(1)}, f32[128,128]{1,0:T(8,128)S(1)}, u32[]{:S(2)}, u32[]{:S(2)}) collective-permute-start(f32[128,128]{1,0:T(8,128)S(1)} %add.118), channel_id=1, source_target_pairs={{0,64},{16,80},{32,96},{48,112},{64,0},{80,16},{96,32},{112,48},{1... | collective-permute-start | bytes 196616 | tf_op jit(solution)/shard_map/ppermute | solution.py:111
  62.2 57.5 %collective-permute-start.17 = (bf16[64,1024]{1,0:T(8,128)(2,1)S(1)}, bf16[64,1024]{1,0:T(8,128)(2,1)S(1)}, u32[]{:S(2)}, u32[]{:S(2)}) collective-permute-start(bf16[64,1024]{1,0:T(8,128)(2,1)S(1)} %maximum_select_fusion.3), channel_id=1, source_target_pairs={{0,64},{16,80},{32,96},{48,112},{64,0},{80,16},{96,32},{112,48},{1... | collective-permute-start | bytes 393224 | tf_op jit(solution)/shard_map/ppermute | solution.py:137
  67.3 18.3 %copy-start.3 = (f32[128,128]{1,0:T(8,128)S(1)}, f32[128,128]{1,0:T(8,128)}, u32[]{:S(2)}) copy-start(f32[128,128]{1,0:T(8,128)} %param.16) | copy-start | bytes 196612
  67.3 18.3 %copy-start.6 = (f32[128,128]{1,0:T(8,128)S(1)}, f32[128,128]{1,0:T(8,128)}, u32[]{:S(2)}) copy-start(f32[128,128]{1,0:T(8,128)} %param.21) | copy-start | bytes 196612
  67.3 10.4 %collective-permute-start.10 = (f32[128,128]{1,0:T(8,128)S(1)}, f32[128,128]{1,0:T(8,128)S(1)}, u32[]{:S(2)}, u32[]{:S(2)}) collective-permute-start(f32[128,128]{1,0:T(8,128)S(1)} %add.119), channel_id=1, source_target_pairs={{15,13},{31,29},{47,45},{63,61},{79,77},{95,93},{111,109},{127,125}} | collective-permute-start | bytes 196616 | tf_op jit(solution)/shard_map/ppermute | solution.py:99
  68.3 9.5 %collective-permute-start.11 = (f32[128,128]{1,0:T(8,128)S(1)}, f32[128,128]{1,0:T(8,128)S(1)}, u32[]{:S(2)}, u32[]{:S(2)}) collective-permute-start(f32[128,128]{1,0:T(8,128)S(1)} %add.119), channel_id=1, source_target_pairs={{15,12},{31,28},{47,44},{63,60},{79,76},{95,92},{111,108},{127,124}} | collective-permute-start | bytes 196616 | tf_op jit(solution)/shard_map/ppermute | solution.py:99
  69.0 8.8 %collective-permute-start.9 = (f32[128,128]{1,0:T(8,128)S(1)}, f32[128,128]{1,0:T(8,128)S(1)}, u32[]{:S(2)}, u32[]{:S(2)}) collective-permute-start(f32[128,128]{1,0:T(8,128)S(1)} %add.119), channel_id=1, source_target_pairs={{15,14},{31,30},{47,46},{63,62},{79,78},{95,94},{111,110},{127,126}} | collective-permute-start | bytes 196616 | tf_op jit(solution)/shard_map/ppermute | solution.py:99
  74.3 3.3 %copy-start = (f32[2048,1024]{1,0:T(8,128)}, f32[2048,1024]{1,0:T(8,128)S(1)}, u32[]{:S(2)}) copy-start(f32[2048,1024]{1,0:T(8,128)S(1)} %convolution_subtract_fusion.1) | copy-start | bytes 25165828
  77.6 13.7 %copy-start.11 = (f32[16,1024]{1,0:T(8,128)S(1)}, f32[16,1024]{1,0:T(8,128)}, u32[]{:S(2)}) copy-start(f32[16,1024]{1,0:T(8,128)} %param.19) | copy-start | bytes 196612
  77.8 3.2 %collective-permute-start.12 = (f32[128,128]{1,0:T(8,128)S(1)}, f32[128,128]{1,0:T(8,128)S(1)}, u32[]{:S(2)}, u32[]{:S(2)}) collective-permute-start(f32[128,128]{1,0:T(8,128)S(1)} %add_select_fusion.1), channel_id=1, source_target_pairs={{15,11},{14,10},{13,9},{12,8},{31,27},{30,26},{29,25},{28,24},{47,... | collective-permute-start | bytes 196616 | tf_op jit(solution)/shard_map/ppermute | solution.py:99
  78.5 2.5 %collective-permute-start.13 = (f32[128,128]{1,0:T(8,128)S(1)}, f32[128,128]{1,0:T(8,128)S(1)}, u32[]{:S(2)}, u32[]{:S(2)}) collective-permute-start(f32[128,128]{1,0:T(8,128)S(1)} %add_select_fusion.1), channel_id=1, source_target_pairs={{15,7},{14,6},{13,5},{12,4},{31,23},{30,22},{29,21},{28,20},{47,39... | collective-permute-start | bytes 196616 | tf_op jit(solution)/shard_map/ppermute | solution.py:99
  79.2 6.4 %collective-permute-start.14 = (f32[128,128]{1,0:T(8,128)S(1)}, f32[128,128]{1,0:T(8,128)S(1)}, u32[]{:S(2)}, u32[]{:S(2)}) collective-permute-start(f32[128,128]{1,0:T(8,128)S(1)} %add_select_fusion.1), channel_id=1, source_target_pairs={{15,3},{14,2},{13,1},{12,0},{31,19},{30,18},{29,17},{28,16},{47,35... | collective-permute-start | bytes 196616 | tf_op jit(solution)/shard_map/ppermute | solution.py:99
  80.5 5.6 %collective-permute-start.4 = (f32[2,16,1024]{2,1,0:T(8,128)S(1)}, f32[2,16,1024]{2,1,0:T(8,128)S(1)}, u32[]{:S(2)}, u32[]{:S(2)}) collective-permute-start(f32[2,16,1024]{2,1,0:T(8,128)S(1)} %slice_select_fusion.6), channel_id=1, source_target_pairs={{0,32},{16,48},{32,0},{48,16},{64,96},{80,112},{96,64},{112,80},{1... | collective-permute-start | bytes 393224 | tf_op jit(solution)/shard_map/ppermute | solution.py:127
  86.3 5.0 %collective-permute-start.5 = (f32[1,16,1024]{2,1,0:T(8,128)S(1)}, f32[1,16,1024]{2,1,0:T(8,128)S(1)}, u32[]{:S(2)}, u32[]{:S(2)}) collective-permute-start(f32[1,16,1024]{2,1,0:T(8,128)S(1)} %slice_select_fusion.8), channel_id=1, source_target_pairs={{0,16},{16,0},{32,48},{48,32},{64,80},{80,64},{96,112},{112,96},{1... | collective-permute-start | bytes 196616 | tf_op jit(solution)/shard_map/ppermute | solution.py:127
  90.6 29.1 %copy-start.8 = (f32[128,128]{1,0:T(8,128)}, f32[128,128]{1,0:T(8,128)S(1)}, u32[]{:S(2)}) copy-start(f32[128,128]{1,0:T(8,128)S(1)} %get-tuple-element.10) | copy-start | bytes 196612
  92.5 35.1 %collective-permute-start.18 = (bf16[16,128]{1,0:T(8,128)(2,1)S(1)}, bf16[16,128]{1,0:T(8,128)(2,1)S(1)}, u32[]{:S(2)}, u32[]{:S(2)}) collective-permute-start(bf16[16,128]{1,0:T(8,128)(2,1)S(1)} %slice.139), channel_id=1, source_target_pairs={{14,15},{30,31},{46,47},{62,63},{78,79},{94,95},{110,111},{126,127}} | collective-permute-start | bytes 12296 | tf_op jit(solution)/shard_map/ppermute | solution.py:99
  93.2 34.5 %collective-permute-start.19 = (bf16[16,128]{1,0:T(8,128)(2,1)S(1)}, bf16[16,128]{1,0:T(8,128)(2,1)S(1)}, u32[]{:S(2)}, u32[]{:S(2)}) collective-permute-start(bf16[16,128]{1,0:T(8,128)(2,1)S(1)} %slice.139), channel_id=1, source_target_pairs={{14,12},{30,28},{46,44},{62,60},{78,76},{94,92},{110,108},{126,124}} | collective-permute-start | bytes 12296 | tf_op jit(solution)/shard_map/ppermute | solution.py:99
  93.9 33.8 %collective-permute-start.20 = (bf16[16,128]{1,0:T(8,128)(2,1)S(1)}, bf16[16,128]{1,0:T(8,128)(2,1)S(1)}, u32[]{:S(2)}, u32[]{:S(2)}) collective-permute-start(bf16[16,128]{1,0:T(8,128)(2,1)S(1)} %slice.139), channel_id=1, source_target_pairs={{14,13},{30,29},{46,45},{62,61},{78,77},{94,93},{110,109},{126,125}} | collective-permute-start | bytes 12296 | tf_op jit(solution)/shard_map/ppermute | solution.py:99
  116.5 3.2 %copy-start.2 = (bf16[2048,128]{1,0:T(8,128)(2,1)S(1)}, bf16[2048,128]{1,0:T(8,128)(2,1)}, u32[]{:S(2)}) copy-start(bf16[2048,128]{1,0:T(8,128)(2,1)} %shard_map.138) | copy-start | bytes 1572868
  127.7 33.7 %copy-start.7 = (f32[128,128]{1,0:T(8,128)S(1)}, f32[128,128]{1,0:T(8,128)}, u32[]{:S(2)}) copy-start(f32[128,128]{1,0:T(8,128)} %param.20) | copy-start | bytes 196612
  127.7 40.7 %copy-start.12 = (f32[16,1024]{1,0:T(8,128)S(1)}, f32[16,1024]{1,0:T(8,128)}, u32[]{:S(2)}) copy-start(f32[16,1024]{1,0:T(8,128)} %param.18) | copy-start | bytes 196612
  127.7 4.2 %collective-permute-start.21 = (bf16[16,128]{1,0:T(8,128)(2,1)S(1)}, bf16[16,128]{1,0:T(8,128)(2,1)S(1)}, u32[]{:S(2)}, u32[]{:S(2)}) collective-permute-start(bf16[16,128]{1,0:T(8,128)(2,1)S(1)} %add_select_fusion.3), channel_id=1, source_target_pairs={{14,10},{15,11},{12,8},{13,9},{30,26},{31,27},{28,24},{29,25},{46,... | collective-permute-start | bytes 12296 | tf_op jit(solution)/shard_map/ppermute | solution.py:99
  128.5 3.4 %collective-permute-start.22 = (bf16[16,128]{1,0:T(8,128)(2,1)S(1)}, bf16[16,128]{1,0:T(8,128)(2,1)S(1)}, u32[]{:S(2)}, u32[]{:S(2)}) collective-permute-start(bf16[16,128]{1,0:T(8,128)(2,1)S(1)} %add_select_fusion.3), channel_id=1, source_target_pairs={{14,6},{15,7},{12,4},{13,5},{30,22},{31,23},{28,20},{29,21},{46,38... | collective-permute-start | bytes 12296 | tf_op jit(solution)/shard_map/ppermute | solution.py:99
  129.2 6.8 %collective-permute-start.23 = (bf16[16,128]{1,0:T(8,128)(2,1)S(1)}, bf16[16,128]{1,0:T(8,128)(2,1)S(1)}, u32[]{:S(2)}, u32[]{:S(2)}) collective-permute-start(bf16[16,128]{1,0:T(8,128)(2,1)S(1)} %add_select_fusion.3), channel_id=1, source_target_pairs={{14,2},{15,3},{12,0},{13,1},{30,18},{31,19},{28,16},{29,17},{46,34... | collective-permute-start | bytes 12296 | tf_op jit(solution)/shard_map/ppermute | solution.py:99
  136.2 4.3 %collective-permute-start.27 = (f32[128,128]{1,0:T(8,128)S(1)}, f32[128,128]{1,0:T(8,128)S(1)}, u32[]{:S(2)}, u32[]{:S(2)}) collective-permute-start(f32[128,128]{1,0:T(8,128)S(1)} %convolution_add_fusion.1), channel_id=1, source_target_pairs={{0,16},{16,0},{32,48},{48,32},{64,80},{80,64},{96,112},{112,96},{1... | collective-permute-start | bytes 196616 | tf_op jit(solution)/shard_map/ppermute | solution.py:111
  140.5 3.2 %collective-permute-start.28 = (f32[128,128]{1,0:T(8,128)S(1)}, f32[128,128]{1,0:T(8,128)S(1)}, u32[]{:S(2)}, u32[]{:S(2)}) collective-permute-start(f32[128,128]{1,0:T(8,128)S(1)} %add.135), channel_id=1, source_target_pairs={{0,32},{16,48},{32,0},{48,16},{64,96},{80,112},{96,64},{112,80},{1... | collective-permute-start | bytes 196616 | tf_op jit(solution)/shard_map/ppermute | solution.py:111
  143.8 4.7 %collective-permute-start.29 = (f32[128,128]{1,0:T(8,128)S(1)}, f32[128,128]{1,0:T(8,128)S(1)}, u32[]{:S(2)}, u32[]{:S(2)}) collective-permute-start(f32[128,128]{1,0:T(8,128)S(1)} %add.136), channel_id=1, source_target_pairs={{0,64},{16,80},{32,96},{48,112},{64,0},{80,16},{96,32},{112,48},{1... | collective-permute-start | bytes 196616 | tf_op jit(solution)/shard_map/ppermute | solution.py:111
  144.4 9.4 %collective-permute-start.24 = (f32[4,16,1024]{2,1,0:T(8,128)S(1)}, f32[4,16,1024]{2,1,0:T(8,128)S(1)}, u32[]{:S(2)}, u32[]{:S(2)}) collective-permute-start(f32[4,16,1024]{2,1,0:T(8,128)S(1)} %bitcast.61), channel_id=1, source_target_pairs={{0,64},{16,80},{32,96},{48,112},{64,0},{80,16},{96,32},{112,48},{1... | collective-permute-start | bytes 786440 | tf_op jit(solution)/shard_map/ppermute | solution.py:127
  148.5 2.7 %collective-permute-start.30 = (f32[128,128]{1,0:T(8,128)S(1)}, f32[128,128]{1,0:T(8,128)S(1)}, u32[]{:S(2)}, u32[]{:S(2)}) collective-permute-start(f32[128,128]{1,0:T(8,128)S(1)} %add.137), channel_id=1, source_target_pairs={{14,15},{30,31},{46,47},{62,63},{78,79},{94,95},{110,111},{126,127}} | collective-permute-start | bytes 196616 | tf_op jit(solution)/shard_map/ppermute | solution.py:99
  149.1 2.0 %collective-permute-start.31 = (f32[128,128]{1,0:T(8,128)S(1)}, f32[128,128]{1,0:T(8,128)S(1)}, u32[]{:S(2)}, u32[]{:S(2)}) collective-permute-start(f32[128,128]{1,0:T(8,128)S(1)} %add.137), channel_id=1, source_target_pairs={{14,12},{30,28},{46,44},{62,60},{78,76},{94,92},{110,108},{126,124}} | collective-permute-start | bytes 196616 | tf_op jit(solution)/shard_map/ppermute | solution.py:99
  149.8 1.3 collective-permute-start.32
  151.2 2.8 %collective-permute-start.33 = (f32[128,128]{1,0:T(8,128)S(1)}, f32[128,128]{1,0:T(8,128)S(1)}, u32[]{:S(2)}, u32[]{:S(2)}) collective-permute-start(f32[128,128]{1,0:T(8,128)S(1)} %add_select_fusion), channel_id=1, source_target_pairs={{14,10},{15,11},{12,8},{13,9},{30,26},{31,27},{28,24},{29,25},{46,... | collective-permute-start | bytes 196616 | tf_op jit(solution)/shard_map/ppermute | solution.py:99
  151.8 2.2 %collective-permute-start.34 = (f32[128,128]{1,0:T(8,128)S(1)}, f32[128,128]{1,0:T(8,128)S(1)}, u32[]{:S(2)}, u32[]{:S(2)}) collective-permute-start(f32[128,128]{1,0:T(8,128)S(1)} %add_select_fusion), channel_id=1, source_target_pairs={{14,6},{15,7},{12,4},{13,5},{30,22},{31,23},{28,20},{29,21},{46,38... | collective-permute-start | bytes 196616 | tf_op jit(solution)/shard_map/ppermute | solution.py:99
  152.5 8.9 %collective-permute-start.35 = (f32[128,128]{1,0:T(8,128)S(1)}, f32[128,128]{1,0:T(8,128)S(1)}, u32[]{:S(2)}, u32[]{:S(2)}) collective-permute-start(f32[128,128]{1,0:T(8,128)S(1)} %add_select_fusion), channel_id=1, source_target_pairs={{14,2},{15,3},{12,0},{13,1},{30,18},{31,19},{28,16},{29,17},{46,34... | collective-permute-start | bytes 196616 | tf_op jit(solution)/shard_map/ppermute | solution.py:99
  153.9 8.1 %collective-permute-start.25 = (f32[2,16,1024]{2,1,0:T(8,128)S(1)}, f32[2,16,1024]{2,1,0:T(8,128)S(1)}, u32[]{:S(2)}, u32[]{:S(2)}) collective-permute-start(f32[2,16,1024]{2,1,0:T(8,128)S(1)} %slice_select_fusion.5), channel_id=1, source_target_pairs={{0,32},{16,48},{32,0},{48,16},{64,96},{80,112},{96,64},{112,80},{1... | collective-permute-start | bytes 393224 | tf_op jit(solution)/shard_map/ppermute | solution.py:127
  162.0 6.4 %collective-permute-start.26 = (f32[1,16,1024]{2,1,0:T(8,128)S(1)}, f32[1,16,1024]{2,1,0:T(8,128)S(1)}, u32[]{:S(2)}, u32[]{:S(2)}) collective-permute-start(f32[1,16,1024]{2,1,0:T(8,128)S(1)} %slice_select_fusion.7), channel_id=1, source_target_pairs={{0,16},{16,0},{32,48},{48,32},{64,80},{80,64},{96,112},{112,96},{1... | collective-permute-start | bytes 196616 | tf_op jit(solution)/shard_map/ppermute | solution.py:127
  167.7 1.6 copy-start.9

commit v11 on v10

--- a/solution.py
+++ b/solution.py
@@ -217,8 +217,10 @@
             jnp.dot(solved_two.T, trail, preferred_element_type=jnp.float32), "row", n_row
         )
         adj_two = adj_row_two - crossed - rest_two
-        adj_next = adj_trail - jnp.dot(solved_two, full_two, preferred_element_type=jnp.float32)
-        stacked = jnp.concatenate([adj_two[:, last:], adj_next[:, last:]], 0)
+        next_panel = adj_trail[:, last:] - jnp.dot(
+            solved_two, full_two[:, last:], preferred_element_type=jnp.float32
+        )
+        stacked = jnp.concatenate([adj_two[:, last:], next_panel], 0)
         solved_one = solve_panel(stacked, inverse_one, root_one)
         head_rows = solved_one[:band]
         tail_rows = solved_one[band:]
@@ -231,7 +233,11 @@
         rest_one = jnp.dot(mirror_one, full_one.astype(jnp.float32), precision=exact_mode)
         head_update = jnp.dot(head_rows, full_one, preferred_element_type=jnp.float32)
         two_left = adj_two - head_update
-        trail_left = adj_next - jnp.dot(tail_rows, full_one, preferred_element_type=jnp.float32)
+        trail_left = adj_trail - jnp.dot(
+            jnp.concatenate([solved_two, tail_rows], 1),
+            jnp.concatenate([full_two, full_one], 0),
+            preferred_element_type=jnp.float32,
+        )
         crossed_one = halving_scatter(
             jnp.dot(head_rows.T, row_two, preferred_element_type=jnp.float32)
             + jnp.dot(tail_rows.T, trail, preferred_element_type=jnp.float32),

time: 170 us -> 163 us (0.959)
  waiting for transfers between devices: 27.6 us -> 24 us
  local copies, waits for them, and re-layouts: 4.95 us -> 1.52 us
  starting transfers between devices: 44.2 us -> 47 us
  matrix products: 25.6 us -> 23.4 us
    ppermute x18, waiting for transfers between devices: 16 us -> 12.4 us  [tree_broadcast(): part = lax.ppermute(value, axis, pairs)]
    unnamed x26 -> x22, local copies, waits for them, and re-layouts: 3.35 us -> 0.06 us
    dot_general x2, matrix products: 9.29 us -> 6.18 us  [the longest x1 4.67 us: per_device(): jnp.dot(jnp.concatenate([solved_two, tail_rows], 1), jnp.concatenate([ful...]
  transfers between devices with their start and end apart: 36 -> 36, of which waited for: 11 -> 11; matrix products, arithmetic and copies ran while one was open for 21% -> 30% of each run, Pallas kernels for 12% -> 24%
where the time goes in v11:
time: 163 us; the launch traced here: 161 us
  starting transfers between devices  47 us (29%)
  Pallas kernels  38.9 us (24%)
  other arithmetic  25.2 us (15%)
  waiting for transfers between devices  24 us (15%)
  matrix products  23.4 us (14%)
    pallas_call x2, Pallas kernels, panel_broadcast(): pl.pallas_call(functools.partial(spread_kernel, root, size), out_shape=ja...  38.9 us
    another operation x4, other arithmetic, inverse_lower(): return lax.linalg.triangular_solve(block, ident, left_side=True, lower=True)  20.5 us
    ppermute x6, starting transfers between devices, halving_scatter(): blocks = keep + lax.ppermute(send, axis, pairs)  16.6 us
    ppermute x18, starting transfers between devices, tree_broadcast(): part = lax.ppermute(value, axis, pairs)  14.1 us
    ppermute x18, waiting for transfers between devices, tree_broadcast(): part = lax.ppermute(value, axis, pairs)  12.4 us
    ppermute x6, waiting for transfers between devices, butterfly_sum(): value = value + lax.ppermute(value, axis, pairs)  9.31 us
    ppermute x6, starting transfers between devices, butterfly_sum(): value = value + lax.ppermute(value, axis, pairs)  9.17 us
    ppermute x6, starting transfers between devices, doubling_gather(): other = lax.ppermute(value, axis, pairs)  7.06 us
  transfers between devices with their start and end apart: 36, of which 11 were waited for; matrix products, arithmetic and copies ran while one was open for 30% of the time, Pallas kernels for 24%

profile of v11, /device:TPU:1, one launch (start us, length us, event | category | flops | bytes accessed | tf_op | source)
XLA Modules:
  0.0 161.4 jit_solution(1591565483438689211)
XLA Ops:
  0.6 1.5 collective-permute-start.15
  2.2 0.8 select_bitcast_fusion.1
  3.1 9.8 %custom-call.4 = f32[1,128,128]{1,2,0:T(8,128)S(1)} custom-call(f32[1,128,128]{2,1,0:T(8,128)S(1)} %select_bitcast_fusion.1), custom_call_target="InvertDiagBlocksLowerTriangular" | custom-call | tf_op jit(solution)/shard_map/triangular_solve/custom-call.1 | solution.py:158
  13.2 3.0 %fusion.x_ref = bf16[2048,128]{1,0:T(8,128)(2,1)} fusion(f32[128,128]{1,0:T(8,128)S(1)} %fusion.21, f32[2048,1024]{1,0:T(8,128)} %param.17), kind=kOutput, calls=%fused_computation.6 | convolution fusion | flops 402915328 | bytes 1638400 | tf_op jit(solution)/shard_map/dot_general | solution.py:197
  16.2 18.4 %shard_map.137 = bf16[2048,128]{1,0:T(8,128)(2,1)} custom-call(bf16[2048,128]{1,0:T(8,128)(2,1)} %fusion.x_ref), custom_call_target="tpu_custom_call" | custom-call | tf_op jit(solution)/shard_map/pallas_call | solution.py:77
  34.6 1.5 fusion.17
  36.1 3.2 %collective-permute-start.3 = (f32[128,128]{1,0:T(8,128)S(1)}, f32[128,128]{1,0:T(8,128)S(1)}, u32[]{:S(2)}, u32[]{:S(2)}) collective-permute-start(f32[128,128]{1,0:T(8,128)S(1)} %fusion.17), channel_id=1, source_target_pairs={{0,16},{16,0},{32,48},{48,32},{64,80},{80,64},{96,112},{112,96},{1... | collective-permute-start | bytes 196616 | tf_op jit(solution)/shard_map/ppermute | solution.py:111
  39.3 3.1 %fusion.60 = f32[128,1024]{1,0:T(8,128)S(1)} fusion(bf16[2048,128]{1,0:T(8,128)(2,1)} %shard_map.137, bf16[2048,1024]{1,0:T(8,128)(2,1)} %param.12), kind=kOutput, calls=%fused_computation.107 | convolution fusion | flops 536870912 | bytes 5242880 | tf_op jit(solution)/shard_map/dot_general | solution.py:217
  42.5 2.8 %collective-permute-start = (f32[4,16,1024]{2,1,0:T(8,128)S(1)}, f32[4,16,1024]{2,1,0:T(8,128)S(1)}, u32[]{:S(2)}, u32[]{:S(2)}) collective-permute-start(f32[4,16,1024]{2,1,0:T(8,128)S(1)} %bitcast.62), channel_id=1, source_target_pairs={{0,64},{16,80},{32,96},{48,112},{64,0},{80,16},{96,32},{112,48},{1... | collective-permute-start | bytes 786440 | tf_op jit(solution)/shard_map/ppermute | solution.py:127
  45.4 9.8 %custom-call.5 = f32[1,128,128]{1,2,0:T(8,128)S(1)} custom-call(f32[1,128,128]{2,1,0:T(8,128)S(1)} %select_bitcast_fusion), custom_call_target="InvertDiagBlocksLowerTriangular" | custom-call | tf_op jit(solution)/shard_map/triangular_solve/custom-call.1 | solution.py:158
  55.6 0.4 collective-permute-start.13
  56.0 1.2 collective-permute-start.16
  57.2 0.4 collective-permute-start.4
  57.6 1.1 collective-permute-done.13
  58.8 1.2 collective-permute-start.14
  60.1 1.7 %collective-permute-done.4 = f32[128,128]{1,0:T(8,128)S(1)} collective-permute-done((f32[128,128]{1,0:T(8,128)S(1)}, f32[128,128]{1,0:T(8,128)S(1)}, u32[]{:S(2)}, u32[]{:S(2)}) %collective-permute-start.4) | collective-permute-done | bytes 65568 | tf_op jit(solution)/shard_map/ppermute | solution.py:111
  61.8 0.5 collective-permute-start.5
  62.4 2.6 %collective-permute-start.17 = (bf16[64,1024]{1,0:T(8,128)(2,1)S(1)}, bf16[64,1024]{1,0:T(8,128)(2,1)S(1)}, u32[]{:S(2)}, u32[]{:S(2)}) collective-permute-start(bf16[64,1024]{1,0:T(8,128)(2,1)S(1)} %maximum_select_fusion.3), channel_id=1, source_target_pairs={{0,64},{16,80},{32,96},{48,112},{64,0},{80,16},{96,32},{112,48},{1... | collective-permute-start | bytes 393224 | tf_op jit(solution)/shard_map/ppermute | solution.py:137
  65.0 2.5 %collective-permute-done.5 = f32[128,128]{1,0:T(8,128)S(1)} collective-permute-done((f32[128,128]{1,0:T(8,128)S(1)}, f32[128,128]{1,0:T(8,128)S(1)}, u32[]{:S(2)}, u32[]{:S(2)}) %collective-permute-start.5) | collective-permute-done | bytes 65568 | tf_op jit(solution)/shard_map/ppermute | solution.py:111
  67.4 0.8 collective-permute-start.8
  68.3 0.7 collective-permute-start.7
  69.0 0.7 collective-permute-start.6
  69.7 1.5 convolution_subtract_fusion.1
  71.4 1.3 collective-permute-start.11
  72.7 0.7 collective-permute-start.10
  73.3 0.7 collective-permute-start.9
  74.1 0.4 collective-permute-start.1
  74.4 4.0 %collective-permute-done.11 = f32[128,128]{1,0:T(8,128)S(1)} collective-permute-done((f32[128,128]{1,0:T(8,128)S(1)}, f32[128,128]{1,0:T(8,128)S(1)}, u32[]{:S(2)}, u32[]{:S(2)}) %collective-permute-start.11) | collective-permute-done | bytes 65568 | tf_op jit(solution)/shard_map/ppermute | solution.py:99
  78.4 1.1 fusion.2
  79.9 5.0 %collective-permute-start.2 = (f32[1,16,1024]{2,1,0:T(8,128)S(1)}, f32[1,16,1024]{2,1,0:T(8,128)S(1)}, u32[]{:S(2)}, u32[]{:S(2)}) collective-permute-start(f32[1,16,1024]{2,1,0:T(8,128)S(1)} %slice_select_fusion.8), channel_id=1, source_target_pairs={{0,16},{16,0},{32,48},{48,32},{64,80},{80,64},{96,112},{112,96},{1... | collective-permute-start | bytes 196616 | tf_op jit(solution)/shard_map/ppermute | solution.py:127
  85.2 0.6 collective-permute-done.2
  86.0 1.0 convolution_convert_fusion
  87.0 0.7 collective-permute-start.20
  87.7 0.7 collective-permute-start.19
  88.4 0.7 collective-permute-start.18
  89.1 0.8 slice.137.x_ref
  89.9 20.5 %shard_map.138 = bf16[2048,128]{1,0:T(8,128)(2,1)} custom-call(bf16[2048,128]{1,0:T(8,128)(2,1)} %slice.137.x_ref), custom_call_target="tpu_custom_call" | custom-call | tf_op jit(solution)/shard_map/pallas_call | solution.py:77
  110.4 3.1 %fusion.62 = f32[128,1024]{1,0:T(8,128)S(1)} fusion(bf16[2048,128]{1,0:T(8,128)(2,1)} %shard_map.138, bf16[2048,1024]{1,0:T(8,128)(2,1)} %param.12), kind=kOutput, calls=%fused_computation.109 | convolution fusion | flops 536870912 | bytes 5242880 | tf_op jit(solution)/shard_map/dot_general | solution.py:243
  113.6 4.7 %convolution_subtract_fusion = bf16[2048,1024]{1,0:T(8,128)(2,1)S(1)} fusion(f32[2048,1024]{1,0:T(8,128)} %param.17, bf16[2048,128]{1,0:T(8,128)(2,1)S(1)} %copy-done.1, bf16[2048,128]{1,0:T(8,128)(2,1)S(1)} %copy-done, bf16[128,1024]{1,0:T(8,128)(2,1)S(1)} %maximum_select_fusion.1, bf16[128,1024]{1,0:T(8,128)(2,1)S(1)} %maximum_select_fusion), kind=kOutput, calls=%fused_computation.1 | convolution fusion | flops 1081081856 | bytes 14155776 | tf_op jit(solution)/shard_map/dot_general | solution.py:236
  118.5 0.4 slice.197
  118.9 2.6 %pad_maximum_fusion = bf16[2048,1024]{1,0:T(8,128)(2,1)} fusion(bf16[2048,128]{1,0:T(8,128)(2,1)S(1)} %fusion.7, bf16[2048,896]{1,0:T(8,128)(2,1)S(1)} %slice.197), kind=kLoop, calls=%fused_computation.2 | loop fusion | flops 8388608 | bytes 8388608 | tf_op jit(solution)/shard_map/concatenate | solution.py:253
  121.6 1.4 collective-permute-start.23
  123.0 0.7 collective-permute-start.22
  123.7 0.7 collective-permute-start.21
  124.4 1.4 fusion.15
  125.8 1.5 collective-permute-done.23
  127.5 4.4 %collective-permute-start.27 = (f32[128,128]{1,0:T(8,128)S(1)}, f32[128,128]{1,0:T(8,128)S(1)}, u32[]{:S(2)}, u32[]{:S(2)}) collective-permute-start(f32[128,128]{1,0:T(8,128)S(1)} %convolution_add_fusion.1), channel_id=1, source_target_pairs={{0,16},{16,0},{32,48},{48,32},{64,80},{80,64},{96,112},{112,96},{1... | collective-permute-start | bytes 196616 | tf_op jit(solution)/shard_map/ppermute | solution.py:111
  132.2 0.6 collective-permute-done.27
  133.0 3.0 %collective-permute-done.28 = f32[128,128]{1,0:T(8,128)S(1)} collective-permute-done((f32[128,128]{1,0:T(8,128)S(1)}, f32[128,128]{1,0:T(8,128)S(1)}, u32[]{:S(2)}, u32[]{:S(2)}) %collective-permute-start.28) | collective-permute-done | bytes 65568 | tf_op jit(solution)/shard_map/ppermute | solution.py:111
  136.0 0.6 collective-permute-start.29
  136.6 2.5 %collective-permute-start.24 = (f32[4,16,1024]{2,1,0:T(8,128)S(1)}, f32[4,16,1024]{2,1,0:T(8,128)S(1)}, u32[]{:S(2)}, u32[]{:S(2)}) collective-permute-start(f32[4,16,1024]{2,1,0:T(8,128)S(1)} %bitcast.63), channel_id=1, source_target_pairs={{0,64},{16,80},{32,96},{48,112},{64,0},{80,16},{96,32},{112,48},{1... | collective-permute-start | bytes 786440 | tf_op jit(solution)/shard_map/ppermute | solution.py:127
  139.1 1.6 collective-permute-done.29
  140.7 0.7 collective-permute-start.32
  141.4 0.7 collective-permute-start.31
  142.1 0.7 collective-permute-start.30
  142.7 0.6 pad_maximum_fusion.2
  143.4 1.3 collective-permute-start.35
  144.7 0.7 collective-permute-start.34
  145.4 0.7 collective-permute-start.33
  146.1 0.5 collective-permute-start.25
  146.6 6.8 %collective-permute-done.35 = f32[128,128]{1,0:T(8,128)S(1)} collective-permute-done((f32[128,128]{1,0:T(8,128)S(1)}, f32[128,128]{1,0:T(8,128)S(1)}, u32[]{:S(2)}, u32[]{:S(2)}) %collective-permute-start.35) | collective-permute-done | bytes 65568 | tf_op jit(solution)/shard_map/ppermute | solution.py:99
  154.1 5.5 %collective-permute-start.26 = (f32[1,16,1024]{2,1,0:T(8,128)S(1)}, f32[1,16,1024]{2,1,0:T(8,128)S(1)}, u32[]{:S(2)}, u32[]{:S(2)}) collective-permute-start(f32[1,16,1024]{2,1,0:T(8,128)S(1)} %slice_select_fusion.7), channel_id=1, source_target_pairs={{0,16},{16,0},{32,48},{48,32},{64,80},{80,64},{96,112},{112,96},{1... | collective-permute-start | bytes 196616 | tf_op jit(solution)/shard_map/ppermute | solution.py:127
  159.9 0.6 collective-permute-done.26
  160.7 0.6 pad_maximum_fusion.1
  (98 shorter events, 4.2 us)
Async XLA Ops:
  0.6 55.3 %collective-permute-start.15 = (bf16[16,1024]{1,0:T(8,128)(2,1)}, bf16[16,1024]{1,0:T(8,128)(2,1)S(1)}, u32[]{:S(2)}, u32[]{:S(2)}) collective-permute-start(bf16[16,1024]{1,0:T(8,128)(2,1)} %param.13), channel_id=1, source_target_pairs={{0,16},{16,0},{32,48},{48,32},{64,80},{80,64},{96,112},{112,96},{1... | collective-permute-start | bytes 98312 | tf_op jit(solution)/shard_map/ppermute | solution.py:137
  2.1 53.4 %collective-permute-start.12 = (bf16[16,1024]{1,0:T(8,128)(2,1)}, bf16[16,1024]{1,0:T(8,128)(2,1)S(1)}, u32[]{:S(2)}, u32[]{:S(2)}) collective-permute-start(bf16[16,1024]{1,0:T(8,128)(2,1)} %param.14), channel_id=1, source_target_pairs={{0,16},{16,0},{32,48},{48,32},{64,80},{80,64},{96,112},{112,96},{1... | collective-permute-start | bytes 98312 | tf_op jit(solution)/shard_map/ppermute | solution.py:137
  16.2 29.2 %copy-start.3 = (f32[128,128]{1,0:T(8,128)S(1)}, f32[128,128]{1,0:T(8,128)}, u32[]{:S(2)}) copy-start(f32[128,128]{1,0:T(8,128)} %param.15) | copy-start | bytes 196612
  16.2 39.3 %copy-start.4 = (bf16[16,1024]{1,0:T(8,128)(2,1)S(1)}, bf16[16,1024]{1,0:T(8,128)(2,1)}, u32[]{:S(2)}) copy-start(bf16[16,1024]{1,0:T(8,128)(2,1)} %param.14) | copy-start | bytes 98308
  34.6 21.4 %copy-start.10 = (bf16[16,1024]{1,0:T(8,128)(2,1)S(1)}, bf16[16,1024]{1,0:T(8,128)(2,1)}, u32[]{:S(2)}) copy-start(bf16[16,1024]{1,0:T(8,128)(2,1)} %param.13) | copy-start | bytes 98308
  36.1 21.1 %collective-permute-start.3 = (f32[128,128]{1,0:T(8,128)S(1)}, f32[128,128]{1,0:T(8,128)S(1)}, u32[]{:S(2)}, u32[]{:S(2)}) collective-permute-start(f32[128,128]{1,0:T(8,128)S(1)} %fusion.17), channel_id=1, source_target_pairs={{0,16},{16,0},{32,48},{48,32},{64,80},{80,64},{96,112},{112,96},{1... | collective-permute-start | bytes 196616 | tf_op jit(solution)/shard_map/ppermute | solution.py:111
  39.3 30.4 %copy-start = (bf16[2048,128]{1,0:T(8,128)(2,1)S(1)}, bf16[2048,128]{1,0:T(8,128)(2,1)}, u32[]{:S(2)}) copy-start(bf16[2048,128]{1,0:T(8,128)(2,1)} %shard_map.137) | copy-start | bytes 1572868
  42.5 36.0 %copy-start.2 = (f32[128,128]{1,0:T(8,128)S(1)}, f32[128,128]{1,0:T(8,128)}, u32[]{:S(2)}) copy-start(f32[128,128]{1,0:T(8,128)} %param.16) | copy-start | bytes 196612
  42.5 31.5 %collective-permute-start = (f32[4,16,1024]{2,1,0:T(8,128)S(1)}, f32[4,16,1024]{2,1,0:T(8,128)S(1)}, u32[]{:S(2)}, u32[]{:S(2)}) collective-permute-start(f32[4,16,1024]{2,1,0:T(8,128)S(1)} %bitcast.62), channel_id=1, source_target_pairs={{0,64},{16,80},{32,96},{48,112},{64,0},{80,16},{96,32},{112,48},{1... | collective-permute-start | bytes 786440 | tf_op jit(solution)/shard_map/ppermute | solution.py:127
  55.6 30.3 %copy-start.7 = (f32[16,1024]{1,0:T(8,128)S(1)}, f32[16,1024]{1,0:T(8,128)}, u32[]{:S(2)}) copy-start(f32[16,1024]{1,0:T(8,128)} %param.19) | copy-start | bytes 196612
  55.6 3.2 %collective-permute-start.13 = (bf16[32,1024]{1,0:T(8,128)(2,1)S(1)}, bf16[32,1024]{1,0:T(8,128)(2,1)S(1)}, u32[]{:S(2)}, u32[]{:S(2)}) collective-permute-start(bf16[32,1024]{1,0:T(8,128)(2,1)S(1)} %maximum_select_fusion.4), channel_id=1, source_target_pairs={{0,32},{16,48},{32,0},{48,16},{64,96},{80,112},{96,64},{112,80},{1... | collective-permute-start | bytes 196616 | tf_op jit(solution)/shard_map/ppermute | solution.py:137
  56.0 6.3 %collective-permute-start.16 = (bf16[32,1024]{1,0:T(8,128)(2,1)S(1)}, bf16[32,1024]{1,0:T(8,128)(2,1)S(1)}, u32[]{:S(2)}, u32[]{:S(2)}) collective-permute-start(bf16[32,1024]{1,0:T(8,128)(2,1)S(1)} %maximum_select_fusion.5), channel_id=1, source_target_pairs={{0,32},{16,48},{32,0},{48,16},{64,96},{80,112},{96,64},{112,80},{1... | collective-permute-start | bytes 196616 | tf_op jit(solution)/shard_map/ppermute | solution.py:137
  57.2 4.6 %collective-permute-start.4 = (f32[128,128]{1,0:T(8,128)S(1)}, f32[128,128]{1,0:T(8,128)S(1)}, u32[]{:S(2)}, u32[]{:S(2)}) collective-permute-start(f32[128,128]{1,0:T(8,128)S(1)} %add.117), channel_id=1, source_target_pairs={{0,32},{16,48},{32,0},{48,16},{64,96},{80,112},{96,64},{112,80},{1... | collective-permute-start | bytes 196616 | tf_op jit(solution)/shard_map/ppermute | solution.py:111
  58.8 10.2 %collective-permute-start.14 = (bf16[64,1024]{1,0:T(8,128)(2,1)S(1)}, bf16[64,1024]{1,0:T(8,128)(2,1)S(1)}, u32[]{:S(2)}, u32[]{:S(2)}) collective-permute-start(bf16[64,1024]{1,0:T(8,128)(2,1)S(1)} %maximum_select_fusion.2), channel_id=1, source_target_pairs={{0,64},{16,80},{32,96},{48,112},{64,0},{80,16},{96,32},{112,48},{1... | collective-permute-start | bytes 393224 | tf_op jit(solution)/shard_map/ppermute | solution.py:137
  61.8 5.6 %collective-permute-start.5 = (f32[128,128]{1,0:T(8,128)S(1)}, f32[128,128]{1,0:T(8,128)S(1)}, u32[]{:S(2)}, u32[]{:S(2)}) collective-permute-start(f32[128,128]{1,0:T(8,128)S(1)} %add.118), channel_id=1, source_target_pairs={{0,64},{16,80},{32,96},{48,112},{64,0},{80,16},{96,32},{112,48},{1... | collective-permute-start | bytes 196616 | tf_op jit(solution)/shard_map/ppermute | solution.py:111
  62.4 8.9 %collective-permute-start.17 = (bf16[64,1024]{1,0:T(8,128)(2,1)S(1)}, bf16[64,1024]{1,0:T(8,128)(2,1)S(1)}, u32[]{:S(2)}, u32[]{:S(2)}) collective-permute-start(bf16[64,1024]{1,0:T(8,128)(2,1)S(1)} %maximum_select_fusion.3), channel_id=1, source_target_pairs={{0,64},{16,80},{32,96},{48,112},{64,0},{80,16},{96,32},{112,48},{1... | collective-permute-start | bytes 393224 | tf_op jit(solution)/shard_map/ppermute | solution.py:137
  67.4 3.9 %collective-permute-start.8 = (f32[128,128]{1,0:T(8,128)S(1)}, f32[128,128]{1,0:T(8,128)S(1)}, u32[]{:S(2)}, u32[]{:S(2)}) collective-permute-start(f32[128,128]{1,0:T(8,128)S(1)} %add.119), channel_id=1, source_target_pairs={{15,12},{31,28},{47,44},{63,60},{79,76},{95,92},{111,108},{127,124}} | collective-permute-start | bytes 196616 | tf_op jit(solution)/shard_map/ppermute | solution.py:99
  68.3 3.0 %collective-permute-start.7 = (f32[128,128]{1,0:T(8,128)S(1)}, f32[128,128]{1,0:T(8,128)S(1)}, u32[]{:S(2)}, u32[]{:S(2)}) collective-permute-start(f32[128,128]{1,0:T(8,128)S(1)} %add.119), channel_id=1, source_target_pairs={{15,13},{31,29},{47,45},{63,61},{79,77},{95,93},{111,109},{127,125}} | collective-permute-start | bytes 196616 | tf_op jit(solution)/shard_map/ppermute | solution.py:99
  69.0 2.4 %collective-permute-start.6 = (f32[128,128]{1,0:T(8,128)S(1)}, f32[128,128]{1,0:T(8,128)S(1)}, u32[]{:S(2)}, u32[]{:S(2)}) collective-permute-start(f32[128,128]{1,0:T(8,128)S(1)} %add.119), channel_id=1, source_target_pairs={{15,14},{31,30},{47,46},{63,62},{79,78},{95,94},{111,110},{127,126}} | collective-permute-start | bytes 196616 | tf_op jit(solution)/shard_map/ppermute | solution.py:99
  71.4 7.1 %collective-permute-start.11 = (f32[128,128]{1,0:T(8,128)S(1)}, f32[128,128]{1,0:T(8,128)S(1)}, u32[]{:S(2)}, u32[]{:S(2)}) collective-permute-start(f32[128,128]{1,0:T(8,128)S(1)} %add_select_fusion.1), channel_id=1, source_target_pairs={{15,3},{14,2},{13,1},{12,0},{31,19},{30,18},{29,17},{28,16},{47,35... | collective-permute-start | bytes 196616 | tf_op jit(solution)/shard_map/ppermute | solution.py:99
  72.7 5.8 %collective-permute-start.10 = (f32[128,128]{1,0:T(8,128)S(1)}, f32[128,128]{1,0:T(8,128)S(1)}, u32[]{:S(2)}, u32[]{:S(2)}) collective-permute-start(f32[128,128]{1,0:T(8,128)S(1)} %add_select_fusion.1), channel_id=1, source_target_pairs={{15,7},{14,6},{13,5},{12,4},{31,23},{30,22},{29,21},{28,20},{47,39... | collective-permute-start | bytes 196616 | tf_op jit(solution)/shard_map/ppermute | solution.py:99
  73.3 5.1 %collective-permute-start.9 = (f32[128,128]{1,0:T(8,128)S(1)}, f32[128,128]{1,0:T(8,128)S(1)}, u32[]{:S(2)}, u32[]{:S(2)}) collective-permute-start(f32[128,128]{1,0:T(8,128)S(1)} %add_select_fusion.1), channel_id=1, source_target_pairs={{15,11},{14,10},{13,9},{12,8},{31,27},{30,26},{29,25},{28,24},{47,... | collective-permute-start | bytes 196616 | tf_op jit(solution)/shard_map/ppermute | solution.py:99
  74.1 5.8 %collective-permute-start.1 = (f32[2,16,1024]{2,1,0:T(8,128)S(1)}, f32[2,16,1024]{2,1,0:T(8,128)S(1)}, u32[]{:S(2)}, u32[]{:S(2)}) collective-permute-start(f32[2,16,1024]{2,1,0:T(8,128)S(1)} %slice_select_fusion.6), channel_id=1, source_target_pairs={{0,32},{16,48},{32,0},{48,16},{64,96},{80,112},{96,64},{112,80},{1... | collective-permute-start | bytes 393224 | tf_op jit(solution)/shard_map/ppermute | solution.py:127
  79.9 5.9 %collective-permute-start.2 = (f32[1,16,1024]{2,1,0:T(8,128)S(1)}, f32[1,16,1024]{2,1,0:T(8,128)S(1)}, u32[]{:S(2)}, u32[]{:S(2)}) collective-permute-start(f32[1,16,1024]{2,1,0:T(8,128)S(1)} %slice_select_fusion.8), channel_id=1, source_target_pairs={{0,16},{16,0},{32,48},{48,32},{64,80},{80,64},{96,112},{112,96},{1... | collective-permute-start | bytes 196616 | tf_op jit(solution)/shard_map/ppermute | solution.py:127
  85.1 28.4 %copy-start.5 = (f32[128,128]{1,0:T(8,128)}, f32[128,128]{1,0:T(8,128)S(1)}, u32[]{:S(2)}) copy-start(f32[128,128]{1,0:T(8,128)S(1)} %get-tuple-element.10) | copy-start | bytes 196612
  87.0 34.5 %collective-permute-start.20 = (bf16[16,128]{1,0:T(8,128)(2,1)S(1)}, bf16[16,128]{1,0:T(8,128)(2,1)S(1)}, u32[]{:S(2)}, u32[]{:S(2)}) collective-permute-start(bf16[16,128]{1,0:T(8,128)(2,1)S(1)} %slice.140), channel_id=1, source_target_pairs={{14,13},{30,29},{46,45},{62,61},{78,77},{94,93},{110,109},{126,125}} | collective-permute-start | bytes 12296 | tf_op jit(solution)/shard_map/ppermute | solution.py:99
  87.7 33.8 %collective-permute-start.19 = (bf16[16,128]{1,0:T(8,128)(2,1)S(1)}, bf16[16,128]{1,0:T(8,128)(2,1)S(1)}, u32[]{:S(2)}, u32[]{:S(2)}) collective-permute-start(bf16[16,128]{1,0:T(8,128)(2,1)S(1)} %slice.140), channel_id=1, source_target_pairs={{14,12},{30,28},{46,44},{62,60},{78,76},{94,92},{110,108},{126,124}} | collective-permute-start | bytes 12296 | tf_op jit(solution)/shard_map/ppermute | solution.py:99
  88.4 33.2 %collective-permute-start.18 = (bf16[16,128]{1,0:T(8,128)(2,1)S(1)}, bf16[16,128]{1,0:T(8,128)(2,1)S(1)}, u32[]{:S(2)}, u32[]{:S(2)}) collective-permute-start(bf16[16,128]{1,0:T(8,128)(2,1)S(1)} %slice.140), channel_id=1, source_target_pairs={{14,15},{30,31},{46,47},{62,63},{78,79},{94,95},{110,111},{126,127}} | collective-permute-start | bytes 12296 | tf_op jit(solution)/shard_map/ppermute | solution.py:99
  110.4 3.2 %copy-start.1 = (bf16[2048,128]{1,0:T(8,128)(2,1)S(1)}, bf16[2048,128]{1,0:T(8,128)(2,1)}, u32[]{:S(2)}) copy-start(bf16[2048,128]{1,0:T(8,128)(2,1)} %shard_map.138) | copy-start | bytes 1572868
  121.6 31.9 %copy-start.9 = (f32[128,128]{1,0:T(8,128)S(1)}, f32[128,128]{1,0:T(8,128)}, u32[]{:S(2)}) copy-start(f32[128,128]{1,0:T(8,128)} %param.20) | copy-start | bytes 196612
  121.6 38.9 %copy-start.8 = (f32[16,1024]{1,0:T(8,128)S(1)}, f32[16,1024]{1,0:T(8,128)}, u32[]{:S(2)}) copy-start(f32[16,1024]{1,0:T(8,128)} %param.18) | copy-start | bytes 196612
  121.6 5.7 %collective-permute-start.23 = (bf16[16,128]{1,0:T(8,128)(2,1)S(1)}, bf16[16,128]{1,0:T(8,128)(2,1)S(1)}, u32[]{:S(2)}, u32[]{:S(2)}) collective-permute-start(bf16[16,128]{1,0:T(8,128)(2,1)S(1)} %add_select_fusion.3), channel_id=1, source_target_pairs={{14,2},{15,3},{12,0},{13,1},{30,18},{31,19},{28,16},{29,17},{46,34... | collective-permute-start | bytes 12296 | tf_op jit(solution)/shard_map/ppermute | solution.py:99
  123.0 4.3 %collective-permute-start.22 = (bf16[16,128]{1,0:T(8,128)(2,1)S(1)}, bf16[16,128]{1,0:T(8,128)(2,1)S(1)}, u32[]{:S(2)}, u32[]{:S(2)}) collective-permute-start(bf16[16,128]{1,0:T(8,128)(2,1)S(1)} %add_select_fusion.3), channel_id=1, source_target_pairs={{14,6},{15,7},{12,4},{13,5},{30,22},{31,23},{28,20},{29,21},{46,38... | collective-permute-start | bytes 12296 | tf_op jit(solution)/shard_map/ppermute | solution.py:99
  123.7 3.6 %collective-permute-start.21 = (bf16[16,128]{1,0:T(8,128)(2,1)S(1)}, bf16[16,128]{1,0:T(8,128)(2,1)S(1)}, u32[]{:S(2)}, u32[]{:S(2)}) collective-permute-start(bf16[16,128]{1,0:T(8,128)(2,1)S(1)} %add_select_fusion.3), channel_id=1, source_target_pairs={{14,10},{15,11},{12,8},{13,9},{30,26},{31,27},{28,24},{29,25},{46,... | collective-permute-start | bytes 12296 | tf_op jit(solution)/shard_map/ppermute | solution.py:99
  127.5 5.3 %collective-permute-start.27 = (f32[128,128]{1,0:T(8,128)S(1)}, f32[128,128]{1,0:T(8,128)S(1)}, u32[]{:S(2)}, u32[]{:S(2)}) collective-permute-start(f32[128,128]{1,0:T(8,128)S(1)} %convolution_add_fusion.1), channel_id=1, source_target_pairs={{0,16},{16,0},{32,48},{48,32},{64,80},{80,64},{96,112},{112,96},{1... | collective-permute-start | bytes 196616 | tf_op jit(solution)/shard_map/ppermute | solution.py:111
  132.8 3.2 %collective-permute-start.28 = (f32[128,128]{1,0:T(8,128)S(1)}, f32[128,128]{1,0:T(8,128)S(1)}, u32[]{:S(2)}, u32[]{:S(2)}) collective-permute-start(f32[128,128]{1,0:T(8,128)S(1)} %add.135), channel_id=1, source_target_pairs={{0,32},{16,48},{32,0},{48,16},{64,96},{80,112},{96,64},{112,80},{1... | collective-permute-start | bytes 196616 | tf_op jit(solution)/shard_map/ppermute | solution.py:111
  136.0 4.7 %collective-permute-start.29 = (f32[128,128]{1,0:T(8,128)S(1)}, f32[128,128]{1,0:T(8,128)S(1)}, u32[]{:S(2)}, u32[]{:S(2)}) collective-permute-start(f32[128,128]{1,0:T(8,128)S(1)} %add.136), channel_id=1, source_target_pairs={{0,64},{16,80},{32,96},{48,112},{64,0},{80,16},{96,32},{112,48},{1... | collective-permute-start | bytes 196616 | tf_op jit(solution)/shard_map/ppermute | solution.py:111
  136.6 9.4 %collective-permute-start.24 = (f32[4,16,1024]{2,1,0:T(8,128)S(1)}, f32[4,16,1024]{2,1,0:T(8,128)S(1)}, u32[]{:S(2)}, u32[]{:S(2)}) collective-permute-start(f32[4,16,1024]{2,1,0:T(8,128)S(1)} %bitcast.63), channel_id=1, source_target_pairs={{0,64},{16,80},{32,96},{48,112},{64,0},{80,16},{96,32},{112,48},{1... | collective-permute-start | bytes 786440 | tf_op jit(solution)/shard_map/ppermute | solution.py:127
  140.7 2.7 %collective-permute-start.32 = (f32[128,128]{1,0:T(8,128)S(1)}, f32[128,128]{1,0:T(8,128)S(1)}, u32[]{:S(2)}, u32[]{:S(2)}) collective-permute-start(f32[128,128]{1,0:T(8,128)S(1)} %add.137), channel_id=1, source_target_pairs={{14,13},{30,29},{46,45},{62,61},{78,77},{94,93},{110,109},{126,125}} | collective-permute-start | bytes 196616 | tf_op jit(solution)/shard_map/ppermute | solution.py:99
  141.4 2.0 %collective-permute-start.31 = (f32[128,128]{1,0:T(8,128)S(1)}, f32[128,128]{1,0:T(8,128)S(1)}, u32[]{:S(2)}, u32[]{:S(2)}) collective-permute-start(f32[128,128]{1,0:T(8,128)S(1)} %add.137), channel_id=1, source_target_pairs={{14,12},{30,28},{46,44},{62,60},{78,76},{94,92},{110,108},{126,124}} | collective-permute-start | bytes 196616 | tf_op jit(solution)/shard_map/ppermute | solution.py:99
  142.1 1.3 collective-permute-start.30
  143.4 10.0 %collective-permute-start.35 = (f32[128,128]{1,0:T(8,128)S(1)}, f32[128,128]{1,0:T(8,128)S(1)}, u32[]{:S(2)}, u32[]{:S(2)}) collective-permute-start(f32[128,128]{1,0:T(8,128)S(1)} %add_select_fusion), channel_id=1, source_target_pairs={{14,2},{15,3},{12,0},{13,1},{30,18},{31,19},{28,16},{29,17},{46,34... | collective-permute-start | bytes 196616 | tf_op jit(solution)/shard_map/ppermute | solution.py:99
  144.7 8.7 %collective-permute-start.34 = (f32[128,128]{1,0:T(8,128)S(1)}, f32[128,128]{1,0:T(8,128)S(1)}, u32[]{:S(2)}, u32[]{:S(2)}) collective-permute-start(f32[128,128]{1,0:T(8,128)S(1)} %add_select_fusion), channel_id=1, source_target_pairs={{14,6},{15,7},{12,4},{13,5},{30,22},{31,23},{28,20},{29,21},{46,38... | collective-permute-start | bytes 196616 | tf_op jit(solution)/shard_map/ppermute | solution.py:99
  145.4 8.0 %collective-permute-start.33 = (f32[128,128]{1,0:T(8,128)S(1)}, f32[128,128]{1,0:T(8,128)S(1)}, u32[]{:S(2)}, u32[]{:S(2)}) collective-permute-start(f32[128,128]{1,0:T(8,128)S(1)} %add_select_fusion), channel_id=1, source_target_pairs={{14,10},{15,11},{12,8},{13,9},{30,26},{31,27},{28,24},{29,25},{46,... | collective-permute-start | bytes 196616 | tf_op jit(solution)/shard_map/ppermute | solution.py:99
  146.1 7.9 %collective-permute-start.25 = (f32[2,16,1024]{2,1,0:T(8,128)S(1)}, f32[2,16,1024]{2,1,0:T(8,128)S(1)}, u32[]{:S(2)}, u32[]{:S(2)}) collective-permute-start(f32[2,16,1024]{2,1,0:T(8,128)S(1)} %slice_select_fusion.5), channel_id=1, source_target_pairs={{0,32},{16,48},{32,0},{48,16},{64,96},{80,112},{96,64},{112,80},{1... | collective-permute-start | bytes 393224 | tf_op jit(solution)/shard_map/ppermute | solution.py:127
  154.1 6.4 %collective-permute-start.26 = (f32[1,16,1024]{2,1,0:T(8,128)S(1)}, f32[1,16,1024]{2,1,0:T(8,128)S(1)}, u32[]{:S(2)}, u32[]{:S(2)}) collective-permute-start(f32[1,16,1024]{2,1,0:T(8,128)S(1)} %slice_select_fusion.7), channel_id=1, source_target_pairs={{0,16},{16,0},{32,48},{48,32},{64,80},{80,64},{96,112},{112,96},{1... | collective-permute-start | bytes 196616 | tf_op jit(solution)/shard_map/ppermute | solution.py:127
  159.8 1.6 copy-start.6

commit v12 on v11

--- a/solution.py
+++ b/solution.py
@@ -227,14 +227,16 @@
         partial_one = jnp.dot(
             head_rows.T, row_two[:, last:], preferred_element_type=jnp.float32
         ) + jnp.dot(tail_rows.T, trail[:, last:], preferred_element_type=jnp.float32)
-        seed_one = jnp.tril(adj_diag_one - summed_block(partial_one, root_one))
+        rows_one = butterfly_sum(partial_one, "row", n_row)
+        tail_late, rows_one = lax.optimization_barrier((tail_rows, rows_one))
+        seed_one = jnp.tril(adj_diag_one - tree_broadcast(rows_one, "col", n_col, root_one))
         grad_diag_one = block_adjoint(diag_one, inverse_one, seed_one)
         mirror_one = own_rows(grad_diag_one + grad_diag_one.T)
         rest_one = jnp.dot(mirror_one, full_one.astype(jnp.float32), precision=exact_mode)
         head_update = jnp.dot(head_rows, full_one, preferred_element_type=jnp.float32)
         two_left = adj_two - head_update
         trail_left = adj_trail - jnp.dot(
-            jnp.concatenate([solved_two, tail_rows], 1),
+            jnp.concatenate([solved_two, tail_late], 1),
             jnp.concatenate([full_two, full_one], 0),
             preferred_element_type=jnp.float32,
         )

time: 163 us -> 159 us (0.975)
  starting transfers between devices: 47 us -> 43.4 us
    ppermute x18, waiting for transfers between devices: 12.4 us -> 7.68 us  [tree_broadcast(): part = lax.ppermute(value, axis, pairs)]
    ppermute x6, starting transfers between devices: 16.6 us -> 13.1 us  [halving_scatter(): blocks = keep + lax.ppermute(send, axis, pairs)]
    ppermute x6, waiting for transfers between devices: 9.31 us -> 12.7 us  [butterfly_sum(): value = value + lax.ppermute(value, axis, pairs)]
  transfers between devices with their start and end apart: 36 -> 36, of which waited for: 11 -> 11; matrix products, arithmetic and copies ran while one was open for 30% -> 30% of each run, Pallas kernels for 24% -> 25%
where the time goes in v12:
time: 159 us; the launch traced here: 156 us
  starting transfers between devices  43.4 us (27%)
  Pallas kernels  38.9 us (24%)
  other arithmetic  25.2 us (16%)
  matrix products  23.4 us (15%)
  waiting for transfers between devices  22.7 us (14%)
    pallas_call x2, Pallas kernels, panel_broadcast(): pl.pallas_call(functools.partial(spread_kernel, root, size), out_shape=ja...  38.9 us
    another operation x4, other arithmetic, inverse_lower(): return lax.linalg.triangular_solve(block, ident, left_side=True, lower=True)  20.5 us
    ppermute x18, starting transfers between devices, tree_broadcast(): part = lax.ppermute(value, axis, pairs)  14 us
    ppermute x6, starting transfers between devices, halving_scatter(): blocks = keep + lax.ppermute(send, axis, pairs)  13.1 us
    ppermute x6, waiting for transfers between devices, butterfly_sum(): value = value + lax.ppermute(value, axis, pairs)  12.7 us
    ppermute x6, starting transfers between devices, butterfly_sum(): value = value + lax.ppermute(value, axis, pairs)  9.16 us
    ppermute x18, waiting for transfers between devices, tree_broadcast(): part = lax.ppermute(value, axis, pairs)  7.68 us
    ppermute x6, starting transfers between devices, doubling_gather(): other = lax.ppermute(value, axis, pairs)  7.06 us
  transfers between devices with their start and end apart: 36, of which 11 were waited for; matrix products, arithmetic and copies ran while one was open for 30% of the time, Pallas kernels for 25%

profile of v12, /device:TPU:1, one launch (start us, length us, event | category | flops | bytes accessed | tf_op | source)
XLA Modules:
  0.0 156.5 jit_solution(7621466170948795029)
XLA Ops:
  0.6 1.5 collective-permute-start.24
  2.2 0.8 select_bitcast_fusion.1
  3.1 9.8 %custom-call.4 = f32[1,128,128]{1,2,0:T(8,128)S(1)} custom-call(f32[1,128,128]{2,1,0:T(8,128)S(1)} %select_bitcast_fusion.1), custom_call_target="InvertDiagBlocksLowerTriangular" | custom-call | tf_op jit(solution)/shard_map/triangular_solve/custom-call.1 | solution.py:158
  13.2 3.0 %fusion.x_ref = bf16[2048,128]{1,0:T(8,128)(2,1)} fusion(f32[128,128]{1,0:T(8,128)S(1)} %fusion.21, f32[2048,1024]{1,0:T(8,128)} %param.17), kind=kOutput, calls=%fused_computation.6 | convolution fusion | flops 402915328 | bytes 1638400 | tf_op jit(solution)/shard_map/dot_general | solution.py:197
  16.2 18.4 %shard_map.137 = bf16[2048,128]{1,0:T(8,128)(2,1)} custom-call(bf16[2048,128]{1,0:T(8,128)(2,1)} %fusion.x_ref), custom_call_target="tpu_custom_call" | custom-call | tf_op jit(solution)/shard_map/pallas_call | solution.py:77
  34.6 1.5 fusion.17
  36.1 3.2 %collective-permute-start.3 = (f32[128,128]{1,0:T(8,128)S(1)}, f32[128,128]{1,0:T(8,128)S(1)}, u32[]{:S(2)}, u32[]{:S(2)}) collective-permute-start(f32[128,128]{1,0:T(8,128)S(1)} %fusion.17), channel_id=1, source_target_pairs={{0,16},{16,0},{32,48},{48,32},{64,80},{80,64},{96,112},{112,96},{1... | collective-permute-start | bytes 196616 | tf_op jit(solution)/shard_map/ppermute | solution.py:111
  39.3 3.1 %fusion.60 = f32[128,1024]{1,0:T(8,128)S(1)} fusion(bf16[2048,128]{1,0:T(8,128)(2,1)} %shard_map.137, bf16[2048,1024]{1,0:T(8,128)(2,1)} %param.12), kind=kOutput, calls=%fused_computation.107 | convolution fusion | flops 536870912 | bytes 5242880 | tf_op jit(solution)/shard_map/dot_general | solution.py:217
  42.5 2.8 %collective-permute-start = (f32[4,16,1024]{2,1,0:T(8,128)S(1)}, f32[4,16,1024]{2,1,0:T(8,128)S(1)}, u32[]{:S(2)}, u32[]{:S(2)}) collective-permute-start(f32[4,16,1024]{2,1,0:T(8,128)S(1)} %bitcast.62), channel_id=1, source_target_pairs={{0,64},{16,80},{32,96},{48,112},{64,0},{80,16},{96,32},{112,48},{1... | collective-permute-start | bytes 786440 | tf_op jit(solution)/shard_map/ppermute | solution.py:127
  45.4 9.8 %custom-call.5 = f32[1,128,128]{1,2,0:T(8,128)S(1)} custom-call(f32[1,128,128]{2,1,0:T(8,128)S(1)} %select_bitcast_fusion), custom_call_target="InvertDiagBlocksLowerTriangular" | custom-call | tf_op jit(solution)/shard_map/triangular_solve/custom-call.1 | solution.py:158
  55.6 0.4 collective-permute-start.13
  56.0 1.2 collective-permute-start.25
  57.2 0.4 collective-permute-start.4
  57.6 1.1 collective-permute-done.13
  58.8 1.2 collective-permute-start.14
  60.1 1.7 %collective-permute-done.4 = f32[128,128]{1,0:T(8,128)S(1)} collective-permute-done((f32[128,128]{1,0:T(8,128)S(1)}, f32[128,128]{1,0:T(8,128)S(1)}, u32[]{:S(2)}, u32[]{:S(2)}) %collective-permute-start.4) | collective-permute-done | bytes 65568 | tf_op jit(solution)/shard_map/ppermute | solution.py:111
  61.8 0.5 collective-permute-start.5
  62.4 2.6 %collective-permute-start.26 = (bf16[64,1024]{1,0:T(8,128)(2,1)S(1)}, bf16[64,1024]{1,0:T(8,128)(2,1)S(1)}, u32[]{:S(2)}, u32[]{:S(2)}) collective-permute-start(bf16[64,1024]{1,0:T(8,128)(2,1)S(1)} %maximum_select_fusion.3), channel_id=1, source_target_pairs={{0,64},{16,80},{32,96},{48,112},{64,0},{80,16},{96,32},{112,48},{1... | collective-permute-start | bytes 393224 | tf_op jit(solution)/shard_map/ppermute | solution.py:137
  65.0 2.5 %collective-permute-done.5 = f32[128,128]{1,0:T(8,128)S(1)} collective-permute-done((f32[128,128]{1,0:T(8,128)S(1)}, f32[128,128]{1,0:T(8,128)S(1)}, u32[]{:S(2)}, u32[]{:S(2)}) %collective-permute-start.5) | collective-permute-done | bytes 65568 | tf_op jit(solution)/shard_map/ppermute | solution.py:111
  67.4 0.8 collective-permute-start.8
  68.3 0.7 collective-permute-start.7
  69.0 0.7 collective-permute-start.6
  69.7 1.5 convolution_subtract_fusion.1
  71.4 1.3 collective-permute-start.11
  72.7 0.7 collective-permute-start.10
  73.3 0.7 collective-permute-start.9
  74.1 0.4 collective-permute-start.1
  74.4 4.0 %collective-permute-done.11 = f32[128,128]{1,0:T(8,128)S(1)} collective-permute-done((f32[128,128]{1,0:T(8,128)S(1)}, f32[128,128]{1,0:T(8,128)S(1)}, u32[]{:S(2)}, u32[]{:S(2)}) %collective-permute-start.11) | collective-permute-done | bytes 65568 | tf_op jit(solution)/shard_map/ppermute | solution.py:99
  78.4 1.1 fusion.2
  79.9 5.0 %collective-permute-start.2 = (f32[1,16,1024]{2,1,0:T(8,128)S(1)}, f32[1,16,1024]{2,1,0:T(8,128)S(1)}, u32[]{:S(2)}, u32[]{:S(2)}) collective-permute-start(f32[1,16,1024]{2,1,0:T(8,128)S(1)} %slice_select_fusion.8), channel_id=1, source_target_pairs={{0,16},{16,0},{32,48},{48,32},{64,80},{80,64},{96,112},{112,96},{1... | collective-permute-start | bytes 196616 | tf_op jit(solution)/shard_map/ppermute | solution.py:127
  85.2 0.6 collective-permute-done.2
  86.1 1.0 convolution_convert_fusion
  87.0 0.7 collective-permute-start.17
  87.7 0.7 collective-permute-start.16
  88.4 0.7 collective-permute-start.15
  89.1 0.8 slice.137.x_ref
  89.9 20.5 %shard_map.138 = bf16[2048,128]{1,0:T(8,128)(2,1)} custom-call(bf16[2048,128]{1,0:T(8,128)(2,1)} %slice.137.x_ref), custom_call_target="tpu_custom_call" | custom-call | tf_op jit(solution)/shard_map/pallas_call | solution.py:77
  110.4 3.1 %fusion.62 = f32[128,1024]{1,0:T(8,128)S(1)} fusion(bf16[2048,128]{1,0:T(8,128)(2,1)} %shard_map.138, bf16[2048,1024]{1,0:T(8,128)(2,1)} %param.12), kind=kOutput, calls=%fused_computation.109 | convolution fusion | flops 536870912 | bytes 5242880 | tf_op jit(solution)/shard_map/dot_general | solution.py:245
  113.6 1.3 collective-permute-start.20
  114.9 0.7 collective-permute-start.19
  115.6 0.7 collective-permute-start.18
  116.2 1.4 fusion.15
  117.6 1.5 collective-permute-done.20
  119.4 4.4 %collective-permute-start.21 = (f32[128,128]{1,0:T(8,128)S(1)}, f32[128,128]{1,0:T(8,128)S(1)}, u32[]{:S(2)}, u32[]{:S(2)}) collective-permute-start(f32[128,128]{1,0:T(8,128)S(1)} %convolution_add_fusion.1), channel_id=1, source_target_pairs={{0,16},{16,0},{32,48},{48,32},{64,80},{80,64},{96,112},{112,96},{1... | collective-permute-start | bytes 196616 | tf_op jit(solution)/shard_map/ppermute | solution.py:111
  124.2 0.4 collective-permute-done.21
  124.8 1.1 collective-permute-start.27
  125.8 2.0 %collective-permute-done.22 = f32[128,128]{1,0:T(8,128)S(1)} collective-permute-done((f32[128,128]{1,0:T(8,128)S(1)}, f32[128,128]{1,0:T(8,128)S(1)}, u32[]{:S(2)}, u32[]{:S(2)}) %collective-permute-start.22) | collective-permute-done | bytes 65568 | tf_op jit(solution)/shard_map/ppermute | solution.py:111
  127.9 0.6 collective-permute-start.23
  128.5 0.6 pad_maximum_fusion.2
  129.1 6.0 %collective-permute-done.23 = f32[128,128]{1,0:T(8,128)S(1)} collective-permute-done((f32[128,128]{1,0:T(8,128)S(1)}, f32[128,128]{1,0:T(8,128)S(1)}, u32[]{:S(2)}, u32[]{:S(2)}) %collective-permute-start.23) | collective-permute-done | bytes 65568 | tf_op jit(solution)/shard_map/ppermute | solution.py:111
  135.2 0.7 collective-permute-start.32
  135.8 0.7 collective-permute-start.31
  136.5 0.7 collective-permute-start.30
  137.2 4.7 %convolution_subtract_fusion = bf16[2048,1024]{1,0:T(8,128)(2,1)S(1)} fusion(f32[2048,1024]{1,0:T(8,128)} %param.17, bf16[2048,128]{1,0:T(8,128)(2,1)S(1)} %copy-done.1, bf16[2048,128]{1,0:T(8,128)(2,1)S(1)} %copy-done, bf16[128,1024]{1,0:T(8,128)(2,1)S(1)} %maximum_select_fusion.1, bf16[128,1024]{1,0:T(8,128)(2,1)S(1)} %maximum_select_fusion), kind=kOutput, calls=%fused_computation.1 | convolution fusion | flops 1081081856 | bytes 14155776 | tf_op jit(solution)/shard_map/dot_general | solution.py:238
  142.1 0.4 slice.197
  142.6 2.6 %pad_maximum_fusion = bf16[2048,1024]{1,0:T(8,128)(2,1)} fusion(bf16[2048,128]{1,0:T(8,128)(2,1)S(1)} %fusion.7, bf16[2048,896]{1,0:T(8,128)(2,1)S(1)} %slice.197), kind=kLoop, calls=%fused_computation.2 | loop fusion | flops 8388608 | bytes 8388608 | tf_op jit(solution)/shard_map/concatenate | solution.py:255
  145.2 1.3 collective-permute-start.35
  146.5 0.7 collective-permute-start.34
  147.2 0.7 collective-permute-start.33
  148.0 1.3 collective-permute-start.28
  149.3 2.2 %collective-permute-done.35 = f32[128,128]{1,0:T(8,128)S(1)} collective-permute-done((f32[128,128]{1,0:T(8,128)S(1)}, f32[128,128]{1,0:T(8,128)S(1)}, u32[]{:S(2)}, u32[]{:S(2)}) %collective-permute-start.35) | collective-permute-done | bytes 65568 | tf_op jit(solution)/shard_map/ppermute | solution.py:99
  152.1 2.6 %collective-permute-start.29 = (f32[1,16,1024]{2,1,0:T(8,128)S(1)}, f32[1,16,1024]{2,1,0:T(8,128)S(1)}, u32[]{:S(2)}, u32[]{:S(2)}) collective-permute-start(f32[1,16,1024]{2,1,0:T(8,128)S(1)} %slice_select_fusion.7), channel_id=1, source_target_pairs={{0,16},{16,0},{32,48},{48,32},{64,80},{80,64},{96,112},{112,96},{1... | collective-permute-start | bytes 196616 | tf_op jit(solution)/shard_map/ppermute | solution.py:127
  155.0 0.6 collective-permute-done.29
  155.8 0.6 pad_maximum_fusion.1
  (98 shorter events, 4.2 us)
Async XLA Ops:
  0.6 55.3 %collective-permute-start.24 = (bf16[16,1024]{1,0:T(8,128)(2,1)}, bf16[16,1024]{1,0:T(8,128)(2,1)S(1)}, u32[]{:S(2)}, u32[]{:S(2)}) collective-permute-start(bf16[16,1024]{1,0:T(8,128)(2,1)} %param.13), channel_id=1, source_target_pairs={{0,16},{16,0},{32,48},{48,32},{64,80},{80,64},{96,112},{112,96},{1... | collective-permute-start | bytes 98312 | tf_op jit(solution)/shard_map/ppermute | solution.py:137
  2.1 53.4 %collective-permute-start.12 = (bf16[16,1024]{1,0:T(8,128)(2,1)}, bf16[16,1024]{1,0:T(8,128)(2,1)S(1)}, u32[]{:S(2)}, u32[]{:S(2)}) collective-permute-start(bf16[16,1024]{1,0:T(8,128)(2,1)} %param.14), channel_id=1, source_target_pairs={{0,16},{16,0},{32,48},{48,32},{64,80},{80,64},{96,112},{112,96},{1... | collective-permute-start | bytes 98312 | tf_op jit(solution)/shard_map/ppermute | solution.py:137
  16.2 29.2 %copy-start.3 = (f32[128,128]{1,0:T(8,128)S(1)}, f32[128,128]{1,0:T(8,128)}, u32[]{:S(2)}) copy-start(f32[128,128]{1,0:T(8,128)} %param.15) | copy-start | bytes 196612
  16.2 39.3 %copy-start.4 = (bf16[16,1024]{1,0:T(8,128)(2,1)S(1)}, bf16[16,1024]{1,0:T(8,128)(2,1)}, u32[]{:S(2)}) copy-start(bf16[16,1024]{1,0:T(8,128)(2,1)} %param.14) | copy-start | bytes 98308
  34.6 21.4 %copy-start.10 = (bf16[16,1024]{1,0:T(8,128)(2,1)S(1)}, bf16[16,1024]{1,0:T(8,128)(2,1)}, u32[]{:S(2)}) copy-start(bf16[16,1024]{1,0:T(8,128)(2,1)} %param.13) | copy-start | bytes 98308
  36.1 21.1 %collective-permute-start.3 = (f32[128,128]{1,0:T(8,128)S(1)}, f32[128,128]{1,0:T(8,128)S(1)}, u32[]{:S(2)}, u32[]{:S(2)}) collective-permute-start(f32[128,128]{1,0:T(8,128)S(1)} %fusion.17), channel_id=1, source_target_pairs={{0,16},{16,0},{32,48},{48,32},{64,80},{80,64},{96,112},{112,96},{1... | collective-permute-start | bytes 196616 | tf_op jit(solution)/shard_map/ppermute | solution.py:111
  39.3 30.4 %copy-start = (bf16[2048,128]{1,0:T(8,128)(2,1)S(1)}, bf16[2048,128]{1,0:T(8,128)(2,1)}, u32[]{:S(2)}) copy-start(bf16[2048,128]{1,0:T(8,128)(2,1)} %shard_map.137) | copy-start | bytes 1572868
  42.5 36.0 %copy-start.2 = (f32[128,128]{1,0:T(8,128)S(1)}, f32[128,128]{1,0:T(8,128)}, u32[]{:S(2)}) copy-start(f32[128,128]{1,0:T(8,128)} %param.16) | copy-start | bytes 196612
  42.5 31.5 %collective-permute-start = (f32[4,16,1024]{2,1,0:T(8,128)S(1)}, f32[4,16,1024]{2,1,0:T(8,128)S(1)}, u32[]{:S(2)}, u32[]{:S(2)}) collective-permute-start(f32[4,16,1024]{2,1,0:T(8,128)S(1)} %bitcast.62), channel_id=1, source_target_pairs={{0,64},{16,80},{32,96},{48,112},{64,0},{80,16},{96,32},{112,48},{1... | collective-permute-start | bytes 786440 | tf_op jit(solution)/shard_map/ppermute | solution.py:127
  55.6 30.3 %copy-start.7 = (f32[16,1024]{1,0:T(8,128)S(1)}, f32[16,1024]{1,0:T(8,128)}, u32[]{:S(2)}) copy-start(f32[16,1024]{1,0:T(8,128)} %param.19) | copy-start | bytes 196612
  55.6 3.2 %collective-permute-start.13 = (bf16[32,1024]{1,0:T(8,128)(2,1)S(1)}, bf16[32,1024]{1,0:T(8,128)(2,1)S(1)}, u32[]{:S(2)}, u32[]{:S(2)}) collective-permute-start(bf16[32,1024]{1,0:T(8,128)(2,1)S(1)} %maximum_select_fusion.4), channel_id=1, source_target_pairs={{0,32},{16,48},{32,0},{48,16},{64,96},{80,112},{96,64},{112,80},{1... | collective-permute-start | bytes 196616 | tf_op jit(solution)/shard_map/ppermute | solution.py:137
  56.0 6.3 %collective-permute-start.25 = (bf16[32,1024]{1,0:T(8,128)(2,1)S(1)}, bf16[32,1024]{1,0:T(8,128)(2,1)S(1)}, u32[]{:S(2)}, u32[]{:S(2)}) collective-permute-start(bf16[32,1024]{1,0:T(8,128)(2,1)S(1)} %maximum_select_fusion.5), channel_id=1, source_target_pairs={{0,32},{16,48},{32,0},{48,16},{64,96},{80,112},{96,64},{112,80},{1... | collective-permute-start | bytes 196616 | tf_op jit(solution)/shard_map/ppermute | solution.py:137
  57.2 4.6 %collective-permute-start.4 = (f32[128,128]{1,0:T(8,128)S(1)}, f32[128,128]{1,0:T(8,128)S(1)}, u32[]{:S(2)}, u32[]{:S(2)}) collective-permute-start(f32[128,128]{1,0:T(8,128)S(1)} %add.117), channel_id=1, source_target_pairs={{0,32},{16,48},{32,0},{48,16},{64,96},{80,112},{96,64},{112,80},{1... | collective-permute-start | bytes 196616 | tf_op jit(solution)/shard_map/ppermute | solution.py:111
  58.8 10.2 %collective-permute-start.14 = (bf16[64,1024]{1,0:T(8,128)(2,1)S(1)}, bf16[64,1024]{1,0:T(8,128)(2,1)S(1)}, u32[]{:S(2)}, u32[]{:S(2)}) collective-permute-start(bf16[64,1024]{1,0:T(8,128)(2,1)S(1)} %maximum_select_fusion.2), channel_id=1, source_target_pairs={{0,64},{16,80},{32,96},{48,112},{64,0},{80,16},{96,32},{112,48},{1... | collective-permute-start | bytes 393224 | tf_op jit(solution)/shard_map/ppermute | solution.py:137
  61.8 5.6 %collective-permute-start.5 = (f32[128,128]{1,0:T(8,128)S(1)}, f32[128,128]{1,0:T(8,128)S(1)}, u32[]{:S(2)}, u32[]{:S(2)}) collective-permute-start(f32[128,128]{1,0:T(8,128)S(1)} %add.118), channel_id=1, source_target_pairs={{0,64},{16,80},{32,96},{48,112},{64,0},{80,16},{96,32},{112,48},{1... | collective-permute-start | bytes 196616 | tf_op jit(solution)/shard_map/ppermute | solution.py:111
  62.4 8.9 %collective-permute-start.26 = (bf16[64,1024]{1,0:T(8,128)(2,1)S(1)}, bf16[64,1024]{1,0:T(8,128)(2,1)S(1)}, u32[]{:S(2)}, u32[]{:S(2)}) collective-permute-start(bf16[64,1024]{1,0:T(8,128)(2,1)S(1)} %maximum_select_fusion.3), channel_id=1, source_target_pairs={{0,64},{16,80},{32,96},{48,112},{64,0},{80,16},{96,32},{112,48},{1... | collective-permute-start | bytes 393224 | tf_op jit(solution)/shard_map/ppermute | solution.py:137
  67.4 3.9 %collective-permute-start.8 = (f32[128,128]{1,0:T(8,128)S(1)}, f32[128,128]{1,0:T(8,128)S(1)}, u32[]{:S(2)}, u32[]{:S(2)}) collective-permute-start(f32[128,128]{1,0:T(8,128)S(1)} %add.119), channel_id=1, source_target_pairs={{15,12},{31,28},{47,44},{63,60},{79,76},{95,92},{111,108},{127,124}} | collective-permute-start | bytes 196616 | tf_op jit(solution)/shard_map/ppermute | solution.py:99
  68.3 3.0 %collective-permute-start.7 = (f32[128,128]{1,0:T(8,128)S(1)}, f32[128,128]{1,0:T(8,128)S(1)}, u32[]{:S(2)}, u32[]{:S(2)}) collective-permute-start(f32[128,128]{1,0:T(8,128)S(1)} %add.119), channel_id=1, source_target_pairs={{15,13},{31,29},{47,45},{63,61},{79,77},{95,93},{111,109},{127,125}} | collective-permute-start | bytes 196616 | tf_op jit(solution)/shard_map/ppermute | solution.py:99
  69.0 2.4 %collective-permute-start.6 = (f32[128,128]{1,0:T(8,128)S(1)}, f32[128,128]{1,0:T(8,128)S(1)}, u32[]{:S(2)}, u32[]{:S(2)}) collective-permute-start(f32[128,128]{1,0:T(8,128)S(1)} %add.119), channel_id=1, source_target_pairs={{15,14},{31,30},{47,46},{63,62},{79,78},{95,94},{111,110},{127,126}} | collective-permute-start | bytes 196616 | tf_op jit(solution)/shard_map/ppermute | solution.py:99
  71.4 7.1 %collective-permute-start.11 = (f32[128,128]{1,0:T(8,128)S(1)}, f32[128,128]{1,0:T(8,128)S(1)}, u32[]{:S(2)}, u32[]{:S(2)}) collective-permute-start(f32[128,128]{1,0:T(8,128)S(1)} %add_select_fusion.1), channel_id=1, source_target_pairs={{15,3},{14,2},{13,1},{12,0},{31,19},{30,18},{29,17},{28,16},{47,35... | collective-permute-start | bytes 196616 | tf_op jit(solution)/shard_map/ppermute | solution.py:99
  72.7 5.8 %collective-permute-start.10 = (f32[128,128]{1,0:T(8,128)S(1)}, f32[128,128]{1,0:T(8,128)S(1)}, u32[]{:S(2)}, u32[]{:S(2)}) collective-permute-start(f32[128,128]{1,0:T(8,128)S(1)} %add_select_fusion.1), channel_id=1, source_target_pairs={{15,7},{14,6},{13,5},{12,4},{31,23},{30,22},{29,21},{28,20},{47,39... | collective-permute-start | bytes 196616 | tf_op jit(solution)/shard_map/ppermute | solution.py:99
  73.3 5.1 %collective-permute-start.9 = (f32[128,128]{1,0:T(8,128)S(1)}, f32[128,128]{1,0:T(8,128)S(1)}, u32[]{:S(2)}, u32[]{:S(2)}) collective-permute-start(f32[128,128]{1,0:T(8,128)S(1)} %add_select_fusion.1), channel_id=1, source_target_pairs={{15,11},{14,10},{13,9},{12,8},{31,27},{30,26},{29,25},{28,24},{47,... | collective-permute-start | bytes 196616 | tf_op jit(solution)/shard_map/ppermute | solution.py:99
  74.1 5.8 %collective-permute-start.1 = (f32[2,16,1024]{2,1,0:T(8,128)S(1)}, f32[2,16,1024]{2,1,0:T(8,128)S(1)}, u32[]{:S(2)}, u32[]{:S(2)}) collective-permute-start(f32[2,16,1024]{2,1,0:T(8,128)S(1)} %slice_select_fusion.6), channel_id=1, source_target_pairs={{0,32},{16,48},{32,0},{48,16},{64,96},{80,112},{96,64},{112,80},{1... | collective-permute-start | bytes 393224 | tf_op jit(solution)/shard_map/ppermute | solution.py:127
  79.9 5.9 %collective-permute-start.2 = (f32[1,16,1024]{2,1,0:T(8,128)S(1)}, f32[1,16,1024]{2,1,0:T(8,128)S(1)}, u32[]{:S(2)}, u32[]{:S(2)}) collective-permute-start(f32[1,16,1024]{2,1,0:T(8,128)S(1)} %slice_select_fusion.8), channel_id=1, source_target_pairs={{0,16},{16,0},{32,48},{48,32},{64,80},{80,64},{96,112},{112,96},{1... | collective-permute-start | bytes 196616 | tf_op jit(solution)/shard_map/ppermute | solution.py:127
  85.1 28.4 %copy-start.5 = (f32[128,128]{1,0:T(8,128)}, f32[128,128]{1,0:T(8,128)S(1)}, u32[]{:S(2)}) copy-start(f32[128,128]{1,0:T(8,128)S(1)} %get-tuple-element.14) | copy-start | bytes 196612
  87.0 26.5 %collective-permute-start.17 = (bf16[16,128]{1,0:T(8,128)(2,1)S(1)}, bf16[16,128]{1,0:T(8,128)(2,1)S(1)}, u32[]{:S(2)}, u32[]{:S(2)}) collective-permute-start(bf16[16,128]{1,0:T(8,128)(2,1)S(1)} %slice.138), channel_id=1, source_target_pairs={{14,13},{30,29},{46,45},{62,61},{78,77},{94,93},{110,109},{126,125}} | collective-permute-start | bytes 12296 | tf_op jit(solution)/shard_map/ppermute | solution.py:99
  87.7 25.8 %collective-permute-start.16 = (bf16[16,128]{1,0:T(8,128)(2,1)S(1)}, bf16[16,128]{1,0:T(8,128)(2,1)S(1)}, u32[]{:S(2)}, u32[]{:S(2)}) collective-permute-start(bf16[16,128]{1,0:T(8,128)(2,1)S(1)} %slice.138), channel_id=1, source_target_pairs={{14,12},{30,28},{46,44},{62,60},{78,76},{94,92},{110,108},{126,124}} | collective-permute-start | bytes 12296 | tf_op jit(solution)/shard_map/ppermute | solution.py:99
  88.4 25.2 %collective-permute-start.15 = (bf16[16,128]{1,0:T(8,128)(2,1)S(1)}, bf16[16,128]{1,0:T(8,128)(2,1)S(1)}, u32[]{:S(2)}, u32[]{:S(2)}) collective-permute-start(bf16[16,128]{1,0:T(8,128)(2,1)S(1)} %slice.138), channel_id=1, source_target_pairs={{14,15},{30,31},{46,47},{62,63},{78,79},{94,95},{110,111},{126,127}} | collective-permute-start | bytes 12296 | tf_op jit(solution)/shard_map/ppermute | solution.py:99
  110.4 5.9 %copy-start.1 = (bf16[2048,128]{1,0:T(8,128)(2,1)S(1)}, bf16[2048,128]{1,0:T(8,128)(2,1)}, u32[]{:S(2)}) copy-start(bf16[2048,128]{1,0:T(8,128)(2,1)} %shard_map.138) | copy-start | bytes 1572868
  113.6 5.6 %collective-permute-start.20 = (bf16[16,128]{1,0:T(8,128)(2,1)S(1)}, bf16[16,128]{1,0:T(8,128)(2,1)S(1)}, u32[]{:S(2)}, u32[]{:S(2)}) collective-permute-start(bf16[16,128]{1,0:T(8,128)(2,1)S(1)} %add_select_fusion.3), channel_id=1, source_target_pairs={{14,2},{15,3},{12,0},{13,1},{30,18},{31,19},{28,16},{29,17},{46,34... | collective-permute-start | bytes 12296 | tf_op jit(solution)/shard_map/ppermute | solution.py:99
  114.9 4.3 %collective-permute-start.19 = (bf16[16,128]{1,0:T(8,128)(2,1)S(1)}, bf16[16,128]{1,0:T(8,128)(2,1)S(1)}, u32[]{:S(2)}, u32[]{:S(2)}) collective-permute-start(bf16[16,128]{1,0:T(8,128)(2,1)S(1)} %add_select_fusion.3), channel_id=1, source_target_pairs={{14,6},{15,7},{12,4},{13,5},{30,22},{31,23},{28,20},{29,21},{46,38... | collective-permute-start | bytes 12296 | tf_op jit(solution)/shard_map/ppermute | solution.py:99
  115.6 3.6 %collective-permute-start.18 = (bf16[16,128]{1,0:T(8,128)(2,1)S(1)}, bf16[16,128]{1,0:T(8,128)(2,1)S(1)}, u32[]{:S(2)}, u32[]{:S(2)}) collective-permute-start(bf16[16,128]{1,0:T(8,128)(2,1)S(1)} %add_select_fusion.3), channel_id=1, source_target_pairs={{14,10},{15,11},{12,8},{13,9},{30,26},{31,27},{28,24},{29,25},{46,... | collective-permute-start | bytes 12296 | tf_op jit(solution)/shard_map/ppermute | solution.py:99
  119.4 5.3 %collective-permute-start.21 = (f32[128,128]{1,0:T(8,128)S(1)}, f32[128,128]{1,0:T(8,128)S(1)}, u32[]{:S(2)}, u32[]{:S(2)}) collective-permute-start(f32[128,128]{1,0:T(8,128)S(1)} %convolution_add_fusion.1), channel_id=1, source_target_pairs={{0,16},{16,0},{32,48},{48,32},{64,80},{80,64},{96,112},{112,96},{1... | collective-permute-start | bytes 196616 | tf_op jit(solution)/shard_map/ppermute | solution.py:111
  124.7 3.2 %collective-permute-start.22 = (f32[128,128]{1,0:T(8,128)S(1)}, f32[128,128]{1,0:T(8,128)S(1)}, u32[]{:S(2)}, u32[]{:S(2)}) collective-permute-start(f32[128,128]{1,0:T(8,128)S(1)} %add.131), channel_id=1, source_target_pairs={{0,32},{16,48},{32,0},{48,16},{64,96},{80,112},{96,64},{112,80},{1... | collective-permute-start | bytes 196616 | tf_op jit(solution)/shard_map/ppermute | solution.py:111
  124.8 23.1 %collective-permute-start.27 = (f32[4,16,1024]{2,1,0:T(8,128)S(1)}, f32[4,16,1024]{2,1,0:T(8,128)S(1)}, u32[]{:S(2)}, u32[]{:S(2)}) collective-permute-start(f32[4,16,1024]{2,1,0:T(8,128)S(1)} %bitcast.63), channel_id=1, source_target_pairs={{0,64},{16,80},{32,96},{48,112},{64,0},{80,16},{96,32},{112,48},{1... | collective-permute-start | bytes 786440 | tf_op jit(solution)/shard_map/ppermute | solution.py:127
  127.9 7.3 %collective-permute-start.23 = (f32[128,128]{1,0:T(8,128)S(1)}, f32[128,128]{1,0:T(8,128)S(1)}, u32[]{:S(2)}, u32[]{:S(2)}) collective-permute-start(f32[128,128]{1,0:T(8,128)S(1)} %add.132), channel_id=1, source_target_pairs={{0,64},{16,80},{32,96},{48,112},{64,0},{80,16},{96,32},{112,48},{1... | collective-permute-start | bytes 196616 | tf_op jit(solution)/shard_map/ppermute | solution.py:111
  135.2 10.0 %collective-permute-start.32 = (f32[128,128]{1,0:T(8,128)S(1)}, f32[128,128]{1,0:T(8,128)S(1)}, u32[]{:S(2)}, u32[]{:S(2)}) collective-permute-start(f32[128,128]{1,0:T(8,128)S(1)} %add.133), channel_id=1, source_target_pairs={{14,13},{30,29},{46,45},{62,61},{78,77},{94,93},{110,109},{126,125}} | collective-permute-start | bytes 196616 | tf_op jit(solution)/shard_map/ppermute | solution.py:99
  135.8 9.4 %collective-permute-start.31 = (f32[128,128]{1,0:T(8,128)S(1)}, f32[128,128]{1,0:T(8,128)S(1)}, u32[]{:S(2)}, u32[]{:S(2)}) collective-permute-start(f32[128,128]{1,0:T(8,128)S(1)} %add.133), channel_id=1, source_target_pairs={{14,12},{30,28},{46,44},{62,60},{78,76},{94,92},{110,108},{126,124}} | collective-permute-start | bytes 196616 | tf_op jit(solution)/shard_map/ppermute | solution.py:99
  136.5 8.7 %collective-permute-start.30 = (f32[128,128]{1,0:T(8,128)S(1)}, f32[128,128]{1,0:T(8,128)S(1)}, u32[]{:S(2)}, u32[]{:S(2)}) collective-permute-start(f32[128,128]{1,0:T(8,128)S(1)} %add.133), channel_id=1, source_target_pairs={{14,15},{30,31},{46,47},{62,63},{78,79},{94,95},{110,111},{126,127}} | collective-permute-start | bytes 196616 | tf_op jit(solution)/shard_map/ppermute | solution.py:99
  142.5 8.9 %copy-start.9 = (f32[128,128]{1,0:T(8,128)S(1)}, f32[128,128]{1,0:T(8,128)}, u32[]{:S(2)}) copy-start(f32[128,128]{1,0:T(8,128)} %param.20) | copy-start | bytes 196612
  142.5 13.0 %copy-start.8 = (f32[16,1024]{1,0:T(8,128)S(1)}, f32[16,1024]{1,0:T(8,128)}, u32[]{:S(2)}) copy-start(f32[16,1024]{1,0:T(8,128)} %param.18) | copy-start | bytes 196612
  145.2 6.2 %collective-permute-start.35 = (f32[128,128]{1,0:T(8,128)S(1)}, f32[128,128]{1,0:T(8,128)S(1)}, u32[]{:S(2)}, u32[]{:S(2)}) collective-permute-start(f32[128,128]{1,0:T(8,128)S(1)} %add_select_fusion), channel_id=1, source_target_pairs={{14,2},{15,3},{12,0},{13,1},{30,18},{31,19},{28,16},{29,17},{46,34... | collective-permute-start | bytes 196616 | tf_op jit(solution)/shard_map/ppermute | solution.py:99
  146.5 4.9 %collective-permute-start.34 = (f32[128,128]{1,0:T(8,128)S(1)}, f32[128,128]{1,0:T(8,128)S(1)}, u32[]{:S(2)}, u32[]{:S(2)}) collective-permute-start(f32[128,128]{1,0:T(8,128)S(1)} %add_select_fusion), channel_id=1, source_target_pairs={{14,6},{15,7},{12,4},{13,5},{30,22},{31,23},{28,20},{29,21},{46,38... | collective-permute-start | bytes 196616 | tf_op jit(solution)/shard_map/ppermute | solution.py:99
  147.2 4.3 %collective-permute-start.33 = (f32[128,128]{1,0:T(8,128)S(1)}, f32[128,128]{1,0:T(8,128)S(1)}, u32[]{:S(2)}, u32[]{:S(2)}) collective-permute-start(f32[128,128]{1,0:T(8,128)S(1)} %add_select_fusion), channel_id=1, source_target_pairs={{14,10},{15,11},{12,8},{13,9},{30,26},{31,27},{28,24},{29,25},{46,... | collective-permute-start | bytes 196616 | tf_op jit(solution)/shard_map/ppermute | solution.py:99
  148.0 4.1 %collective-permute-start.28 = (f32[2,16,1024]{2,1,0:T(8,128)S(1)}, f32[2,16,1024]{2,1,0:T(8,128)S(1)}, u32[]{:S(2)}, u32[]{:S(2)}) collective-permute-start(f32[2,16,1024]{2,1,0:T(8,128)S(1)} %slice_select_fusion.5), channel_id=1, source_target_pairs={{0,32},{16,48},{32,0},{48,16},{64,96},{80,112},{96,64},{112,80},{1... | collective-permute-start | bytes 393224 | tf_op jit(solution)/shard_map/ppermute | solution.py:127
  152.1 3.5 %collective-permute-start.29 = (f32[1,16,1024]{2,1,0:T(8,128)S(1)}, f32[1,16,1024]{2,1,0:T(8,128)S(1)}, u32[]{:S(2)}, u32[]{:S(2)}) collective-permute-start(f32[1,16,1024]{2,1,0:T(8,128)S(1)} %slice_select_fusion.7), channel_id=1, source_target_pairs={{0,16},{16,0},{32,48},{48,32},{64,80},{80,64},{96,112},{112,96},{1... | collective-permute-start | bytes 196616 | tf_op jit(solution)/shard_map/ppermute | solution.py:127
  154.9 1.6 %copy-start.6 = (f32[128,128]{1,0:T(8,128)}, f32[128,128]{1,0:T(8,128)S(1)}, u32[]{:S(2)}) copy-start(f32[128,128]{1,0:T(8,128)S(1)} %get-tuple-element.16) | copy-start | bytes 196612

commit v13 on v12

--- a/solution.py
+++ b/solution.py
@@ -242,7 +242,7 @@
         )
         crossed_one = halving_scatter(
             jnp.dot(head_rows.T, row_two, preferred_element_type=jnp.float32)
-            + jnp.dot(tail_rows.T, trail, preferred_element_type=jnp.float32),
+            + jnp.dot(tail_late.T, trail, preferred_element_type=jnp.float32),
             "row",
             n_row,
         )

time: 159 us -> 161 us (1.013)
    ppermute x6, waiting for transfers between devices: 1.18 us -> 4.47 us  [halving_scatter(): blocks = keep + lax.ppermute(send, axis, pairs)]
  transfers between devices with their start and end apart: 36 -> 36, of which waited for: 11 -> 12; matrix products, arithmetic and copies ran while one was open for 30% -> 31% of each run, Pallas kernels for 25% -> 24%
where the time goes in v13:
time: 161 us; the launch traced here: 159 us
  starting transfers between devices  44.9 us (28%)
  Pallas kernels  38.9 us (24%)
  other arithmetic  25.2 us (16%)
  matrix products  23.5 us (15%)
  waiting for transfers between devices  23.5 us (15%)
    pallas_call x2, Pallas kernels, panel_broadcast(): pl.pallas_call(functools.partial(spread_kernel, root, size), out_shape=ja...  38.9 us
    another operation x4, other arithmetic, inverse_lower(): return lax.linalg.triangular_solve(block, ident, left_side=True, lower=True)  20.5 us
    ppermute x6, starting transfers between devices, halving_scatter(): blocks = keep + lax.ppermute(send, axis, pairs)  14.4 us
    ppermute x18, starting transfers between devices, tree_broadcast(): part = lax.ppermute(value, axis, pairs)  14.3 us
    ppermute x6, waiting for transfers between devices, butterfly_sum(): value = value + lax.ppermute(value, axis, pairs)  11.5 us
    ppermute x6, starting transfers between devices, butterfly_sum(): value = value + lax.ppermute(value, axis, pairs)  9.17 us
    ppermute x6, starting transfers between devices, doubling_gather(): other = lax.ppermute(value, axis, pairs)  7.06 us
    ppermute x18, waiting for transfers between devices, tree_broadcast(): part = lax.ppermute(value, axis, pairs)  6.39 us
  transfers between devices with their start and end apart: 36, of which 12 were waited for; matrix products, arithmetic and copies ran while one was open for 31% of the time, Pallas kernels for 24%

profile of v13, /device:TPU:1, one launch (start us, length us, event | category | flops | bytes accessed | tf_op | source)
XLA Modules:
  0.0 158.9 jit_solution(12804432089053222641)
XLA Ops:
  0.6 1.5 collective-permute-start.24
  2.2 0.8 select_bitcast_fusion.1
  3.1 9.8 %custom-call.4 = f32[1,128,128]{1,2,0:T(8,128)S(1)} custom-call(f32[1,128,128]{2,1,0:T(8,128)S(1)} %select_bitcast_fusion.1), custom_call_target="InvertDiagBlocksLowerTriangular" | custom-call | tf_op jit(solution)/shard_map/triangular_solve/custom-call.1 | solution.py:158
  13.2 3.0 %fusion.x_ref = bf16[2048,128]{1,0:T(8,128)(2,1)} fusion(f32[128,128]{1,0:T(8,128)S(1)} %fusion.21, f32[2048,1024]{1,0:T(8,128)} %param.17), kind=kOutput, calls=%fused_computation.6 | convolution fusion | flops 402915328 | bytes 1638400 | tf_op jit(solution)/shard_map/dot_general | solution.py:197
  16.2 18.4 %shard_map.137 = bf16[2048,128]{1,0:T(8,128)(2,1)} custom-call(bf16[2048,128]{1,0:T(8,128)(2,1)} %fusion.x_ref), custom_call_target="tpu_custom_call" | custom-call | tf_op jit(solution)/shard_map/pallas_call | solution.py:77
  34.6 1.5 fusion.17
  36.1 3.2 %collective-permute-start.3 = (f32[128,128]{1,0:T(8,128)S(1)}, f32[128,128]{1,0:T(8,128)S(1)}, u32[]{:S(2)}, u32[]{:S(2)}) collective-permute-start(f32[128,128]{1,0:T(8,128)S(1)} %fusion.17), channel_id=1, source_target_pairs={{0,16},{16,0},{32,48},{48,32},{64,80},{80,64},{96,112},{112,96},{1... | collective-permute-start | bytes 196616 | tf_op jit(solution)/shard_map/ppermute | solution.py:111
  39.3 3.1 %fusion.60 = f32[128,1024]{1,0:T(8,128)S(1)} fusion(bf16[2048,128]{1,0:T(8,128)(2,1)} %shard_map.137, bf16[2048,1024]{1,0:T(8,128)(2,1)} %param.12), kind=kOutput, calls=%fused_computation.107 | convolution fusion | flops 536870912 | bytes 5242880 | tf_op jit(solution)/shard_map/dot_general | solution.py:217
  42.5 2.8 %collective-permute-start = (f32[4,16,1024]{2,1,0:T(8,128)S(1)}, f32[4,16,1024]{2,1,0:T(8,128)S(1)}, u32[]{:S(2)}, u32[]{:S(2)}) collective-permute-start(f32[4,16,1024]{2,1,0:T(8,128)S(1)} %bitcast.62), channel_id=1, source_target_pairs={{0,64},{16,80},{32,96},{48,112},{64,0},{80,16},{96,32},{112,48},{1... | collective-permute-start | bytes 786440 | tf_op jit(solution)/shard_map/ppermute | solution.py:127
  45.4 9.8 %custom-call.5 = f32[1,128,128]{1,2,0:T(8,128)S(1)} custom-call(f32[1,128,128]{2,1,0:T(8,128)S(1)} %select_bitcast_fusion), custom_call_target="InvertDiagBlocksLowerTriangular" | custom-call | tf_op jit(solution)/shard_map/triangular_solve/custom-call.1 | solution.py:158
  55.6 0.4 collective-permute-start.13
  56.0 1.2 collective-permute-start.25
  57.2 0.4 collective-permute-start.4
  57.6 1.1 collective-permute-done.13
  58.8 1.2 collective-permute-start.14
  60.1 1.7 %collective-permute-done.4 = f32[128,128]{1,0:T(8,128)S(1)} collective-permute-done((f32[128,128]{1,0:T(8,128)S(1)}, f32[128,128]{1,0:T(8,128)S(1)}, u32[]{:S(2)}, u32[]{:S(2)}) %collective-permute-start.4) | collective-permute-done | bytes 65568 | tf_op jit(solution)/shard_map/ppermute | solution.py:111
  61.8 0.5 collective-permute-start.5
  62.4 2.6 %collective-permute-start.26 = (bf16[64,1024]{1,0:T(8,128)(2,1)S(1)}, bf16[64,1024]{1,0:T(8,128)(2,1)S(1)}, u32[]{:S(2)}, u32[]{:S(2)}) collective-permute-start(bf16[64,1024]{1,0:T(8,128)(2,1)S(1)} %maximum_select_fusion.3), channel_id=1, source_target_pairs={{0,64},{16,80},{32,96},{48,112},{64,0},{80,16},{96,32},{112,48},{1... | collective-permute-start | bytes 393224 | tf_op jit(solution)/shard_map/ppermute | solution.py:137
  65.0 2.5 %collective-permute-done.5 = f32[128,128]{1,0:T(8,128)S(1)} collective-permute-done((f32[128,128]{1,0:T(8,128)S(1)}, f32[128,128]{1,0:T(8,128)S(1)}, u32[]{:S(2)}, u32[]{:S(2)}) %collective-permute-start.5) | collective-permute-done | bytes 65568 | tf_op jit(solution)/shard_map/ppermute | solution.py:111
  67.4 0.8 collective-permute-start.8
  68.3 0.7 collective-permute-start.7
  69.0 0.7 collective-permute-start.6
  69.7 1.5 convolution_subtract_fusion.1
  71.3 1.3 collective-permute-start.11
  72.6 0.7 collective-permute-start.10
  73.3 0.7 collective-permute-start.9
  74.0 0.4 collective-permute-start.1
  74.4 4.0 %collective-permute-done.11 = f32[128,128]{1,0:T(8,128)S(1)} collective-permute-done((f32[128,128]{1,0:T(8,128)S(1)}, f32[128,128]{1,0:T(8,128)S(1)}, u32[]{:S(2)}, u32[]{:S(2)}) %collective-permute-start.11) | collective-permute-done | bytes 65568 | tf_op jit(solution)/shard_map/ppermute | solution.py:99
  78.4 1.1 fusion.2
  79.9 5.0 %collective-permute-start.2 = (f32[1,16,1024]{2,1,0:T(8,128)S(1)}, f32[1,16,1024]{2,1,0:T(8,128)S(1)}, u32[]{:S(2)}, u32[]{:S(2)}) collective-permute-start(f32[1,16,1024]{2,1,0:T(8,128)S(1)} %slice_select_fusion.8), channel_id=1, source_target_pairs={{0,16},{16,0},{32,48},{48,32},{64,80},{80,64},{96,112},{112,96},{1... | collective-permute-start | bytes 196616 | tf_op jit(solution)/shard_map/ppermute | solution.py:127
  85.2 0.6 collective-permute-done.2
  86.1 1.0 convolution_convert_fusion
  87.0 0.7 collective-permute-start.17
  87.7 0.7 collective-permute-start.16
  88.4 0.7 collective-permute-start.15
  89.1 0.8 slice.137.x_ref
  89.9 20.5 %shard_map.138 = bf16[2048,128]{1,0:T(8,128)(2,1)} custom-call(bf16[2048,128]{1,0:T(8,128)(2,1)} %slice.137.x_ref), custom_call_target="tpu_custom_call" | custom-call | tf_op jit(solution)/shard_map/pallas_call | solution.py:77
  110.5 1.4 collective-permute-start.20
  111.9 0.7 collective-permute-start.19
  112.6 0.7 collective-permute-start.18
  113.3 1.5 fusion.15
  114.8 1.4 collective-permute-done.20
  116.4 4.4 %collective-permute-start.21 = (f32[128,128]{1,0:T(8,128)S(1)}, f32[128,128]{1,0:T(8,128)S(1)}, u32[]{:S(2)}, u32[]{:S(2)}) collective-permute-start(f32[128,128]{1,0:T(8,128)S(1)} %convolution_add_fusion.1), channel_id=1, source_target_pairs={{0,16},{16,0},{32,48},{48,32},{64,80},{80,64},{96,112},{112,96},{1... | collective-permute-start | bytes 196616 | tf_op jit(solution)/shard_map/ppermute | solution.py:111
  120.9 0.8 collective-permute-done.21
  121.8 3.1 %collective-permute-done.22 = f32[128,128]{1,0:T(8,128)S(1)} collective-permute-done((f32[128,128]{1,0:T(8,128)S(1)}, f32[128,128]{1,0:T(8,128)S(1)}, u32[]{:S(2)}, u32[]{:S(2)}) %collective-permute-start.22) | collective-permute-done | bytes 65568 | tf_op jit(solution)/shard_map/ppermute | solution.py:111
  124.9 0.6 collective-permute-start.23
  125.5 0.6 pad_maximum_fusion.2
  126.1 3.5 %collective-permute-done.23 = f32[128,128]{1,0:T(8,128)S(1)} collective-permute-done((f32[128,128]{1,0:T(8,128)S(1)}, f32[128,128]{1,0:T(8,128)S(1)}, u32[]{:S(2)}, u32[]{:S(2)}) %collective-permute-start.23) | collective-permute-done | bytes 65568 | tf_op jit(solution)/shard_map/ppermute | solution.py:111
  129.6 0.7 collective-permute-start.32
  130.3 0.7 collective-permute-start.31
  131.0 0.7 collective-permute-start.30
  131.6 3.1 %fusion.62 = f32[128,1024]{1,0:T(8,128)S(1)} fusion(bf16[2048,128]{1,0:T(8,128)(2,1)} %shard_map.138, bf16[2048,1024]{1,0:T(8,128)(2,1)} %param.12), kind=kOutput, calls=%fused_computation.109 | convolution fusion | flops 536870912 | bytes 5242880 | tf_op jit(solution)/shard_map/dot_general | solution.py:245
  134.8 4.7 %convolution_subtract_fusion = bf16[2048,1024]{1,0:T(8,128)(2,1)S(1)} fusion(f32[2048,1024]{1,0:T(8,128)} %param.17, bf16[2048,128]{1,0:T(8,128)(2,1)S(1)} %copy-done.1, bf16[2048,128]{1,0:T(8,128)(2,1)S(1)} %copy-done, bf16[128,1024]{1,0:T(8,128)(2,1)S(1)} %maximum_select_fusion.1, bf16[128,1024]{1,0:T(8,128)(2,1)S(1)} %maximum_select_fusion), kind=kOutput, calls=%fused_computation.1 | convolution fusion | flops 1081081856 | bytes 14155776 | tf_op jit(solution)/shard_map/dot_general | solution.py:238
  140.0 0.4 slice.197
  140.4 0.6 collective-permute-start.27
  141.1 1.4 collective-permute-start.35
  142.5 0.7 collective-permute-start.34
  143.2 0.7 collective-permute-start.33
  143.9 2.6 %pad_maximum_fusion = bf16[2048,1024]{1,0:T(8,128)(2,1)} fusion(bf16[2048,128]{1,0:T(8,128)(2,1)S(1)} %fusion.7, bf16[2048,896]{1,0:T(8,128)(2,1)S(1)} %slice.197), kind=kLoop, calls=%fused_computation.2 | loop fusion | flops 8388608 | bytes 8388608 | tf_op jit(solution)/shard_map/concatenate | solution.py:255
  146.5 0.9 collective-permute-done.35
  148.4 3.3 %collective-permute-done.28 = f32[2,16,1024]{2,1,0:T(8,128)S(1)} collective-permute-done((f32[2,16,1024]{2,1,0:T(8,128)S(1)}, f32[2,16,1024]{2,1,0:T(8,128)S(1)}, u32[]{:S(2)}, u32[]{:S(2)}) %collective-permute-start.28) | collective-permute-done | bytes 131104 | tf_op jit(solution)/shard_map/ppermute | solution.py:127
  151.8 5.3 %collective-permute-start.29 = (f32[1,16,1024]{2,1,0:T(8,128)S(1)}, f32[1,16,1024]{2,1,0:T(8,128)S(1)}, u32[]{:S(2)}, u32[]{:S(2)}) collective-permute-start(f32[1,16,1024]{2,1,0:T(8,128)S(1)} %slice_select_fusion.7), channel_id=1, source_target_pairs={{0,16},{16,0},{32,48},{48,32},{64,80},{80,64},{96,112},{112,96},{1... | collective-permute-start | bytes 196616 | tf_op jit(solution)/shard_map/ppermute | solution.py:127
  157.4 0.6 collective-permute-done.29
  158.2 0.6 pad_maximum_fusion.1
  (98 shorter events, 4.5 us)
Async XLA Ops:
  0.6 55.3 %collective-permute-start.24 = (bf16[16,1024]{1,0:T(8,128)(2,1)}, bf16[16,1024]{1,0:T(8,128)(2,1)S(1)}, u32[]{:S(2)}, u32[]{:S(2)}) collective-permute-start(bf16[16,1024]{1,0:T(8,128)(2,1)} %param.13), channel_id=1, source_target_pairs={{0,16},{16,0},{32,48},{48,32},{64,80},{80,64},{96,112},{112,96},{1... | collective-permute-start | bytes 98312 | tf_op jit(solution)/shard_map/ppermute | solution.py:137
  2.1 53.4 %collective-permute-start.12 = (bf16[16,1024]{1,0:T(8,128)(2,1)}, bf16[16,1024]{1,0:T(8,128)(2,1)S(1)}, u32[]{:S(2)}, u32[]{:S(2)}) collective-permute-start(bf16[16,1024]{1,0:T(8,128)(2,1)} %param.14), channel_id=1, source_target_pairs={{0,16},{16,0},{32,48},{48,32},{64,80},{80,64},{96,112},{112,96},{1... | collective-permute-start | bytes 98312 | tf_op jit(solution)/shard_map/ppermute | solution.py:137
  16.2 29.2 %copy-start.3 = (f32[128,128]{1,0:T(8,128)S(1)}, f32[128,128]{1,0:T(8,128)}, u32[]{:S(2)}) copy-start(f32[128,128]{1,0:T(8,128)} %param.15) | copy-start | bytes 196612
  16.2 39.4 %copy-start.4 = (bf16[16,1024]{1,0:T(8,128)(2,1)S(1)}, bf16[16,1024]{1,0:T(8,128)(2,1)}, u32[]{:S(2)}) copy-start(bf16[16,1024]{1,0:T(8,128)(2,1)} %param.14) | copy-start | bytes 98308
  34.6 21.4 %copy-start.10 = (bf16[16,1024]{1,0:T(8,128)(2,1)S(1)}, bf16[16,1024]{1,0:T(8,128)(2,1)}, u32[]{:S(2)}) copy-start(bf16[16,1024]{1,0:T(8,128)(2,1)} %param.13) | copy-start | bytes 98308
  36.1 21.1 %collective-permute-start.3 = (f32[128,128]{1,0:T(8,128)S(1)}, f32[128,128]{1,0:T(8,128)S(1)}, u32[]{:S(2)}, u32[]{:S(2)}) collective-permute-start(f32[128,128]{1,0:T(8,128)S(1)} %fusion.17), channel_id=1, source_target_pairs={{0,16},{16,0},{32,48},{48,32},{64,80},{80,64},{96,112},{112,96},{1... | collective-permute-start | bytes 196616 | tf_op jit(solution)/shard_map/ppermute | solution.py:111
  39.3 30.4 %copy-start = (bf16[2048,128]{1,0:T(8,128)(2,1)S(1)}, bf16[2048,128]{1,0:T(8,128)(2,1)}, u32[]{:S(2)}) copy-start(bf16[2048,128]{1,0:T(8,128)(2,1)} %shard_map.137) | copy-start | bytes 1572868
  42.5 36.0 %copy-start.2 = (f32[128,128]{1,0:T(8,128)S(1)}, f32[128,128]{1,0:T(8,128)}, u32[]{:S(2)}) copy-start(f32[128,128]{1,0:T(8,128)} %param.16) | copy-start | bytes 196612
  42.5 43.3 %copy-start.7 = (f32[16,1024]{1,0:T(8,128)S(1)}, f32[16,1024]{1,0:T(8,128)}, u32[]{:S(2)}) copy-start(f32[16,1024]{1,0:T(8,128)} %param.19) | copy-start | bytes 196612
  42.5 31.4 %collective-permute-start = (f32[4,16,1024]{2,1,0:T(8,128)S(1)}, f32[4,16,1024]{2,1,0:T(8,128)S(1)}, u32[]{:S(2)}, u32[]{:S(2)}) collective-permute-start(f32[4,16,1024]{2,1,0:T(8,128)S(1)} %bitcast.62), channel_id=1, source_target_pairs={{0,64},{16,80},{32,96},{48,112},{64,0},{80,16},{96,32},{112,48},{1... | collective-permute-start | bytes 786440 | tf_op jit(solution)/shard_map/ppermute | solution.py:127
  55.6 3.2 %collective-permute-start.13 = (bf16[32,1024]{1,0:T(8,128)(2,1)S(1)}, bf16[32,1024]{1,0:T(8,128)(2,1)S(1)}, u32[]{:S(2)}, u32[]{:S(2)}) collective-permute-start(bf16[32,1024]{1,0:T(8,128)(2,1)S(1)} %maximum_select_fusion.4), channel_id=1, source_target_pairs={{0,32},{16,48},{32,0},{48,16},{64,96},{80,112},{96,64},{112,80},{1... | collective-permute-start | bytes 196616 | tf_op jit(solution)/shard_map/ppermute | solution.py:137
  56.0 6.3 %collective-permute-start.25 = (bf16[32,1024]{1,0:T(8,128)(2,1)S(1)}, bf16[32,1024]{1,0:T(8,128)(2,1)S(1)}, u32[]{:S(2)}, u32[]{:S(2)}) collective-permute-start(bf16[32,1024]{1,0:T(8,128)(2,1)S(1)} %maximum_select_fusion.5), channel_id=1, source_target_pairs={{0,32},{16,48},{32,0},{48,16},{64,96},{80,112},{96,64},{112,80},{1... | collective-permute-start | bytes 196616 | tf_op jit(solution)/shard_map/ppermute | solution.py:137
  57.2 4.6 %collective-permute-start.4 = (f32[128,128]{1,0:T(8,128)S(1)}, f32[128,128]{1,0:T(8,128)S(1)}, u32[]{:S(2)}, u32[]{:S(2)}) collective-permute-start(f32[128,128]{1,0:T(8,128)S(1)} %add.117), channel_id=1, source_target_pairs={{0,32},{16,48},{32,0},{48,16},{64,96},{80,112},{96,64},{112,80},{1... | collective-permute-start | bytes 196616 | tf_op jit(solution)/shard_map/ppermute | solution.py:111
  58.8 10.2 %collective-permute-start.14 = (bf16[64,1024]{1,0:T(8,128)(2,1)S(1)}, bf16[64,1024]{1,0:T(8,128)(2,1)S(1)}, u32[]{:S(2)}, u32[]{:S(2)}) collective-permute-start(bf16[64,1024]{1,0:T(8,128)(2,1)S(1)} %maximum_select_fusion.2), channel_id=1, source_target_pairs={{0,64},{16,80},{32,96},{48,112},{64,0},{80,16},{96,32},{112,48},{1... | collective-permute-start | bytes 393224 | tf_op jit(solution)/shard_map/ppermute | solution.py:137
  61.8 5.6 %collective-permute-start.5 = (f32[128,128]{1,0:T(8,128)S(1)}, f32[128,128]{1,0:T(8,128)S(1)}, u32[]{:S(2)}, u32[]{:S(2)}) collective-permute-start(f32[128,128]{1,0:T(8,128)S(1)} %add.118), channel_id=1, source_target_pairs={{0,64},{16,80},{32,96},{48,112},{64,0},{80,16},{96,32},{112,48},{1... | collective-permute-start | bytes 196616 | tf_op jit(solution)/shard_map/ppermute | solution.py:111
  62.4 26.7 %collective-permute-start.26 = (bf16[64,1024]{1,0:T(8,128)(2,1)S(1)}, bf16[64,1024]{1,0:T(8,128)(2,1)S(1)}, u32[]{:S(2)}, u32[]{:S(2)}) collective-permute-start(bf16[64,1024]{1,0:T(8,128)(2,1)S(1)} %maximum_select_fusion.3), channel_id=1, source_target_pairs={{0,64},{16,80},{32,96},{48,112},{64,0},{80,16},{96,32},{112,48},{1... | collective-permute-start | bytes 393224 | tf_op jit(solution)/shard_map/ppermute | solution.py:137
  67.4 3.8 %collective-permute-start.8 = (f32[128,128]{1,0:T(8,128)S(1)}, f32[128,128]{1,0:T(8,128)S(1)}, u32[]{:S(2)}, u32[]{:S(2)}) collective-permute-start(f32[128,128]{1,0:T(8,128)S(1)} %add.119), channel_id=1, source_target_pairs={{15,12},{31,28},{47,44},{63,60},{79,76},{95,92},{111,108},{127,124}} | collective-permute-start | bytes 196616 | tf_op jit(solution)/shard_map/ppermute | solution.py:99
  68.3 3.0 %collective-permute-start.7 = (f32[128,128]{1,0:T(8,128)S(1)}, f32[128,128]{1,0:T(8,128)S(1)}, u32[]{:S(2)}, u32[]{:S(2)}) collective-permute-start(f32[128,128]{1,0:T(8,128)S(1)} %add.119), channel_id=1, source_target_pairs={{15,13},{31,29},{47,45},{63,61},{79,77},{95,93},{111,109},{127,125}} | collective-permute-start | bytes 196616 | tf_op jit(solution)/shard_map/ppermute | solution.py:99
  69.0 2.3 %collective-permute-start.6 = (f32[128,128]{1,0:T(8,128)S(1)}, f32[128,128]{1,0:T(8,128)S(1)}, u32[]{:S(2)}, u32[]{:S(2)}) collective-permute-start(f32[128,128]{1,0:T(8,128)S(1)} %add.119), channel_id=1, source_target_pairs={{15,14},{31,30},{47,46},{63,62},{79,78},{95,94},{111,110},{127,126}} | collective-permute-start | bytes 196616 | tf_op jit(solution)/shard_map/ppermute | solution.py:99
  71.3 7.1 %collective-permute-start.11 = (f32[128,128]{1,0:T(8,128)S(1)}, f32[128,128]{1,0:T(8,128)S(1)}, u32[]{:S(2)}, u32[]{:S(2)}) collective-permute-start(f32[128,128]{1,0:T(8,128)S(1)} %add_select_fusion.1), channel_id=1, source_target_pairs={{15,3},{14,2},{13,1},{12,0},{31,19},{30,18},{29,17},{28,16},{47,35... | collective-permute-start | bytes 196616 | tf_op jit(solution)/shard_map/ppermute | solution.py:99
  72.6 5.8 %collective-permute-start.10 = (f32[128,128]{1,0:T(8,128)S(1)}, f32[128,128]{1,0:T(8,128)S(1)}, u32[]{:S(2)}, u32[]{:S(2)}) collective-permute-start(f32[128,128]{1,0:T(8,128)S(1)} %add_select_fusion.1), channel_id=1, source_target_pairs={{15,7},{14,6},{13,5},{12,4},{31,23},{30,22},{29,21},{28,20},{47,39... | collective-permute-start | bytes 196616 | tf_op jit(solution)/shard_map/ppermute | solution.py:99
  73.3 5.2 %collective-permute-start.9 = (f32[128,128]{1,0:T(8,128)S(1)}, f32[128,128]{1,0:T(8,128)S(1)}, u32[]{:S(2)}, u32[]{:S(2)}) collective-permute-start(f32[128,128]{1,0:T(8,128)S(1)} %add_select_fusion.1), channel_id=1, source_target_pairs={{15,11},{14,10},{13,9},{12,8},{31,27},{30,26},{29,25},{28,24},{47,... | collective-permute-start | bytes 196616 | tf_op jit(solution)/shard_map/ppermute | solution.py:99
  74.0 5.8 %collective-permute-start.1 = (f32[2,16,1024]{2,1,0:T(8,128)S(1)}, f32[2,16,1024]{2,1,0:T(8,128)S(1)}, u32[]{:S(2)}, u32[]{:S(2)}) collective-permute-start(f32[2,16,1024]{2,1,0:T(8,128)S(1)} %slice_select_fusion.6), channel_id=1, source_target_pairs={{0,32},{16,48},{32,0},{48,16},{64,96},{80,112},{96,64},{112,80},{1... | collective-permute-start | bytes 393224 | tf_op jit(solution)/shard_map/ppermute | solution.py:127
  79.9 5.9 %collective-permute-start.2 = (f32[1,16,1024]{2,1,0:T(8,128)S(1)}, f32[1,16,1024]{2,1,0:T(8,128)S(1)}, u32[]{:S(2)}, u32[]{:S(2)}) collective-permute-start(f32[1,16,1024]{2,1,0:T(8,128)S(1)} %slice_select_fusion.8), channel_id=1, source_target_pairs={{0,16},{16,0},{32,48},{48,32},{64,80},{80,64},{96,112},{112,96},{1... | collective-permute-start | bytes 196616 | tf_op jit(solution)/shard_map/ppermute | solution.py:127
  85.1 49.6 %copy-start.5 = (f32[128,128]{1,0:T(8,128)}, f32[128,128]{1,0:T(8,128)S(1)}, u32[]{:S(2)}) copy-start(f32[128,128]{1,0:T(8,128)S(1)} %get-tuple-element.14) | copy-start | bytes 196612
  87.0 23.4 %collective-permute-start.17 = (bf16[16,128]{1,0:T(8,128)(2,1)S(1)}, bf16[16,128]{1,0:T(8,128)(2,1)S(1)}, u32[]{:S(2)}, u32[]{:S(2)}) collective-permute-start(bf16[16,128]{1,0:T(8,128)(2,1)S(1)} %slice.138), channel_id=1, source_target_pairs={{14,13},{30,29},{46,45},{62,61},{78,77},{94,93},{110,109},{126,125}} | collective-permute-start | bytes 12296 | tf_op jit(solution)/shard_map/ppermute | solution.py:99
  87.7 22.8 %collective-permute-start.16 = (bf16[16,128]{1,0:T(8,128)(2,1)S(1)}, bf16[16,128]{1,0:T(8,128)(2,1)S(1)}, u32[]{:S(2)}, u32[]{:S(2)}) collective-permute-start(bf16[16,128]{1,0:T(8,128)(2,1)S(1)} %slice.138), channel_id=1, source_target_pairs={{14,12},{30,28},{46,44},{62,60},{78,76},{94,92},{110,108},{126,124}} | collective-permute-start | bytes 12296 | tf_op jit(solution)/shard_map/ppermute | solution.py:99
  88.4 22.1 %collective-permute-start.15 = (bf16[16,128]{1,0:T(8,128)(2,1)S(1)}, bf16[16,128]{1,0:T(8,128)(2,1)S(1)}, u32[]{:S(2)}, u32[]{:S(2)}) collective-permute-start(bf16[16,128]{1,0:T(8,128)(2,1)S(1)} %slice.138), channel_id=1, source_target_pairs={{14,15},{30,31},{46,47},{62,63},{78,79},{94,95},{110,111},{126,127}} | collective-permute-start | bytes 12296 | tf_op jit(solution)/shard_map/ppermute | solution.py:99
  110.4 24.3 %copy-start.1 = (bf16[2048,128]{1,0:T(8,128)(2,1)S(1)}, bf16[2048,128]{1,0:T(8,128)(2,1)}, u32[]{:S(2)}) copy-start(bf16[2048,128]{1,0:T(8,128)(2,1)} %shard_map.138) | copy-start | bytes 1572868
  110.5 5.7 %collective-permute-start.20 = (bf16[16,128]{1,0:T(8,128)(2,1)S(1)}, bf16[16,128]{1,0:T(8,128)(2,1)S(1)}, u32[]{:S(2)}, u32[]{:S(2)}) collective-permute-start(bf16[16,128]{1,0:T(8,128)(2,1)S(1)} %add_select_fusion.3), channel_id=1, source_target_pairs={{14,2},{15,3},{12,0},{13,1},{30,18},{31,19},{28,16},{29,17},{46,34... | collective-permute-start | bytes 12296 | tf_op jit(solution)/shard_map/ppermute | solution.py:99
  111.9 4.3 %collective-permute-start.19 = (bf16[16,128]{1,0:T(8,128)(2,1)S(1)}, bf16[16,128]{1,0:T(8,128)(2,1)S(1)}, u32[]{:S(2)}, u32[]{:S(2)}) collective-permute-start(bf16[16,128]{1,0:T(8,128)(2,1)S(1)} %add_select_fusion.3), channel_id=1, source_target_pairs={{14,6},{15,7},{12,4},{13,5},{30,22},{31,23},{28,20},{29,21},{46,38... | collective-permute-start | bytes 12296 | tf_op jit(solution)/shard_map/ppermute | solution.py:99
  112.6 3.6 %collective-permute-start.18 = (bf16[16,128]{1,0:T(8,128)(2,1)S(1)}, bf16[16,128]{1,0:T(8,128)(2,1)S(1)}, u32[]{:S(2)}, u32[]{:S(2)}) collective-permute-start(bf16[16,128]{1,0:T(8,128)(2,1)S(1)} %add_select_fusion.3), channel_id=1, source_target_pairs={{14,10},{15,11},{12,8},{13,9},{30,26},{31,27},{28,24},{29,25},{46,... | collective-permute-start | bytes 12296 | tf_op jit(solution)/shard_map/ppermute | solution.py:99
  116.4 5.3 %collective-permute-start.21 = (f32[128,128]{1,0:T(8,128)S(1)}, f32[128,128]{1,0:T(8,128)S(1)}, u32[]{:S(2)}, u32[]{:S(2)}) collective-permute-start(f32[128,128]{1,0:T(8,128)S(1)} %convolution_add_fusion.1), channel_id=1, source_target_pairs={{0,16},{16,0},{32,48},{48,32},{64,80},{80,64},{96,112},{112,96},{1... | collective-permute-start | bytes 196616 | tf_op jit(solution)/shard_map/ppermute | solution.py:111
  121.7 3.2 %collective-permute-start.22 = (f32[128,128]{1,0:T(8,128)S(1)}, f32[128,128]{1,0:T(8,128)S(1)}, u32[]{:S(2)}, u32[]{:S(2)}) collective-permute-start(f32[128,128]{1,0:T(8,128)S(1)} %add.131), channel_id=1, source_target_pairs={{0,32},{16,48},{32,0},{48,16},{64,96},{80,112},{96,64},{112,80},{1... | collective-permute-start | bytes 196616 | tf_op jit(solution)/shard_map/ppermute | solution.py:111
  124.9 4.7 %collective-permute-start.23 = (f32[128,128]{1,0:T(8,128)S(1)}, f32[128,128]{1,0:T(8,128)S(1)}, u32[]{:S(2)}, u32[]{:S(2)}) collective-permute-start(f32[128,128]{1,0:T(8,128)S(1)} %add.132), channel_id=1, source_target_pairs={{0,64},{16,80},{32,96},{48,112},{64,0},{80,16},{96,32},{112,48},{1... | collective-permute-start | bytes 196616 | tf_op jit(solution)/shard_map/ppermute | solution.py:111
  129.6 11.4 %collective-permute-start.32 = (f32[128,128]{1,0:T(8,128)S(1)}, f32[128,128]{1,0:T(8,128)S(1)}, u32[]{:S(2)}, u32[]{:S(2)}) collective-permute-start(f32[128,128]{1,0:T(8,128)S(1)} %add.133), channel_id=1, source_target_pairs={{14,13},{30,29},{46,45},{62,61},{78,77},{94,93},{110,109},{126,125}} | collective-permute-start | bytes 196616 | tf_op jit(solution)/shard_map/ppermute | solution.py:99
  130.3 10.7 %collective-permute-start.31 = (f32[128,128]{1,0:T(8,128)S(1)}, f32[128,128]{1,0:T(8,128)S(1)}, u32[]{:S(2)}, u32[]{:S(2)}) collective-permute-start(f32[128,128]{1,0:T(8,128)S(1)} %add.133), channel_id=1, source_target_pairs={{14,12},{30,28},{46,44},{62,60},{78,76},{94,92},{110,108},{126,124}} | collective-permute-start | bytes 196616 | tf_op jit(solution)/shard_map/ppermute | solution.py:99
  131.0 10.1 %collective-permute-start.30 = (f32[128,128]{1,0:T(8,128)S(1)}, f32[128,128]{1,0:T(8,128)S(1)}, u32[]{:S(2)}, u32[]{:S(2)}) collective-permute-start(f32[128,128]{1,0:T(8,128)S(1)} %add.133), channel_id=1, source_target_pairs={{14,15},{30,31},{46,47},{62,63},{78,79},{94,95},{110,111},{126,127}} | collective-permute-start | bytes 196616 | tf_op jit(solution)/shard_map/ppermute | solution.py:99
  140.4 7.3 %collective-permute-start.27 = (f32[4,16,1024]{2,1,0:T(8,128)S(1)}, f32[4,16,1024]{2,1,0:T(8,128)S(1)}, u32[]{:S(2)}, u32[]{:S(2)}) collective-permute-start(f32[4,16,1024]{2,1,0:T(8,128)S(1)} %bitcast.63), channel_id=1, source_target_pairs={{0,64},{16,80},{32,96},{48,112},{64,0},{80,16},{96,32},{112,48},{1... | collective-permute-start | bytes 786440 | tf_op jit(solution)/shard_map/ppermute | solution.py:127
  141.1 6.4 %copy-start.9 = (f32[128,128]{1,0:T(8,128)S(1)}, f32[128,128]{1,0:T(8,128)}, u32[]{:S(2)}) copy-start(f32[128,128]{1,0:T(8,128)} %param.20) | copy-start | bytes 196612
  141.1 16.9 %copy-start.8 = (f32[16,1024]{1,0:T(8,128)S(1)}, f32[16,1024]{1,0:T(8,128)}, u32[]{:S(2)}) copy-start(f32[16,1024]{1,0:T(8,128)} %param.18) | copy-start | bytes 196612
  141.1 6.4 %collective-permute-start.35 = (f32[128,128]{1,0:T(8,128)S(1)}, f32[128,128]{1,0:T(8,128)S(1)}, u32[]{:S(2)}, u32[]{:S(2)}) collective-permute-start(f32[128,128]{1,0:T(8,128)S(1)} %add_select_fusion), channel_id=1, source_target_pairs={{14,2},{15,3},{12,0},{13,1},{30,18},{31,19},{28,16},{29,17},{46,34... | collective-permute-start | bytes 196616 | tf_op jit(solution)/shard_map/ppermute | solution.py:99
  142.5 4.9 %collective-permute-start.34 = (f32[128,128]{1,0:T(8,128)S(1)}, f32[128,128]{1,0:T(8,128)S(1)}, u32[]{:S(2)}, u32[]{:S(2)}) collective-permute-start(f32[128,128]{1,0:T(8,128)S(1)} %add_select_fusion), channel_id=1, source_target_pairs={{14,6},{15,7},{12,4},{13,5},{30,22},{31,23},{28,20},{29,21},{46,38... | collective-permute-start | bytes 196616 | tf_op jit(solution)/shard_map/ppermute | solution.py:99
  143.2 4.3 %collective-permute-start.33 = (f32[128,128]{1,0:T(8,128)S(1)}, f32[128,128]{1,0:T(8,128)S(1)}, u32[]{:S(2)}, u32[]{:S(2)}) collective-permute-start(f32[128,128]{1,0:T(8,128)S(1)} %add_select_fusion), channel_id=1, source_target_pairs={{14,10},{15,11},{12,8},{13,9},{30,26},{31,27},{28,24},{29,25},{46,... | collective-permute-start | bytes 196616 | tf_op jit(solution)/shard_map/ppermute | solution.py:99
  147.8 3.9 %collective-permute-start.28 = (f32[2,16,1024]{2,1,0:T(8,128)S(1)}, f32[2,16,1024]{2,1,0:T(8,128)S(1)}, u32[]{:S(2)}, u32[]{:S(2)}) collective-permute-start(f32[2,16,1024]{2,1,0:T(8,128)S(1)} %slice_select_fusion.5), channel_id=1, source_target_pairs={{0,32},{16,48},{32,0},{48,16},{64,96},{80,112},{96,64},{112,80},{1... | collective-permute-start | bytes 393224 | tf_op jit(solution)/shard_map/ppermute | solution.py:127
  151.8 6.2 %collective-permute-start.29 = (f32[1,16,1024]{2,1,0:T(8,128)S(1)}, f32[1,16,1024]{2,1,0:T(8,128)S(1)}, u32[]{:S(2)}, u32[]{:S(2)}) collective-permute-start(f32[1,16,1024]{2,1,0:T(8,128)S(1)} %slice_select_fusion.7), channel_id=1, source_target_pairs={{0,16},{16,0},{32,48},{48,32},{64,80},{80,64},{96,112},{112,96},{1... | collective-permute-start | bytes 196616 | tf_op jit(solution)/shard_map/ppermute | solution.py:127
  157.3 1.6 copy-start.6

commit v14 on v12

--- a/solution.py
+++ b/solution.py
@@ -194,7 +194,7 @@
             return lax.dynamic_slice_in_dim(matrix, row_start, band, 0)
 
         def solve_panel(rows, inverse, root):
-            local = jnp.dot(rows, inverse, precision=exact_mode).astype(jnp.bfloat16)
+            local = jnp.dot(rows, inverse, precision=lax.Precision.HIGH).astype(jnp.bfloat16)
             head = local.shape[0] % (16 * n_col)
             tail = panel_broadcast(local[head:], n_col, root, n_col - 1 - root)
             if head == 0:

time: 159 us -> 158 us (level)
  no operation moved by 1% of the time
where the time goes in v14:
time: 158 us; the launch traced here: 156 us
  starting transfers between devices  43.3 us (27%)
  Pallas kernels  38.9 us (25%)
  other arithmetic  25.2 us (16%)
  matrix products  22.6 us (14%)
  waiting for transfers between devices  22.6 us (14%)
    pallas_call x2, Pallas kernels, panel_broadcast(): pl.pallas_call(functools.partial(spread_kernel, root, size), out_shape=ja...  38.9 us
    another operation x4, other arithmetic, inverse_lower(): return lax.linalg.triangular_solve(block, ident, left_side=True, lower=True)  20.5 us
    ppermute x18, starting transfers between devices, tree_broadcast(): part = lax.ppermute(value, axis, pairs)  14 us
    ppermute x6, starting transfers between devices, halving_scatter(): blocks = keep + lax.ppermute(send, axis, pairs)  13.1 us
    ppermute x6, waiting for transfers between devices, butterfly_sum(): value = value + lax.ppermute(value, axis, pairs)  12.8 us
    ppermute x6, starting transfers between devices, butterfly_sum(): value = value + lax.ppermute(value, axis, pairs)  9.12 us
    ppermute x18, waiting for transfers between devices, tree_broadcast(): part = lax.ppermute(value, axis, pairs)  7.53 us
    ppermute x6, starting transfers between devices, doubling_gather(): other = lax.ppermute(value, axis, pairs)  7.08 us
  transfers between devices with their start and end apart: 36, of which 11 were waited for; matrix products, arithmetic and copies ran while one was open for 30% of the time, Pallas kernels for 25%

profile of v14, /device:TPU:1, one launch (start us, length us, event | category | flops | bytes accessed | tf_op | source)
XLA Modules:
  0.0 155.5 jit_solution(16521580014920166673)
XLA Ops:
  0.6 1.5 collective-permute-start.24
  2.2 0.8 select_bitcast_fusion.1
  3.1 9.8 %custom-call.4 = f32[1,128,128]{1,2,0:T(8,128)S(1)} custom-call(f32[1,128,128]{2,1,0:T(8,128)S(1)} %select_bitcast_fusion.1), custom_call_target="InvertDiagBlocksLowerTriangular" | custom-call | tf_op jit(solution)/shard_map/triangular_solve/custom-call.1 | solution.py:158
  13.2 2.6 %fusion.x_ref = bf16[2048,128]{1,0:T(8,128)(2,1)} fusion(f32[128,128]{1,0:T(8,128)S(1)} %fusion.21, f32[2048,1024]{1,0:T(8,128)} %param.17), kind=kOutput, calls=%fused_computation.6 | convolution fusion | flops 201588736 | bytes 1638400 | tf_op jit(solution)/shard_map/dot_general | solution.py:197
  15.8 18.4 %shard_map.137 = bf16[2048,128]{1,0:T(8,128)(2,1)} custom-call(bf16[2048,128]{1,0:T(8,128)(2,1)} %fusion.x_ref), custom_call_target="tpu_custom_call" | custom-call | tf_op jit(solution)/shard_map/pallas_call | solution.py:77
  34.2 1.5 fusion.17
  35.7 3.2 %collective-permute-start.3 = (f32[128,128]{1,0:T(8,128)S(1)}, f32[128,128]{1,0:T(8,128)S(1)}, u32[]{:S(2)}, u32[]{:S(2)}) collective-permute-start(f32[128,128]{1,0:T(8,128)S(1)} %fusion.17), channel_id=1, source_target_pairs={{0,16},{16,0},{32,48},{48,32},{64,80},{80,64},{96,112},{112,96},{1... | collective-permute-start | bytes 196616 | tf_op jit(solution)/shard_map/ppermute | solution.py:111
  38.9 3.1 %fusion.60 = f32[128,1024]{1,0:T(8,128)S(1)} fusion(bf16[2048,128]{1,0:T(8,128)(2,1)} %shard_map.137, bf16[2048,1024]{1,0:T(8,128)(2,1)} %param.12), kind=kOutput, calls=%fused_computation.107 | convolution fusion | flops 536870912 | bytes 5242880 | tf_op jit(solution)/shard_map/dot_general | solution.py:217
  42.1 2.8 %collective-permute-start = (f32[4,16,1024]{2,1,0:T(8,128)S(1)}, f32[4,16,1024]{2,1,0:T(8,128)S(1)}, u32[]{:S(2)}, u32[]{:S(2)}) collective-permute-start(f32[4,16,1024]{2,1,0:T(8,128)S(1)} %bitcast.62), channel_id=1, source_target_pairs={{0,64},{16,80},{32,96},{48,112},{64,0},{80,16},{96,32},{112,48},{1... | collective-permute-start | bytes 786440 | tf_op jit(solution)/shard_map/ppermute | solution.py:127
  45.0 9.8 %custom-call.5 = f32[1,128,128]{1,2,0:T(8,128)S(1)} custom-call(f32[1,128,128]{2,1,0:T(8,128)S(1)} %select_bitcast_fusion), custom_call_target="InvertDiagBlocksLowerTriangular" | custom-call | tf_op jit(solution)/shard_map/triangular_solve/custom-call.1 | solution.py:158
  55.2 0.4 collective-permute-start.13
  55.6 1.2 collective-permute-start.25
  56.8 0.4 collective-permute-start.4
  57.2 1.1 collective-permute-done.13
  58.4 1.2 collective-permute-start.14
  59.7 1.8 %collective-permute-done.4 = f32[128,128]{1,0:T(8,128)S(1)} collective-permute-done((f32[128,128]{1,0:T(8,128)S(1)}, f32[128,128]{1,0:T(8,128)S(1)}, u32[]{:S(2)}, u32[]{:S(2)}) %collective-permute-start.4) | collective-permute-done | bytes 65568 | tf_op jit(solution)/shard_map/ppermute | solution.py:111
  61.4 0.5 collective-permute-start.5
  61.9 2.7 %collective-permute-start.26 = (bf16[64,1024]{1,0:T(8,128)(2,1)S(1)}, bf16[64,1024]{1,0:T(8,128)(2,1)S(1)}, u32[]{:S(2)}, u32[]{:S(2)}) collective-permute-start(bf16[64,1024]{1,0:T(8,128)(2,1)S(1)} %maximum_select_fusion.3), channel_id=1, source_target_pairs={{0,64},{16,80},{32,96},{48,112},{64,0},{80,16},{96,32},{112,48},{1... | collective-permute-start | bytes 393224 | tf_op jit(solution)/shard_map/ppermute | solution.py:137
  64.6 2.5 %collective-permute-done.5 = f32[128,128]{1,0:T(8,128)S(1)} collective-permute-done((f32[128,128]{1,0:T(8,128)S(1)}, f32[128,128]{1,0:T(8,128)S(1)}, u32[]{:S(2)}, u32[]{:S(2)}) %collective-permute-start.5) | collective-permute-done | bytes 65568 | tf_op jit(solution)/shard_map/ppermute | solution.py:111
  67.1 0.7 collective-permute-start.8
  67.7 0.7 collective-permute-start.7
  68.4 0.8 collective-permute-start.6
  69.3 1.5 convolution_subtract_fusion.1
  71.0 1.3 collective-permute-start.11
  72.3 0.7 collective-permute-start.10
  73.0 0.7 collective-permute-start.9
  73.7 0.3 collective-permute-start.1
  74.0 3.8 %collective-permute-done.11 = f32[128,128]{1,0:T(8,128)S(1)} collective-permute-done((f32[128,128]{1,0:T(8,128)S(1)}, f32[128,128]{1,0:T(8,128)S(1)}, u32[]{:S(2)}, u32[]{:S(2)}) %collective-permute-start.11) | collective-permute-done | bytes 65568 | tf_op jit(solution)/shard_map/ppermute | solution.py:99
  77.9 1.1 fusion.2
  79.4 5.0 %collective-permute-start.2 = (f32[1,16,1024]{2,1,0:T(8,128)S(1)}, f32[1,16,1024]{2,1,0:T(8,128)S(1)}, u32[]{:S(2)}, u32[]{:S(2)}) collective-permute-start(f32[1,16,1024]{2,1,0:T(8,128)S(1)} %slice_select_fusion.8), channel_id=1, source_target_pairs={{0,16},{16,0},{32,48},{48,32},{64,80},{80,64},{96,112},{112,96},{1... | collective-permute-start | bytes 196616 | tf_op jit(solution)/shard_map/ppermute | solution.py:127
  84.7 0.6 collective-permute-done.2
  85.5 0.6 convolution_convert_fusion
  86.1 0.7 collective-permute-start.17
  86.7 0.7 collective-permute-start.16
  87.4 0.7 collective-permute-start.15
  88.1 0.8 slice.137.x_ref
  88.9 20.5 %shard_map.138 = bf16[2048,128]{1,0:T(8,128)(2,1)} custom-call(bf16[2048,128]{1,0:T(8,128)(2,1)} %slice.137.x_ref), custom_call_target="tpu_custom_call" | custom-call | tf_op jit(solution)/shard_map/pallas_call | solution.py:77
  109.4 3.1 %fusion.62 = f32[128,1024]{1,0:T(8,128)S(1)} fusion(bf16[2048,128]{1,0:T(8,128)(2,1)} %shard_map.138, bf16[2048,1024]{1,0:T(8,128)(2,1)} %param.12), kind=kOutput, calls=%fused_computation.109 | convolution fusion | flops 536870912 | bytes 5242880 | tf_op jit(solution)/shard_map/dot_general | solution.py:245
  112.6 1.3 collective-permute-start.20
  113.9 0.7 collective-permute-start.19
  114.6 0.7 collective-permute-start.18
  115.3 1.4 fusion.15
  116.7 1.5 collective-permute-done.20
  118.4 4.4 %collective-permute-start.21 = (f32[128,128]{1,0:T(8,128)S(1)}, f32[128,128]{1,0:T(8,128)S(1)}, u32[]{:S(2)}, u32[]{:S(2)}) collective-permute-start(f32[128,128]{1,0:T(8,128)S(1)} %convolution_add_fusion.1), channel_id=1, source_target_pairs={{0,16},{16,0},{32,48},{48,32},{64,80},{80,64},{96,112},{112,96},{1... | collective-permute-start | bytes 196616 | tf_op jit(solution)/shard_map/ppermute | solution.py:111
  123.2 0.4 collective-permute-done.21
  123.8 1.0 collective-permute-start.27
  124.9 2.0 %collective-permute-done.22 = f32[128,128]{1,0:T(8,128)S(1)} collective-permute-done((f32[128,128]{1,0:T(8,128)S(1)}, f32[128,128]{1,0:T(8,128)S(1)}, u32[]{:S(2)}, u32[]{:S(2)}) %collective-permute-start.22) | collective-permute-done | bytes 65568 | tf_op jit(solution)/shard_map/ppermute | solution.py:111
  126.9 0.6 collective-permute-start.23
  127.5 0.6 pad_maximum_fusion.2
  128.1 6.1 %collective-permute-done.23 = f32[128,128]{1,0:T(8,128)S(1)} collective-permute-done((f32[128,128]{1,0:T(8,128)S(1)}, f32[128,128]{1,0:T(8,128)S(1)}, u32[]{:S(2)}, u32[]{:S(2)}) %collective-permute-start.23) | collective-permute-done | bytes 65568 | tf_op jit(solution)/shard_map/ppermute | solution.py:111
  134.2 0.7 collective-permute-start.32
  134.9 0.7 collective-permute-start.31
  135.6 0.7 collective-permute-start.30
  136.2 4.7 %convolution_subtract_fusion = bf16[2048,1024]{1,0:T(8,128)(2,1)S(1)} fusion(f32[2048,1024]{1,0:T(8,128)} %param.17, bf16[2048,128]{1,0:T(8,128)(2,1)S(1)} %copy-done.1, bf16[2048,128]{1,0:T(8,128)(2,1)S(1)} %copy-done, bf16[128,1024]{1,0:T(8,128)(2,1)S(1)} %maximum_select_fusion.1, bf16[128,1024]{1,0:T(8,128)(2,1)S(1)} %maximum_select_fusion), kind=kOutput, calls=%fused_computation.1 | convolution fusion | flops 1081081856 | bytes 14155776 | tf_op jit(solution)/shard_map/dot_general | solution.py:238
  141.1 0.4 slice.197
  141.6 2.6 %pad_maximum_fusion = bf16[2048,1024]{1,0:T(8,128)(2,1)} fusion(bf16[2048,128]{1,0:T(8,128)(2,1)S(1)} %fusion.7, bf16[2048,896]{1,0:T(8,128)(2,1)S(1)} %slice.197), kind=kLoop, calls=%fused_computation.2 | loop fusion | flops 8388608 | bytes 8388608 | tf_op jit(solution)/shard_map/concatenate | solution.py:255
  144.3 1.3 collective-permute-start.35
  145.6 0.7 collective-permute-start.34
  146.2 0.7 collective-permute-start.33
  147.0 1.3 collective-permute-start.28
  148.3 2.2 %collective-permute-done.35 = f32[128,128]{1,0:T(8,128)S(1)} collective-permute-done((f32[128,128]{1,0:T(8,128)S(1)}, f32[128,128]{1,0:T(8,128)S(1)}, u32[]{:S(2)}, u32[]{:S(2)}) %collective-permute-start.35) | collective-permute-done | bytes 65568 | tf_op jit(solution)/shard_map/ppermute | solution.py:99
  151.2 2.6 %collective-permute-start.29 = (f32[1,16,1024]{2,1,0:T(8,128)S(1)}, f32[1,16,1024]{2,1,0:T(8,128)S(1)}, u32[]{:S(2)}, u32[]{:S(2)}) collective-permute-start(f32[1,16,1024]{2,1,0:T(8,128)S(1)} %slice_select_fusion.7), channel_id=1, source_target_pairs={{0,16},{16,0},{32,48},{48,32},{64,80},{80,64},{96,112},{112,96},{1... | collective-permute-start | bytes 196616 | tf_op jit(solution)/shard_map/ppermute | solution.py:127
  154.0 0.6 collective-permute-done.29
  154.9 0.6 pad_maximum_fusion.1
  (98 shorter events, 4.2 us)
Async XLA Ops:
  0.6 54.9 %collective-permute-start.24 = (bf16[16,1024]{1,0:T(8,128)(2,1)}, bf16[16,1024]{1,0:T(8,128)(2,1)S(1)}, u32[]{:S(2)}, u32[]{:S(2)}) collective-permute-start(bf16[16,1024]{1,0:T(8,128)(2,1)} %param.13), channel_id=1, source_target_pairs={{0,16},{16,0},{32,48},{48,32},{64,80},{80,64},{96,112},{112,96},{1... | collective-permute-start | bytes 98312 | tf_op jit(solution)/shard_map/ppermute | solution.py:137
  2.1 53.0 %collective-permute-start.12 = (bf16[16,1024]{1,0:T(8,128)(2,1)}, bf16[16,1024]{1,0:T(8,128)(2,1)S(1)}, u32[]{:S(2)}, u32[]{:S(2)}) collective-permute-start(bf16[16,1024]{1,0:T(8,128)(2,1)} %param.14), channel_id=1, source_target_pairs={{0,16},{16,0},{32,48},{48,32},{64,80},{80,64},{96,112},{112,96},{1... | collective-permute-start | bytes 98312 | tf_op jit(solution)/shard_map/ppermute | solution.py:137
  15.8 29.2 %copy-start.3 = (f32[128,128]{1,0:T(8,128)S(1)}, f32[128,128]{1,0:T(8,128)}, u32[]{:S(2)}) copy-start(f32[128,128]{1,0:T(8,128)} %param.15) | copy-start | bytes 196612
  15.8 39.4 %copy-start.4 = (bf16[16,1024]{1,0:T(8,128)(2,1)S(1)}, bf16[16,1024]{1,0:T(8,128)(2,1)}, u32[]{:S(2)}) copy-start(bf16[16,1024]{1,0:T(8,128)(2,1)} %param.14) | copy-start | bytes 98308
  34.2 21.4 %copy-start.10 = (bf16[16,1024]{1,0:T(8,128)(2,1)S(1)}, bf16[16,1024]{1,0:T(8,128)(2,1)}, u32[]{:S(2)}) copy-start(bf16[16,1024]{1,0:T(8,128)(2,1)} %param.13) | copy-start | bytes 98308
  35.7 21.1 %collective-permute-start.3 = (f32[128,128]{1,0:T(8,128)S(1)}, f32[128,128]{1,0:T(8,128)S(1)}, u32[]{:S(2)}, u32[]{:S(2)}) collective-permute-start(f32[128,128]{1,0:T(8,128)S(1)} %fusion.17), channel_id=1, source_target_pairs={{0,16},{16,0},{32,48},{48,32},{64,80},{80,64},{96,112},{112,96},{1... | collective-permute-start | bytes 196616 | tf_op jit(solution)/shard_map/ppermute | solution.py:111
  38.9 30.4 %copy-start = (bf16[2048,128]{1,0:T(8,128)(2,1)S(1)}, bf16[2048,128]{1,0:T(8,128)(2,1)}, u32[]{:S(2)}) copy-start(bf16[2048,128]{1,0:T(8,128)(2,1)} %shard_map.137) | copy-start | bytes 1572868
  42.1 35.8 %copy-start.2 = (f32[128,128]{1,0:T(8,128)S(1)}, f32[128,128]{1,0:T(8,128)}, u32[]{:S(2)}) copy-start(f32[128,128]{1,0:T(8,128)} %param.16) | copy-start | bytes 196612
  42.1 31.5 %collective-permute-start = (f32[4,16,1024]{2,1,0:T(8,128)S(1)}, f32[4,16,1024]{2,1,0:T(8,128)S(1)}, u32[]{:S(2)}, u32[]{:S(2)}) collective-permute-start(f32[4,16,1024]{2,1,0:T(8,128)S(1)} %bitcast.62), channel_id=1, source_target_pairs={{0,64},{16,80},{32,96},{48,112},{64,0},{80,16},{96,32},{112,48},{1... | collective-permute-start | bytes 786440 | tf_op jit(solution)/shard_map/ppermute | solution.py:127
  55.2 30.1 %copy-start.7 = (f32[16,1024]{1,0:T(8,128)S(1)}, f32[16,1024]{1,0:T(8,128)}, u32[]{:S(2)}) copy-start(f32[16,1024]{1,0:T(8,128)} %param.19) | copy-start | bytes 196612
  55.2 3.2 %collective-permute-start.13 = (bf16[32,1024]{1,0:T(8,128)(2,1)S(1)}, bf16[32,1024]{1,0:T(8,128)(2,1)S(1)}, u32[]{:S(2)}, u32[]{:S(2)}) collective-permute-start(bf16[32,1024]{1,0:T(8,128)(2,1)S(1)} %maximum_select_fusion.4), channel_id=1, source_target_pairs={{0,32},{16,48},{32,0},{48,16},{64,96},{80,112},{96,64},{112,80},{1... | collective-permute-start | bytes 196616 | tf_op jit(solution)/shard_map/ppermute | solution.py:137
  55.6 6.3 %collective-permute-start.25 = (bf16[32,1024]{1,0:T(8,128)(2,1)S(1)}, bf16[32,1024]{1,0:T(8,128)(2,1)S(1)}, u32[]{:S(2)}, u32[]{:S(2)}) collective-permute-start(bf16[32,1024]{1,0:T(8,128)(2,1)S(1)} %maximum_select_fusion.5), channel_id=1, source_target_pairs={{0,32},{16,48},{32,0},{48,16},{64,96},{80,112},{96,64},{112,80},{1... | collective-permute-start | bytes 196616 | tf_op jit(solution)/shard_map/ppermute | solution.py:137
  56.8 4.6 %collective-permute-start.4 = (f32[128,128]{1,0:T(8,128)S(1)}, f32[128,128]{1,0:T(8,128)S(1)}, u32[]{:S(2)}, u32[]{:S(2)}) collective-permute-start(f32[128,128]{1,0:T(8,128)S(1)} %add.117), channel_id=1, source_target_pairs={{0,32},{16,48},{32,0},{48,16},{64,96},{80,112},{96,64},{112,80},{1... | collective-permute-start | bytes 196616 | tf_op jit(solution)/shard_map/ppermute | solution.py:111
  58.4 10.0 %collective-permute-start.14 = (bf16[64,1024]{1,0:T(8,128)(2,1)S(1)}, bf16[64,1024]{1,0:T(8,128)(2,1)S(1)}, u32[]{:S(2)}, u32[]{:S(2)}) collective-permute-start(bf16[64,1024]{1,0:T(8,128)(2,1)S(1)} %maximum_select_fusion.2), channel_id=1, source_target_pairs={{0,64},{16,80},{32,96},{48,112},{64,0},{80,16},{96,32},{112,48},{1... | collective-permute-start | bytes 393224 | tf_op jit(solution)/shard_map/ppermute | solution.py:137
  61.4 5.6 %collective-permute-start.5 = (f32[128,128]{1,0:T(8,128)S(1)}, f32[128,128]{1,0:T(8,128)S(1)}, u32[]{:S(2)}, u32[]{:S(2)}) collective-permute-start(f32[128,128]{1,0:T(8,128)S(1)} %add.118), channel_id=1, source_target_pairs={{0,64},{16,80},{32,96},{48,112},{64,0},{80,16},{96,32},{112,48},{1... | collective-permute-start | bytes 196616 | tf_op jit(solution)/shard_map/ppermute | solution.py:111
  61.9 8.9 %collective-permute-start.26 = (bf16[64,1024]{1,0:T(8,128)(2,1)S(1)}, bf16[64,1024]{1,0:T(8,128)(2,1)S(1)}, u32[]{:S(2)}, u32[]{:S(2)}) collective-permute-start(bf16[64,1024]{1,0:T(8,128)(2,1)S(1)} %maximum_select_fusion.3), channel_id=1, source_target_pairs={{0,64},{16,80},{32,96},{48,112},{64,0},{80,16},{96,32},{112,48},{1... | collective-permute-start | bytes 393224 | tf_op jit(solution)/shard_map/ppermute | solution.py:137
  67.1 3.9 %collective-permute-start.8 = (f32[128,128]{1,0:T(8,128)S(1)}, f32[128,128]{1,0:T(8,128)S(1)}, u32[]{:S(2)}, u32[]{:S(2)}) collective-permute-start(f32[128,128]{1,0:T(8,128)S(1)} %add.119), channel_id=1, source_target_pairs={{15,12},{31,28},{47,44},{63,60},{79,76},{95,92},{111,108},{127,124}} | collective-permute-start | bytes 196616 | tf_op jit(solution)/shard_map/ppermute | solution.py:99
  67.7 3.2 %collective-permute-start.7 = (f32[128,128]{1,0:T(8,128)S(1)}, f32[128,128]{1,0:T(8,128)S(1)}, u32[]{:S(2)}, u32[]{:S(2)}) collective-permute-start(f32[128,128]{1,0:T(8,128)S(1)} %add.119), channel_id=1, source_target_pairs={{15,13},{31,29},{47,45},{63,61},{79,77},{95,93},{111,109},{127,125}} | collective-permute-start | bytes 196616 | tf_op jit(solution)/shard_map/ppermute | solution.py:99
  68.4 2.5 %collective-permute-start.6 = (f32[128,128]{1,0:T(8,128)S(1)}, f32[128,128]{1,0:T(8,128)S(1)}, u32[]{:S(2)}, u32[]{:S(2)}) collective-permute-start(f32[128,128]{1,0:T(8,128)S(1)} %add.119), channel_id=1, source_target_pairs={{15,14},{31,30},{47,46},{63,62},{79,78},{95,94},{111,110},{127,126}} | collective-permute-start | bytes 196616 | tf_op jit(solution)/shard_map/ppermute | solution.py:99
  71.0 6.9 %collective-permute-start.11 = (f32[128,128]{1,0:T(8,128)S(1)}, f32[128,128]{1,0:T(8,128)S(1)}, u32[]{:S(2)}, u32[]{:S(2)}) collective-permute-start(f32[128,128]{1,0:T(8,128)S(1)} %add_select_fusion.1), channel_id=1, source_target_pairs={{15,3},{14,2},{13,1},{12,0},{31,19},{30,18},{29,17},{28,16},{47,35... | collective-permute-start | bytes 196616 | tf_op jit(solution)/shard_map/ppermute | solution.py:99
  72.3 5.6 %collective-permute-start.10 = (f32[128,128]{1,0:T(8,128)S(1)}, f32[128,128]{1,0:T(8,128)S(1)}, u32[]{:S(2)}, u32[]{:S(2)}) collective-permute-start(f32[128,128]{1,0:T(8,128)S(1)} %add_select_fusion.1), channel_id=1, source_target_pairs={{15,7},{14,6},{13,5},{12,4},{31,23},{30,22},{29,21},{28,20},{47,39... | collective-permute-start | bytes 196616 | tf_op jit(solution)/shard_map/ppermute | solution.py:99
  73.0 4.9 %collective-permute-start.9 = (f32[128,128]{1,0:T(8,128)S(1)}, f32[128,128]{1,0:T(8,128)S(1)}, u32[]{:S(2)}, u32[]{:S(2)}) collective-permute-start(f32[128,128]{1,0:T(8,128)S(1)} %add_select_fusion.1), channel_id=1, source_target_pairs={{15,11},{14,10},{13,9},{12,8},{31,27},{30,26},{29,25},{28,24},{47,... | collective-permute-start | bytes 196616 | tf_op jit(solution)/shard_map/ppermute | solution.py:99
  73.7 5.6 %collective-permute-start.1 = (f32[2,16,1024]{2,1,0:T(8,128)S(1)}, f32[2,16,1024]{2,1,0:T(8,128)S(1)}, u32[]{:S(2)}, u32[]{:S(2)}) collective-permute-start(f32[2,16,1024]{2,1,0:T(8,128)S(1)} %slice_select_fusion.6), channel_id=1, source_target_pairs={{0,32},{16,48},{32,0},{48,16},{64,96},{80,112},{96,64},{112,80},{1... | collective-permute-start | bytes 393224 | tf_op jit(solution)/shard_map/ppermute | solution.py:127
  79.4 5.9 %collective-permute-start.2 = (f32[1,16,1024]{2,1,0:T(8,128)S(1)}, f32[1,16,1024]{2,1,0:T(8,128)S(1)}, u32[]{:S(2)}, u32[]{:S(2)}) collective-permute-start(f32[1,16,1024]{2,1,0:T(8,128)S(1)} %slice_select_fusion.8), channel_id=1, source_target_pairs={{0,16},{16,0},{32,48},{48,32},{64,80},{80,64},{96,112},{112,96},{1... | collective-permute-start | bytes 196616 | tf_op jit(solution)/shard_map/ppermute | solution.py:127
  84.6 28.0 %copy-start.5 = (f32[128,128]{1,0:T(8,128)}, f32[128,128]{1,0:T(8,128)S(1)}, u32[]{:S(2)}) copy-start(f32[128,128]{1,0:T(8,128)S(1)} %get-tuple-element.14) | copy-start | bytes 196612
  86.1 26.5 %collective-permute-start.17 = (bf16[16,128]{1,0:T(8,128)(2,1)S(1)}, bf16[16,128]{1,0:T(8,128)(2,1)S(1)}, u32[]{:S(2)}, u32[]{:S(2)}) collective-permute-start(bf16[16,128]{1,0:T(8,128)(2,1)S(1)} %slice.138), channel_id=1, source_target_pairs={{14,13},{30,29},{46,45},{62,61},{78,77},{94,93},{110,109},{126,125}} | collective-permute-start | bytes 12296 | tf_op jit(solution)/shard_map/ppermute | solution.py:99
  86.7 25.8 %collective-permute-start.16 = (bf16[16,128]{1,0:T(8,128)(2,1)S(1)}, bf16[16,128]{1,0:T(8,128)(2,1)S(1)}, u32[]{:S(2)}, u32[]{:S(2)}) collective-permute-start(bf16[16,128]{1,0:T(8,128)(2,1)S(1)} %slice.138), channel_id=1, source_target_pairs={{14,12},{30,28},{46,44},{62,60},{78,76},{94,92},{110,108},{126,124}} | collective-permute-start | bytes 12296 | tf_op jit(solution)/shard_map/ppermute | solution.py:99
  87.4 25.2 %collective-permute-start.15 = (bf16[16,128]{1,0:T(8,128)(2,1)S(1)}, bf16[16,128]{1,0:T(8,128)(2,1)S(1)}, u32[]{:S(2)}, u32[]{:S(2)}) collective-permute-start(bf16[16,128]{1,0:T(8,128)(2,1)S(1)} %slice.138), channel_id=1, source_target_pairs={{14,15},{30,31},{46,47},{62,63},{78,79},{94,95},{110,111},{126,127}} | collective-permute-start | bytes 12296 | tf_op jit(solution)/shard_map/ppermute | solution.py:99
  109.4 5.9 %copy-start.1 = (bf16[2048,128]{1,0:T(8,128)(2,1)S(1)}, bf16[2048,128]{1,0:T(8,128)(2,1)}, u32[]{:S(2)}) copy-start(bf16[2048,128]{1,0:T(8,128)(2,1)} %shard_map.138) | copy-start | bytes 1572868
  112.6 5.6 %collective-permute-start.20 = (bf16[16,128]{1,0:T(8,128)(2,1)S(1)}, bf16[16,128]{1,0:T(8,128)(2,1)S(1)}, u32[]{:S(2)}, u32[]{:S(2)}) collective-permute-start(bf16[16,128]{1,0:T(8,128)(2,1)S(1)} %add_select_fusion.3), channel_id=1, source_target_pairs={{14,2},{15,3},{12,0},{13,1},{30,18},{31,19},{28,16},{29,17},{46,34... | collective-permute-start | bytes 12296 | tf_op jit(solution)/shard_map/ppermute | solution.py:99
  113.9 4.3 %collective-permute-start.19 = (bf16[16,128]{1,0:T(8,128)(2,1)S(1)}, bf16[16,128]{1,0:T(8,128)(2,1)S(1)}, u32[]{:S(2)}, u32[]{:S(2)}) collective-permute-start(bf16[16,128]{1,0:T(8,128)(2,1)S(1)} %add_select_fusion.3), channel_id=1, source_target_pairs={{14,6},{15,7},{12,4},{13,5},{30,22},{31,23},{28,20},{29,21},{46,38... | collective-permute-start | bytes 12296 | tf_op jit(solution)/shard_map/ppermute | solution.py:99
  114.6 3.6 %collective-permute-start.18 = (bf16[16,128]{1,0:T(8,128)(2,1)S(1)}, bf16[16,128]{1,0:T(8,128)(2,1)S(1)}, u32[]{:S(2)}, u32[]{:S(2)}) collective-permute-start(bf16[16,128]{1,0:T(8,128)(2,1)S(1)} %add_select_fusion.3), channel_id=1, source_target_pairs={{14,10},{15,11},{12,8},{13,9},{30,26},{31,27},{28,24},{29,25},{46,... | collective-permute-start | bytes 12296 | tf_op jit(solution)/shard_map/ppermute | solution.py:99
  118.4 5.3 %collective-permute-start.21 = (f32[128,128]{1,0:T(8,128)S(1)}, f32[128,128]{1,0:T(8,128)S(1)}, u32[]{:S(2)}, u32[]{:S(2)}) collective-permute-start(f32[128,128]{1,0:T(8,128)S(1)} %convolution_add_fusion.1), channel_id=1, source_target_pairs={{0,16},{16,0},{32,48},{48,32},{64,80},{80,64},{96,112},{112,96},{1... | collective-permute-start | bytes 196616 | tf_op jit(solution)/shard_map/ppermute | solution.py:111
  123.7 3.2 %collective-permute-start.22 = (f32[128,128]{1,0:T(8,128)S(1)}, f32[128,128]{1,0:T(8,128)S(1)}, u32[]{:S(2)}, u32[]{:S(2)}) collective-permute-start(f32[128,128]{1,0:T(8,128)S(1)} %add.131), channel_id=1, source_target_pairs={{0,32},{16,48},{32,0},{48,16},{64,96},{80,112},{96,64},{112,80},{1... | collective-permute-start | bytes 196616 | tf_op jit(solution)/shard_map/ppermute | solution.py:111
  123.8 23.1 %collective-permute-start.27 = (f32[4,16,1024]{2,1,0:T(8,128)S(1)}, f32[4,16,1024]{2,1,0:T(8,128)S(1)}, u32[]{:S(2)}, u32[]{:S(2)}) collective-permute-start(f32[4,16,1024]{2,1,0:T(8,128)S(1)} %bitcast.63), channel_id=1, source_target_pairs={{0,64},{16,80},{32,96},{48,112},{64,0},{80,16},{96,32},{112,48},{1... | collective-permute-start | bytes 786440 | tf_op jit(solution)/shard_map/ppermute | solution.py:127
  126.9 7.3 %collective-permute-start.23 = (f32[128,128]{1,0:T(8,128)S(1)}, f32[128,128]{1,0:T(8,128)S(1)}, u32[]{:S(2)}, u32[]{:S(2)}) collective-permute-start(f32[128,128]{1,0:T(8,128)S(1)} %add.132), channel_id=1, source_target_pairs={{0,64},{16,80},{32,96},{48,112},{64,0},{80,16},{96,32},{112,48},{1... | collective-permute-start | bytes 196616 | tf_op jit(solution)/shard_map/ppermute | solution.py:111
  134.2 10.0 %collective-permute-start.32 = (f32[128,128]{1,0:T(8,128)S(1)}, f32[128,128]{1,0:T(8,128)S(1)}, u32[]{:S(2)}, u32[]{:S(2)}) collective-permute-start(f32[128,128]{1,0:T(8,128)S(1)} %add.133), channel_id=1, source_target_pairs={{14,13},{30,29},{46,45},{62,61},{78,77},{94,93},{110,109},{126,125}} | collective-permute-start | bytes 196616 | tf_op jit(solution)/shard_map/ppermute | solution.py:99
  134.9 9.4 %collective-permute-start.31 = (f32[128,128]{1,0:T(8,128)S(1)}, f32[128,128]{1,0:T(8,128)S(1)}, u32[]{:S(2)}, u32[]{:S(2)}) collective-permute-start(f32[128,128]{1,0:T(8,128)S(1)} %add.133), channel_id=1, source_target_pairs={{14,12},{30,28},{46,44},{62,60},{78,76},{94,92},{110,108},{126,124}} | collective-permute-start | bytes 196616 | tf_op jit(solution)/shard_map/ppermute | solution.py:99
  135.6 8.7 %collective-permute-start.30 = (f32[128,128]{1,0:T(8,128)S(1)}, f32[128,128]{1,0:T(8,128)S(1)}, u32[]{:S(2)}, u32[]{:S(2)}) collective-permute-start(f32[128,128]{1,0:T(8,128)S(1)} %add.133), channel_id=1, source_target_pairs={{14,15},{30,31},{46,47},{62,63},{78,79},{94,95},{110,111},{126,127}} | collective-permute-start | bytes 196616 | tf_op jit(solution)/shard_map/ppermute | solution.py:99
  141.6 8.9 %copy-start.9 = (f32[128,128]{1,0:T(8,128)S(1)}, f32[128,128]{1,0:T(8,128)}, u32[]{:S(2)}) copy-start(f32[128,128]{1,0:T(8,128)} %param.20) | copy-start | bytes 196612
  141.6 13.0 %copy-start.8 = (f32[16,1024]{1,0:T(8,128)S(1)}, f32[16,1024]{1,0:T(8,128)}, u32[]{:S(2)}) copy-start(f32[16,1024]{1,0:T(8,128)} %param.18) | copy-start | bytes 196612
  144.3 6.2 %collective-permute-start.35 = (f32[128,128]{1,0:T(8,128)S(1)}, f32[128,128]{1,0:T(8,128)S(1)}, u32[]{:S(2)}, u32[]{:S(2)}) collective-permute-start(f32[128,128]{1,0:T(8,128)S(1)} %add_select_fusion), channel_id=1, source_target_pairs={{14,2},{15,3},{12,0},{13,1},{30,18},{31,19},{28,16},{29,17},{46,34... | collective-permute-start | bytes 196616 | tf_op jit(solution)/shard_map/ppermute | solution.py:99
  145.6 4.9 %collective-permute-start.34 = (f32[128,128]{1,0:T(8,128)S(1)}, f32[128,128]{1,0:T(8,128)S(1)}, u32[]{:S(2)}, u32[]{:S(2)}) collective-permute-start(f32[128,128]{1,0:T(8,128)S(1)} %add_select_fusion), channel_id=1, source_target_pairs={{14,6},{15,7},{12,4},{13,5},{30,22},{31,23},{28,20},{29,21},{46,38... | collective-permute-start | bytes 196616 | tf_op jit(solution)/shard_map/ppermute | solution.py:99
  146.2 4.3 %collective-permute-start.33 = (f32[128,128]{1,0:T(8,128)S(1)}, f32[128,128]{1,0:T(8,128)S(1)}, u32[]{:S(2)}, u32[]{:S(2)}) collective-permute-start(f32[128,128]{1,0:T(8,128)S(1)} %add_select_fusion), channel_id=1, source_target_pairs={{14,10},{15,11},{12,8},{13,9},{30,26},{31,27},{28,24},{29,25},{46,... | collective-permute-start | bytes 196616 | tf_op jit(solution)/shard_map/ppermute | solution.py:99
  147.0 4.1 %collective-permute-start.28 = (f32[2,16,1024]{2,1,0:T(8,128)S(1)}, f32[2,16,1024]{2,1,0:T(8,128)S(1)}, u32[]{:S(2)}, u32[]{:S(2)}) collective-permute-start(f32[2,16,1024]{2,1,0:T(8,128)S(1)} %slice_select_fusion.5), channel_id=1, source_target_pairs={{0,32},{16,48},{32,0},{48,16},{64,96},{80,112},{96,64},{112,80},{1... | collective-permute-start | bytes 393224 | tf_op jit(solution)/shard_map/ppermute | solution.py:127
  151.2 3.5 %collective-permute-start.29 = (f32[1,16,1024]{2,1,0:T(8,128)S(1)}, f32[1,16,1024]{2,1,0:T(8,128)S(1)}, u32[]{:S(2)}, u32[]{:S(2)}) collective-permute-start(f32[1,16,1024]{2,1,0:T(8,128)S(1)} %slice_select_fusion.7), channel_id=1, source_target_pairs={{0,16},{16,0},{32,48},{48,32},{64,80},{80,64},{96,112},{112,96},{1... | collective-permute-start | bytes 196616 | tf_op jit(solution)/shard_map/ppermute | solution.py:127
  153.9 1.6 %copy-start.6 = (f32[128,128]{1,0:T(8,128)}, f32[128,128]{1,0:T(8,128)S(1)}, u32[]{:S(2)}) copy-start(f32[128,128]{1,0:T(8,128)S(1)} %get-tuple-element.16) | copy-start | bytes 196612

commit v15 on v12

--- a/solution.py
+++ b/solution.py
@@ -208,13 +208,15 @@
         inverse_two = inverse_lower(diag_two)
         solved_two = solve_panel(adj_trail[:, last:], inverse_two, root_two)
         partial_two = jnp.dot(solved_two.T, trail[:, last:], preferred_element_type=jnp.float32)
-        seed_two = jnp.tril(adj_diag_two - summed_block(partial_two, root_two))
+        rows_two = butterfly_sum(partial_two, "row", n_row)
+        solved_late, rows_two = lax.optimization_barrier((solved_two, rows_two))
+        seed_two = jnp.tril(adj_diag_two - tree_broadcast(rows_two, "col", n_col, root_two))
         grad_diag_two = block_adjoint(diag_two, inverse_two, seed_two)
         mirror_two = own_rows(grad_diag_two + grad_diag_two.T)
         rest_two = jnp.dot(mirror_two, full_two.astype(jnp.float32), precision=exact_mode)
         inverse_one = inverse_lower(diag_one)
         crossed = halving_scatter(
-            jnp.dot(solved_two.T, trail, preferred_element_type=jnp.float32), "row", n_row
+            jnp.dot(solved_late.T, trail, preferred_element_type=jnp.float32), "row", n_row
         )
         adj_two = adj_row_two - crossed - rest_two
         next_panel = adj_trail[:, last:] - jnp.dot(

time: 159 us -> 161 us (1.013)
  starting transfers between devices: 43.4 us -> 45.3 us
    ppermute x6, starting transfers between devices: 9.16 us -> 13 us  [butterfly_sum(): value = value + lax.ppermute(value, axis, pairs)]
    ppermute x6, waiting for transfers between devices: 1.18 us -> 4.34 us  [halving_scatter(): blocks = keep + lax.ppermute(send, axis, pairs)]
  transfers between devices with their start and end apart: 36 -> 36, of which waited for: 11 -> 11; matrix products, arithmetic and copies ran while one was open for 30% -> 30% of each run, Pallas kernels for 25% -> 24%
where the time goes in v15:
time: 161 us; the launch traced here: 159 us
  starting transfers between devices  45.3 us (28%)
  Pallas kernels  37.5 us (23%)
  other arithmetic  26 us (16%)
  waiting for transfers between devices  24.1 us (15%)
  matrix products  22.5 us (14%)
    pallas_call x2, Pallas kernels, panel_broadcast(): pl.pallas_call(functools.partial(spread_kernel, root, size), out_shape=ja...  37.5 us
    another operation x4, other arithmetic, inverse_lower(): return lax.linalg.triangular_solve(block, ident, left_side=True, lower=True)  21.3 us
    ppermute x18, starting transfers between devices, tree_broadcast(): part = lax.ppermute(value, axis, pairs)  14 us
    ppermute x6, starting transfers between devices, butterfly_sum(): value = value + lax.ppermute(value, axis, pairs)  13 us
    ppermute x6, starting transfers between devices, halving_scatter(): blocks = keep + lax.ppermute(send, axis, pairs)  12 us
    ppermute x6, waiting for transfers between devices, butterfly_sum(): value = value + lax.ppermute(value, axis, pairs)  11.2 us
    ppermute x18, waiting for transfers between devices, tree_broadcast(): part = lax.ppermute(value, axis, pairs)  7.71 us
    ppermute x6, starting transfers between devices, doubling_gather(): other = lax.ppermute(value, axis, pairs)  6.34 us
  transfers between devices with their start and end apart: 36, of which 11 were waited for; matrix products, arithmetic and copies ran while one was open for 30% of the time, Pallas kernels for 24%

profile of v15, /device:TPU:1, one launch (start us, length us, event | category | flops | bytes accessed | tf_op | source)
XLA Modules:
  0.0 158.5 jit_solution(249598533950349744)
XLA Ops:
  0.7 1.5 collective-permute-start.24
  2.2 0.8 select_bitcast_fusion.1
  3.1 9.8 %custom-call.4 = f32[1,128,128]{1,2,0:T(8,128)S(1)} custom-call(f32[1,128,128]{2,1,0:T(8,128)S(1)} %select_bitcast_fusion.1), custom_call_target="InvertDiagBlocksLowerTriangular" | custom-call | tf_op jit(solution)/shard_map/triangular_solve/custom-call.1 | solution.py:158
  13.2 3.0 %fusion.x_ref = bf16[2048,128]{1,0:T(8,128)(2,1)} fusion(f32[128,128]{1,0:T(8,128)S(1)} %fusion.21, f32[2048,1024]{1,0:T(8,128)} %param.17), kind=kOutput, calls=%fused_computation.6 | convolution fusion | flops 402915328 | bytes 1638400 | tf_op jit(solution)/shard_map/dot_general | solution.py:197
  16.2 18.3 %shard_map.137 = bf16[2048,128]{1,0:T(8,128)(2,1)} custom-call(bf16[2048,128]{1,0:T(8,128)(2,1)} %fusion.x_ref), custom_call_target="tpu_custom_call" | custom-call | tf_op jit(solution)/shard_map/pallas_call | solution.py:77
  34.5 1.5 fusion.17
  36.1 3.2 %collective-permute-start = (f32[128,128]{1,0:T(8,128)S(1)}, f32[128,128]{1,0:T(8,128)S(1)}, u32[]{:S(2)}, u32[]{:S(2)}) collective-permute-start(f32[128,128]{1,0:T(8,128)S(1)} %fusion.17), channel_id=1, source_target_pairs={{0,16},{16,0},{32,48},{48,32},{64,80},{80,64},{96,112},{112,96},{1... | collective-permute-start | bytes 196616 | tf_op jit(solution)/shard_map/ppermute | solution.py:111
  39.3 0.8 select_bitcast_fusion
  40.1 9.8 %custom-call.5 = f32[1,128,128]{1,2,0:T(8,128)S(1)} custom-call(f32[1,128,128]{2,1,0:T(8,128)S(1)} %select_bitcast_fusion), custom_call_target="InvertDiagBlocksLowerTriangular" | custom-call | tf_op jit(solution)/shard_map/triangular_solve/custom-call.1 | solution.py:158
  50.4 1.3 collective-permute-start.25
  51.7 0.3 collective-permute-start.13
  52.1 1.3 collective-permute-start.1
  53.4 0.8 collective-permute-done.25
  54.2 2.8 %collective-permute-start.26 = (bf16[64,1024]{1,0:T(8,128)(2,1)S(1)}, bf16[64,1024]{1,0:T(8,128)(2,1)S(1)}, u32[]{:S(2)}, u32[]{:S(2)}) collective-permute-start(bf16[64,1024]{1,0:T(8,128)(2,1)S(1)} %maximum_select_fusion.3), channel_id=1, source_target_pairs={{0,64},{16,80},{32,96},{48,112},{64,0},{80,16},{96,32},{112,48},{1... | collective-permute-start | bytes 393224 | tf_op jit(solution)/shard_map/ppermute | solution.py:137
  57.1 2.8 %collective-permute-start.2 = (f32[128,128]{1,0:T(8,128)S(1)}, f32[128,128]{1,0:T(8,128)S(1)}, u32[]{:S(2)}, u32[]{:S(2)}) collective-permute-start(f32[128,128]{1,0:T(8,128)S(1)} %add.115), channel_id=1, source_target_pairs={{0,64},{16,80},{32,96},{48,112},{64,0},{80,16},{96,32},{112,48},{1... | collective-permute-start | bytes 196616 | tf_op jit(solution)/shard_map/ppermute | solution.py:111
  60.2 2.6 %collective-permute-done.2 = f32[128,128]{1,0:T(8,128)S(1)} collective-permute-done((f32[128,128]{1,0:T(8,128)S(1)}, f32[128,128]{1,0:T(8,128)S(1)}, u32[]{:S(2)}, u32[]{:S(2)}) %collective-permute-start.2) | collective-permute-done | bytes 65568 | tf_op jit(solution)/shard_map/ppermute | solution.py:111
  62.9 0.8 collective-permute-start.8
  63.7 0.7 collective-permute-start.7
  64.3 0.7 collective-permute-start.6
  65.0 3.1 %fusion.60 = f32[128,1024]{1,0:T(8,128)S(1)} fusion(bf16[2048,128]{1,0:T(8,128)(2,1)} %shard_map.137, bf16[2048,1024]{1,0:T(8,128)(2,1)} %param.12), kind=kOutput, calls=%fused_computation.107 | convolution fusion | flops 536870912 | bytes 5242880 | tf_op jit(solution)/shard_map/dot_general | solution.py:219
  68.2 2.1 %collective-permute-start.3 = (f32[4,16,1024]{2,1,0:T(8,128)S(1)}, f32[4,16,1024]{2,1,0:T(8,128)S(1)}, u32[]{:S(2)}, u32[]{:S(2)}) collective-permute-start(f32[4,16,1024]{2,1,0:T(8,128)S(1)} %bitcast.63), channel_id=1, source_target_pairs={{0,64},{16,80},{32,96},{48,112},{64,0},{80,16},{96,32},{112,48},{1... | collective-permute-start | bytes 786440 | tf_op jit(solution)/shard_map/ppermute | solution.py:127
  70.4 1.5 convolution_subtract_fusion.1
  72.0 1.3 collective-permute-start.11
  73.3 0.7 collective-permute-start.10
  73.9 0.7 collective-permute-start.9
  74.7 3.6 %collective-permute-done.11 = f32[128,128]{1,0:T(8,128)S(1)} collective-permute-done((f32[128,128]{1,0:T(8,128)S(1)}, f32[128,128]{1,0:T(8,128)S(1)}, u32[]{:S(2)}, u32[]{:S(2)}) %collective-permute-start.11) | collective-permute-done | bytes 65568 | tf_op jit(solution)/shard_map/ppermute | solution.py:99
  78.7 0.4 collective-permute-start.4
  79.4 3.2 %collective-permute-done.4 = f32[2,16,1024]{2,1,0:T(8,128)S(1)} collective-permute-done((f32[2,16,1024]{2,1,0:T(8,128)S(1)}, f32[2,16,1024]{2,1,0:T(8,128)S(1)}, u32[]{:S(2)}, u32[]{:S(2)}) %collective-permute-start.4) | collective-permute-done | bytes 131104 | tf_op jit(solution)/shard_map/ppermute | solution.py:127
  82.6 5.0 %collective-permute-start.5 = (f32[1,16,1024]{2,1,0:T(8,128)S(1)}, f32[1,16,1024]{2,1,0:T(8,128)S(1)}, u32[]{:S(2)}, u32[]{:S(2)}) collective-permute-start(f32[1,16,1024]{2,1,0:T(8,128)S(1)} %slice_select_fusion.8), channel_id=1, source_target_pairs={{0,16},{16,0},{32,48},{48,32},{64,80},{80,64},{96,112},{112,96},{1... | collective-permute-start | bytes 196616 | tf_op jit(solution)/shard_map/ppermute | solution.py:127
  87.9 0.6 collective-permute-done.5
  88.8 1.0 convolution_convert_fusion
  89.8 0.7 collective-permute-start.17
  90.4 0.7 collective-permute-start.16
  91.1 0.7 collective-permute-start.15
  91.8 0.8 slice.137.x_ref
  92.6 19.2 %shard_map.138 = bf16[2048,128]{1,0:T(8,128)(2,1)} custom-call(bf16[2048,128]{1,0:T(8,128)(2,1)} %slice.137.x_ref), custom_call_target="tpu_custom_call" | custom-call | tf_op jit(solution)/shard_map/pallas_call | solution.py:77
  111.8 3.1 %fusion.62 = f32[128,1024]{1,0:T(8,128)S(1)} fusion(bf16[2048,128]{1,0:T(8,128)(2,1)} %shard_map.138, bf16[2048,1024]{1,0:T(8,128)(2,1)} %param.12), kind=kOutput, calls=%fused_computation.109 | convolution fusion | flops 536870912 | bytes 5242880 | tf_op jit(solution)/shard_map/dot_general | solution.py:247
  115.0 1.3 collective-permute-start.20
  116.3 0.7 collective-permute-start.19
  117.0 0.7 collective-permute-start.18
  117.7 1.4 fusion.15
  119.1 1.5 collective-permute-done.20
  120.8 4.4 %collective-permute-start.21 = (f32[128,128]{1,0:T(8,128)S(1)}, f32[128,128]{1,0:T(8,128)S(1)}, u32[]{:S(2)}, u32[]{:S(2)}) collective-permute-start(f32[128,128]{1,0:T(8,128)S(1)} %convolution_add_fusion.1), channel_id=1, source_target_pairs={{0,16},{16,0},{32,48},{48,32},{64,80},{80,64},{96,112},{112,96},{1... | collective-permute-start | bytes 196616 | tf_op jit(solution)/shard_map/ppermute | solution.py:111
  125.6 0.4 collective-permute-done.21
  126.1 0.7 collective-permute-start.22
  126.8 0.8 collective-permute-start.27
  127.6 1.7 %collective-permute-done.22 = f32[128,128]{1,0:T(8,128)S(1)} collective-permute-done((f32[128,128]{1,0:T(8,128)S(1)}, f32[128,128]{1,0:T(8,128)S(1)}, u32[]{:S(2)}, u32[]{:S(2)}) %collective-permute-start.22) | collective-permute-done | bytes 65568 | tf_op jit(solution)/shard_map/ppermute | solution.py:111
  129.3 0.6 collective-permute-start.23
  129.9 0.6 pad_maximum_fusion.2
  130.6 6.4 %collective-permute-done.23 = f32[128,128]{1,0:T(8,128)S(1)} collective-permute-done((f32[128,128]{1,0:T(8,128)S(1)}, f32[128,128]{1,0:T(8,128)S(1)}, u32[]{:S(2)}, u32[]{:S(2)}) %collective-permute-start.23) | collective-permute-done | bytes 65568 | tf_op jit(solution)/shard_map/ppermute | solution.py:111
  137.0 0.7 collective-permute-start.32
  137.7 0.7 collective-permute-start.31
  138.3 0.7 collective-permute-start.30
  139.0 4.7 %convolution_subtract_fusion = bf16[2048,1024]{1,0:T(8,128)(2,1)S(1)} fusion(f32[2048,1024]{1,0:T(8,128)} %param.17, bf16[2048,128]{1,0:T(8,128)(2,1)S(1)} %copy-done.1, bf16[2048,128]{1,0:T(8,128)(2,1)S(1)} %copy-done, bf16[128,1024]{1,0:T(8,128)(2,1)S(1)} %maximum_select_fusion.1, bf16[128,1024]{1,0:T(8,128)(2,1)S(1)} %maximum_select_fusion), kind=kOutput, calls=%fused_computation.1 | convolution fusion | flops 1081081856 | bytes 14155776 | tf_op jit(solution)/shard_map/dot_general | solution.py:240
  143.9 0.4 slice.197
  144.4 2.6 %pad_maximum_fusion = bf16[2048,1024]{1,0:T(8,128)(2,1)} fusion(bf16[2048,128]{1,0:T(8,128)(2,1)S(1)} %fusion.7, bf16[2048,896]{1,0:T(8,128)(2,1)S(1)} %slice.197), kind=kLoop, calls=%fused_computation.2 | loop fusion | flops 8388608 | bytes 8388608 | tf_op jit(solution)/shard_map/concatenate | solution.py:257
  147.1 1.3 collective-permute-start.35
  148.4 0.7 collective-permute-start.34
  149.1 0.7 collective-permute-start.33
  149.8 1.0 collective-permute-start.28
  150.7 2.5 %collective-permute-done.35 = f32[128,128]{1,0:T(8,128)S(1)} collective-permute-done((f32[128,128]{1,0:T(8,128)S(1)}, f32[128,128]{1,0:T(8,128)S(1)}, u32[]{:S(2)}, u32[]{:S(2)}) %collective-permute-start.35) | collective-permute-done | bytes 65568 | tf_op jit(solution)/shard_map/ppermute | solution.py:99
  154.0 2.7 %collective-permute-start.29 = (f32[1,16,1024]{2,1,0:T(8,128)S(1)}, f32[1,16,1024]{2,1,0:T(8,128)S(1)}, u32[]{:S(2)}, u32[]{:S(2)}) collective-permute-start(f32[1,16,1024]{2,1,0:T(8,128)S(1)} %slice_select_fusion.7), channel_id=1, source_target_pairs={{0,16},{16,0},{32,48},{48,32},{64,80},{80,64},{96,112},{112,96},{1... | collective-permute-start | bytes 196616 | tf_op jit(solution)/shard_map/ppermute | solution.py:127
  157.0 0.6 collective-permute-done.29
  157.9 0.6 pad_maximum_fusion.1
  (100 shorter events, 4.7 us)
Async XLA Ops:
  0.6 49.7 %copy-start.11 = (bf16[16,1024]{1,0:T(8,128)(2,1)S(1)}, bf16[16,1024]{1,0:T(8,128)(2,1)}, u32[]{:S(2)}) copy-start(bf16[16,1024]{1,0:T(8,128)(2,1)} %param.13) | copy-start | bytes 98308
  0.6 51.1 %copy-start.4 = (bf16[16,1024]{1,0:T(8,128)(2,1)S(1)}, bf16[16,1024]{1,0:T(8,128)(2,1)}, u32[]{:S(2)}) copy-start(bf16[16,1024]{1,0:T(8,128)(2,1)} %param.14) | copy-start | bytes 98308
  0.7 49.7 %collective-permute-start.24 = (bf16[16,1024]{1,0:T(8,128)(2,1)}, bf16[16,1024]{1,0:T(8,128)(2,1)S(1)}, u32[]{:S(2)}, u32[]{:S(2)}) collective-permute-start(bf16[16,1024]{1,0:T(8,128)(2,1)} %param.13), channel_id=1, source_target_pairs={{0,16},{16,0},{32,48},{48,32},{64,80},{80,64},{96,112},{112,96},{1... | collective-permute-start | bytes 98312 | tf_op jit(solution)/shard_map/ppermute | solution.py:137
  2.2 49.5 %collective-permute-start.12 = (bf16[16,1024]{1,0:T(8,128)(2,1)}, bf16[16,1024]{1,0:T(8,128)(2,1)S(1)}, u32[]{:S(2)}, u32[]{:S(2)}) collective-permute-start(bf16[16,1024]{1,0:T(8,128)(2,1)} %param.14), channel_id=1, source_target_pairs={{0,16},{16,0},{32,48},{48,32},{64,80},{80,64},{96,112},{112,96},{1... | collective-permute-start | bytes 98312 | tf_op jit(solution)/shard_map/ppermute | solution.py:137
  36.1 16.0 %collective-permute-start = (f32[128,128]{1,0:T(8,128)S(1)}, f32[128,128]{1,0:T(8,128)S(1)}, u32[]{:S(2)}, u32[]{:S(2)}) collective-permute-start(f32[128,128]{1,0:T(8,128)S(1)} %fusion.17), channel_id=1, source_target_pairs={{0,16},{16,0},{32,48},{48,32},{64,80},{80,64},{96,112},{112,96},{1... | collective-permute-start | bytes 196616 | tf_op jit(solution)/shard_map/ppermute | solution.py:111
  50.3 20.1 %copy-start = (bf16[2048,128]{1,0:T(8,128)(2,1)S(1)}, bf16[2048,128]{1,0:T(8,128)(2,1)}, u32[]{:S(2)}) copy-start(bf16[2048,128]{1,0:T(8,128)(2,1)} %shard_map.137) | copy-start | bytes 1572868
  50.4 3.8 %collective-permute-start.25 = (bf16[32,1024]{1,0:T(8,128)(2,1)S(1)}, bf16[32,1024]{1,0:T(8,128)(2,1)S(1)}, u32[]{:S(2)}, u32[]{:S(2)}) collective-permute-start(bf16[32,1024]{1,0:T(8,128)(2,1)S(1)} %maximum_select_fusion.5), channel_id=1, source_target_pairs={{0,32},{16,48},{32,0},{48,16},{64,96},{80,112},{96,64},{112,80},{1... | collective-permute-start | bytes 196616 | tf_op jit(solution)/shard_map/ppermute | solution.py:137
  51.7 8.2 %collective-permute-start.13 = (bf16[32,1024]{1,0:T(8,128)(2,1)S(1)}, bf16[32,1024]{1,0:T(8,128)(2,1)S(1)}, u32[]{:S(2)}, u32[]{:S(2)}) collective-permute-start(bf16[32,1024]{1,0:T(8,128)(2,1)S(1)} %maximum_select_fusion.4), channel_id=1, source_target_pairs={{0,32},{16,48},{32,0},{48,16},{64,96},{80,112},{96,64},{112,80},{1... | collective-permute-start | bytes 196616 | tf_op jit(solution)/shard_map/ppermute | solution.py:137
  52.1 5.0 %collective-permute-start.1 = (f32[128,128]{1,0:T(8,128)S(1)}, f32[128,128]{1,0:T(8,128)S(1)}, u32[]{:S(2)}, u32[]{:S(2)}) collective-permute-start(f32[128,128]{1,0:T(8,128)S(1)} %add.114), channel_id=1, source_target_pairs={{0,32},{16,48},{32,0},{48,16},{64,96},{80,112},{96,64},{112,80},{1... | collective-permute-start | bytes 196616 | tf_op jit(solution)/shard_map/ppermute | solution.py:111
  54.2 20.4 %collective-permute-start.26 = (bf16[64,1024]{1,0:T(8,128)(2,1)S(1)}, bf16[64,1024]{1,0:T(8,128)(2,1)S(1)}, u32[]{:S(2)}, u32[]{:S(2)}) collective-permute-start(bf16[64,1024]{1,0:T(8,128)(2,1)S(1)} %maximum_select_fusion.3), channel_id=1, source_target_pairs={{0,64},{16,80},{32,96},{48,112},{64,0},{80,16},{96,32},{112,48},{1... | collective-permute-start | bytes 393224 | tf_op jit(solution)/shard_map/ppermute | solution.py:137
  57.1 5.8 %collective-permute-start.2 = (f32[128,128]{1,0:T(8,128)S(1)}, f32[128,128]{1,0:T(8,128)S(1)}, u32[]{:S(2)}, u32[]{:S(2)}) collective-permute-start(f32[128,128]{1,0:T(8,128)S(1)} %add.115), channel_id=1, source_target_pairs={{0,64},{16,80},{32,96},{48,112},{64,0},{80,16},{96,32},{112,48},{1... | collective-permute-start | bytes 196616 | tf_op jit(solution)/shard_map/ppermute | solution.py:111
  59.9 8.2 %collective-permute-start.14 = (bf16[64,1024]{1,0:T(8,128)(2,1)S(1)}, bf16[64,1024]{1,0:T(8,128)(2,1)S(1)}, u32[]{:S(2)}, u32[]{:S(2)}) collective-permute-start(bf16[64,1024]{1,0:T(8,128)(2,1)S(1)} %maximum_select_fusion.2), channel_id=1, source_target_pairs={{0,64},{16,80},{32,96},{48,112},{64,0},{80,16},{96,32},{112,48},{1... | collective-permute-start | bytes 393224 | tf_op jit(solution)/shard_map/ppermute | solution.py:137
  62.8 15.4 %copy-start.2 = (f32[128,128]{1,0:T(8,128)S(1)}, f32[128,128]{1,0:T(8,128)}, u32[]{:S(2)}) copy-start(f32[128,128]{1,0:T(8,128)} %param.16) | copy-start | bytes 196612
  62.9 15.4 %copy-start.9 = (f32[128,128]{1,0:T(8,128)S(1)}, f32[128,128]{1,0:T(8,128)}, u32[]{:S(2)}) copy-start(f32[128,128]{1,0:T(8,128)} %param.21) | copy-start | bytes 196612
  62.9 9.0 %collective-permute-start.8 = (f32[128,128]{1,0:T(8,128)S(1)}, f32[128,128]{1,0:T(8,128)S(1)}, u32[]{:S(2)}, u32[]{:S(2)}) collective-permute-start(f32[128,128]{1,0:T(8,128)S(1)} %add.116), channel_id=1, source_target_pairs={{15,12},{31,28},{47,44},{63,60},{79,76},{95,92},{111,108},{127,124}} | collective-permute-start | bytes 196616 | tf_op jit(solution)/shard_map/ppermute | solution.py:99
  63.7 8.2 %collective-permute-start.7 = (f32[128,128]{1,0:T(8,128)S(1)}, f32[128,128]{1,0:T(8,128)S(1)}, u32[]{:S(2)}, u32[]{:S(2)}) collective-permute-start(f32[128,128]{1,0:T(8,128)S(1)} %add.116), channel_id=1, source_target_pairs={{15,13},{31,29},{47,45},{63,61},{79,77},{95,93},{111,109},{127,125}} | collective-permute-start | bytes 196616 | tf_op jit(solution)/shard_map/ppermute | solution.py:99
  64.3 7.6 %collective-permute-start.6 = (f32[128,128]{1,0:T(8,128)S(1)}, f32[128,128]{1,0:T(8,128)S(1)}, u32[]{:S(2)}, u32[]{:S(2)}) collective-permute-start(f32[128,128]{1,0:T(8,128)S(1)} %add.116), channel_id=1, source_target_pairs={{15,14},{31,30},{47,46},{63,62},{79,78},{95,94},{111,110},{127,126}} | collective-permute-start | bytes 196616 | tf_op jit(solution)/shard_map/ppermute | solution.py:99
  68.1 20.4 %copy-start.7 = (f32[16,1024]{1,0:T(8,128)S(1)}, f32[16,1024]{1,0:T(8,128)}, u32[]{:S(2)}) copy-start(f32[16,1024]{1,0:T(8,128)} %param.19) | copy-start | bytes 196612
  68.2 10.4 %collective-permute-start.3 = (f32[4,16,1024]{2,1,0:T(8,128)S(1)}, f32[4,16,1024]{2,1,0:T(8,128)S(1)}, u32[]{:S(2)}, u32[]{:S(2)}) collective-permute-start(f32[4,16,1024]{2,1,0:T(8,128)S(1)} %bitcast.63), channel_id=1, source_target_pairs={{0,64},{16,80},{32,96},{48,112},{64,0},{80,16},{96,32},{112,48},{1... | collective-permute-start | bytes 786440 | tf_op jit(solution)/shard_map/ppermute | solution.py:127
  72.0 6.3 %collective-permute-start.11 = (f32[128,128]{1,0:T(8,128)S(1)}, f32[128,128]{1,0:T(8,128)S(1)}, u32[]{:S(2)}, u32[]{:S(2)}) collective-permute-start(f32[128,128]{1,0:T(8,128)S(1)} %add_select_fusion.1), channel_id=1, source_target_pairs={{15,3},{14,2},{13,1},{12,0},{31,19},{30,18},{29,17},{28,16},{47,35... | collective-permute-start | bytes 196616 | tf_op jit(solution)/shard_map/ppermute | solution.py:99
  73.3 5.0 %collective-permute-start.10 = (f32[128,128]{1,0:T(8,128)S(1)}, f32[128,128]{1,0:T(8,128)S(1)}, u32[]{:S(2)}, u32[]{:S(2)}) collective-permute-start(f32[128,128]{1,0:T(8,128)S(1)} %add_select_fusion.1), channel_id=1, source_target_pairs={{15,7},{14,6},{13,5},{12,4},{31,23},{30,22},{29,21},{28,20},{47,39... | collective-permute-start | bytes 196616 | tf_op jit(solution)/shard_map/ppermute | solution.py:99
  73.9 4.4 %collective-permute-start.9 = (f32[128,128]{1,0:T(8,128)S(1)}, f32[128,128]{1,0:T(8,128)S(1)}, u32[]{:S(2)}, u32[]{:S(2)}) collective-permute-start(f32[128,128]{1,0:T(8,128)S(1)} %add_select_fusion.1), channel_id=1, source_target_pairs={{15,11},{14,10},{13,9},{12,8},{31,27},{30,26},{29,25},{28,24},{47,... | collective-permute-start | bytes 196616 | tf_op jit(solution)/shard_map/ppermute | solution.py:99
  78.7 3.9 %collective-permute-start.4 = (f32[2,16,1024]{2,1,0:T(8,128)S(1)}, f32[2,16,1024]{2,1,0:T(8,128)S(1)}, u32[]{:S(2)}, u32[]{:S(2)}) collective-permute-start(f32[2,16,1024]{2,1,0:T(8,128)S(1)} %slice_select_fusion.6), channel_id=1, source_target_pairs={{0,32},{16,48},{32,0},{48,16},{64,96},{80,112},{96,64},{112,80},{1... | collective-permute-start | bytes 393224 | tf_op jit(solution)/shard_map/ppermute | solution.py:127
  82.6 5.9 %collective-permute-start.5 = (f32[1,16,1024]{2,1,0:T(8,128)S(1)}, f32[1,16,1024]{2,1,0:T(8,128)S(1)}, u32[]{:S(2)}, u32[]{:S(2)}) collective-permute-start(f32[1,16,1024]{2,1,0:T(8,128)S(1)} %slice_select_fusion.8), channel_id=1, source_target_pairs={{0,16},{16,0},{32,48},{48,32},{64,80},{80,64},{96,112},{112,96},{1... | collective-permute-start | bytes 196616 | tf_op jit(solution)/shard_map/ppermute | solution.py:127
  87.8 27.1 %copy-start.5 = (f32[128,128]{1,0:T(8,128)}, f32[128,128]{1,0:T(8,128)S(1)}, u32[]{:S(2)}) copy-start(f32[128,128]{1,0:T(8,128)S(1)} %get-tuple-element.18) | copy-start | bytes 196612
  89.8 25.2 %collective-permute-start.17 = (bf16[16,128]{1,0:T(8,128)(2,1)S(1)}, bf16[16,128]{1,0:T(8,128)(2,1)S(1)}, u32[]{:S(2)}, u32[]{:S(2)}) collective-permute-start(bf16[16,128]{1,0:T(8,128)(2,1)S(1)} %slice.138), channel_id=1, source_target_pairs={{14,13},{30,29},{46,45},{62,61},{78,77},{94,93},{110,109},{126,125}} | collective-permute-start | bytes 12296 | tf_op jit(solution)/shard_map/ppermute | solution.py:99
  90.4 24.6 %collective-permute-start.16 = (bf16[16,128]{1,0:T(8,128)(2,1)S(1)}, bf16[16,128]{1,0:T(8,128)(2,1)S(1)}, u32[]{:S(2)}, u32[]{:S(2)}) collective-permute-start(bf16[16,128]{1,0:T(8,128)(2,1)S(1)} %slice.138), channel_id=1, source_target_pairs={{14,12},{30,28},{46,44},{62,60},{78,76},{94,92},{110,108},{126,124}} | collective-permute-start | bytes 12296 | tf_op jit(solution)/shard_map/ppermute | solution.py:99
  91.1 23.9 %collective-permute-start.15 = (bf16[16,128]{1,0:T(8,128)(2,1)S(1)}, bf16[16,128]{1,0:T(8,128)(2,1)S(1)}, u32[]{:S(2)}, u32[]{:S(2)}) collective-permute-start(bf16[16,128]{1,0:T(8,128)(2,1)S(1)} %slice.138), channel_id=1, source_target_pairs={{14,15},{30,31},{46,47},{62,63},{78,79},{94,95},{110,111},{126,127}} | collective-permute-start | bytes 12296 | tf_op jit(solution)/shard_map/ppermute | solution.py:99
  111.8 5.9 %copy-start.1 = (bf16[2048,128]{1,0:T(8,128)(2,1)S(1)}, bf16[2048,128]{1,0:T(8,128)(2,1)}, u32[]{:S(2)}) copy-start(bf16[2048,128]{1,0:T(8,128)(2,1)} %shard_map.138) | copy-start | bytes 1572868
  115.0 5.6 %collective-permute-start.20 = (bf16[16,128]{1,0:T(8,128)(2,1)S(1)}, bf16[16,128]{1,0:T(8,128)(2,1)S(1)}, u32[]{:S(2)}, u32[]{:S(2)}) collective-permute-start(bf16[16,128]{1,0:T(8,128)(2,1)S(1)} %add_select_fusion.3), channel_id=1, source_target_pairs={{14,2},{15,3},{12,0},{13,1},{30,18},{31,19},{28,16},{29,17},{46,34... | collective-permute-start | bytes 12296 | tf_op jit(solution)/shard_map/ppermute | solution.py:99
  116.3 4.3 %collective-permute-start.19 = (bf16[16,128]{1,0:T(8,128)(2,1)S(1)}, bf16[16,128]{1,0:T(8,128)(2,1)S(1)}, u32[]{:S(2)}, u32[]{:S(2)}) collective-permute-start(bf16[16,128]{1,0:T(8,128)(2,1)S(1)} %add_select_fusion.3), channel_id=1, source_target_pairs={{14,6},{15,7},{12,4},{13,5},{30,22},{31,23},{28,20},{29,21},{46,38... | collective-permute-start | bytes 12296 | tf_op jit(solution)/shard_map/ppermute | solution.py:99
  117.0 3.6 %collective-permute-start.18 = (bf16[16,128]{1,0:T(8,128)(2,1)S(1)}, bf16[16,128]{1,0:T(8,128)(2,1)S(1)}, u32[]{:S(2)}, u32[]{:S(2)}) collective-permute-start(bf16[16,128]{1,0:T(8,128)(2,1)S(1)} %add_select_fusion.3), channel_id=1, source_target_pairs={{14,10},{15,11},{12,8},{13,9},{30,26},{31,27},{28,24},{29,25},{46,... | collective-permute-start | bytes 12296 | tf_op jit(solution)/shard_map/ppermute | solution.py:99
  120.8 5.3 %collective-permute-start.21 = (f32[128,128]{1,0:T(8,128)S(1)}, f32[128,128]{1,0:T(8,128)S(1)}, u32[]{:S(2)}, u32[]{:S(2)}) collective-permute-start(f32[128,128]{1,0:T(8,128)S(1)} %convolution_add_fusion.1), channel_id=1, source_target_pairs={{0,16},{16,0},{32,48},{48,32},{64,80},{80,64},{96,112},{112,96},{1... | collective-permute-start | bytes 196616 | tf_op jit(solution)/shard_map/ppermute | solution.py:111
  126.1 3.2 %collective-permute-start.22 = (f32[128,128]{1,0:T(8,128)S(1)}, f32[128,128]{1,0:T(8,128)S(1)}, u32[]{:S(2)}, u32[]{:S(2)}) collective-permute-start(f32[128,128]{1,0:T(8,128)S(1)} %add.131), channel_id=1, source_target_pairs={{0,32},{16,48},{32,0},{48,16},{64,96},{80,112},{96,64},{112,80},{1... | collective-permute-start | bytes 196616 | tf_op jit(solution)/shard_map/ppermute | solution.py:111
  126.8 22.9 %collective-permute-start.27 = (f32[4,16,1024]{2,1,0:T(8,128)S(1)}, f32[4,16,1024]{2,1,0:T(8,128)S(1)}, u32[]{:S(2)}, u32[]{:S(2)}) collective-permute-start(f32[4,16,1024]{2,1,0:T(8,128)S(1)} %bitcast.62), channel_id=1, source_target_pairs={{0,64},{16,80},{32,96},{48,112},{64,0},{80,16},{96,32},{112,48},{1... | collective-permute-start | bytes 786440 | tf_op jit(solution)/shard_map/ppermute | solution.py:127
  129.3 7.7 %collective-permute-start.23 = (f32[128,128]{1,0:T(8,128)S(1)}, f32[128,128]{1,0:T(8,128)S(1)}, u32[]{:S(2)}, u32[]{:S(2)}) collective-permute-start(f32[128,128]{1,0:T(8,128)S(1)} %add.132), channel_id=1, source_target_pairs={{0,64},{16,80},{32,96},{48,112},{64,0},{80,16},{96,32},{112,48},{1... | collective-permute-start | bytes 196616 | tf_op jit(solution)/shard_map/ppermute | solution.py:111
  137.0 10.0 %collective-permute-start.32 = (f32[128,128]{1,0:T(8,128)S(1)}, f32[128,128]{1,0:T(8,128)S(1)}, u32[]{:S(2)}, u32[]{:S(2)}) collective-permute-start(f32[128,128]{1,0:T(8,128)S(1)} %add.133), channel_id=1, source_target_pairs={{14,13},{30,29},{46,45},{62,61},{78,77},{94,93},{110,109},{126,125}} | collective-permute-start | bytes 196616 | tf_op jit(solution)/shard_map/ppermute | solution.py:99
  137.7 9.4 %collective-permute-start.31 = (f32[128,128]{1,0:T(8,128)S(1)}, f32[128,128]{1,0:T(8,128)S(1)}, u32[]{:S(2)}, u32[]{:S(2)}) collective-permute-start(f32[128,128]{1,0:T(8,128)S(1)} %add.133), channel_id=1, source_target_pairs={{14,12},{30,28},{46,44},{62,60},{78,76},{94,92},{110,108},{126,124}} | collective-permute-start | bytes 196616 | tf_op jit(solution)/shard_map/ppermute | solution.py:99
  138.3 8.7 %collective-permute-start.30 = (f32[128,128]{1,0:T(8,128)S(1)}, f32[128,128]{1,0:T(8,128)S(1)}, u32[]{:S(2)}, u32[]{:S(2)}) collective-permute-start(f32[128,128]{1,0:T(8,128)S(1)} %add.133), channel_id=1, source_target_pairs={{14,15},{30,31},{46,47},{62,63},{78,79},{94,95},{110,111},{126,127}} | collective-permute-start | bytes 196616 | tf_op jit(solution)/shard_map/ppermute | solution.py:99
  144.4 8.9 %copy-start.3 = (f32[128,128]{1,0:T(8,128)S(1)}, f32[128,128]{1,0:T(8,128)}, u32[]{:S(2)}) copy-start(f32[128,128]{1,0:T(8,128)} %param.15) | copy-start | bytes 196612
  144.4 8.9 %copy-start.10 = (f32[128,128]{1,0:T(8,128)S(1)}, f32[128,128]{1,0:T(8,128)}, u32[]{:S(2)}) copy-start(f32[128,128]{1,0:T(8,128)} %param.20) | copy-start | bytes 196612
  144.4 13.2 %copy-start.8 = (f32[16,1024]{1,0:T(8,128)S(1)}, f32[16,1024]{1,0:T(8,128)}, u32[]{:S(2)}) copy-start(f32[16,1024]{1,0:T(8,128)} %param.18) | copy-start | bytes 196612
  147.1 6.2 %collective-permute-start.35 = (f32[128,128]{1,0:T(8,128)S(1)}, f32[128,128]{1,0:T(8,128)S(1)}, u32[]{:S(2)}, u32[]{:S(2)}) collective-permute-start(f32[128,128]{1,0:T(8,128)S(1)} %add_select_fusion), channel_id=1, source_target_pairs={{14,2},{15,3},{12,0},{13,1},{30,18},{31,19},{28,16},{29,17},{46,34... | collective-permute-start | bytes 196616 | tf_op jit(solution)/shard_map/ppermute | solution.py:99
  148.4 4.9 %collective-permute-start.34 = (f32[128,128]{1,0:T(8,128)S(1)}, f32[128,128]{1,0:T(8,128)S(1)}, u32[]{:S(2)}, u32[]{:S(2)}) collective-permute-start(f32[128,128]{1,0:T(8,128)S(1)} %add_select_fusion), channel_id=1, source_target_pairs={{14,6},{15,7},{12,4},{13,5},{30,22},{31,23},{28,20},{29,21},{46,38... | collective-permute-start | bytes 196616 | tf_op jit(solution)/shard_map/ppermute | solution.py:99
  149.1 4.3 %collective-permute-start.33 = (f32[128,128]{1,0:T(8,128)S(1)}, f32[128,128]{1,0:T(8,128)S(1)}, u32[]{:S(2)}, u32[]{:S(2)}) collective-permute-start(f32[128,128]{1,0:T(8,128)S(1)} %add_select_fusion), channel_id=1, source_target_pairs={{14,10},{15,11},{12,8},{13,9},{30,26},{31,27},{28,24},{29,25},{46,... | collective-permute-start | bytes 196616 | tf_op jit(solution)/shard_map/ppermute | solution.py:99
  149.8 4.1 %collective-permute-start.28 = (f32[2,16,1024]{2,1,0:T(8,128)S(1)}, f32[2,16,1024]{2,1,0:T(8,128)S(1)}, u32[]{:S(2)}, u32[]{:S(2)}) collective-permute-start(f32[2,16,1024]{2,1,0:T(8,128)S(1)} %slice_select_fusion.5), channel_id=1, source_target_pairs={{0,32},{16,48},{32,0},{48,16},{64,96},{80,112},{96,64},{112,80},{1... | collective-permute-start | bytes 393224 | tf_op jit(solution)/shard_map/ppermute | solution.py:127
  154.0 3.6 %collective-permute-start.29 = (f32[1,16,1024]{2,1,0:T(8,128)S(1)}, f32[1,16,1024]{2,1,0:T(8,128)S(1)}, u32[]{:S(2)}, u32[]{:S(2)}) collective-permute-start(f32[1,16,1024]{2,1,0:T(8,128)S(1)} %slice_select_fusion.7), channel_id=1, source_target_pairs={{0,16},{16,0},{32,48},{48,32},{64,80},{80,64},{96,112},{112,96},{1... | collective-permute-start | bytes 196616 | tf_op jit(solution)/shard_map/ppermute | solution.py:127
  156.9 1.6 %copy-start.6 = (f32[128,128]{1,0:T(8,128)}, f32[128,128]{1,0:T(8,128)S(1)}, u32[]{:S(2)}) copy-start(f32[128,128]{1,0:T(8,128)S(1)} %get-tuple-element.20) | copy-start | bytes 196612

commit v16 on v15

--- a/solution.py
+++ b/solution.py
@@ -209,14 +209,14 @@
         solved_two = solve_panel(adj_trail[:, last:], inverse_two, root_two)
         partial_two = jnp.dot(solved_two.T, trail[:, last:], preferred_element_type=jnp.float32)
         rows_two = butterfly_sum(partial_two, "row", n_row)
-        solved_late, rows_two = lax.optimization_barrier((solved_two, rows_two))
+        diag_one_late, rows_two = lax.optimization_barrier((diag_one, rows_two))
+        inverse_one = inverse_lower(diag_one_late)
         seed_two = jnp.tril(adj_diag_two - tree_broadcast(rows_two, "col", n_col, root_two))
         grad_diag_two = block_adjoint(diag_two, inverse_two, seed_two)
         mirror_two = own_rows(grad_diag_two + grad_diag_two.T)
         rest_two = jnp.dot(mirror_two, full_two.astype(jnp.float32), precision=exact_mode)
-        inverse_one = inverse_lower(diag_one)
         crossed = halving_scatter(
-            jnp.dot(solved_late.T, trail, preferred_element_type=jnp.float32), "row", n_row
+            jnp.dot(solved_two.T, trail, preferred_element_type=jnp.float32), "row", n_row
         )
         adj_two = adj_row_two - crossed - rest_two
         next_panel = adj_trail[:, last:] - jnp.dot(

time: 161 us -> 167 us (1.037)
  Pallas kernels: 37.5 us -> 40.4 us
  matrix products: 22.5 us -> 24.9 us
    ppermute x6, waiting for transfers between devices: 0.85 us -> 5.41 us  [doubling_gather(): other = lax.ppermute(value, axis, pairs)]
    ppermute x6, waiting for transfers between devices: 4.34 us -> 1.18 us  [halving_scatter(): blocks = keep + lax.ppermute(send, axis, pairs)]
    pallas_call x2, Pallas kernels: 37.5 us -> 40.4 us  [panel_broadcast(): pl.pallas_call(functools.partial(spread_kernel, root, size), out_shape=ja...]
  transfers between devices with their start and end apart: 36 -> 36, of which waited for: 11 -> 11; matrix products, arithmetic and copies ran while one was open for 30% -> 30% of each run, Pallas kernels for 24% -> 25%
where the time goes in v16:
time: 167 us; the launch traced here: 165 us
  starting transfers between devices  46.1 us (28%)
  Pallas kernels  40.4 us (24%)
  other arithmetic  26.7 us (16%)
  matrix products  24.9 us (15%)
  waiting for transfers between devices  23.7 us (14%)
    pallas_call x2, Pallas kernels, panel_broadcast(): pl.pallas_call(functools.partial(spread_kernel, root, size), out_shape=ja...  40.4 us
    another operation x4, other arithmetic, inverse_lower(): return lax.linalg.triangular_solve(block, ident, left_side=True, lower=True)  20.5 us
    ppermute x18, starting transfers between devices, tree_broadcast(): part = lax.ppermute(value, axis, pairs)  15.3 us
    ppermute x6, starting transfers between devices, halving_scatter(): blocks = keep + lax.ppermute(send, axis, pairs)  12.3 us
    ppermute x6, starting transfers between devices, butterfly_sum(): value = value + lax.ppermute(value, axis, pairs)  12.2 us
    ppermute x6, waiting for transfers between devices, butterfly_sum(): value = value + lax.ppermute(value, axis, pairs)  10.5 us
    ppermute x18, waiting for transfers between devices, tree_broadcast(): part = lax.ppermute(value, axis, pairs)  6.64 us
    ppermute x6, starting transfers between devices, doubling_gather(): other = lax.ppermute(value, axis, pairs)  6.35 us
  transfers between devices with their start and end apart: 36, of which 11 were waited for; matrix products, arithmetic and copies ran while one was open for 30% of the time, Pallas kernels for 25%

profile of v16, /device:TPU:1, one launch (start us, length us, event | category | flops | bytes accessed | tf_op | source)
XLA Modules:
  0.0 164.6 jit_solution(18402744458151909924)
XLA Ops:
  0.6 1.5 collective-permute-start.24
  2.2 0.8 select_bitcast_fusion.1
  3.1 9.8 %custom-call.4 = f32[1,128,128]{1,2,0:T(8,128)S(1)} custom-call(f32[1,128,128]{2,1,0:T(8,128)S(1)} %select_bitcast_fusion.1), custom_call_target="InvertDiagBlocksLowerTriangular" | custom-call | tf_op jit(solution)/shard_map/triangular_solve/custom-call.1 | solution.py:158
  13.2 3.0 %fusion.x_ref = bf16[2048,128]{1,0:T(8,128)(2,1)} fusion(f32[128,128]{1,0:T(8,128)S(1)} %fusion.21, f32[2048,1024]{1,0:T(8,128)} %param.17), kind=kOutput, calls=%fused_computation.6 | convolution fusion | flops 402915328 | bytes 1638400 | tf_op jit(solution)/shard_map/dot_general | solution.py:197
  16.2 18.3 %shard_map.137 = bf16[2048,128]{1,0:T(8,128)(2,1)} custom-call(bf16[2048,128]{1,0:T(8,128)(2,1)} %fusion.x_ref), custom_call_target="tpu_custom_call" | custom-call | tf_op jit(solution)/shard_map/pallas_call | solution.py:77
  34.5 1.5 fusion.17
  36.1 3.2 %collective-permute-start.3 = (f32[128,128]{1,0:T(8,128)S(1)}, f32[128,128]{1,0:T(8,128)S(1)}, u32[]{:S(2)}, u32[]{:S(2)}) collective-permute-start(f32[128,128]{1,0:T(8,128)S(1)} %fusion.17), channel_id=1, source_target_pairs={{0,16},{16,0},{32,48},{48,32},{64,80},{80,64},{96,112},{112,96},{1... | collective-permute-start | bytes 196616 | tf_op jit(solution)/shard_map/ppermute | solution.py:111
  39.3 3.1 %fusion.60 = f32[128,1024]{1,0:T(8,128)S(1)} fusion(bf16[2048,128]{1,0:T(8,128)(2,1)} %shard_map.137, bf16[2048,1024]{1,0:T(8,128)(2,1)} %param.12), kind=kOutput, calls=%fused_computation.107 | convolution fusion | flops 536870912 | bytes 5242880 | tf_op jit(solution)/shard_map/dot_general | solution.py:219
  42.5 2.8 %collective-permute-start = (f32[4,16,1024]{2,1,0:T(8,128)S(1)}, f32[4,16,1024]{2,1,0:T(8,128)S(1)}, u32[]{:S(2)}, u32[]{:S(2)}) collective-permute-start(f32[4,16,1024]{2,1,0:T(8,128)S(1)} %bitcast.62), channel_id=1, source_target_pairs={{0,64},{16,80},{32,96},{48,112},{64,0},{80,16},{96,32},{112,48},{1... | collective-permute-start | bytes 786440 | tf_op jit(solution)/shard_map/ppermute | solution.py:127
  45.3 0.6 select_subtract_fusion
  46.4 1.2 collective-permute-start.13
  48.1 5.4 %collective-permute-done.25 = bf16[32,1024]{1,0:T(8,128)(2,1)S(1)} collective-permute-done((bf16[32,1024]{1,0:T(8,128)(2,1)S(1)}, bf16[32,1024]{1,0:T(8,128)(2,1)S(1)}, u32[]{:S(2)}, u32[]{:S(2)}) %collective-permute-start.25) | collective-permute-done | bytes 65568 | tf_op jit(solution)/shard_map/ppermute | solution.py:137
  53.5 1.8 %collective-permute-start.26 = (bf16[64,1024]{1,0:T(8,128)(2,1)S(1)}, bf16[64,1024]{1,0:T(8,128)(2,1)S(1)}, u32[]{:S(2)}, u32[]{:S(2)}) collective-permute-start(bf16[64,1024]{1,0:T(8,128)(2,1)S(1)} %maximum_select_fusion.3), channel_id=1, source_target_pairs={{0,64},{16,80},{32,96},{48,112},{64,0},{80,16},{96,32},{112,48},{1... | collective-permute-start | bytes 393224 | tf_op jit(solution)/shard_map/ppermute | solution.py:137
  55.3 0.9 collective-permute-done.4
  56.3 1.8 %collective-permute-start.5 = (f32[128,128]{1,0:T(8,128)S(1)}, f32[128,128]{1,0:T(8,128)S(1)}, u32[]{:S(2)}, u32[]{:S(2)}) collective-permute-start(f32[128,128]{1,0:T(8,128)S(1)} %add.118), channel_id=1, source_target_pairs={{0,64},{16,80},{32,96},{48,112},{64,0},{80,16},{96,32},{112,48},{1... | collective-permute-start | bytes 196616 | tf_op jit(solution)/shard_map/ppermute | solution.py:111
  58.1 1.3 collective-permute-start.14
  59.4 1.9 %collective-permute-done.5 = f32[128,128]{1,0:T(8,128)S(1)} collective-permute-done((f32[128,128]{1,0:T(8,128)S(1)}, f32[128,128]{1,0:T(8,128)S(1)}, u32[]{:S(2)}, u32[]{:S(2)}) %collective-permute-start.5) | collective-permute-done | bytes 65568 | tf_op jit(solution)/shard_map/ppermute | solution.py:111
  61.4 1.3 collective-permute-start.8
  62.6 1.3 collective-permute-start.7
  63.9 9.8 %custom-call.5 = f32[1,128,128]{1,2,0:T(8,128)S(1)} custom-call(f32[1,128,128]{2,1,0:T(8,128)S(1)} %select_bitcast_fusion), custom_call_target="InvertDiagBlocksLowerTriangular" | custom-call | tf_op jit(solution)/shard_map/triangular_solve/custom-call.1 | solution.py:158
  74.0 0.7 collective-permute-start.6
  74.8 1.5 convolution_subtract_fusion.1
  76.4 0.9 add_select_fusion.1
  77.3 1.3 collective-permute-start.11
  78.6 0.7 collective-permute-start.10
  79.3 0.7 collective-permute-start.9
  80.0 1.2 collective-permute-start.1
  81.3 2.3 %collective-permute-done.11 = f32[128,128]{1,0:T(8,128)S(1)} collective-permute-done((f32[128,128]{1,0:T(8,128)S(1)}, f32[128,128]{1,0:T(8,128)S(1)}, u32[]{:S(2)}, u32[]{:S(2)}) %collective-permute-start.11) | collective-permute-done | bytes 65568 | tf_op jit(solution)/shard_map/ppermute | solution.py:99
  83.5 1.1 fusion.2
  85.0 3.9 %collective-permute-start.2 = (f32[1,16,1024]{2,1,0:T(8,128)S(1)}, f32[1,16,1024]{2,1,0:T(8,128)S(1)}, u32[]{:S(2)}, u32[]{:S(2)}) collective-permute-start(f32[1,16,1024]{2,1,0:T(8,128)S(1)} %slice_select_fusion.8), channel_id=1, source_target_pairs={{0,16},{16,0},{32,48},{48,32},{64,80},{80,64},{96,112},{112,96},{1... | collective-permute-start | bytes 196616 | tf_op jit(solution)/shard_map/ppermute | solution.py:127
  89.2 0.6 collective-permute-done.2
  89.8 1.1 fusion.25
  90.9 1.0 convolution_convert_fusion
  91.9 0.7 collective-permute-start.17
  92.6 0.7 collective-permute-start.16
  93.2 0.7 collective-permute-start.15
  93.9 0.8 slice.137.x_ref
  94.7 22.0 %shard_map.138 = bf16[2048,128]{1,0:T(8,128)(2,1)} custom-call(bf16[2048,128]{1,0:T(8,128)(2,1)} %slice.137.x_ref), custom_call_target="tpu_custom_call" | custom-call | tf_op jit(solution)/shard_map/pallas_call | solution.py:77
  116.8 3.1 %fusion.62 = f32[128,1024]{1,0:T(8,128)S(1)} fusion(bf16[2048,128]{1,0:T(8,128)(2,1)} %shard_map.138, bf16[2048,1024]{1,0:T(8,128)(2,1)} %param.12), kind=kOutput, calls=%fused_computation.109 | convolution fusion | flops 536870912 | bytes 5242880 | tf_op jit(solution)/shard_map/dot_general | solution.py:247
  120.0 1.3 collective-permute-start.20
  121.3 0.7 collective-permute-start.19
  122.0 0.7 collective-permute-start.18
  122.6 1.4 fusion.15
  124.0 1.5 collective-permute-done.20
  125.8 4.4 %collective-permute-start.21 = (f32[128,128]{1,0:T(8,128)S(1)}, f32[128,128]{1,0:T(8,128)S(1)}, u32[]{:S(2)}, u32[]{:S(2)}) collective-permute-start(f32[128,128]{1,0:T(8,128)S(1)} %convolution_add_fusion.1), channel_id=1, source_target_pairs={{0,16},{16,0},{32,48},{48,32},{64,80},{80,64},{96,112},{112,96},{1... | collective-permute-start | bytes 196616 | tf_op jit(solution)/shard_map/ppermute | solution.py:111
  131.0 0.9 collective-permute-start.22
  132.0 0.9 collective-permute-start.27
  132.9 1.3 collective-permute-done.22
  134.2 1.4 collective-permute-start.23
  135.7 0.6 pad_maximum_fusion.2
  136.3 5.9 %collective-permute-done.23 = f32[128,128]{1,0:T(8,128)S(1)} collective-permute-done((f32[128,128]{1,0:T(8,128)S(1)}, f32[128,128]{1,0:T(8,128)S(1)}, u32[]{:S(2)}, u32[]{:S(2)}) %collective-permute-start.23) | collective-permute-done | bytes 65568 | tf_op jit(solution)/shard_map/ppermute | solution.py:111
  142.2 0.7 collective-permute-start.32
  142.9 0.7 collective-permute-start.31
  143.6 0.9 collective-permute-start.30
  144.5 4.7 %convolution_subtract_fusion = bf16[2048,1024]{1,0:T(8,128)(2,1)S(1)} fusion(f32[2048,1024]{1,0:T(8,128)} %param.17, bf16[2048,128]{1,0:T(8,128)(2,1)S(1)} %copy-done.1, bf16[2048,128]{1,0:T(8,128)(2,1)S(1)} %copy-done, bf16[128,1024]{1,0:T(8,128)(2,1)S(1)} %maximum_select_fusion.1, bf16[128,1024]{1,0:T(8,128)(2,1)S(1)} %maximum_select_fusion), kind=kOutput, calls=%fused_computation.1 | convolution fusion | flops 1081081856 | bytes 14155776 | tf_op jit(solution)/shard_map/dot_general | solution.py:240
  149.8 2.6 %pad_maximum_fusion = bf16[2048,1024]{1,0:T(8,128)(2,1)} fusion(bf16[2048,128]{1,0:T(8,128)(2,1)S(1)} %fusion.7, bf16[2048,896]{1,0:T(8,128)(2,1)S(1)} %slice.197), kind=kLoop, calls=%fused_computation.2 | loop fusion | flops 8388608 | bytes 8388608 | tf_op jit(solution)/shard_map/concatenate | solution.py:257
  152.5 1.3 collective-permute-start.35
  153.8 0.7 collective-permute-start.34
  154.5 0.7 collective-permute-start.33
  155.2 0.7 collective-permute-start.28
  155.9 2.8 %collective-permute-done.35 = f32[128,128]{1,0:T(8,128)S(1)} collective-permute-done((f32[128,128]{1,0:T(8,128)S(1)}, f32[128,128]{1,0:T(8,128)S(1)}, u32[]{:S(2)}, u32[]{:S(2)}) %collective-permute-start.35) | collective-permute-done | bytes 65568 | tf_op jit(solution)/shard_map/ppermute | solution.py:99
  159.4 2.7 %collective-permute-start.29 = (f32[1,16,1024]{2,1,0:T(8,128)S(1)}, f32[1,16,1024]{2,1,0:T(8,128)S(1)}, u32[]{:S(2)}, u32[]{:S(2)}) collective-permute-start(f32[1,16,1024]{2,1,0:T(8,128)S(1)} %slice_select_fusion.7), channel_id=1, source_target_pairs={{0,16},{16,0},{32,48},{48,32},{64,80},{80,64},{96,112},{112,96},{1... | collective-permute-start | bytes 196616 | tf_op jit(solution)/shard_map/ppermute | solution.py:127
  163.0 0.9 fusion.23
  164.0 0.6 pad_maximum_fusion.1
  (96 shorter events, 5.9 us)
Async XLA Ops:
  0.6 45.3 %collective-permute-start.24 = (bf16[16,1024]{1,0:T(8,128)(2,1)}, bf16[16,1024]{1,0:T(8,128)(2,1)S(1)}, u32[]{:S(2)}, u32[]{:S(2)}) collective-permute-start(bf16[16,1024]{1,0:T(8,128)(2,1)} %param.13), channel_id=1, source_target_pairs={{0,16},{16,0},{32,48},{48,32},{64,80},{80,64},{96,112},{112,96},{1... | collective-permute-start | bytes 98312 | tf_op jit(solution)/shard_map/ppermute | solution.py:137
  2.1 44.3 %collective-permute-start.12 = (bf16[16,1024]{1,0:T(8,128)(2,1)}, bf16[16,1024]{1,0:T(8,128)(2,1)S(1)}, u32[]{:S(2)}, u32[]{:S(2)}) collective-permute-start(bf16[16,1024]{1,0:T(8,128)(2,1)} %param.14), channel_id=1, source_target_pairs={{0,16},{16,0},{32,48},{48,32},{64,80},{80,64},{96,112},{112,96},{1... | collective-permute-start | bytes 98312 | tf_op jit(solution)/shard_map/ppermute | solution.py:137
  16.2 29.8 %copy-start.9 = (bf16[16,1024]{1,0:T(8,128)(2,1)S(1)}, bf16[16,1024]{1,0:T(8,128)(2,1)}, u32[]{:S(2)}) copy-start(bf16[16,1024]{1,0:T(8,128)(2,1)} %param.13) | copy-start | bytes 98308
  16.2 30.2 %copy-start.4 = (bf16[16,1024]{1,0:T(8,128)(2,1)S(1)}, bf16[16,1024]{1,0:T(8,128)(2,1)}, u32[]{:S(2)}) copy-start(bf16[16,1024]{1,0:T(8,128)(2,1)} %param.14) | copy-start | bytes 98308
  36.1 27.8 %copy-start.3 = (f32[128,128]{1,0:T(8,128)S(1)}, f32[128,128]{1,0:T(8,128)}, u32[]{:S(2)}) copy-start(f32[128,128]{1,0:T(8,128)} %param.15) | copy-start | bytes 196612
  36.1 11.6 %collective-permute-start.3 = (f32[128,128]{1,0:T(8,128)S(1)}, f32[128,128]{1,0:T(8,128)S(1)}, u32[]{:S(2)}, u32[]{:S(2)}) collective-permute-start(f32[128,128]{1,0:T(8,128)S(1)} %fusion.17), channel_id=1, source_target_pairs={{0,16},{16,0},{32,48},{48,32},{64,80},{80,64},{96,112},{112,96},{1... | collective-permute-start | bytes 196616 | tf_op jit(solution)/shard_map/ppermute | solution.py:111
  39.3 35.5 %copy-start = (bf16[2048,128]{1,0:T(8,128)(2,1)S(1)}, bf16[2048,128]{1,0:T(8,128)(2,1)}, u32[]{:S(2)}) copy-start(bf16[2048,128]{1,0:T(8,128)(2,1)} %shard_map.137) | copy-start | bytes 1572868
  42.4 41.1 %copy-start.2 = (f32[128,128]{1,0:T(8,128)S(1)}, f32[128,128]{1,0:T(8,128)}, u32[]{:S(2)}) copy-start(f32[128,128]{1,0:T(8,128)} %param.16) | copy-start | bytes 196612
  42.5 37.4 %collective-permute-start = (f32[4,16,1024]{2,1,0:T(8,128)S(1)}, f32[4,16,1024]{2,1,0:T(8,128)S(1)}, u32[]{:S(2)}, u32[]{:S(2)}) collective-permute-start(f32[4,16,1024]{2,1,0:T(8,128)S(1)} %bitcast.62), channel_id=1, source_target_pairs={{0,64},{16,80},{32,96},{48,112},{64,0},{80,16},{96,32},{112,48},{1... | collective-permute-start | bytes 786440 | tf_op jit(solution)/shard_map/ppermute | solution.py:127
  46.0 7.5 %collective-permute-start.25 = (bf16[32,1024]{1,0:T(8,128)(2,1)S(1)}, bf16[32,1024]{1,0:T(8,128)(2,1)S(1)}, u32[]{:S(2)}, u32[]{:S(2)}) collective-permute-start(bf16[32,1024]{1,0:T(8,128)(2,1)S(1)} %maximum_select_fusion.5), channel_id=1, source_target_pairs={{0,32},{16,48},{32,0},{48,16},{64,96},{80,112},{96,64},{112,80},{1... | collective-permute-start | bytes 196616 | tf_op jit(solution)/shard_map/ppermute | solution.py:137
  46.4 11.7 %collective-permute-start.13 = (bf16[32,1024]{1,0:T(8,128)(2,1)S(1)}, bf16[32,1024]{1,0:T(8,128)(2,1)S(1)}, u32[]{:S(2)}, u32[]{:S(2)}) collective-permute-start(bf16[32,1024]{1,0:T(8,128)(2,1)S(1)} %maximum_select_fusion.4), channel_id=1, source_target_pairs={{0,32},{16,48},{32,0},{48,16},{64,96},{80,112},{96,64},{112,80},{1... | collective-permute-start | bytes 196616 | tf_op jit(solution)/shard_map/ppermute | solution.py:137
  47.7 8.6 %collective-permute-start.4 = (f32[128,128]{1,0:T(8,128)S(1)}, f32[128,128]{1,0:T(8,128)S(1)}, u32[]{:S(2)}, u32[]{:S(2)}) collective-permute-start(f32[128,128]{1,0:T(8,128)S(1)} %add.117), channel_id=1, source_target_pairs={{0,32},{16,48},{32,0},{48,16},{64,96},{80,112},{96,64},{112,80},{1... | collective-permute-start | bytes 196616 | tf_op jit(solution)/shard_map/ppermute | solution.py:111
  53.5 22.8 %collective-permute-start.26 = (bf16[64,1024]{1,0:T(8,128)(2,1)S(1)}, bf16[64,1024]{1,0:T(8,128)(2,1)S(1)}, u32[]{:S(2)}, u32[]{:S(2)}) collective-permute-start(bf16[64,1024]{1,0:T(8,128)(2,1)S(1)} %maximum_select_fusion.3), channel_id=1, source_target_pairs={{0,64},{16,80},{32,96},{48,112},{64,0},{80,16},{96,32},{112,48},{1... | collective-permute-start | bytes 393224 | tf_op jit(solution)/shard_map/ppermute | solution.py:137
  56.3 5.1 %collective-permute-start.5 = (f32[128,128]{1,0:T(8,128)S(1)}, f32[128,128]{1,0:T(8,128)S(1)}, u32[]{:S(2)}, u32[]{:S(2)}) collective-permute-start(f32[128,128]{1,0:T(8,128)S(1)} %add.118), channel_id=1, source_target_pairs={{0,64},{16,80},{32,96},{48,112},{64,0},{80,16},{96,32},{112,48},{1... | collective-permute-start | bytes 196616 | tf_op jit(solution)/shard_map/ppermute | solution.py:111
  58.1 15.9 %collective-permute-start.14 = (bf16[64,1024]{1,0:T(8,128)(2,1)S(1)}, bf16[64,1024]{1,0:T(8,128)(2,1)S(1)}, u32[]{:S(2)}, u32[]{:S(2)}) collective-permute-start(bf16[64,1024]{1,0:T(8,128)(2,1)S(1)} %maximum_select_fusion.2), channel_id=1, source_target_pairs={{0,64},{16,80},{32,96},{48,112},{64,0},{80,16},{96,32},{112,48},{1... | collective-permute-start | bytes 393224 | tf_op jit(solution)/shard_map/ppermute | solution.py:137
  61.4 15.0 %collective-permute-start.8 = (f32[128,128]{1,0:T(8,128)S(1)}, f32[128,128]{1,0:T(8,128)}, u32[]{:S(2)}, u32[]{:S(2)}) collective-permute-start(f32[128,128]{1,0:T(8,128)S(1)} %add.119), channel_id=1, source_target_pairs={{15,12},{31,28},{47,44},{63,60},{79,76},{95,92},{111,108},{127,124}} | collective-permute-start | bytes 196616 | tf_op jit(solution)/shard_map/ppermute | solution.py:99
  62.6 13.7 %collective-permute-start.7 = (f32[128,128]{1,0:T(8,128)S(1)}, f32[128,128]{1,0:T(8,128)}, u32[]{:S(2)}, u32[]{:S(2)}) collective-permute-start(f32[128,128]{1,0:T(8,128)S(1)} %add.119), channel_id=1, source_target_pairs={{15,13},{31,29},{47,45},{63,61},{79,77},{95,93},{111,109},{127,125}} | collective-permute-start | bytes 196616 | tf_op jit(solution)/shard_map/ppermute | solution.py:99
  74.0 2.4 %collective-permute-start.6 = (f32[128,128]{1,0:T(8,128)S(1)}, f32[128,128]{1,0:T(8,128)S(1)}, u32[]{:S(2)}, u32[]{:S(2)}) collective-permute-start(f32[128,128]{1,0:T(8,128)S(1)} %add.119), channel_id=1, source_target_pairs={{15,14},{31,30},{47,46},{63,62},{79,78},{95,94},{111,110},{127,126}} | collective-permute-start | bytes 196616 | tf_op jit(solution)/shard_map/ppermute | solution.py:99
  77.3 6.2 %collective-permute-start.11 = (f32[128,128]{1,0:T(8,128)S(1)}, f32[128,128]{1,0:T(8,128)S(1)}, u32[]{:S(2)}, u32[]{:S(2)}) collective-permute-start(f32[128,128]{1,0:T(8,128)S(1)} %add_select_fusion.1), channel_id=1, source_target_pairs={{15,3},{14,2},{13,1},{12,0},{31,19},{30,18},{29,17},{28,16},{47,35... | collective-permute-start | bytes 196616 | tf_op jit(solution)/shard_map/ppermute | solution.py:99
  78.6 4.9 %collective-permute-start.10 = (f32[128,128]{1,0:T(8,128)S(1)}, f32[128,128]{1,0:T(8,128)S(1)}, u32[]{:S(2)}, u32[]{:S(2)}) collective-permute-start(f32[128,128]{1,0:T(8,128)S(1)} %add_select_fusion.1), channel_id=1, source_target_pairs={{15,7},{14,6},{13,5},{12,4},{31,23},{30,22},{29,21},{28,20},{47,39... | collective-permute-start | bytes 196616 | tf_op jit(solution)/shard_map/ppermute | solution.py:99
  79.3 4.3 %collective-permute-start.9 = (f32[128,128]{1,0:T(8,128)S(1)}, f32[128,128]{1,0:T(8,128)S(1)}, u32[]{:S(2)}, u32[]{:S(2)}) collective-permute-start(f32[128,128]{1,0:T(8,128)S(1)} %add_select_fusion.1), channel_id=1, source_target_pairs={{15,11},{14,10},{13,9},{12,8},{31,27},{30,26},{29,25},{28,24},{47,... | collective-permute-start | bytes 196616 | tf_op jit(solution)/shard_map/ppermute | solution.py:99
  80.0 4.9 %collective-permute-start.1 = (f32[2,16,1024]{2,1,0:T(8,128)S(1)}, f32[2,16,1024]{2,1,0:T(8,128)S(1)}, u32[]{:S(2)}, u32[]{:S(2)}) collective-permute-start(f32[2,16,1024]{2,1,0:T(8,128)S(1)} %slice_select_fusion.6), channel_id=1, source_target_pairs={{0,32},{16,48},{32,0},{48,16},{64,96},{80,112},{96,64},{112,80},{1... | collective-permute-start | bytes 393224 | tf_op jit(solution)/shard_map/ppermute | solution.py:127
  85.0 4.8 %collective-permute-start.2 = (f32[1,16,1024]{2,1,0:T(8,128)S(1)}, f32[1,16,1024]{2,1,0:T(8,128)S(1)}, u32[]{:S(2)}, u32[]{:S(2)}) collective-permute-start(f32[1,16,1024]{2,1,0:T(8,128)S(1)} %slice_select_fusion.8), channel_id=1, source_target_pairs={{0,16},{16,0},{32,48},{48,32},{64,80},{80,64},{96,112},{112,96},{1... | collective-permute-start | bytes 196616 | tf_op jit(solution)/shard_map/ppermute | solution.py:127
  89.1 30.8 %copy-start.5 = (f32[128,128]{1,0:T(8,128)}, f32[128,128]{1,0:T(8,128)S(1)}, u32[]{:S(2)}) copy-start(f32[128,128]{1,0:T(8,128)S(1)} %get-tuple-element.18) | copy-start | bytes 196612
  91.9 28.0 %collective-permute-start.17 = (bf16[16,128]{1,0:T(8,128)(2,1)S(1)}, bf16[16,128]{1,0:T(8,128)(2,1)S(1)}, u32[]{:S(2)}, u32[]{:S(2)}) collective-permute-start(bf16[16,128]{1,0:T(8,128)(2,1)S(1)} %slice.138), channel_id=1, source_target_pairs={{14,13},{30,29},{46,45},{62,61},{78,77},{94,93},{110,109},{126,125}} | collective-permute-start | bytes 12296 | tf_op jit(solution)/shard_map/ppermute | solution.py:99
  92.6 27.4 %collective-permute-start.16 = (bf16[16,128]{1,0:T(8,128)(2,1)S(1)}, bf16[16,128]{1,0:T(8,128)(2,1)S(1)}, u32[]{:S(2)}, u32[]{:S(2)}) collective-permute-start(bf16[16,128]{1,0:T(8,128)(2,1)S(1)} %slice.138), channel_id=1, source_target_pairs={{14,12},{30,28},{46,44},{62,60},{78,76},{94,92},{110,108},{126,124}} | collective-permute-start | bytes 12296 | tf_op jit(solution)/shard_map/ppermute | solution.py:99
  93.2 26.7 %collective-permute-start.15 = (bf16[16,128]{1,0:T(8,128)(2,1)S(1)}, bf16[16,128]{1,0:T(8,128)(2,1)S(1)}, u32[]{:S(2)}, u32[]{:S(2)}) collective-permute-start(bf16[16,128]{1,0:T(8,128)(2,1)S(1)} %slice.138), channel_id=1, source_target_pairs={{14,15},{30,31},{46,47},{62,63},{78,79},{94,95},{110,111},{126,127}} | collective-permute-start | bytes 12296 | tf_op jit(solution)/shard_map/ppermute | solution.py:99
  116.8 5.9 %copy-start.1 = (bf16[2048,128]{1,0:T(8,128)(2,1)S(1)}, bf16[2048,128]{1,0:T(8,128)(2,1)}, u32[]{:S(2)}) copy-start(bf16[2048,128]{1,0:T(8,128)(2,1)} %shard_map.138) | copy-start | bytes 1572868
  120.0 5.6 %collective-permute-start.20 = (bf16[16,128]{1,0:T(8,128)(2,1)S(1)}, bf16[16,128]{1,0:T(8,128)(2,1)S(1)}, u32[]{:S(2)}, u32[]{:S(2)}) collective-permute-start(bf16[16,128]{1,0:T(8,128)(2,1)S(1)} %add_select_fusion.3), channel_id=1, source_target_pairs={{14,2},{15,3},{12,0},{13,1},{30,18},{31,19},{28,16},{29,17},{46,34... | collective-permute-start | bytes 12296 | tf_op jit(solution)/shard_map/ppermute | solution.py:99
  121.3 4.3 %collective-permute-start.19 = (bf16[16,128]{1,0:T(8,128)(2,1)S(1)}, bf16[16,128]{1,0:T(8,128)(2,1)S(1)}, u32[]{:S(2)}, u32[]{:S(2)}) collective-permute-start(bf16[16,128]{1,0:T(8,128)(2,1)S(1)} %add_select_fusion.3), channel_id=1, source_target_pairs={{14,6},{15,7},{12,4},{13,5},{30,22},{31,23},{28,20},{29,21},{46,38... | collective-permute-start | bytes 12296 | tf_op jit(solution)/shard_map/ppermute | solution.py:99
  122.0 3.6 %collective-permute-start.18 = (bf16[16,128]{1,0:T(8,128)(2,1)S(1)}, bf16[16,128]{1,0:T(8,128)(2,1)S(1)}, u32[]{:S(2)}, u32[]{:S(2)}) collective-permute-start(bf16[16,128]{1,0:T(8,128)(2,1)S(1)} %add_select_fusion.3), channel_id=1, source_target_pairs={{14,10},{15,11},{12,8},{13,9},{30,26},{31,27},{28,24},{29,25},{46,... | collective-permute-start | bytes 12296 | tf_op jit(solution)/shard_map/ppermute | solution.py:99
  125.8 5.3 %collective-permute-start.21 = (f32[128,128]{1,0:T(8,128)S(1)}, f32[128,128]{1,0:T(8,128)S(1)}, u32[]{:S(2)}, u32[]{:S(2)}) collective-permute-start(f32[128,128]{1,0:T(8,128)S(1)} %convolution_add_fusion.1), channel_id=1, source_target_pairs={{0,16},{16,0},{32,48},{48,32},{64,80},{80,64},{96,112},{112,96},{1... | collective-permute-start | bytes 196616 | tf_op jit(solution)/shard_map/ppermute | solution.py:111
  131.0 3.2 %collective-permute-start.22 = (f32[128,128]{1,0:T(8,128)S(1)}, f32[128,128]{1,0:T(8,128)S(1)}, u32[]{:S(2)}, u32[]{:S(2)}) collective-permute-start(f32[128,128]{1,0:T(8,128)S(1)} %add.131), channel_id=1, source_target_pairs={{0,32},{16,48},{32,0},{48,16},{64,96},{80,112},{96,64},{112,80},{1... | collective-permute-start | bytes 196616 | tf_op jit(solution)/shard_map/ppermute | solution.py:111
  132.0 23.2 %collective-permute-start.27 = (f32[4,16,1024]{2,1,0:T(8,128)S(1)}, f32[4,16,1024]{2,1,0:T(8,128)S(1)}, u32[]{:S(2)}, u32[]{:S(2)}) collective-permute-start(f32[4,16,1024]{2,1,0:T(8,128)S(1)} %bitcast.63), channel_id=1, source_target_pairs={{0,64},{16,80},{32,96},{48,112},{64,0},{80,16},{96,32},{112,48},{1... | collective-permute-start | bytes 786440 | tf_op jit(solution)/shard_map/ppermute | solution.py:127
  134.2 8.0 %collective-permute-start.23 = (f32[128,128]{1,0:T(8,128)S(1)}, f32[128,128]{1,0:T(8,128)S(1)}, u32[]{:S(2)}, u32[]{:S(2)}) collective-permute-start(f32[128,128]{1,0:T(8,128)S(1)} %add.132), channel_id=1, source_target_pairs={{0,64},{16,80},{32,96},{48,112},{64,0},{80,16},{96,32},{112,48},{1... | collective-permute-start | bytes 196616 | tf_op jit(solution)/shard_map/ppermute | solution.py:111
  142.2 10.3 %collective-permute-start.32 = (f32[128,128]{1,0:T(8,128)S(1)}, f32[128,128]{1,0:T(8,128)S(1)}, u32[]{:S(2)}, u32[]{:S(2)}) collective-permute-start(f32[128,128]{1,0:T(8,128)S(1)} %add.133), channel_id=1, source_target_pairs={{14,13},{30,29},{46,45},{62,61},{78,77},{94,93},{110,109},{126,125}} | collective-permute-start | bytes 196616 | tf_op jit(solution)/shard_map/ppermute | solution.py:99
  142.9 9.6 %collective-permute-start.31 = (f32[128,128]{1,0:T(8,128)S(1)}, f32[128,128]{1,0:T(8,128)S(1)}, u32[]{:S(2)}, u32[]{:S(2)}) collective-permute-start(f32[128,128]{1,0:T(8,128)S(1)} %add.133), channel_id=1, source_target_pairs={{14,12},{30,28},{46,44},{62,60},{78,76},{94,92},{110,108},{126,124}} | collective-permute-start | bytes 196616 | tf_op jit(solution)/shard_map/ppermute | solution.py:99
  143.6 8.9 %collective-permute-start.30 = (f32[128,128]{1,0:T(8,128)S(1)}, f32[128,128]{1,0:T(8,128)S(1)}, u32[]{:S(2)}, u32[]{:S(2)}) collective-permute-start(f32[128,128]{1,0:T(8,128)S(1)} %add.133), channel_id=1, source_target_pairs={{14,15},{30,31},{46,47},{62,63},{78,79},{94,95},{110,111},{126,127}} | collective-permute-start | bytes 196616 | tf_op jit(solution)/shard_map/ppermute | solution.py:99
  149.8 8.9 %copy-start.8 = (f32[128,128]{1,0:T(8,128)S(1)}, f32[128,128]{1,0:T(8,128)}, u32[]{:S(2)}) copy-start(f32[128,128]{1,0:T(8,128)} %param.20) | copy-start | bytes 196612
  149.8 13.2 %copy-start.7 = (f32[16,1024]{1,0:T(8,128)S(1)}, f32[16,1024]{1,0:T(8,128)}, u32[]{:S(2)}) copy-start(f32[16,1024]{1,0:T(8,128)} %param.18) | copy-start | bytes 196612
  152.5 6.2 %collective-permute-start.35 = (f32[128,128]{1,0:T(8,128)S(1)}, f32[128,128]{1,0:T(8,128)S(1)}, u32[]{:S(2)}, u32[]{:S(2)}) collective-permute-start(f32[128,128]{1,0:T(8,128)S(1)} %add_select_fusion), channel_id=1, source_target_pairs={{14,2},{15,3},{12,0},{13,1},{30,18},{31,19},{28,16},{29,17},{46,34... | collective-permute-start | bytes 196616 | tf_op jit(solution)/shard_map/ppermute | solution.py:99
  153.8 4.9 %collective-permute-start.34 = (f32[128,128]{1,0:T(8,128)S(1)}, f32[128,128]{1,0:T(8,128)S(1)}, u32[]{:S(2)}, u32[]{:S(2)}) collective-permute-start(f32[128,128]{1,0:T(8,128)S(1)} %add_select_fusion), channel_id=1, source_target_pairs={{14,6},{15,7},{12,4},{13,5},{30,22},{31,23},{28,20},{29,21},{46,38... | collective-permute-start | bytes 196616 | tf_op jit(solution)/shard_map/ppermute | solution.py:99
  154.5 4.3 %collective-permute-start.33 = (f32[128,128]{1,0:T(8,128)S(1)}, f32[128,128]{1,0:T(8,128)S(1)}, u32[]{:S(2)}, u32[]{:S(2)}) collective-permute-start(f32[128,128]{1,0:T(8,128)S(1)} %add_select_fusion), channel_id=1, source_target_pairs={{14,10},{15,11},{12,8},{13,9},{30,26},{31,27},{28,24},{29,25},{46,... | collective-permute-start | bytes 196616 | tf_op jit(solution)/shard_map/ppermute | solution.py:99
  155.2 4.1 %collective-permute-start.28 = (f32[2,16,1024]{2,1,0:T(8,128)S(1)}, f32[2,16,1024]{2,1,0:T(8,128)S(1)}, u32[]{:S(2)}, u32[]{:S(2)}) collective-permute-start(f32[2,16,1024]{2,1,0:T(8,128)S(1)} %slice_select_fusion.5), channel_id=1, source_target_pairs={{0,32},{16,48},{32,0},{48,16},{64,96},{80,112},{96,64},{112,80},{1... | collective-permute-start | bytes 393224 | tf_op jit(solution)/shard_map/ppermute | solution.py:127
  159.4 3.6 %collective-permute-start.29 = (f32[1,16,1024]{2,1,0:T(8,128)S(1)}, f32[1,16,1024]{2,1,0:T(8,128)S(1)}, u32[]{:S(2)}, u32[]{:S(2)}) collective-permute-start(f32[1,16,1024]{2,1,0:T(8,128)S(1)} %slice_select_fusion.7), channel_id=1, source_target_pairs={{0,16},{16,0},{32,48},{48,32},{64,80},{80,64},{96,112},{112,96},{1... | collective-permute-start | bytes 196616 | tf_op jit(solution)/shard_map/ppermute | solution.py:127
  162.3 2.3 %copy-start.6 = (f32[128,128]{1,0:T(8,128)}, f32[128,128]{1,0:T(8,128)S(1)}, u32[]{:S(2)}) copy-start(f32[128,128]{1,0:T(8,128)S(1)} %get-tuple-element.20) | copy-start | bytes 196612

commit v17 on v12

--- a/solution.py
+++ b/solution.py
@@ -124,7 +124,7 @@
         keep = jnp.where(high, halves[1], halves[0])
         send = jnp.where(high, halves[0], halves[1])
         pairs = [(i, i ^ step) for i in range(size)]
-        blocks = keep + lax.ppermute(send, axis, pairs)
+        blocks = keep + lax.ppermute(send.astype(jnp.bfloat16), axis, pairs).astype(jnp.float32)
         step //= 2
     return blocks.reshape(band, value.shape[1])
 

time: 159 us -> 152 us (0.956)
  waiting for transfers between devices: 22.7 us -> 18.7 us
  Pallas kernels: 38.9 us -> 37.2 us
    ppermute x6, starting transfers between devices: 9.16 us -> 13.1 us  [butterfly_sum(): value = value + lax.ppermute(value, axis, pairs)]
    ppermute x6, starting transfers between devices: 13.1 us -> 9.69 us  [halving_scatter(): lax.ppermute(send.astype(jnp.bfloat16), axis, pairs).astype(jnp.float32)]
    ppermute x6, waiting for transfers between devices: 12.7 us -> 9.57 us  [butterfly_sum(): value = value + lax.ppermute(value, axis, pairs)]
    pallas_call x2, Pallas kernels: 38.9 us -> 37.2 us  [panel_broadcast(): pl.pallas_call(functools.partial(spread_kernel, root, size), out_shape=ja...]
  transfers between devices with their start and end apart: 36 -> 36, of which waited for: 11 -> 10; matrix products, arithmetic and copies ran while one was open for 30% -> 31% of each run, Pallas kernels for 25% -> 25%
where the time goes in v17:
time: 152 us; the launch traced here: 150 us
  starting transfers between devices  43.7 us (29%)
  Pallas kernels  37.2 us (24%)
  other arithmetic  25.2 us (17%)
  matrix products  22.6 us (15%)
  waiting for transfers between devices  18.7 us (12%)
  local copies, waits for them, and re-layouts  1.53 us (1%)
  between operations  1.52 us (1%)
    pallas_call x2, Pallas kernels, panel_broadcast(): pl.pallas_call(functools.partial(spread_kernel, root, size), out_shape=ja...  37.2 us
    another operation x4, other arithmetic, inverse_lower(): return lax.linalg.triangular_solve(block, ident, left_side=True, lower=True)  20.5 us
    ppermute x18, starting transfers between devices, tree_broadcast(): part = lax.ppermute(value, axis, pairs)  14 us
    ppermute x6, starting transfers between devices, butterfly_sum(): value = value + lax.ppermute(value, axis, pairs)  13.1 us
    ppermute x6, starting transfers between devices, halving_scatter(): lax.ppermute(send.astype(jnp.bfloat16), axis, pairs).astype(jnp.float32)  9.69 us
    ppermute x6, waiting for transfers between devices, butterfly_sum(): value = value + lax.ppermute(value, axis, pairs)  9.57 us
    ppermute x6, starting transfers between devices, doubling_gather(): other = lax.ppermute(value, axis, pairs)  6.99 us
    ppermute x18, waiting for transfers between devices, tree_broadcast(): part = lax.ppermute(value, axis, pairs)  6.57 us
  transfers between devices with their start and end apart: 36, of which 10 were waited for; matrix products, arithmetic and copies ran while one was open for 31% of the time, Pallas kernels for 25%

profile of v17, /device:TPU:1, one launch (start us, length us, event | category | flops | bytes accessed | tf_op | source)
XLA Modules:
  0.0 150.4 jit_solution(6600922526953763894)
XLA Ops:
  0.6 1.5 collective-permute-start.24
  2.2 0.8 select_bitcast_fusion.1
  3.1 9.8 %custom-call.4 = f32[1,128,128]{1,2,0:T(8,128)S(1)} custom-call(f32[1,128,128]{2,1,0:T(8,128)S(1)} %select_bitcast_fusion.1), custom_call_target="InvertDiagBlocksLowerTriangular" | custom-call | tf_op jit(solution)/shard_map/triangular_solve/custom-call.1 | solution.py:158
  12.9 0.3 fusion.21
  13.2 3.0 %fusion.x_ref = bf16[2048,128]{1,0:T(8,128)(2,1)} fusion(f32[128,128]{1,0:T(8,128)S(1)} %fusion.21, f32[2048,1024]{1,0:T(8,128)} %param.17), kind=kOutput, calls=%fused_computation.6 | convolution fusion | flops 402915328 | bytes 1638400 | tf_op jit(solution)/shard_map/dot_general | solution.py:197
  16.2 18.4 %shard_map.137 = bf16[2048,128]{1,0:T(8,128)(2,1)} custom-call(bf16[2048,128]{1,0:T(8,128)(2,1)} %fusion.x_ref), custom_call_target="tpu_custom_call" | custom-call | tf_op jit(solution)/shard_map/pallas_call | solution.py:77
  34.6 1.5 %fusion.17 = f32[128,128]{1,0:T(8,128)S(1)} fusion(bf16[2048,128]{1,0:T(8,128)(2,1)} %shard_map.137, bf16[2048,1024]{1,0:T(8,128)(2,1)} %param.12), kind=kOutput, calls=%fused_computation.29 | convolution fusion | flops 67108864 | bytes 1114112 | tf_op jit(solution)/shard_map/dot_general | solution.py:210
  36.1 3.2 %collective-permute-start.3 = (f32[128,128]{1,0:T(8,128)S(1)}, f32[128,128]{1,0:T(8,128)S(1)}, u32[]{:S(2)}, u32[]{:S(2)}) collective-permute-start(f32[128,128]{1,0:T(8,128)S(1)} %fusion.17), channel_id=1, source_target_pairs={{0,16},{16,0},{32,48},{48,32},{64,80},{80,64},{96,112},{112,96},{1... | collective-permute-start | bytes 196616 | tf_op jit(solution)/shard_map/ppermute | solution.py:111
  39.3 3.1 %fusion.60 = f32[128,1024]{1,0:T(8,128)S(1)} fusion(bf16[2048,128]{1,0:T(8,128)(2,1)} %shard_map.137, bf16[2048,1024]{1,0:T(8,128)(2,1)} %param.12), kind=kOutput, calls=%fused_computation.109 | convolution fusion | flops 536870912 | bytes 5242880 | tf_op jit(solution)/shard_map/dot_general | solution.py:217
  42.6 2.8 %collective-permute-start = (bf16[4,16,1024]{2,1,0:T(8,128)(2,1)S(1)}, bf16[4,16,1024]{2,1,0:T(8,128)(2,1)S(1)}, u32[]{:S(2)}, u32[]{:S(2)}) collective-permute-start(bf16[4,16,1024]{2,1,0:T(8,128)(2,1)S(1)} %bitcast.62), channel_id=1, source_target_pairs={{0,64},{16,80},{32,96},{48,112},{64,0},{80,16},{96,32},{112,48},{1... | collective-permute-start | bytes 393224 | tf_op jit(solution)/shard_map/ppermute | solution.py:127
  45.4 9.8 %custom-call.5 = f32[1,128,128]{1,2,0:T(8,128)S(1)} custom-call(f32[1,128,128]{2,1,0:T(8,128)S(1)} %select_bitcast_fusion), custom_call_target="InvertDiagBlocksLowerTriangular" | custom-call | tf_op jit(solution)/shard_map/triangular_solve/custom-call.1 | solution.py:158
  55.7 0.4 collective-permute-start.25
  56.1 1.2 collective-permute-start.13
  57.4 0.4 collective-permute-start.4
  57.7 1.1 collective-permute-done.25
  58.9 1.2 collective-permute-start.26
  60.1 1.8 %collective-permute-done.4 = f32[128,128]{1,0:T(8,128)S(1)} collective-permute-done((f32[128,128]{1,0:T(8,128)S(1)}, f32[128,128]{1,0:T(8,128)S(1)}, u32[]{:S(2)}, u32[]{:S(2)}) %collective-permute-start.4) | collective-permute-done | bytes 65568 | tf_op jit(solution)/shard_map/ppermute | solution.py:111
  62.0 0.5 collective-permute-start.5
  62.5 1.3 collective-permute-start.1
  63.8 2.6 %collective-permute-start.14 = (bf16[64,1024]{1,0:T(8,128)(2,1)S(1)}, bf16[64,1024]{1,0:T(8,128)(2,1)S(1)}, u32[]{:S(2)}, u32[]{:S(2)}) collective-permute-start(bf16[64,1024]{1,0:T(8,128)(2,1)S(1)} %maximum_select_fusion.2), channel_id=1, source_target_pairs={{0,64},{16,80},{32,96},{48,112},{64,0},{80,16},{96,32},{112,48},{1... | collective-permute-start | bytes 393224 | tf_op jit(solution)/shard_map/ppermute | solution.py:137
  66.4 1.2 collective-permute-done.5
  67.6 0.7 collective-permute-start.8
  68.3 0.7 collective-permute-start.7
  68.9 0.7 collective-permute-start.6
  69.7 1.4 collective-permute-done.14
  71.1 2.1 %collective-permute-start.2 = (bf16[1,16,1024]{2,1,0:T(8,128)(2,1)S(1)}, bf16[1,16,1024]{2,1,0:T(8,128)(2,1)S(1)}, u32[]{:S(2)}, u32[]{:S(2)}) collective-permute-start(bf16[1,16,1024]{2,1,0:T(8,128)(2,1)S(1)} %select_convert_fusion.5), channel_id=1, source_target_pairs={{0,16},{16,0},{32,48},{48,32},{64,80},{80,64},{96,112},{112,96},{1... | collective-permute-start | bytes 98312 | tf_op jit(solution)/shard_map/ppermute | solution.py:127
  73.3 1.5 %convolution_subtract_fusion.1 = f32[2048,128]{1,0:T(8,128)S(1)} fusion(bf16[2048,128]{1,0:T(8,128)(2,1)S(1)} %copy-done, f32[2048,1024]{1,0:T(8,128)} %param.17, bf16[128,1024]{1,0:T(8,128)(2,1)S(1)} %maximum_select_fusion), kind=kOutput, calls=%fused_computation.4 | convolution fusion | flops 67371008 | bytes 2654208 | tf_op jit(solution)/shard_map/dot_general | solution.py:220
  74.9 1.3 collective-permute-start.11
  76.2 0.7 collective-permute-start.10
  76.8 0.7 collective-permute-start.9
  77.6 3.5 %collective-permute-done.11 = f32[128,128]{1,0:T(8,128)S(1)} collective-permute-done((f32[128,128]{1,0:T(8,128)S(1)}, f32[128,128]{1,0:T(8,128)S(1)}, u32[]{:S(2)}, u32[]{:S(2)}) %collective-permute-start.11) | collective-permute-done | bytes 65568 | tf_op jit(solution)/shard_map/ppermute | solution.py:99
  81.1 0.3 fusion.2
  82.3 1.0 convolution_convert_fusion
  83.3 0.7 collective-permute-start.17
  84.0 0.7 collective-permute-start.16
  84.6 0.7 collective-permute-start.15
  85.3 0.8 slice.137.x_ref
  86.1 18.8 %shard_map.138 = bf16[2048,128]{1,0:T(8,128)(2,1)} custom-call(bf16[2048,128]{1,0:T(8,128)(2,1)} %slice.137.x_ref), custom_call_target="tpu_custom_call" | custom-call | tf_op jit(solution)/shard_map/pallas_call | solution.py:77
  105.0 3.1 %fusion.62 = f32[128,1024]{1,0:T(8,128)S(1)} fusion(bf16[2048,128]{1,0:T(8,128)(2,1)} %shard_map.138, bf16[2048,1024]{1,0:T(8,128)(2,1)} %param.12), kind=kOutput, calls=%fused_computation.111 | convolution fusion | flops 536870912 | bytes 5242880 | tf_op jit(solution)/shard_map/dot_general | solution.py:245
  108.2 1.3 collective-permute-start.20
  109.5 0.7 collective-permute-start.19
  110.1 0.7 collective-permute-start.18
  110.8 1.4 fusion.15
  112.2 1.5 %collective-permute-done.20 = bf16[16,128]{1,0:T(8,128)(2,1)S(1)} collective-permute-done((bf16[16,128]{1,0:T(8,128)(2,1)S(1)}, bf16[16,128]{1,0:T(8,128)(2,1)S(1)}, u32[]{:S(2)}, u32[]{:S(2)}) %collective-permute-start.20) | collective-permute-done | bytes 4128 | tf_op jit(solution)/shard_map/ppermute | solution.py:99
  114.4 6.3 %collective-permute-start.21 = (f32[128,128]{1,0:T(8,128)S(1)}, f32[128,128]{1,0:T(8,128)S(1)}, u32[]{:S(2)}, u32[]{:S(2)}) collective-permute-start(f32[128,128]{1,0:T(8,128)S(1)} %convolution_add_fusion.1), channel_id=1, source_target_pairs={{0,16},{16,0},{32,48},{48,32},{64,80},{80,64},{96,112},{112,96},{1... | collective-permute-start | bytes 196616 | tf_op jit(solution)/shard_map/ppermute | solution.py:111
  120.9 0.7 collective-permute-done.21
  121.8 0.6 pad_maximum_fusion.2
  122.5 4.2 %collective-permute-done.22 = f32[128,128]{1,0:T(8,128)S(1)} collective-permute-done((f32[128,128]{1,0:T(8,128)S(1)}, f32[128,128]{1,0:T(8,128)S(1)}, u32[]{:S(2)}, u32[]{:S(2)}) %collective-permute-start.22) | collective-permute-done | bytes 65568 | tf_op jit(solution)/shard_map/ppermute | solution.py:111
  126.7 2.5 %collective-permute-start.23 = (f32[128,128]{1,0:T(8,128)S(1)}, f32[128,128]{1,0:T(8,128)S(1)}, u32[]{:S(2)}, u32[]{:S(2)}) collective-permute-start(f32[128,128]{1,0:T(8,128)S(1)} %add.132), channel_id=1, source_target_pairs={{0,64},{16,80},{32,96},{48,112},{64,0},{80,16},{96,32},{112,48},{1... | collective-permute-start | bytes 196616 | tf_op jit(solution)/shard_map/ppermute | solution.py:111
  129.3 0.5 collective-permute-start.28
  129.8 1.6 %collective-permute-done.23 = f32[128,128]{1,0:T(8,128)S(1)} collective-permute-done((f32[128,128]{1,0:T(8,128)S(1)}, f32[128,128]{1,0:T(8,128)S(1)}, u32[]{:S(2)}, u32[]{:S(2)}) %collective-permute-start.23) | collective-permute-done | bytes 65568 | tf_op jit(solution)/shard_map/ppermute | solution.py:111
  131.4 0.7 collective-permute-start.32
  132.1 0.7 collective-permute-start.31
  132.8 0.7 collective-permute-start.30
  133.4 4.7 %convolution_subtract_fusion = bf16[2048,1024]{1,0:T(8,128)(2,1)S(1)} fusion(f32[2048,1024]{1,0:T(8,128)} %param.17, bf16[2048,128]{1,0:T(8,128)(2,1)S(1)} %copy-done.1, bf16[2048,128]{1,0:T(8,128)(2,1)S(1)} %copy-done, bf16[128,1024]{1,0:T(8,128)(2,1)S(1)} %maximum_select_fusion.1, bf16[128,1024]{1,0:T(8,128)(2,1)S(1)} %maximum_select_fusion), kind=kOutput, calls=%fused_computation.1 | convolution fusion | flops 1081081856 | bytes 14155776 | tf_op jit(solution)/shard_map/dot_general | solution.py:238
  138.4 0.4 slice.197
  138.8 2.7 %collective-permute-start.29 = (bf16[1,16,1024]{2,1,0:T(8,128)(2,1)S(1)}, bf16[1,16,1024]{2,1,0:T(8,128)(2,1)S(1)}, u32[]{:S(2)}, u32[]{:S(2)}) collective-permute-start(bf16[1,16,1024]{2,1,0:T(8,128)(2,1)S(1)} %select_convert_fusion.4), channel_id=1, source_target_pairs={{0,16},{16,0},{32,48},{48,32},{64,80},{80,64},{96,112},{112,96},{1... | collective-permute-start | bytes 98312 | tf_op jit(solution)/shard_map/ppermute | solution.py:127
  141.6 1.4 collective-permute-start.35
  143.1 0.7 collective-permute-start.34
  143.7 0.7 collective-permute-start.33
  144.4 2.6 %pad_maximum_fusion = bf16[2048,1024]{1,0:T(8,128)(2,1)} fusion(bf16[2048,128]{1,0:T(8,128)(2,1)S(1)} %fusion.7, bf16[2048,896]{1,0:T(8,128)(2,1)S(1)} %slice.197), kind=kLoop, calls=%fused_computation.2 | loop fusion | flops 8388608 | bytes 8388608 | tf_op jit(solution)/shard_map/concatenate | solution.py:255
  147.0 1.5 %collective-permute-done.35 = f32[128,128]{1,0:T(8,128)S(1)} collective-permute-done((f32[128,128]{1,0:T(8,128)S(1)}, f32[128,128]{1,0:T(8,128)S(1)}, u32[]{:S(2)}, u32[]{:S(2)}) %collective-permute-start.35) | collective-permute-done | bytes 65568 | tf_op jit(solution)/shard_map/ppermute | solution.py:99
  148.6 0.3 fusion.1
  149.8 0.6 pad_maximum_fusion.1
  (102 shorter events, 3.9 us)
Async XLA Ops:
  0.6 55.0 %collective-permute-start.24 = (bf16[16,1024]{1,0:T(8,128)(2,1)}, bf16[16,1024]{1,0:T(8,128)(2,1)S(1)}, u32[]{:S(2)}, u32[]{:S(2)}) collective-permute-start(bf16[16,1024]{1,0:T(8,128)(2,1)} %param.13), channel_id=1, source_target_pairs={{0,16},{16,0},{32,48},{48,32},{64,80},{80,64},{96,112},{112,96},{1... | collective-permute-start | bytes 98312 | tf_op jit(solution)/shard_map/ppermute | solution.py:137
  2.1 54.0 %collective-permute-start.12 = (bf16[16,1024]{1,0:T(8,128)(2,1)}, bf16[16,1024]{1,0:T(8,128)(2,1)S(1)}, u32[]{:S(2)}, u32[]{:S(2)}) collective-permute-start(bf16[16,1024]{1,0:T(8,128)(2,1)} %param.14), channel_id=1, source_target_pairs={{0,16},{16,0},{32,48},{48,32},{64,80},{80,64},{96,112},{112,96},{1... | collective-permute-start | bytes 98312 | tf_op jit(solution)/shard_map/ppermute | solution.py:137
  16.2 29.2 %copy-start.3 = (f32[128,128]{1,0:T(8,128)S(1)}, f32[128,128]{1,0:T(8,128)}, u32[]{:S(2)}) copy-start(f32[128,128]{1,0:T(8,128)} %param.15) | copy-start | bytes 196612
  34.6 21.1 %copy-start.11 = (bf16[16,1024]{1,0:T(8,128)(2,1)S(1)}, bf16[16,1024]{1,0:T(8,128)(2,1)}, u32[]{:S(2)}) copy-start(bf16[16,1024]{1,0:T(8,128)(2,1)} %param.13) | copy-start | bytes 98308
  34.6 21.5 %copy-start.4 = (bf16[16,1024]{1,0:T(8,128)(2,1)S(1)}, bf16[16,1024]{1,0:T(8,128)(2,1)}, u32[]{:S(2)}) copy-start(bf16[16,1024]{1,0:T(8,128)(2,1)} %param.14) | copy-start | bytes 98308
  36.1 21.2 %collective-permute-start.3 = (f32[128,128]{1,0:T(8,128)S(1)}, f32[128,128]{1,0:T(8,128)S(1)}, u32[]{:S(2)}, u32[]{:S(2)}) collective-permute-start(f32[128,128]{1,0:T(8,128)S(1)} %fusion.17), channel_id=1, source_target_pairs={{0,16},{16,0},{32,48},{48,32},{64,80},{80,64},{96,112},{112,96},{1... | collective-permute-start | bytes 196616 | tf_op jit(solution)/shard_map/ppermute | solution.py:111
  39.3 33.9 %copy-start = (bf16[2048,128]{1,0:T(8,128)(2,1)S(1)}, bf16[2048,128]{1,0:T(8,128)(2,1)}, u32[]{:S(2)}) copy-start(bf16[2048,128]{1,0:T(8,128)(2,1)} %shard_map.137) | copy-start | bytes 1572868
  42.5 38.6 %copy-start.2 = (f32[128,128]{1,0:T(8,128)S(1)}, f32[128,128]{1,0:T(8,128)}, u32[]{:S(2)}) copy-start(f32[128,128]{1,0:T(8,128)} %param.16) | copy-start | bytes 196612
  42.5 38.6 %copy-start.7 = (f32[128,128]{1,0:T(8,128)S(1)}, f32[128,128]{1,0:T(8,128)}, u32[]{:S(2)}) copy-start(f32[128,128]{1,0:T(8,128)} %param.21) | copy-start | bytes 196612
  42.6 19.9 %collective-permute-start = (bf16[4,16,1024]{2,1,0:T(8,128)(2,1)S(1)}, bf16[4,16,1024]{2,1,0:T(8,128)(2,1)S(1)}, u32[]{:S(2)}, u32[]{:S(2)}) collective-permute-start(bf16[4,16,1024]{2,1,0:T(8,128)(2,1)S(1)} %bitcast.62), channel_id=1, source_target_pairs={{0,64},{16,80},{32,96},{48,112},{64,0},{80,16},{96,32},{112,48},{1... | collective-permute-start | bytes 393224 | tf_op jit(solution)/shard_map/ppermute | solution.py:127
  45.4 36.6 %copy-start.9 = (f32[16,1024]{1,0:T(8,128)S(1)}, f32[16,1024]{1,0:T(8,128)}, u32[]{:S(2)}) copy-start(f32[16,1024]{1,0:T(8,128)} %param.19) | copy-start | bytes 196612
  55.7 3.2 %collective-permute-start.25 = (bf16[32,1024]{1,0:T(8,128)(2,1)S(1)}, bf16[32,1024]{1,0:T(8,128)(2,1)S(1)}, u32[]{:S(2)}, u32[]{:S(2)}) collective-permute-start(bf16[32,1024]{1,0:T(8,128)(2,1)S(1)} %maximum_select_fusion.5), channel_id=1, source_target_pairs={{0,32},{16,48},{32,0},{48,16},{64,96},{80,112},{96,64},{112,80},{1... | collective-permute-start | bytes 196616 | tf_op jit(solution)/shard_map/ppermute | solution.py:137
  56.1 7.7 %collective-permute-start.13 = (bf16[32,1024]{1,0:T(8,128)(2,1)S(1)}, bf16[32,1024]{1,0:T(8,128)(2,1)S(1)}, u32[]{:S(2)}, u32[]{:S(2)}) collective-permute-start(bf16[32,1024]{1,0:T(8,128)(2,1)S(1)} %maximum_select_fusion.4), channel_id=1, source_target_pairs={{0,32},{16,48},{32,0},{48,16},{64,96},{80,112},{96,64},{112,80},{1... | collective-permute-start | bytes 196616 | tf_op jit(solution)/shard_map/ppermute | solution.py:137
  57.4 4.6 %collective-permute-start.4 = (f32[128,128]{1,0:T(8,128)S(1)}, f32[128,128]{1,0:T(8,128)S(1)}, u32[]{:S(2)}, u32[]{:S(2)}) collective-permute-start(f32[128,128]{1,0:T(8,128)S(1)} %add.117), channel_id=1, source_target_pairs={{0,32},{16,48},{32,0},{48,16},{64,96},{80,112},{96,64},{112,80},{1... | collective-permute-start | bytes 196616 | tf_op jit(solution)/shard_map/ppermute | solution.py:111
  58.9 18.6 %collective-permute-start.26 = (bf16[64,1024]{1,0:T(8,128)(2,1)S(1)}, bf16[64,1024]{1,0:T(8,128)(2,1)S(1)}, u32[]{:S(2)}, u32[]{:S(2)}) collective-permute-start(bf16[64,1024]{1,0:T(8,128)(2,1)S(1)} %maximum_select_fusion.3), channel_id=1, source_target_pairs={{0,64},{16,80},{32,96},{48,112},{64,0},{80,16},{96,32},{112,48},{1... | collective-permute-start | bytes 393224 | tf_op jit(solution)/shard_map/ppermute | solution.py:137
  62.0 5.6 %collective-permute-start.5 = (f32[128,128]{1,0:T(8,128)S(1)}, f32[128,128]{1,0:T(8,128)S(1)}, u32[]{:S(2)}, u32[]{:S(2)}) collective-permute-start(f32[128,128]{1,0:T(8,128)S(1)} %add.118), channel_id=1, source_target_pairs={{0,64},{16,80},{32,96},{48,112},{64,0},{80,16},{96,32},{112,48},{1... | collective-permute-start | bytes 196616 | tf_op jit(solution)/shard_map/ppermute | solution.py:111
  62.5 6.4 %collective-permute-start.1 = (bf16[2,16,1024]{2,1,0:T(8,128)(2,1)S(1)}, bf16[2,16,1024]{2,1,0:T(8,128)(2,1)S(1)}, u32[]{:S(2)}, u32[]{:S(2)}) collective-permute-start(bf16[2,16,1024]{2,1,0:T(8,128)(2,1)S(1)} %select_convert_fusion.3), channel_id=1, source_target_pairs={{0,32},{16,48},{32,0},{48,16},{64,96},{80,112},{96,64},{112,80},{1... | collective-permute-start | bytes 196616 | tf_op jit(solution)/shard_map/ppermute | solution.py:127
  63.8 7.3 %collective-permute-start.14 = (bf16[64,1024]{1,0:T(8,128)(2,1)S(1)}, bf16[64,1024]{1,0:T(8,128)(2,1)S(1)}, u32[]{:S(2)}, u32[]{:S(2)}) collective-permute-start(bf16[64,1024]{1,0:T(8,128)(2,1)S(1)} %maximum_select_fusion.2), channel_id=1, source_target_pairs={{0,64},{16,80},{32,96},{48,112},{64,0},{80,16},{96,32},{112,48},{1... | collective-permute-start | bytes 393224 | tf_op jit(solution)/shard_map/ppermute | solution.py:137
  67.6 7.2 %collective-permute-start.8 = (f32[128,128]{1,0:T(8,128)S(1)}, f32[128,128]{1,0:T(8,128)S(1)}, u32[]{:S(2)}, u32[]{:S(2)}) collective-permute-start(f32[128,128]{1,0:T(8,128)S(1)} %add.119), channel_id=1, source_target_pairs={{15,12},{31,28},{47,44},{63,60},{79,76},{95,92},{111,108},{127,124}} | collective-permute-start | bytes 196616 | tf_op jit(solution)/shard_map/ppermute | solution.py:99
  68.3 6.6 %collective-permute-start.7 = (f32[128,128]{1,0:T(8,128)S(1)}, f32[128,128]{1,0:T(8,128)S(1)}, u32[]{:S(2)}, u32[]{:S(2)}) collective-permute-start(f32[128,128]{1,0:T(8,128)S(1)} %add.119), channel_id=1, source_target_pairs={{15,13},{31,29},{47,45},{63,61},{79,77},{95,93},{111,109},{127,125}} | collective-permute-start | bytes 196616 | tf_op jit(solution)/shard_map/ppermute | solution.py:99
  68.9 5.9 %collective-permute-start.6 = (f32[128,128]{1,0:T(8,128)S(1)}, f32[128,128]{1,0:T(8,128)S(1)}, u32[]{:S(2)}, u32[]{:S(2)}) collective-permute-start(f32[128,128]{1,0:T(8,128)S(1)} %add.119), channel_id=1, source_target_pairs={{15,14},{31,30},{47,46},{63,62},{79,78},{95,94},{111,110},{127,126}} | collective-permute-start | bytes 196616 | tf_op jit(solution)/shard_map/ppermute | solution.py:99
  71.1 11.0 %collective-permute-start.2 = (bf16[1,16,1024]{2,1,0:T(8,128)(2,1)S(1)}, bf16[1,16,1024]{2,1,0:T(8,128)(2,1)S(1)}, u32[]{:S(2)}, u32[]{:S(2)}) collective-permute-start(bf16[1,16,1024]{2,1,0:T(8,128)(2,1)S(1)} %select_convert_fusion.5), channel_id=1, source_target_pairs={{0,16},{16,0},{32,48},{48,32},{64,80},{80,64},{96,112},{112,96},{1... | collective-permute-start | bytes 98312 | tf_op jit(solution)/shard_map/ppermute | solution.py:127
  74.9 6.2 %collective-permute-start.11 = (f32[128,128]{1,0:T(8,128)S(1)}, f32[128,128]{1,0:T(8,128)S(1)}, u32[]{:S(2)}, u32[]{:S(2)}) collective-permute-start(f32[128,128]{1,0:T(8,128)S(1)} %add_select_fusion.1), channel_id=1, source_target_pairs={{15,3},{14,2},{13,1},{12,0},{31,19},{30,18},{29,17},{28,16},{47,35... | collective-permute-start | bytes 196616 | tf_op jit(solution)/shard_map/ppermute | solution.py:99
  76.2 4.9 %collective-permute-start.10 = (f32[128,128]{1,0:T(8,128)S(1)}, f32[128,128]{1,0:T(8,128)S(1)}, u32[]{:S(2)}, u32[]{:S(2)}) collective-permute-start(f32[128,128]{1,0:T(8,128)S(1)} %add_select_fusion.1), channel_id=1, source_target_pairs={{15,7},{14,6},{13,5},{12,4},{31,23},{30,22},{29,21},{28,20},{47,39... | collective-permute-start | bytes 196616 | tf_op jit(solution)/shard_map/ppermute | solution.py:99
  76.8 4.3 %collective-permute-start.9 = (f32[128,128]{1,0:T(8,128)S(1)}, f32[128,128]{1,0:T(8,128)S(1)}, u32[]{:S(2)}, u32[]{:S(2)}) collective-permute-start(f32[128,128]{1,0:T(8,128)S(1)} %add_select_fusion.1), channel_id=1, source_target_pairs={{15,11},{14,10},{13,9},{12,8},{31,27},{30,26},{29,25},{28,24},{47,... | collective-permute-start | bytes 196616 | tf_op jit(solution)/shard_map/ppermute | solution.py:99
  81.9 26.2 %copy-start.5 = (f32[128,128]{1,0:T(8,128)}, f32[128,128]{1,0:T(8,128)S(1)}, u32[]{:S(2)}) copy-start(f32[128,128]{1,0:T(8,128)S(1)} %get-tuple-element.10) | copy-start | bytes 196612
  83.3 24.8 %collective-permute-start.17 = (bf16[16,128]{1,0:T(8,128)(2,1)S(1)}, bf16[16,128]{1,0:T(8,128)(2,1)S(1)}, u32[]{:S(2)}, u32[]{:S(2)}) collective-permute-start(bf16[16,128]{1,0:T(8,128)(2,1)S(1)} %slice.138), channel_id=1, source_target_pairs={{14,13},{30,29},{46,45},{62,61},{78,77},{94,93},{110,109},{126,125}} | collective-permute-start | bytes 12296 | tf_op jit(solution)/shard_map/ppermute | solution.py:99
  84.0 24.2 %collective-permute-start.16 = (bf16[16,128]{1,0:T(8,128)(2,1)S(1)}, bf16[16,128]{1,0:T(8,128)(2,1)S(1)}, u32[]{:S(2)}, u32[]{:S(2)}) collective-permute-start(bf16[16,128]{1,0:T(8,128)(2,1)S(1)} %slice.138), channel_id=1, source_target_pairs={{14,12},{30,28},{46,44},{62,60},{78,76},{94,92},{110,108},{126,124}} | collective-permute-start | bytes 12296 | tf_op jit(solution)/shard_map/ppermute | solution.py:99
  84.6 23.5 %collective-permute-start.15 = (bf16[16,128]{1,0:T(8,128)(2,1)S(1)}, bf16[16,128]{1,0:T(8,128)(2,1)S(1)}, u32[]{:S(2)}, u32[]{:S(2)}) collective-permute-start(bf16[16,128]{1,0:T(8,128)(2,1)S(1)} %slice.138), channel_id=1, source_target_pairs={{14,15},{30,31},{46,47},{62,63},{78,79},{94,95},{110,111},{126,127}} | collective-permute-start | bytes 12296 | tf_op jit(solution)/shard_map/ppermute | solution.py:99
  104.9 5.9 %copy-start.1 = (bf16[2048,128]{1,0:T(8,128)(2,1)S(1)}, bf16[2048,128]{1,0:T(8,128)(2,1)}, u32[]{:S(2)}) copy-start(bf16[2048,128]{1,0:T(8,128)(2,1)} %shard_map.138) | copy-start | bytes 1572868
  108.2 5.6 %collective-permute-start.20 = (bf16[16,128]{1,0:T(8,128)(2,1)S(1)}, bf16[16,128]{1,0:T(8,128)(2,1)S(1)}, u32[]{:S(2)}, u32[]{:S(2)}) collective-permute-start(bf16[16,128]{1,0:T(8,128)(2,1)S(1)} %add_select_fusion.3), channel_id=1, source_target_pairs={{14,2},{15,3},{12,0},{13,1},{30,18},{31,19},{28,16},{29,17},{46,34... | collective-permute-start | bytes 12296 | tf_op jit(solution)/shard_map/ppermute | solution.py:99
  109.5 4.3 %collective-permute-start.19 = (bf16[16,128]{1,0:T(8,128)(2,1)S(1)}, bf16[16,128]{1,0:T(8,128)(2,1)S(1)}, u32[]{:S(2)}, u32[]{:S(2)}) collective-permute-start(bf16[16,128]{1,0:T(8,128)(2,1)S(1)} %add_select_fusion.3), channel_id=1, source_target_pairs={{14,6},{15,7},{12,4},{13,5},{30,22},{31,23},{28,20},{29,21},{46,38... | collective-permute-start | bytes 12296 | tf_op jit(solution)/shard_map/ppermute | solution.py:99
  110.1 3.6 %collective-permute-start.18 = (bf16[16,128]{1,0:T(8,128)(2,1)S(1)}, bf16[16,128]{1,0:T(8,128)(2,1)S(1)}, u32[]{:S(2)}, u32[]{:S(2)}) collective-permute-start(bf16[16,128]{1,0:T(8,128)(2,1)S(1)} %add_select_fusion.3), channel_id=1, source_target_pairs={{14,10},{15,11},{12,8},{13,9},{30,26},{31,27},{28,24},{29,25},{46,... | collective-permute-start | bytes 12296 | tf_op jit(solution)/shard_map/ppermute | solution.py:99
  114.4 7.2 %collective-permute-start.21 = (f32[128,128]{1,0:T(8,128)S(1)}, f32[128,128]{1,0:T(8,128)S(1)}, u32[]{:S(2)}, u32[]{:S(2)}) collective-permute-start(f32[128,128]{1,0:T(8,128)S(1)} %convolution_add_fusion.1), channel_id=1, source_target_pairs={{0,16},{16,0},{32,48},{48,32},{64,80},{80,64},{96,112},{112,96},{1... | collective-permute-start | bytes 196616 | tf_op jit(solution)/shard_map/ppermute | solution.py:111
  120.7 8.5 %collective-permute-start.27 = (bf16[4,16,1024]{2,1,0:T(8,128)(2,1)S(1)}, bf16[4,16,1024]{2,1,0:T(8,128)(2,1)S(1)}, u32[]{:S(2)}, u32[]{:S(2)}) collective-permute-start(bf16[4,16,1024]{2,1,0:T(8,128)(2,1)S(1)} %bitcast.63), channel_id=1, source_target_pairs={{0,64},{16,80},{32,96},{48,112},{64,0},{80,16},{96,32},{112,48},{1... | collective-permute-start | bytes 393224 | tf_op jit(solution)/shard_map/ppermute | solution.py:127
  121.6 5.0 %collective-permute-start.22 = (f32[128,128]{1,0:T(8,128)S(1)}, f32[128,128]{1,0:T(8,128)S(1)}, u32[]{:S(2)}, u32[]{:S(2)}) collective-permute-start(f32[128,128]{1,0:T(8,128)S(1)} %add.131), channel_id=1, source_target_pairs={{0,32},{16,48},{32,0},{48,16},{64,96},{80,112},{96,64},{112,80},{1... | collective-permute-start | bytes 196616 | tf_op jit(solution)/shard_map/ppermute | solution.py:111
  126.7 4.7 %collective-permute-start.23 = (f32[128,128]{1,0:T(8,128)S(1)}, f32[128,128]{1,0:T(8,128)S(1)}, u32[]{:S(2)}, u32[]{:S(2)}) collective-permute-start(f32[128,128]{1,0:T(8,128)S(1)} %add.132), channel_id=1, source_target_pairs={{0,64},{16,80},{32,96},{48,112},{64,0},{80,16},{96,32},{112,48},{1... | collective-permute-start | bytes 196616 | tf_op jit(solution)/shard_map/ppermute | solution.py:111
  129.3 9.1 %collective-permute-start.28 = (bf16[2,16,1024]{2,1,0:T(8,128)(2,1)S(1)}, bf16[2,16,1024]{2,1,0:T(8,128)(2,1)S(1)}, u32[]{:S(2)}, u32[]{:S(2)}) collective-permute-start(bf16[2,16,1024]{2,1,0:T(8,128)(2,1)S(1)} %select_convert_fusion.2), channel_id=1, source_target_pairs={{0,32},{16,48},{32,0},{48,16},{64,96},{80,112},{96,64},{112,80},{1... | collective-permute-start | bytes 196616 | tf_op jit(solution)/shard_map/ppermute | solution.py:127
  131.4 10.1 %collective-permute-start.32 = (f32[128,128]{1,0:T(8,128)S(1)}, f32[128,128]{1,0:T(8,128)S(1)}, u32[]{:S(2)}, u32[]{:S(2)}) collective-permute-start(f32[128,128]{1,0:T(8,128)S(1)} %add.133), channel_id=1, source_target_pairs={{14,13},{30,29},{46,45},{62,61},{78,77},{94,93},{110,109},{126,125}} | collective-permute-start | bytes 196616 | tf_op jit(solution)/shard_map/ppermute | solution.py:99
  132.1 9.5 %collective-permute-start.31 = (f32[128,128]{1,0:T(8,128)S(1)}, f32[128,128]{1,0:T(8,128)S(1)}, u32[]{:S(2)}, u32[]{:S(2)}) collective-permute-start(f32[128,128]{1,0:T(8,128)S(1)} %add.133), channel_id=1, source_target_pairs={{14,12},{30,28},{46,44},{62,60},{78,76},{94,92},{110,108},{126,124}} | collective-permute-start | bytes 196616 | tf_op jit(solution)/shard_map/ppermute | solution.py:99
  132.8 8.8 %collective-permute-start.30 = (f32[128,128]{1,0:T(8,128)S(1)}, f32[128,128]{1,0:T(8,128)S(1)}, u32[]{:S(2)}, u32[]{:S(2)}) collective-permute-start(f32[128,128]{1,0:T(8,128)S(1)} %add.133), channel_id=1, source_target_pairs={{14,15},{30,31},{46,47},{62,63},{78,79},{94,95},{110,111},{126,127}} | collective-permute-start | bytes 196616 | tf_op jit(solution)/shard_map/ppermute | solution.py:99
  138.8 10.7 %collective-permute-start.29 = (bf16[1,16,1024]{2,1,0:T(8,128)(2,1)S(1)}, bf16[1,16,1024]{2,1,0:T(8,128)(2,1)S(1)}, u32[]{:S(2)}, u32[]{:S(2)}) collective-permute-start(bf16[1,16,1024]{2,1,0:T(8,128)(2,1)S(1)} %select_convert_fusion.4), channel_id=1, source_target_pairs={{0,16},{16,0},{32,48},{48,32},{64,80},{80,64},{96,112},{112,96},{1... | collective-permute-start | bytes 98312 | tf_op jit(solution)/shard_map/ppermute | solution.py:127
  141.6 7.0 %copy-start.8 = (f32[128,128]{1,0:T(8,128)S(1)}, f32[128,128]{1,0:T(8,128)}, u32[]{:S(2)}) copy-start(f32[128,128]{1,0:T(8,128)} %param.20) | copy-start | bytes 196612
  141.6 7.9 %copy-start.10 = (f32[16,1024]{1,0:T(8,128)S(1)}, f32[16,1024]{1,0:T(8,128)}, u32[]{:S(2)}) copy-start(f32[16,1024]{1,0:T(8,128)} %param.18) | copy-start | bytes 196612
  141.6 6.9 %collective-permute-start.35 = (f32[128,128]{1,0:T(8,128)S(1)}, f32[128,128]{1,0:T(8,128)S(1)}, u32[]{:S(2)}, u32[]{:S(2)}) collective-permute-start(f32[128,128]{1,0:T(8,128)S(1)} %add_select_fusion), channel_id=1, source_target_pairs={{14,2},{15,3},{12,0},{13,1},{30,18},{31,19},{28,16},{29,17},{46,34... | collective-permute-start | bytes 196616 | tf_op jit(solution)/shard_map/ppermute | solution.py:99
  143.1 5.5 %collective-permute-start.34 = (f32[128,128]{1,0:T(8,128)S(1)}, f32[128,128]{1,0:T(8,128)S(1)}, u32[]{:S(2)}, u32[]{:S(2)}) collective-permute-start(f32[128,128]{1,0:T(8,128)S(1)} %add_select_fusion), channel_id=1, source_target_pairs={{14,6},{15,7},{12,4},{13,5},{30,22},{31,23},{28,20},{29,21},{46,38... | collective-permute-start | bytes 196616 | tf_op jit(solution)/shard_map/ppermute | solution.py:99
  143.7 4.8 %collective-permute-start.33 = (f32[128,128]{1,0:T(8,128)S(1)}, f32[128,128]{1,0:T(8,128)S(1)}, u32[]{:S(2)}, u32[]{:S(2)}) collective-permute-start(f32[128,128]{1,0:T(8,128)S(1)} %add_select_fusion), channel_id=1, source_target_pairs={{14,10},{15,11},{12,8},{13,9},{30,26},{31,27},{28,24},{29,25},{46,... | collective-permute-start | bytes 196616 | tf_op jit(solution)/shard_map/ppermute | solution.py:99
  149.4 1.0 copy-start.6

commit v18 on v17

--- a/solution.py
+++ b/solution.py
@@ -203,7 +203,8 @@
 
         def summed_block(partial_value, root):
             rows_sum = butterfly_sum(partial_value, "row", n_row)
-            return tree_broadcast(rows_sum, "col", n_col, root)
+            sent = tree_broadcast(rows_sum.astype(jnp.bfloat16), "col", n_col, root)
+            return sent.astype(jnp.float32)
 
         inverse_two = inverse_lower(diag_two)
         solved_two = solve_panel(adj_trail[:, last:], inverse_two, root_two)
@@ -229,7 +230,8 @@
         ) + jnp.dot(tail_rows.T, trail[:, last:], preferred_element_type=jnp.float32)
         rows_one = butterfly_sum(partial_one, "row", n_row)
         tail_late, rows_one = lax.optimization_barrier((tail_rows, rows_one))
-        seed_one = jnp.tril(adj_diag_one - tree_broadcast(rows_one, "col", n_col, root_one))
+        sent_one = tree_broadcast(rows_one.astype(jnp.bfloat16), "col", n_col, root_one)
+        seed_one = jnp.tril(adj_diag_one - sent_one.astype(jnp.float32))
         grad_diag_one = block_adjoint(diag_one, inverse_one, seed_one)
         mirror_one = own_rows(grad_diag_one + grad_diag_one.T)
         rest_one = jnp.dot(mirror_one, full_one.astype(jnp.float32), precision=exact_mode)

time: 152 us -> 153 us (level)
  Pallas kernels: 37.2 us -> 35.5 us
    pallas_call x2, Pallas kernels: 37.2 us -> 35.5 us  [panel_broadcast(): pl.pallas_call(functools.partial(spread_kernel, root, size), out_shape=ja...]
  transfers between devices with their start and end apart: 36 -> 36, of which waited for: 10 -> 8; matrix products, arithmetic and copies ran while one was open for 31% -> 31% of each run, Pallas kernels for 25% -> 23%
where the time goes in v18:
time: 153 us; the launch traced here: 151 us
  starting transfers between devices  44.9 us (29%)
  Pallas kernels  35.5 us (23%)
  other arithmetic  25.2 us (16%)
  matrix products  22.6 us (15%)
  waiting for transfers between devices  19.9 us (13%)
  local copies, waits for them, and re-layouts  1.53 us (1%)
  between operations  1.53 us (1%)
    pallas_call x2, Pallas kernels, panel_broadcast(): pl.pallas_call(functools.partial(spread_kernel, root, size), out_shape=ja...  35.5 us
    another operation x4, other arithmetic, inverse_lower(): return lax.linalg.triangular_solve(block, ident, left_side=True, lower=True)  20.5 us
    ppermute x6, starting transfers between devices, butterfly_sum(): value = value + lax.ppermute(value, axis, pairs)  14.5 us
    ppermute x18, starting transfers between devices, tree_broadcast(): part = lax.ppermute(value, axis, pairs)  13.9 us
    ppermute x6, waiting for transfers between devices, butterfly_sum(): value = value + lax.ppermute(value, axis, pairs)  11 us
    ppermute x6, starting transfers between devices, halving_scatter(): lax.ppermute(send.astype(jnp.bfloat16), axis, pairs).astype(jnp.float32)  10.6 us
    ppermute x18, waiting for transfers between devices, tree_broadcast(): part = lax.ppermute(value, axis, pairs)  7.33 us
    ppermute x6, starting transfers between devices, doubling_gather(): other = lax.ppermute(value, axis, pairs)  5.94 us
  transfers between devices with their start and end apart: 36, of which 8 were waited for; matrix products, arithmetic and copies ran while one was open for 31% of the time, Pallas kernels for 23%

profile of v18, /device:TPU:1, one launch (start us, length us, event | category | flops | bytes accessed | tf_op | source)
XLA Modules:
  0.0 151.2 jit_solution(1342188367607861690)
XLA Ops:
  0.6 1.5 collective-permute-start.24
  2.2 0.8 select_bitcast_fusion.1
  3.1 9.8 %custom-call.4 = f32[1,128,128]{1,2,0:T(8,128)S(1)} custom-call(f32[1,128,128]{2,1,0:T(8,128)S(1)} %select_bitcast_fusion.1), custom_call_target="InvertDiagBlocksLowerTriangular" | custom-call | tf_op jit(solution)/shard_map/triangular_solve/custom-call.1 | solution.py:158
  12.9 0.3 fusion.21
  13.2 3.0 %fusion.x_ref = bf16[2048,128]{1,0:T(8,128)(2,1)} fusion(f32[128,128]{1,0:T(8,128)S(1)} %fusion.21, f32[2048,1024]{1,0:T(8,128)} %param.17), kind=kOutput, calls=%fused_computation.6 | convolution fusion | flops 402915328 | bytes 1638400 | tf_op jit(solution)/shard_map/dot_general | solution.py:197
  16.2 18.4 %shard_map.137 = bf16[2048,128]{1,0:T(8,128)(2,1)} custom-call(bf16[2048,128]{1,0:T(8,128)(2,1)} %fusion.x_ref), custom_call_target="tpu_custom_call" | custom-call | tf_op jit(solution)/shard_map/pallas_call | solution.py:77
  34.6 1.5 %fusion.17 = f32[128,128]{1,0:T(8,128)S(1)} fusion(bf16[2048,128]{1,0:T(8,128)(2,1)} %shard_map.137, bf16[2048,1024]{1,0:T(8,128)(2,1)} %param.12), kind=kOutput, calls=%fused_computation.29 | convolution fusion | flops 67108864 | bytes 1114112 | tf_op jit(solution)/shard_map/dot_general | solution.py:211
  36.1 3.2 %collective-permute-start.3 = (f32[128,128]{1,0:T(8,128)S(1)}, f32[128,128]{1,0:T(8,128)S(1)}, u32[]{:S(2)}, u32[]{:S(2)}) collective-permute-start(f32[128,128]{1,0:T(8,128)S(1)} %fusion.17), channel_id=1, source_target_pairs={{0,16},{16,0},{32,48},{48,32},{64,80},{80,64},{96,112},{112,96},{1... | collective-permute-start | bytes 196616 | tf_op jit(solution)/shard_map/ppermute | solution.py:111
  39.3 3.1 %fusion.62 = f32[128,1024]{1,0:T(8,128)S(1)} fusion(bf16[2048,128]{1,0:T(8,128)(2,1)} %shard_map.137, bf16[2048,1024]{1,0:T(8,128)(2,1)} %param.12), kind=kOutput, calls=%fused_computation.112 | convolution fusion | flops 536870912 | bytes 5242880 | tf_op jit(solution)/shard_map/dot_general | solution.py:218
  42.6 2.8 %collective-permute-start = (bf16[4,16,1024]{2,1,0:T(8,128)(2,1)S(1)}, bf16[4,16,1024]{2,1,0:T(8,128)(2,1)S(1)}, u32[]{:S(2)}, u32[]{:S(2)}) collective-permute-start(bf16[4,16,1024]{2,1,0:T(8,128)(2,1)S(1)} %bitcast.62), channel_id=1, source_target_pairs={{0,64},{16,80},{32,96},{48,112},{64,0},{80,16},{96,32},{112,48},{1... | collective-permute-start | bytes 393224 | tf_op jit(solution)/shard_map/ppermute | solution.py:127
  45.4 9.8 %custom-call.5 = f32[1,128,128]{1,2,0:T(8,128)S(1)} custom-call(f32[1,128,128]{2,1,0:T(8,128)S(1)} %select_bitcast_fusion), custom_call_target="InvertDiagBlocksLowerTriangular" | custom-call | tf_op jit(solution)/shard_map/triangular_solve/custom-call.1 | solution.py:158
  55.3 0.3 fusion.19
  55.7 0.4 collective-permute-start.25
  56.1 1.2 collective-permute-start.13
  57.4 0.4 collective-permute-start.4
  57.7 1.1 collective-permute-done.25
  58.9 1.2 collective-permute-start.26
  60.1 0.4 collective-permute-done.13
  60.6 1.5 %collective-permute-start.14 = (bf16[64,1024]{1,0:T(8,128)(2,1)S(1)}, bf16[64,1024]{1,0:T(8,128)(2,1)S(1)}, u32[]{:S(2)}, u32[]{:S(2)}) collective-permute-start(bf16[64,1024]{1,0:T(8,128)(2,1)S(1)} %maximum_select_fusion.2), channel_id=1, source_target_pairs={{0,64},{16,80},{32,96},{48,112},{64,0},{80,16},{96,32},{112,48},{1... | collective-permute-start | bytes 393224 | tf_op jit(solution)/shard_map/ppermute | solution.py:137
  62.1 1.8 %collective-permute-start.5 = (f32[128,128]{1,0:T(8,128)S(1)}, f32[128,128]{1,0:T(8,128)S(1)}, u32[]{:S(2)}, u32[]{:S(2)}) collective-permute-start(f32[128,128]{1,0:T(8,128)S(1)} %add.118), channel_id=1, source_target_pairs={{0,64},{16,80},{32,96},{48,112},{64,0},{80,16},{96,32},{112,48},{1... | collective-permute-start | bytes 196616 | tf_op jit(solution)/shard_map/ppermute | solution.py:111
  64.2 3.9 %collective-permute-done.5 = f32[128,128]{1,0:T(8,128)S(1)} collective-permute-done((f32[128,128]{1,0:T(8,128)S(1)}, f32[128,128]{1,0:T(8,128)S(1)}, u32[]{:S(2)}, u32[]{:S(2)}) %collective-permute-start.5) | collective-permute-done | bytes 65568 | tf_op jit(solution)/shard_map/ppermute | solution.py:111
  68.1 0.7 collective-permute-start.8
  68.8 0.7 collective-permute-start.7
  69.5 0.7 collective-permute-start.6
  70.2 3.5 %collective-permute-start.2 = (bf16[1,16,1024]{2,1,0:T(8,128)(2,1)S(1)}, bf16[1,16,1024]{2,1,0:T(8,128)(2,1)S(1)}, u32[]{:S(2)}, u32[]{:S(2)}) collective-permute-start(bf16[1,16,1024]{2,1,0:T(8,128)(2,1)S(1)} %select_convert_fusion.5), channel_id=1, source_target_pairs={{0,16},{16,0},{32,48},{48,32},{64,80},{80,64},{96,112},{112,96},{1... | collective-permute-start | bytes 98312 | tf_op jit(solution)/shard_map/ppermute | solution.py:127
  73.8 1.3 collective-permute-start.11
  75.1 0.7 collective-permute-start.10
  75.8 0.7 collective-permute-start.9
  76.5 1.5 convolution_subtract_fusion.1
  78.1 5.2 %collective-permute-done.11 = bf16[128,128]{1,0:T(8,128)(2,1)S(1)} collective-permute-done((bf16[128,128]{1,0:T(8,128)(2,1)S(1)}, bf16[128,128]{1,0:T(8,128)(2,1)S(1)}, u32[]{:S(2)}, u32[]{:S(2)}) %collective-permute-start.11) | collective-permute-done | bytes 32800 | tf_op jit(solution)/shard_map/ppermute | solution.py:99
  83.3 0.3 fusion.2
  84.5 1.0 convolution_convert_fusion
  85.5 0.7 collective-permute-start.17
  86.1 0.7 collective-permute-start.16
  86.8 0.7 collective-permute-start.15
  87.5 0.8 slice.137.x_ref
  88.3 17.2 %shard_map.138 = bf16[2048,128]{1,0:T(8,128)(2,1)} custom-call(bf16[2048,128]{1,0:T(8,128)(2,1)} %slice.137.x_ref), custom_call_target="tpu_custom_call" | custom-call | tf_op jit(solution)/shard_map/pallas_call | solution.py:77
  105.5 3.1 %fusion.64 = f32[128,1024]{1,0:T(8,128)S(1)} fusion(bf16[2048,128]{1,0:T(8,128)(2,1)} %shard_map.138, bf16[2048,1024]{1,0:T(8,128)(2,1)} %param.12), kind=kOutput, calls=%fused_computation.114 | convolution fusion | flops 536870912 | bytes 5242880 | tf_op jit(solution)/shard_map/dot_general | solution.py:247
  108.7 1.3 collective-permute-start.20
  110.0 0.7 collective-permute-start.19
  110.6 0.7 collective-permute-start.18
  111.3 1.4 fusion.15
  112.7 1.5 %collective-permute-done.20 = bf16[16,128]{1,0:T(8,128)(2,1)S(1)} collective-permute-done((bf16[16,128]{1,0:T(8,128)(2,1)S(1)}, bf16[16,128]{1,0:T(8,128)(2,1)S(1)}, u32[]{:S(2)}, u32[]{:S(2)}) %collective-permute-start.20) | collective-permute-done | bytes 4128 | tf_op jit(solution)/shard_map/ppermute | solution.py:99
  114.9 6.3 %collective-permute-start.21 = (f32[128,128]{1,0:T(8,128)S(1)}, f32[128,128]{1,0:T(8,128)S(1)}, u32[]{:S(2)}, u32[]{:S(2)}) collective-permute-start(f32[128,128]{1,0:T(8,128)S(1)} %convolution_add_fusion.1), channel_id=1, source_target_pairs={{0,16},{16,0},{32,48},{48,32},{64,80},{80,64},{96,112},{112,96},{1... | collective-permute-start | bytes 196616 | tf_op jit(solution)/shard_map/ppermute | solution.py:111
  121.3 1.2 collective-permute-start.27
  122.5 1.1 collective-permute-start.22
  123.6 0.6 pad_maximum_fusion.2
  124.2 4.2 %collective-permute-done.22 = f32[128,128]{1,0:T(8,128)S(1)} collective-permute-done((f32[128,128]{1,0:T(8,128)S(1)}, f32[128,128]{1,0:T(8,128)S(1)}, u32[]{:S(2)}, u32[]{:S(2)}) %collective-permute-start.22) | collective-permute-done | bytes 65568 | tf_op jit(solution)/shard_map/ppermute | solution.py:111
  128.5 1.6 %collective-permute-start.23 = (f32[128,128]{1,0:T(8,128)S(1)}, f32[128,128]{1,0:T(8,128)S(1)}, u32[]{:S(2)}, u32[]{:S(2)}) collective-permute-start(f32[128,128]{1,0:T(8,128)S(1)} %add.132), channel_id=1, source_target_pairs={{0,64},{16,80},{32,96},{48,112},{64,0},{80,16},{96,32},{112,48},{1... | collective-permute-start | bytes 196616 | tf_op jit(solution)/shard_map/ppermute | solution.py:111
  130.3 2.8 %collective-permute-done.23 = f32[128,128]{1,0:T(8,128)S(1)} collective-permute-done((f32[128,128]{1,0:T(8,128)S(1)}, f32[128,128]{1,0:T(8,128)S(1)}, u32[]{:S(2)}, u32[]{:S(2)}) %collective-permute-start.23) | collective-permute-done | bytes 65568 | tf_op jit(solution)/shard_map/ppermute | solution.py:111
  133.2 0.7 collective-permute-start.32
  133.9 0.7 collective-permute-start.31
  134.5 0.7 collective-permute-start.30
  135.2 4.7 %convolution_subtract_fusion = bf16[2048,1024]{1,0:T(8,128)(2,1)S(1)} fusion(f32[2048,1024]{1,0:T(8,128)} %param.17, bf16[2048,128]{1,0:T(8,128)(2,1)S(1)} %copy-done.1, bf16[2048,128]{1,0:T(8,128)(2,1)S(1)} %copy-done, bf16[128,1024]{1,0:T(8,128)(2,1)S(1)} %maximum_select_fusion.1, bf16[128,1024]{1,0:T(8,128)(2,1)S(1)} %maximum_select_fusion), kind=kOutput, calls=%fused_computation.1 | convolution fusion | flops 1081081856 | bytes 14155776 | tf_op jit(solution)/shard_map/dot_general | solution.py:240
  140.2 0.4 slice.197
  140.6 2.6 %collective-permute-start.29 = (bf16[1,16,1024]{2,1,0:T(8,128)(2,1)S(1)}, bf16[1,16,1024]{2,1,0:T(8,128)(2,1)S(1)}, u32[]{:S(2)}, u32[]{:S(2)}) collective-permute-start(bf16[1,16,1024]{2,1,0:T(8,128)(2,1)S(1)} %select_convert_fusion.4), channel_id=1, source_target_pairs={{0,16},{16,0},{32,48},{48,32},{64,80},{80,64},{96,112},{112,96},{1... | collective-permute-start | bytes 98312 | tf_op jit(solution)/shard_map/ppermute | solution.py:127
  143.3 1.4 collective-permute-start.35
  144.7 0.7 collective-permute-start.34
  145.4 0.7 collective-permute-start.33
  146.1 2.6 %pad_maximum_fusion = bf16[2048,1024]{1,0:T(8,128)(2,1)} fusion(bf16[2048,128]{1,0:T(8,128)(2,1)S(1)} %fusion.7, bf16[2048,896]{1,0:T(8,128)(2,1)S(1)} %slice.197), kind=kLoop, calls=%fused_computation.2 | loop fusion | flops 8388608 | bytes 8388608 | tf_op jit(solution)/shard_map/concatenate | solution.py:257
  148.7 0.6 collective-permute-done.35
  149.3 0.3 fusion.1
  149.6 0.3 fusion.65
  150.5 0.6 pad_maximum_fusion.1
  (102 shorter events, 3.4 us)
Async XLA Ops:
  0.6 55.0 %collective-permute-start.24 = (bf16[16,1024]{1,0:T(8,128)(2,1)}, bf16[16,1024]{1,0:T(8,128)(2,1)S(1)}, u32[]{:S(2)}, u32[]{:S(2)}) collective-permute-start(bf16[16,1024]{1,0:T(8,128)(2,1)} %param.13), channel_id=1, source_target_pairs={{0,16},{16,0},{32,48},{48,32},{64,80},{80,64},{96,112},{112,96},{1... | collective-permute-start | bytes 98312 | tf_op jit(solution)/shard_map/ppermute | solution.py:137
  2.1 54.0 %collective-permute-start.12 = (bf16[16,1024]{1,0:T(8,128)(2,1)}, bf16[16,1024]{1,0:T(8,128)(2,1)S(1)}, u32[]{:S(2)}, u32[]{:S(2)}) collective-permute-start(bf16[16,1024]{1,0:T(8,128)(2,1)} %param.14), channel_id=1, source_target_pairs={{0,16},{16,0},{32,48},{48,32},{64,80},{80,64},{96,112},{112,96},{1... | collective-permute-start | bytes 98312 | tf_op jit(solution)/shard_map/ppermute | solution.py:137
  16.2 29.2 %copy-start.3 = (f32[128,128]{1,0:T(8,128)S(1)}, f32[128,128]{1,0:T(8,128)}, u32[]{:S(2)}) copy-start(f32[128,128]{1,0:T(8,128)} %param.15) | copy-start | bytes 196612
  34.6 21.1 %copy-start.11 = (bf16[16,1024]{1,0:T(8,128)(2,1)S(1)}, bf16[16,1024]{1,0:T(8,128)(2,1)}, u32[]{:S(2)}) copy-start(bf16[16,1024]{1,0:T(8,128)(2,1)} %param.13) | copy-start | bytes 98308
  34.6 21.5 %copy-start.4 = (bf16[16,1024]{1,0:T(8,128)(2,1)S(1)}, bf16[16,1024]{1,0:T(8,128)(2,1)}, u32[]{:S(2)}) copy-start(bf16[16,1024]{1,0:T(8,128)(2,1)} %param.14) | copy-start | bytes 98308
  36.1 21.2 %collective-permute-start.3 = (f32[128,128]{1,0:T(8,128)S(1)}, f32[128,128]{1,0:T(8,128)S(1)}, u32[]{:S(2)}, u32[]{:S(2)}) collective-permute-start(f32[128,128]{1,0:T(8,128)S(1)} %fusion.17), channel_id=1, source_target_pairs={{0,16},{16,0},{32,48},{48,32},{64,80},{80,64},{96,112},{112,96},{1... | collective-permute-start | bytes 196616 | tf_op jit(solution)/shard_map/ppermute | solution.py:111
  39.3 37.1 %copy-start = (bf16[2048,128]{1,0:T(8,128)(2,1)S(1)}, bf16[2048,128]{1,0:T(8,128)(2,1)}, u32[]{:S(2)}) copy-start(bf16[2048,128]{1,0:T(8,128)(2,1)} %shard_map.137) | copy-start | bytes 1572868
  42.5 40.8 %copy-start.2 = (f32[128,128]{1,0:T(8,128)S(1)}, f32[128,128]{1,0:T(8,128)}, u32[]{:S(2)}) copy-start(f32[128,128]{1,0:T(8,128)} %param.16) | copy-start | bytes 196612
  42.5 40.8 %copy-start.7 = (f32[128,128]{1,0:T(8,128)S(1)}, f32[128,128]{1,0:T(8,128)}, u32[]{:S(2)}) copy-start(f32[128,128]{1,0:T(8,128)} %param.21) | copy-start | bytes 196612
  42.5 41.7 %copy-start.9 = (f32[16,1024]{1,0:T(8,128)S(1)}, f32[16,1024]{1,0:T(8,128)}, u32[]{:S(2)}) copy-start(f32[16,1024]{1,0:T(8,128)} %param.19) | copy-start | bytes 196612
  42.6 21.3 %collective-permute-start = (bf16[4,16,1024]{2,1,0:T(8,128)(2,1)S(1)}, bf16[4,16,1024]{2,1,0:T(8,128)(2,1)S(1)}, u32[]{:S(2)}, u32[]{:S(2)}) collective-permute-start(bf16[4,16,1024]{2,1,0:T(8,128)(2,1)S(1)} %bitcast.62), channel_id=1, source_target_pairs={{0,64},{16,80},{32,96},{48,112},{64,0},{80,16},{96,32},{112,48},{1... | collective-permute-start | bytes 393224 | tf_op jit(solution)/shard_map/ppermute | solution.py:127
  55.7 3.2 %collective-permute-start.25 = (bf16[32,1024]{1,0:T(8,128)(2,1)S(1)}, bf16[32,1024]{1,0:T(8,128)(2,1)S(1)}, u32[]{:S(2)}, u32[]{:S(2)}) collective-permute-start(bf16[32,1024]{1,0:T(8,128)(2,1)S(1)} %maximum_select_fusion.5), channel_id=1, source_target_pairs={{0,32},{16,48},{32,0},{48,16},{64,96},{80,112},{96,64},{112,80},{1... | collective-permute-start | bytes 196616 | tf_op jit(solution)/shard_map/ppermute | solution.py:137
  56.1 4.4 %collective-permute-start.13 = (bf16[32,1024]{1,0:T(8,128)(2,1)S(1)}, bf16[32,1024]{1,0:T(8,128)(2,1)S(1)}, u32[]{:S(2)}, u32[]{:S(2)}) collective-permute-start(bf16[32,1024]{1,0:T(8,128)(2,1)S(1)} %maximum_select_fusion.4), channel_id=1, source_target_pairs={{0,32},{16,48},{32,0},{48,16},{64,96},{80,112},{96,64},{112,80},{1... | collective-permute-start | bytes 196616 | tf_op jit(solution)/shard_map/ppermute | solution.py:137
  57.4 4.7 %collective-permute-start.4 = (f32[128,128]{1,0:T(8,128)S(1)}, f32[128,128]{1,0:T(8,128)S(1)}, u32[]{:S(2)}, u32[]{:S(2)}) collective-permute-start(f32[128,128]{1,0:T(8,128)S(1)} %add.117), channel_id=1, source_target_pairs={{0,32},{16,48},{32,0},{48,16},{64,96},{80,112},{96,64},{112,80},{1... | collective-permute-start | bytes 196616 | tf_op jit(solution)/shard_map/ppermute | solution.py:111
  58.9 19.1 %collective-permute-start.26 = (bf16[64,1024]{1,0:T(8,128)(2,1)S(1)}, bf16[64,1024]{1,0:T(8,128)(2,1)S(1)}, u32[]{:S(2)}, u32[]{:S(2)}) collective-permute-start(bf16[64,1024]{1,0:T(8,128)(2,1)S(1)} %maximum_select_fusion.3), channel_id=1, source_target_pairs={{0,64},{16,80},{32,96},{48,112},{64,0},{80,16},{96,32},{112,48},{1... | collective-permute-start | bytes 393224 | tf_op jit(solution)/shard_map/ppermute | solution.py:137
  60.6 15.2 %collective-permute-start.14 = (bf16[64,1024]{1,0:T(8,128)(2,1)S(1)}, bf16[64,1024]{1,0:T(8,128)(2,1)S(1)}, u32[]{:S(2)}, u32[]{:S(2)}) collective-permute-start(bf16[64,1024]{1,0:T(8,128)(2,1)S(1)} %maximum_select_fusion.2), channel_id=1, source_target_pairs={{0,64},{16,80},{32,96},{48,112},{64,0},{80,16},{96,32},{112,48},{1... | collective-permute-start | bytes 393224 | tf_op jit(solution)/shard_map/ppermute | solution.py:137
  62.1 6.0 %collective-permute-start.5 = (f32[128,128]{1,0:T(8,128)S(1)}, f32[128,128]{1,0:T(8,128)S(1)}, u32[]{:S(2)}, u32[]{:S(2)}) collective-permute-start(f32[128,128]{1,0:T(8,128)S(1)} %add.118), channel_id=1, source_target_pairs={{0,64},{16,80},{32,96},{48,112},{64,0},{80,16},{96,32},{112,48},{1... | collective-permute-start | bytes 196616 | tf_op jit(solution)/shard_map/ppermute | solution.py:111
  64.0 5.5 %collective-permute-start.1 = (bf16[2,16,1024]{2,1,0:T(8,128)(2,1)S(1)}, bf16[2,16,1024]{2,1,0:T(8,128)(2,1)S(1)}, u32[]{:S(2)}, u32[]{:S(2)}) collective-permute-start(bf16[2,16,1024]{2,1,0:T(8,128)(2,1)S(1)} %select_convert_fusion.3), channel_id=1, source_target_pairs={{0,32},{16,48},{32,0},{48,16},{64,96},{80,112},{96,64},{112,80},{1... | collective-permute-start | bytes 196616 | tf_op jit(solution)/shard_map/ppermute | solution.py:127
  68.1 2.1 %collective-permute-start.8 = (bf16[128,128]{1,0:T(8,128)(2,1)S(1)}, bf16[128,128]{1,0:T(8,128)(2,1)S(1)}, u32[]{:S(2)}, u32[]{:S(2)}) collective-permute-start(bf16[128,128]{1,0:T(8,128)(2,1)S(1)} %add_convert_fusion), channel_id=1, source_target_pairs={{15,12},{31,28},{47,44},{63,60},{79,76},{95,92},{111,108},{127,124}} | collective-permute-start | bytes 98312 | tf_op jit(solution)/shard_map/ppermute | solution.py:99
  68.8 4.9 %collective-permute-start.7 = (bf16[128,128]{1,0:T(8,128)(2,1)S(1)}, bf16[128,128]{1,0:T(8,128)(2,1)S(1)}, u32[]{:S(2)}, u32[]{:S(2)}) collective-permute-start(bf16[128,128]{1,0:T(8,128)(2,1)S(1)} %add_convert_fusion), channel_id=1, source_target_pairs={{15,13},{31,29},{47,45},{63,61},{79,77},{95,93},{111,109},{127,125}} | collective-permute-start | bytes 98312 | tf_op jit(solution)/shard_map/ppermute | solution.py:99
  69.5 4.3 %collective-permute-start.6 = (bf16[128,128]{1,0:T(8,128)(2,1)S(1)}, bf16[128,128]{1,0:T(8,128)(2,1)S(1)}, u32[]{:S(2)}, u32[]{:S(2)}) collective-permute-start(bf16[128,128]{1,0:T(8,128)(2,1)S(1)} %add_convert_fusion), channel_id=1, source_target_pairs={{15,14},{31,30},{47,46},{63,62},{79,78},{95,94},{111,110},{127,126}} | collective-permute-start | bytes 98312 | tf_op jit(solution)/shard_map/ppermute | solution.py:99
  70.2 14.0 %collective-permute-start.2 = (bf16[1,16,1024]{2,1,0:T(8,128)(2,1)S(1)}, bf16[1,16,1024]{2,1,0:T(8,128)(2,1)S(1)}, u32[]{:S(2)}, u32[]{:S(2)}) collective-permute-start(bf16[1,16,1024]{2,1,0:T(8,128)(2,1)S(1)} %select_convert_fusion.5), channel_id=1, source_target_pairs={{0,16},{16,0},{32,48},{48,32},{64,80},{80,64},{96,112},{112,96},{1... | collective-permute-start | bytes 98312 | tf_op jit(solution)/shard_map/ppermute | solution.py:127
  73.8 9.5 %collective-permute-start.11 = (bf16[128,128]{1,0:T(8,128)(2,1)S(1)}, bf16[128,128]{1,0:T(8,128)(2,1)S(1)}, u32[]{:S(2)}, u32[]{:S(2)}) collective-permute-start(bf16[128,128]{1,0:T(8,128)(2,1)S(1)} %add_select_fusion.1), channel_id=1, source_target_pairs={{15,3},{14,2},{13,1},{12,0},{31,19},{30,18},{29,17},{28,16},{47,35... | collective-permute-start | bytes 98312 | tf_op jit(solution)/shard_map/ppermute | solution.py:99
  75.1 8.2 %collective-permute-start.10 = (bf16[128,128]{1,0:T(8,128)(2,1)S(1)}, bf16[128,128]{1,0:T(8,128)(2,1)S(1)}, u32[]{:S(2)}, u32[]{:S(2)}) collective-permute-start(bf16[128,128]{1,0:T(8,128)(2,1)S(1)} %add_select_fusion.1), channel_id=1, source_target_pairs={{15,7},{14,6},{13,5},{12,4},{31,23},{30,22},{29,21},{28,20},{47,39... | collective-permute-start | bytes 98312 | tf_op jit(solution)/shard_map/ppermute | solution.py:99
  75.8 7.5 %collective-permute-start.9 = (bf16[128,128]{1,0:T(8,128)(2,1)S(1)}, bf16[128,128]{1,0:T(8,128)(2,1)S(1)}, u32[]{:S(2)}, u32[]{:S(2)}) collective-permute-start(bf16[128,128]{1,0:T(8,128)(2,1)S(1)} %add_select_fusion.1), channel_id=1, source_target_pairs={{15,11},{14,10},{13,9},{12,8},{31,27},{30,26},{29,25},{28,24},{47,... | collective-permute-start | bytes 98312 | tf_op jit(solution)/shard_map/ppermute | solution.py:99
  84.1 24.5 %copy-start.5 = (f32[128,128]{1,0:T(8,128)}, f32[128,128]{1,0:T(8,128)S(1)}, u32[]{:S(2)}) copy-start(f32[128,128]{1,0:T(8,128)S(1)} %get-tuple-element.10) | copy-start | bytes 196612
  85.5 23.2 %collective-permute-start.17 = (bf16[16,128]{1,0:T(8,128)(2,1)S(1)}, bf16[16,128]{1,0:T(8,128)(2,1)S(1)}, u32[]{:S(2)}, u32[]{:S(2)}) collective-permute-start(bf16[16,128]{1,0:T(8,128)(2,1)S(1)} %slice.138), channel_id=1, source_target_pairs={{14,13},{30,29},{46,45},{62,61},{78,77},{94,93},{110,109},{126,125}} | collective-permute-start | bytes 12296 | tf_op jit(solution)/shard_map/ppermute | solution.py:99
  86.1 22.5 %collective-permute-start.16 = (bf16[16,128]{1,0:T(8,128)(2,1)S(1)}, bf16[16,128]{1,0:T(8,128)(2,1)S(1)}, u32[]{:S(2)}, u32[]{:S(2)}) collective-permute-start(bf16[16,128]{1,0:T(8,128)(2,1)S(1)} %slice.138), channel_id=1, source_target_pairs={{14,12},{30,28},{46,44},{62,60},{78,76},{94,92},{110,108},{126,124}} | collective-permute-start | bytes 12296 | tf_op jit(solution)/shard_map/ppermute | solution.py:99
  86.8 21.9 %collective-permute-start.15 = (bf16[16,128]{1,0:T(8,128)(2,1)S(1)}, bf16[16,128]{1,0:T(8,128)(2,1)S(1)}, u32[]{:S(2)}, u32[]{:S(2)}) collective-permute-start(bf16[16,128]{1,0:T(8,128)(2,1)S(1)} %slice.138), channel_id=1, source_target_pairs={{14,15},{30,31},{46,47},{62,63},{78,79},{94,95},{110,111},{126,127}} | collective-permute-start | bytes 12296 | tf_op jit(solution)/shard_map/ppermute | solution.py:99
  105.5 5.9 %copy-start.1 = (bf16[2048,128]{1,0:T(8,128)(2,1)S(1)}, bf16[2048,128]{1,0:T(8,128)(2,1)}, u32[]{:S(2)}) copy-start(bf16[2048,128]{1,0:T(8,128)(2,1)} %shard_map.138) | copy-start | bytes 1572868
  108.7 5.6 %collective-permute-start.20 = (bf16[16,128]{1,0:T(8,128)(2,1)S(1)}, bf16[16,128]{1,0:T(8,128)(2,1)S(1)}, u32[]{:S(2)}, u32[]{:S(2)}) collective-permute-start(bf16[16,128]{1,0:T(8,128)(2,1)S(1)} %add_select_fusion.3), channel_id=1, source_target_pairs={{14,2},{15,3},{12,0},{13,1},{30,18},{31,19},{28,16},{29,17},{46,34... | collective-permute-start | bytes 12296 | tf_op jit(solution)/shard_map/ppermute | solution.py:99
  110.0 4.3 %collective-permute-start.19 = (bf16[16,128]{1,0:T(8,128)(2,1)S(1)}, bf16[16,128]{1,0:T(8,128)(2,1)S(1)}, u32[]{:S(2)}, u32[]{:S(2)}) collective-permute-start(bf16[16,128]{1,0:T(8,128)(2,1)S(1)} %add_select_fusion.3), channel_id=1, source_target_pairs={{14,6},{15,7},{12,4},{13,5},{30,22},{31,23},{28,20},{29,21},{46,38... | collective-permute-start | bytes 12296 | tf_op jit(solution)/shard_map/ppermute | solution.py:99
  110.6 3.6 %collective-permute-start.18 = (bf16[16,128]{1,0:T(8,128)(2,1)S(1)}, bf16[16,128]{1,0:T(8,128)(2,1)S(1)}, u32[]{:S(2)}, u32[]{:S(2)}) collective-permute-start(bf16[16,128]{1,0:T(8,128)(2,1)S(1)} %add_select_fusion.3), channel_id=1, source_target_pairs={{14,10},{15,11},{12,8},{13,9},{30,26},{31,27},{28,24},{29,25},{46,... | collective-permute-start | bytes 12296 | tf_op jit(solution)/shard_map/ppermute | solution.py:99
  114.9 7.5 %collective-permute-start.21 = (f32[128,128]{1,0:T(8,128)S(1)}, f32[128,128]{1,0:T(8,128)S(1)}, u32[]{:S(2)}, u32[]{:S(2)}) collective-permute-start(f32[128,128]{1,0:T(8,128)S(1)} %convolution_add_fusion.1), channel_id=1, source_target_pairs={{0,16},{16,0},{32,48},{48,32},{64,80},{80,64},{96,112},{112,96},{1... | collective-permute-start | bytes 196616 | tf_op jit(solution)/shard_map/ppermute | solution.py:111
  121.3 8.8 %collective-permute-start.27 = (bf16[4,16,1024]{2,1,0:T(8,128)(2,1)S(1)}, bf16[4,16,1024]{2,1,0:T(8,128)(2,1)S(1)}, u32[]{:S(2)}, u32[]{:S(2)}) collective-permute-start(bf16[4,16,1024]{2,1,0:T(8,128)(2,1)S(1)} %bitcast.63), channel_id=1, source_target_pairs={{0,64},{16,80},{32,96},{48,112},{64,0},{80,16},{96,32},{112,48},{1... | collective-permute-start | bytes 393224 | tf_op jit(solution)/shard_map/ppermute | solution.py:127
  122.5 6.0 %collective-permute-start.22 = (f32[128,128]{1,0:T(8,128)S(1)}, f32[128,128]{1,0:T(8,128)S(1)}, u32[]{:S(2)}, u32[]{:S(2)}) collective-permute-start(f32[128,128]{1,0:T(8,128)S(1)} %add.131), channel_id=1, source_target_pairs={{0,32},{16,48},{32,0},{48,16},{64,96},{80,112},{96,64},{112,80},{1... | collective-permute-start | bytes 196616 | tf_op jit(solution)/shard_map/ppermute | solution.py:111
  128.5 4.7 %collective-permute-start.23 = (f32[128,128]{1,0:T(8,128)S(1)}, f32[128,128]{1,0:T(8,128)S(1)}, u32[]{:S(2)}, u32[]{:S(2)}) collective-permute-start(f32[128,128]{1,0:T(8,128)S(1)} %add.132), channel_id=1, source_target_pairs={{0,64},{16,80},{32,96},{48,112},{64,0},{80,16},{96,32},{112,48},{1... | collective-permute-start | bytes 196616 | tf_op jit(solution)/shard_map/ppermute | solution.py:111
  130.2 10.0 %collective-permute-start.28 = (bf16[2,16,1024]{2,1,0:T(8,128)(2,1)S(1)}, bf16[2,16,1024]{2,1,0:T(8,128)(2,1)S(1)}, u32[]{:S(2)}, u32[]{:S(2)}) collective-permute-start(bf16[2,16,1024]{2,1,0:T(8,128)(2,1)S(1)} %select_convert_fusion.2), channel_id=1, source_target_pairs={{0,32},{16,48},{32,0},{48,16},{64,96},{80,112},{96,64},{112,80},{1... | collective-permute-start | bytes 196616 | tf_op jit(solution)/shard_map/ppermute | solution.py:127
  133.2 10.1 %collective-permute-start.32 = (bf16[128,128]{1,0:T(8,128)(2,1)S(1)}, bf16[128,128]{1,0:T(8,128)(2,1)S(1)}, u32[]{:S(2)}, u32[]{:S(2)}) collective-permute-start(bf16[128,128]{1,0:T(8,128)(2,1)S(1)} %add.133), channel_id=1, source_target_pairs={{14,13},{30,29},{46,45},{62,61},{78,77},{94,93},{110,109},{126,125}} | collective-permute-start | bytes 98312 | tf_op jit(solution)/shard_map/ppermute | solution.py:99
  133.9 9.4 %collective-permute-start.31 = (bf16[128,128]{1,0:T(8,128)(2,1)S(1)}, bf16[128,128]{1,0:T(8,128)(2,1)S(1)}, u32[]{:S(2)}, u32[]{:S(2)}) collective-permute-start(bf16[128,128]{1,0:T(8,128)(2,1)S(1)} %add.133), channel_id=1, source_target_pairs={{14,12},{30,28},{46,44},{62,60},{78,76},{94,92},{110,108},{126,124}} | collective-permute-start | bytes 98312 | tf_op jit(solution)/shard_map/ppermute | solution.py:99
  134.5 8.7 %collective-permute-start.30 = (bf16[128,128]{1,0:T(8,128)(2,1)S(1)}, bf16[128,128]{1,0:T(8,128)(2,1)S(1)}, u32[]{:S(2)}, u32[]{:S(2)}) collective-permute-start(bf16[128,128]{1,0:T(8,128)(2,1)S(1)} %add.133), channel_id=1, source_target_pairs={{14,15},{30,31},{46,47},{62,63},{78,79},{94,95},{110,111},{126,127}} | collective-permute-start | bytes 98312 | tf_op jit(solution)/shard_map/ppermute | solution.py:99
  140.6 9.6 %collective-permute-start.29 = (bf16[1,16,1024]{2,1,0:T(8,128)(2,1)S(1)}, bf16[1,16,1024]{2,1,0:T(8,128)(2,1)S(1)}, u32[]{:S(2)}, u32[]{:S(2)}) collective-permute-start(bf16[1,16,1024]{2,1,0:T(8,128)(2,1)S(1)} %select_convert_fusion.4), channel_id=1, source_target_pairs={{0,16},{16,0},{32,48},{48,32},{64,80},{80,64},{96,112},{112,96},{1... | collective-permute-start | bytes 98312 | tf_op jit(solution)/shard_map/ppermute | solution.py:127
  143.3 6.0 %copy-start.8 = (f32[128,128]{1,0:T(8,128)S(1)}, f32[128,128]{1,0:T(8,128)}, u32[]{:S(2)}) copy-start(f32[128,128]{1,0:T(8,128)} %param.20) | copy-start | bytes 196612
  143.3 7.0 %copy-start.10 = (f32[16,1024]{1,0:T(8,128)S(1)}, f32[16,1024]{1,0:T(8,128)}, u32[]{:S(2)}) copy-start(f32[16,1024]{1,0:T(8,128)} %param.18) | copy-start | bytes 196612
  143.3 6.0 %collective-permute-start.35 = (bf16[128,128]{1,0:T(8,128)(2,1)S(1)}, bf16[128,128]{1,0:T(8,128)(2,1)S(1)}, u32[]{:S(2)}, u32[]{:S(2)}) collective-permute-start(bf16[128,128]{1,0:T(8,128)(2,1)S(1)} %add_select_fusion), channel_id=1, source_target_pairs={{14,2},{15,3},{12,0},{13,1},{30,18},{31,19},{28,16},{29,17},{46,34... | collective-permute-start | bytes 98312 | tf_op jit(solution)/shard_map/ppermute | solution.py:99
  144.7 4.6 %collective-permute-start.34 = (bf16[128,128]{1,0:T(8,128)(2,1)S(1)}, bf16[128,128]{1,0:T(8,128)(2,1)S(1)}, u32[]{:S(2)}, u32[]{:S(2)}) collective-permute-start(bf16[128,128]{1,0:T(8,128)(2,1)S(1)} %add_select_fusion), channel_id=1, source_target_pairs={{14,6},{15,7},{12,4},{13,5},{30,22},{31,23},{28,20},{29,21},{46,38... | collective-permute-start | bytes 98312 | tf_op jit(solution)/shard_map/ppermute | solution.py:99
  145.4 3.9 %collective-permute-start.33 = (bf16[128,128]{1,0:T(8,128)(2,1)S(1)}, bf16[128,128]{1,0:T(8,128)(2,1)S(1)}, u32[]{:S(2)}, u32[]{:S(2)}) collective-permute-start(bf16[128,128]{1,0:T(8,128)(2,1)S(1)} %add_select_fusion), channel_id=1, source_target_pairs={{14,10},{15,11},{12,8},{13,9},{30,26},{31,27},{28,24},{29,25},{46,... | collective-permute-start | bytes 98312 | tf_op jit(solution)/shard_map/ppermute | solution.py:99
  150.1 1.0 copy-start.6
